TPU v7x, 32 devices: a whole 2x2x4 slice. The times are simulated.
32 devices in a mesh: dp: 16 (over z, y, x), tensor: 2 (over core).
Axes of the slice: x: 2, y: 2, z: 4, core: 2. Of those that a mesh axis runs over, the one named last changes fastest.
Arguments:
- frames: bfloat16 [32, 512, 1536], P('dp', 'tensor'), may hold values from -6 to 6
- text_states: bfloat16 [32, 64, 1536], P('dp'), may hold values from -6 to 6
- norm_gain: bfloat16 [3, 1536], P(None, 'dp'), may hold values from 0.25 to 1.75
- norm_shift: bfloat16 [3, 1536], P(None, 'dp'), may hold values from -2.5 to 2.5
- self_project: bfloat16 [3, 1536, 1536], P(None, 'dp', 'tensor'), may hold values from -0.15625 to 0.15625
- self_output: bfloat16 [1536, 1536], P('tensor', 'dp'), may hold values from -0.625 to 0.625
- cross_query: bfloat16 [1536, 1536], P('dp', 'tensor'), may hold values from -0.15625 to 0.15625
- cross_memory: bfloat16 [2, 1536, 1536], P(None, 'dp', 'tensor'), may hold values from -0.15625 to 0.15625
- cross_output: bfloat16 [1536, 1536], P('tensor', 'dp'), may hold values from -0.4375 to 0.4375
- feed_input: bfloat16 [1536, 6144], P('dp', 'tensor'), may hold values from -0.15625 to 0.15625
- feed_output: bfloat16 [6144, 1536], P('tensor', 'dp'), may hold values from -0.078125 to 0.078125
- upstream: bfloat16 [32, 512, 1536], P('dp', 'tensor'), may hold values from -6 to 6
Outputs:
- layer_out: bfloat16 [32, 512, 1536], P('dp', 'tensor')
- input_grad: float32 [32, 512, 1536], P('dp', 'tensor')
- text_grad: float32 [32, 64, 1536], P('dp')
- gain_grad: float32 [3, 1536], P(None, 'dp')
- shift_grad: float32 [3, 1536], P(None, 'dp')
- self_project_grad: float32 [3, 1536, 1536], P(None, 'dp', 'tensor')
- self_output_grad: float32 [1536, 1536], P('tensor', 'dp')
- cross_query_grad: float32 [1536, 1536], P('dp', 'tensor')
- cross_memory_grad: float32 [2, 1536, 1536], P(None, 'dp', 'tensor')
- cross_output_grad: float32 [1536, 1536], P('tensor', 'dp')
- feed_input_grad: float32 [1536, 6144], P('dp', 'tensor')
- feed_output_grad: float32 [6144, 1536], P('tensor', 'dp')
All inputs are finite; a program needn't handle non-finite values.
Results may differ from a plain program's by a relative error of at most 0.028.
Values may be sent and summed in bfloat16 or wider, within the bound.
No kernel may reach another device: no remote copies, remote signals or barrier semaphores. Data moves between devices by JAX's collectives and lax.ppermute only.
A program may use at most 256 MiB of HBM per device.

v0:
```python
import math

import jax
import jax.numpy as jnp
from jax import lax
from jax.sharding import PartitionSpec as P

HEAD_DIM = 64


epsilon = 1e-05


def norm_rows(values, gain_row, shift_row):
    row_mean = jnp.mean(values, axis=-1, keepdims=True)
    centred = values - row_mean
    row_var = jnp.mean(centred * centred, axis=-1, keepdims=True)
    return centred * lax.rsqrt(row_var + epsilon) * gain_row + shift_row


def norm_back(values, gain_row, shift_row, grad_rows):
    pull_back = jax.vjp(norm_rows, values, gain_row, shift_row)[1]
    return pull_back(grad_rows)


def gelu_exact(values):
    return jax.nn.gelu(values, approximate=False)


def product(left_side, right_side):
    return jnp.dot(left_side, right_side, preferred_element_type=jnp.float32)


def contract_rows(left_side, right_side):
    return lax.dot_general(
        left_side, right_side, (((0,), (0,)), ((), ())), preferred_element_type=jnp.float32
    )


def times_transposed(left_side, right_side):
    return lax.dot_general(
        left_side, right_side, (((1,), (1,)), ((), ())), preferred_element_type=jnp.float32
    )


def split_heads(matrix):
    return matrix.reshape(matrix.shape[0], matrix.shape[1] // HEAD_DIM, HEAD_DIM)


def spread_rows(row_block):
    return lax.all_gather(row_block, "tensor", axis=0, tiled=True)


def spread_grads(row_block):
    return lax.all_gather(row_block, "tensor", axis=0, tiled=True)


def branch_sum(left_side, weight):
    return lax.psum_scatter(
        product(left_side, weight).astype(jnp.bfloat16), "tensor", scatter_dimension=0, tiled=True
    ).astype(jnp.float32)


def input_sum(grad_pairs):
    result_rows = None
    for grad_part, weight in grad_pairs:
        piece_rows = times_transposed(grad_part, weight)
        result_rows = piece_rows if result_rows is None else result_rows + piece_rows
    return lax.psum_scatter(
        result_rows.astype(jnp.bfloat16), "tensor", scatter_dimension=0, tiled=True
    ).astype(jnp.float32)


def causal_mask(begin_row, block_size, end_row):
    row_place = begin_row + jnp.arange(block_size, dtype=jnp.int32)
    col_place = jnp.arange(end_row, dtype=jnp.int32)
    return col_place[None, :] <= row_place[:, None]


def block_scores(query_heads, key_heads, begin_row, end_row, scale):
    scores = (
        jnp.einsum("qhd,khd->hqk", query_heads, key_heads, preferred_element_type=jnp.float32)
        * scale
    )
    allowed = causal_mask(begin_row, end_row - begin_row, end_row)
    return jnp.where(allowed[None], scores, -1e30)


def causal_forward(queries, keys, values):
    length = queries.shape[0]
    block_size = min(512, length)
    scale = 1.0 / math.sqrt(HEAD_DIM)
    query_heads = split_heads(queries)
    key_heads = split_heads(keys)
    value_heads = split_heads(values)
    scores = block_scores(query_heads, key_heads, 0, block_size, scale)
    row_top = jnp.max(scores, axis=-1, keepdims=True)
    exp_terms = jnp.exp(scores - row_top)
    row_total = jnp.sum(exp_terms, axis=-1, keepdims=True)
    chances = (exp_terms / row_total).astype(jnp.bfloat16)
    outputs = jnp.einsum("hqk,khd->qhd", chances, value_heads, preferred_element_type=jnp.float32)
    log_totals = row_top[..., 0] + jnp.log(row_total[..., 0])
    return (outputs.reshape(length, -1), log_totals)


def causal_backward(queries, keys, values, log_totals, out_grad):
    length = queries.shape[0]
    block_size = min(512, length)
    scale = 1.0 / math.sqrt(HEAD_DIM)
    query_heads = split_heads(queries)
    key_heads = split_heads(keys)
    value_heads = split_heads(values)
    grad_heads = split_heads(out_grad)
    key_grad = jnp.zeros(key_heads.shape, jnp.float32)
    value_grad = jnp.zeros(value_heads.shape, jnp.float32)
    scores = block_scores(query_heads, key_heads, 0, block_size, scale)
    chances = jnp.exp(scores - log_totals[:, 0:block_size, None])
    chance_grad = jnp.einsum(
        "qhd,khd->hqk", grad_heads, value_heads, preferred_element_type=jnp.float32
    )
    row_dot = jnp.sum(chances * chance_grad, axis=-1, keepdims=True)
    score_grad = (chances * (chance_grad - row_dot)).astype(jnp.bfloat16)
    value_grad = value_grad.at[:block_size].add(
        jnp.einsum(
            "hqk,qhd->khd",
            chances.astype(jnp.bfloat16),
            grad_heads,
            preferred_element_type=jnp.float32,
        )
    )
    query_grads = (
        jnp.einsum("hqk,khd->qhd", score_grad, key_heads, preferred_element_type=jnp.float32)
        * scale
    )
    key_grad = key_grad.at[:block_size].add(
        jnp.einsum("hqk,qhd->khd", score_grad, query_heads, preferred_element_type=jnp.float32)
        * scale
    )
    query_grad = query_grads.reshape(length, -1).astype(jnp.bfloat16)
    return (
        query_grad,
        key_grad.reshape(length, -1).astype(jnp.bfloat16),
        value_grad.reshape(length, -1).astype(jnp.bfloat16),
    )


def cross_forward(queries, keys, values):
    scale = 1.0 / math.sqrt(HEAD_DIM)
    scores = (
        jnp.einsum(
            "qhd,khd->hqk",
            split_heads(queries),
            split_heads(keys),
            preferred_element_type=jnp.float32,
        )
        * scale
    )
    chances = jax.nn.softmax(scores, axis=-1)
    attended = jnp.einsum(
        "hqk,khd->qhd",
        chances.astype(jnp.bfloat16),
        split_heads(values),
        preferred_element_type=jnp.float32,
    )
    return (attended.reshape(queries.shape[0], -1), chances)


def cross_backward(queries, keys, values, chances, out_grad):
    scale = 1.0 / math.sqrt(HEAD_DIM)
    grad_heads = split_heads(out_grad)
    key_heads = split_heads(keys)
    chance_grad = jnp.einsum(
        "qhd,khd->hqk", grad_heads, split_heads(values), preferred_element_type=jnp.float32
    )
    row_dot = jnp.sum(chances * chance_grad, axis=-1, keepdims=True)
    score_grad = (chances * (chance_grad - row_dot)).astype(jnp.bfloat16)
    value_grad = jnp.einsum(
        "hqk,qhd->khd", chances.astype(jnp.bfloat16), grad_heads, preferred_element_type=jnp.float32
    )
    query_grad = (
        jnp.einsum("hqk,khd->qhd", score_grad, key_heads, preferred_element_type=jnp.float32)
        * scale
    )
    key_grad = (
        jnp.einsum(
            "hqk,qhd->khd", score_grad, split_heads(queries), preferred_element_type=jnp.float32
        )
        * scale
    )
    return (
        query_grad.reshape(queries.shape[0], -1).astype(jnp.bfloat16),
        key_grad.reshape(keys.shape[0], -1).astype(jnp.bfloat16),
        value_grad.reshape(keys.shape[0], -1).astype(jnp.bfloat16),
    )


def per_device(
    frames,
    text_states,
    norm_gain,
    norm_shift,
    self_project,
    self_output,
    cross_query,
    cross_memory,
    cross_output,
    feed_input,
    feed_output,
    upstream,
):
    layer_outs = []
    input_grads = []
    text_grads = []
    grad_totals = None
    for clip_index in range(frames.shape[0]):
        forward_set = (
            lax.all_gather(norm_gain, "dp", axis=1, tiled=True),
            lax.all_gather(norm_shift, "dp", axis=1, tiled=True),
            lax.all_gather(self_project, "dp", axis=1, tiled=True),
            lax.all_gather(self_output, "dp", axis=1, tiled=True),
            lax.all_gather(cross_query, "dp", axis=0, tiled=True),
            lax.all_gather(cross_memory, "dp", axis=1, tiled=True),
            lax.all_gather(cross_output, "dp", axis=1, tiled=True),
            lax.all_gather(feed_input, "dp", axis=0, tiled=True),
            lax.all_gather(feed_output, "dp", axis=1, tiled=True),
        )
        gain_rows = forward_set[0].astype(jnp.float32)
        shift_rows = forward_set[1].astype(jnp.float32)
        frame_rows = frames[clip_index].astype(jnp.float32)
        texts = text_states[clip_index]
        normed_one = spread_rows(
            norm_rows(frame_rows, gain_rows[0], shift_rows[0]).astype(jnp.bfloat16)
        )
        queries = product(normed_one, forward_set[2][0]).astype(jnp.bfloat16)
        keys_self = product(normed_one, forward_set[2][1]).astype(jnp.bfloat16)
        values_self = product(normed_one, forward_set[2][2]).astype(jnp.bfloat16)
        attended, log_totals = causal_forward(queries, keys_self, values_self)
        attended = attended.astype(jnp.bfloat16)
        after_self = frame_rows + branch_sum(attended, forward_set[3])
        normed_two = spread_rows(
            norm_rows(after_self, gain_rows[1], shift_rows[1]).astype(jnp.bfloat16)
        )
        cross_queries = product(normed_two, forward_set[4]).astype(jnp.bfloat16)
        cross_keys = product(texts, forward_set[5][0]).astype(jnp.bfloat16)
        cross_values = product(texts, forward_set[5][1]).astype(jnp.bfloat16)
        cross_att, cross_chances = cross_forward(cross_queries, cross_keys, cross_values)
        cross_att = cross_att.astype(jnp.bfloat16)
        after_cross = after_self + branch_sum(cross_att, forward_set[6])
        normed_three = spread_rows(
            norm_rows(after_cross, gain_rows[2], shift_rows[2]).astype(jnp.bfloat16)
        )
        pre_act = product(normed_three, forward_set[7])
        hidden = gelu_exact(pre_act).astype(jnp.bfloat16)
        layer_out = after_cross + branch_sum(hidden, forward_set[8])
        layer_outs.append(layer_out.astype(jnp.bfloat16))
        backward_set = (
            lax.all_gather(norm_gain, "dp", axis=1, tiled=True),
            lax.all_gather(norm_shift, "dp", axis=1, tiled=True),
            lax.all_gather(self_project, "dp", axis=1, tiled=True),
            lax.all_gather(self_output, "dp", axis=1, tiled=True),
            lax.all_gather(cross_query, "dp", axis=0, tiled=True),
            lax.all_gather(cross_memory, "dp", axis=1, tiled=True),
            lax.all_gather(cross_output, "dp", axis=1, tiled=True),
            lax.all_gather(feed_input, "dp", axis=0, tiled=True),
            lax.all_gather(feed_output, "dp", axis=1, tiled=True),
        )
        back_gain = backward_set[0].astype(jnp.float32)
        back_shift = backward_set[1].astype(jnp.float32)
        out_grad = upstream[clip_index]
        feed_grad = spread_grads(out_grad)
        grad_feed_out = contract_rows(hidden, feed_grad)
        hidden_grad = times_transposed(feed_grad, backward_set[8])
        pre_grad = jax.vjp(gelu_exact, pre_act)[1](hidden_grad)[0].astype(jnp.bfloat16)
        grad_feed_in = contract_rows(normed_three, pre_grad)
        norm_grad_three = input_sum(((pre_grad, backward_set[7]),))
        cross_grad_in, gain_three, shift_three = norm_back(
            after_cross, back_gain[2], back_shift[2], norm_grad_three
        )
        cross_res_grad = out_grad.astype(jnp.float32) + cross_grad_in
        cross_out_grad = spread_grads(cross_res_grad.astype(jnp.bfloat16))
        grad_cross_out = contract_rows(cross_att, cross_out_grad)
        cross_att_grad = times_transposed(cross_out_grad, backward_set[6]).astype(jnp.bfloat16)
        cquery_grad, ckey_grad, cvalue_grad = cross_backward(
            cross_queries, cross_keys, cross_values, cross_chances, cross_att_grad
        )
        grad_cross_query = contract_rows(normed_two, cquery_grad)
        grad_memory = jnp.stack(
            [contract_rows(texts, ckey_grad), contract_rows(texts, cvalue_grad)]
        )
        text_part = times_transposed(ckey_grad, backward_set[5][0]) + times_transposed(
            cvalue_grad, backward_set[5][1]
        )
        text_grads.append(lax.psum(text_part.astype(jnp.bfloat16), "tensor").astype(jnp.float32))
        norm_grad_two = input_sum(((cquery_grad, backward_set[4]),))
        self_grad_in, gain_two, shift_two = norm_back(
            after_self, back_gain[1], back_shift[1], norm_grad_two
        )
        self_res_grad = cross_res_grad + self_grad_in
        self_out_grad = spread_grads(self_res_grad.astype(jnp.bfloat16))
        grad_self_out = contract_rows(attended, self_out_grad)
        attended_grad = times_transposed(self_out_grad, backward_set[3]).astype(jnp.bfloat16)
        query_grad, key_grad, value_grad = causal_backward(
            queries, keys_self, values_self, log_totals, attended_grad
        )
        grad_project = jnp.stack(
            [
                contract_rows(normed_one, query_grad),
                contract_rows(normed_one, key_grad),
                contract_rows(normed_one, value_grad),
            ]
        )
        norm_grad_one = input_sum(
            (
                (query_grad, backward_set[2][0]),
                (key_grad, backward_set[2][1]),
                (value_grad, backward_set[2][2]),
            )
        )
        frame_grad_in, gain_one, shift_one = norm_back(
            frame_rows, back_gain[0], back_shift[0], norm_grad_one
        )
        input_grads.append(self_res_grad + frame_grad_in)
        clip_grads = (
            jnp.stack([gain_one, gain_two, gain_three]),
            jnp.stack([shift_one, shift_two, shift_three]),
            grad_project,
            grad_self_out,
            grad_cross_query,
            grad_memory,
            grad_cross_out,
            grad_feed_in,
            grad_feed_out,
        )
        grad_totals = (
            clip_grads if grad_totals is None else jax.tree.map(jnp.add, grad_totals, clip_grads)
        )
    gain_sum, shift_sum = (
        lax.psum(grad_totals[0].astype(jnp.bfloat16), "tensor").astype(jnp.float32),
        lax.psum(grad_totals[1].astype(jnp.bfloat16), "tensor").astype(jnp.float32),
    )
    weight_grads = (
        lax.psum_scatter(
            gain_sum.astype(jnp.bfloat16), "dp", scatter_dimension=1, tiled=True
        ).astype(jnp.float32),
        lax.psum_scatter(
            shift_sum.astype(jnp.bfloat16), "dp", scatter_dimension=1, tiled=True
        ).astype(jnp.float32),
        lax.psum_scatter(
            grad_totals[2].astype(jnp.bfloat16), "dp", scatter_dimension=1, tiled=True
        ).astype(jnp.float32),
        lax.psum_scatter(
            grad_totals[3].astype(jnp.bfloat16), "dp", scatter_dimension=1, tiled=True
        ).astype(jnp.float32),
        lax.psum_scatter(
            grad_totals[4].astype(jnp.bfloat16), "dp", scatter_dimension=0, tiled=True
        ).astype(jnp.float32),
        lax.psum_scatter(
            grad_totals[5].astype(jnp.bfloat16), "dp", scatter_dimension=1, tiled=True
        ).astype(jnp.float32),
        lax.psum_scatter(
            grad_totals[6].astype(jnp.bfloat16), "dp", scatter_dimension=1, tiled=True
        ).astype(jnp.float32),
        lax.psum_scatter(
            grad_totals[7].astype(jnp.bfloat16), "dp", scatter_dimension=0, tiled=True
        ).astype(jnp.float32),
        lax.psum_scatter(
            grad_totals[8].astype(jnp.bfloat16), "dp", scatter_dimension=1, tiled=True
        ).astype(jnp.float32),
    )
    return (
        jnp.stack(layer_outs),
        jnp.stack(input_grads),
        jnp.stack(text_grads),
        weight_grads[0],
        weight_grads[1],
        weight_grads[2],
        weight_grads[3],
        weight_grads[4],
        weight_grads[5],
        weight_grads[6],
        weight_grads[7],
        weight_grads[8],
    )


def solution(mesh):
    in_specs = (
        P("dp", "tensor", None),
        P("dp", None, None),
        P(None, "dp"),
        P(None, "dp"),
        P(None, "dp", "tensor"),
        P("tensor", "dp"),
        P("dp", "tensor"),
        P(None, "dp", "tensor"),
        P("tensor", "dp"),
        P("dp", "tensor"),
        P("tensor", "dp"),
        P("dp", "tensor", None),
    )
    out_specs = (
        P("dp", "tensor", None),
        P("dp", "tensor", None),
        P("dp", None, None),
        P(None, "dp"),
        P(None, "dp"),
        P(None, "dp", "tensor"),
        P("tensor", "dp"),
        P("dp", "tensor"),
        P(None, "dp", "tensor"),
        P("tensor", "dp"),
        P("dp", "tensor"),
        P("tensor", "dp"),
    )
    return jax.shard_map(
        per_device, mesh=mesh, in_specs=in_specs, out_specs=out_specs, check_vma=False
    )
```

profile of v0, /device:TPU:0, one launch (start us, length us, event | category | flops | bytes accessed | tf_op | source)
XLA Modules:
  0.0 2552.1 jit_solution(1254650275084944020)
XLA Ops:
  11.1 42.5 %all-gather.2 = bf16[16,96,3]{1,2,0:T(4,128)(2,1)S(1)} all-gather(bf16[1,96,3]{1,2,0:T(4,128)(2,1)S(1)} %bitcast.511), channel_id=1, replica_groups=mesh['dp'=16,'tensor'=2] {'dp'}, dimensions={0}, use_global_device_ids=true | all-gather | bytes 9792 | tf_op jit(solution)/shard_map/all_gather | solution.py:217
  53.8 35.5 %all-gather.3 = bf16[16,96,3]{1,2,0:T(4,128)(2,1)S(1)} all-gather(bf16[1,96,3]{1,2,0:T(4,128)(2,1)S(1)} %bitcast.512), channel_id=1, replica_groups=mesh['dp'=16,'tensor'=2] {'dp'}, dimensions={0}, use_global_device_ids=true | all-gather | bytes 9792 | tf_op jit(solution)/shard_map/all_gather | solution.py:218
  93.0 6.1 all-gather.24.cloned.1.call-done
  99.1 104.5 %all-gather.26.cloned.1.call-done = bf16[3,1536,768]{2,1,0:T(8,128)(2,1)} async-done(((bf16[3,96,768]{2,1,0:T(8,128)(2,1)}), bf16[3,1536,768]{2,1,0:T(8,128)(2,1)}) %all-gather.26.cloned.1.call-update) | async-done | bytes 7077904 | tf_op jit(solution)/shard_map/all_gather | solution.py:219
  207.4 4.7 fusion.109
  213.5 4.7 fusion.111
  230.8 36.1 %all-gather.28.cloned.1.call-done = bf16[768,1536]{0,1:T(8,128)(2,1)} async-done(((bf16[768,96]{0,1:T(8,128)(2,1)}), bf16[768,1536]{0,1:T(8,128)(2,1)}) %all-gather.28.cloned.1.call-update) | async-done | bytes 2359312 | tf_op jit(solution)/shard_map/all_gather | solution.py:220
  266.9 4.2 convolution_convert_fusion.5
  271.6 7.2 reduce-scatter.25.cloned.1.call-done
  281.8 11.2 all-gather.44.cloned.1.call-done
  296.8 4.7 fusion.110
  302.9 4.7 fusion.112
  325.4 8.6 reduce-scatter.31.cloned.1.call-done
  340.2 77.6 %all-gather.30.cloned.1.call-done = bf16[2,1536,768]{2,1,0:T(8,128)(2,1)} async-done(((bf16[2,96,768]{2,1,0:T(8,128)(2,1)}), bf16[2,1536,768]{2,1,0:T(8,128)(2,1)}) %all-gather.30.cloned.1.call-update) | async-done | bytes 4718608 | tf_op jit(solution)/shard_map/all_gather | solution.py:222
  424.9 56.5 %all-gather.34.cloned.1.call-done = bf16[1536,768]{1,0:T(8,128)(2,1)} async-done(((bf16[96,768]{1,0:T(8,128)(2,1)}), bf16[1536,768]{1,0:T(8,128)(2,1)}) %all-gather.34.cloned.1.call-update) | async-done | bytes 2359312 | tf_op jit(solution)/shard_map/all_gather | solution.py:221
  481.4 10.3 all-gather.32.cloned.1.call-done
  491.8 4.4 convolution_convert_fusion.15
  504.2 53.6 %all-gather.36.cloned.1.call-done = bf16[768,1536]{0,1:T(8,128)(2,1)} async-done(((bf16[768,96]{0,1:T(8,128)(2,1)}), bf16[768,1536]{0,1:T(8,128)(2,1)}) %all-gather.36.cloned.1.call-update) | async-done | bytes 2359312 | tf_op jit(solution)/shard_map/all_gather | solution.py:223
  557.8 4.5 convolution_convert_fusion.4
  569.6 4.4 convolution_convert_fusion.14
  585.9 8.0 reduce-scatter.33.cloned.1.call-done
  602.1 117.4 %all-gather.40.cloned.1.call-done = bf16[1536,3072]{1,0:T(8,128)(2,1)} async-done(((bf16[96,3072]{1,0:T(8,128)(2,1)}), bf16[1536,3072]{1,0:T(8,128)(2,1)}) %all-gather.40.cloned.1.call-update) | async-done | bytes 9437200 | tf_op jit(solution)/shard_map/all_gather | solution.py:224
  719.5 10.0 all-gather.48.cloned.1.call-done
  729.5 21.6 multiply_convert_fusion.2
  751.1 116.4 %all-gather.42.cloned.1.call-done = bf16[3072,1536]{0,1:T(8,128)(2,1)} async-done(((bf16[3072,96]{0,1:T(8,128)(2,1)}), bf16[3072,1536]{0,1:T(8,128)(2,1)}) %all-gather.42.cloned.1.call-update) | async-done | bytes 9437200 | tf_op jit(solution)/shard_map/all_gather | solution.py:225
  867.5 12.3 add_convert_fusion.2
  881.6 6.3 convolution_convert_fusion.6
  888.3 21.8 multiply_convert_fusion.3
  910.1 12.1 add_convert_fusion.3
  923.9 8.9 convolution_convert_fusion.7
  933.0 9.0 convolution_convert_fusion.8
  942.3 10.4 convolution_convert_fusion.9
  957.3 8.6 reduce-scatter.29.cloned.1.call-done
  972.6 10.4 all-gather.54.cloned.1.call-done
  1007.9 12.4 reduce-scatter.39.cloned.1.call-done
  1028.4 4.1 fusion.186
  1032.7 6.9 all-gather.52.cloned.1.call-done
  1044.3 7.9 all-gather.56.cloned.1.call-done
  1052.1 4.4 convolution_convert_fusion.10
  1058.0 6.4 fusion.196
  1064.4 7.6 fusion.116
  1071.9 20.1 multiply_reduce_fusion.1
  1092.0 23.5 multiply_convert_fusion.1
  1115.5 4.9 multiply_convert_fusion.4
  1129.6 3.9 multiply_convert_fusion.9
  1138.2 5.0 multiply_convert_fusion.8
  1150.8 4.4 fusion.30
  1174.8 9.5 fusion.7
  1184.3 12.5 copy.158
  1211.6 5.0 fusion.197
  1223.0 6.0 add_convert_fusion.6
  1229.2 11.3 fusion.200
  1240.6 11.4 add_convert_fusion.1
  1252.1 11.6 fusion.85
  1263.7 11.7 add_convert_fusion
  1296.7 83.6 %all-reduce.6.cloned.1.call-done = bf16[2,1536,768]{2,0,1:T(2,128)(2,1)} async-done(((bf16[2,1536,768]{2,0,1:T(2,128)(2,1)}), bf16[2,1536,768]{2,0,1:T(2,128)(2,1)}) %all-reduce.6.cloned.1.call-update) | async-done | bytes 4718608
  1382.3 131.5 %reduce-scatter.53.cloned.1.call-done = bf16[96,768]{1,0:T(8,128)(2,1)} async-done(((bf16[1536,768]{1,0:T(8,128)(2,1)}), bf16[96,768]{1,0:T(8,128)(2,1)}) %reduce-scatter.53.cloned.1.call-update) | async-done | bytes 147472 | tf_op jit(solution)/shard_map/reduce_scatter | solution.py:354
  1515.4 131.8 %reduce-scatter.55.cloned.1.call-done = bf16[768,96]{0,1:T(8,128)(2,1)} async-done(((bf16[768,1536]{0,1:T(8,128)(2,1)}), bf16[768,96]{0,1:T(8,128)(2,1)}) %reduce-scatter.55.cloned.1.call-update) | async-done | bytes 147472 | tf_op jit(solution)/shard_map/reduce_scatter | solution.py:360
  1653.3 120.4 %reduce-scatter.61.cloned.1.call-done = bf16[96,3]{1,0:T(8,128)(2,1)} async-done(((bf16[1536,3]{1,0:T(8,128)(2,1)}), bf16[96,3]{1,0:T(8,128)(2,1)}) %reduce-scatter.61.cloned.1.call-update) | async-done | bytes 592
  1774.6 126.0 %reduce-scatter.63.cloned.1.call-done = bf16[96,3]{1,0:T(8,128)(2,1)} async-done(((bf16[1536,3]{1,0:T(8,128)(2,1)}), bf16[96,3]{1,0:T(8,128)(2,1)}) %reduce-scatter.63.cloned.1.call-update) | async-done | bytes 592
  1905.0 129.1 %reduce-scatter.51.cloned.1.call-done = bf16[768,96]{0,1:T(8,128)(2,1)} async-done(((bf16[768,1536]{0,1:T(8,128)(2,1)}), bf16[768,96]{0,1:T(8,128)(2,1)}) %reduce-scatter.51.cloned.1.call-update) | async-done | bytes 147472 | tf_op jit(solution)/shard_map/reduce_scatter | solution.py:351
  2035.7 174.3 %reduce-scatter.57.cloned.1.call-done = bf16[96,3072]{1,0:T(8,128)(2,1)} async-done(((bf16[1536,3072]{1,0:T(8,128)(2,1)}), bf16[96,3072]{1,0:T(8,128)(2,1)}) %reduce-scatter.57.cloned.1.call-update) | async-done | bytes 589840 | tf_op jit(solution)/shard_map/reduce_scatter | solution.py:363
  2212.2 173.9 %reduce-scatter.59.cloned.1.call-done = bf16[3072,96]{0,1:T(8,128)(2,1)} async-done(((bf16[3072,1536]{0,1:T(8,128)(2,1)}), bf16[3072,96]{0,1:T(8,128)(2,1)}) %reduce-scatter.59.cloned.1.call-update) | async-done | bytes 589840 | tf_op jit(solution)/shard_map/reduce_scatter | solution.py:366
  2388.4 154.7 %reduce-scatter.49.cloned.1.call-done = bf16[3,96,768]{2,1,0:T(8,128)(2,1)} async-done(((bf16[3,1536,768]{2,1,0:T(8,128)(2,1)}), bf16[3,96,768]{2,1,0:T(8,128)(2,1)}) %reduce-scatter.49.cloned.1.call-update) | async-done | bytes 442384 | tf_op jit(solution)/shard_map/reduce_scatter | solution.py:348
  (598 shorter events, 259.3 us)
Async XLA Ops:
  7.2 82.9 %copy-start = (bf16[2,256,1536]{2,1,0:T(8,128)(2,1)S(1)}, bf16[2,256,1536]{2,1,0:T(8,128)(2,1)}, u32[]{:S(2)}) copy-start(bf16[2,256,1536]{2,1,0:T(8,128)(2,1)} %param.28) | copy-start | bytes 4718596
  7.2 46.6 %copy-start.141 = (bf16[3,96]{1,0:T(4,128)(2,1)S(1)}, bf16[3,96]{1,0:T(4,128)(2,1)}, u32[]{:S(2)}) copy-start(bf16[3,96]{1,0:T(4,128)(2,1)} %param.31) | copy-start | bytes 1732
  7.2 91.8 %all-gather.24.cloned.1.call-start = ((), (), s32[]{:S(2)}) async-start(), calls=%async_computation.20 | async-start | bytes 2359296 | tf_op jit(solution)/shard_map/all_gather | solution.py:51
  9.0 198.1 %copy-start.98 = (f32[256]{0:T(256)}, f32[256]{0:T(256)S(1)}, u32[]{:S(2)}) copy-start(f32[256]{0:T(256)S(1)} %broadcast_multiply_fusion.5) | copy-start | bytes 3076
  10.5 196.6 %copy-start.116 = (f32[256]{0:T(256)}, f32[256]{0:T(256)S(1)}, u32[]{:S(2)}) copy-start(f32[256]{0:T(256)S(1)} %fusion.165) | copy-start | bytes 3076
  53.7 226.7 %copy-start.75 = (f32[1536]{0:T(1024)}, f32[1536]{0:T(1024)S(1)}, u32[]{:S(2)}) copy-start(f32[1536]{0:T(1024)S(1)} %get-tuple-element.176) | copy-start | bytes 18436
  53.8 283.1 %copy-start.81 = (f32[1536]{0:T(1024)}, f32[1536]{0:T(1024)S(1)}, u32[]{:S(2)}) copy-start(f32[1536]{0:T(1024)S(1)} %get-tuple-element.175) | copy-start | bytes 18436
  53.8 543.2 %copy-start.94 = (f32[1536]{0:T(1024)}, f32[1536]{0:T(1024)S(1)}, u32[]{:S(2)}) copy-start(f32[1536]{0:T(1024)S(1)} %get-tuple-element.174) | copy-start | bytes 18436
  91.3 112.2 %all-gather.26.cloned.1.call-start = ((), (), s32[]{:S(2)}) async-start(), calls=%async_computation.21 | async-start | bytes 7520256 | tf_op jit(solution)/shard_map/all_gather | solution.py:219
  92.1 174.9 %all-gather.28.cloned.1.call-start = ((), (), s32[]{:S(2)}) async-start(), calls=%async_computation.22 | async-start | bytes 2506752 | tf_op jit(solution)/shard_map/all_gather | solution.py:220
  92.8 186.0 %reduce-scatter.25.cloned.1.call-start = ((), (), s32[]{:S(2)}) async-start(), calls=%async_computation.23 | async-start | bytes 2359296 | tf_op jit(solution)/shard_map/reduce_scatter | solution.py:59
  92.9 221.6 %copy-start.19 = (pred[512,512]{0,1:T(8,128)(4,1)}, pred[512,512]{0,1:T(8,128)(4,1)S(1)}, u32[]{:S(2)}) copy-start(pred[512,512]{0,1:T(8,128)(4,1)S(1)} %iota_compare_fusion) | copy-start | bytes 786436
  230.8 40.4 %copy-start.151 = (bf16[12,64,512]{2,1,0:T(8,128)(2,1)}, bf16[12,64,512]{2,1,0:T(8,128)(2,1)S(1)}, u32[]{:S(2)}) copy-start(bf16[12,64,512]{2,1,0:T(8,128)(2,1)S(1)} %fusion.120) | copy-start | bytes 2359300
  271.2 21.7 all-gather.44.cloned.1.call-start
  280.4 16.1 copy-start.128
  281.7 52.3 %reduce-scatter.31.cloned.1.call-start = ((), (), s32[]{:S(2)}) async-start(), calls=%async_computation.34 | async-start | bytes 2359296 | tf_op jit(solution)/shard_map/reduce_scatter | solution.py:59
  323.7 94.1 %all-gather.30.cloned.1.call-start = ((), (), s32[]{:S(2)}) async-start(), calls=%async_computation.24 | async-start | bytes 5013504 | tf_op jit(solution)/shard_map/all_gather | solution.py:222
  324.4 157.0 %all-gather.34.cloned.1.call-start = ((), (), s32[]{:S(2)}) async-start(), calls=%async_computation.26 | async-start | bytes 2506752 | tf_op jit(solution)/shard_map/all_gather | solution.py:221
  325.2 166.6 %all-gather.32.cloned.1.call-start = ((), (), s32[]{:S(2)}) async-start(), calls=%async_computation.25 | async-start | bytes 2359296 | tf_op jit(solution)/shard_map/all_gather | solution.py:51
  336.8 80.9 %copy-start.64 = (bf16[2,64,1536]{2,1,0:T(8,128)(2,1)S(1)}, bf16[2,64,1536]{2,1,0:T(8,128)(2,1)}, u32[]{:S(2)}) copy-start(bf16[2,64,1536]{2,1,0:T(8,128)(2,1)} %param.29) | copy-start | bytes 1179652
  339.5 218.3 %all-gather.36.cloned.1.call-start = ((), (), s32[]{:S(2)}) async-start(), calls=%async_computation.27 | async-start | bytes 2506752 | tf_op jit(solution)/shard_map/all_gather | solution.py:223
  340.1 229.5 %all-gather.46.cloned.1.call-start = ((), (), s32[]{:S(2)}) async-start(), calls=%async_computation.35 | async-start | bytes 2359296 | tf_op jit(solution)/shard_map/all_gather | solution.py:51
  421.7 76.8 %copy-start.60 = (bf16[64,768]{0,1:T(8,128)(2,1)}, bf16[64,768]{0,1:T(8,128)(2,1)S(1)}, u32[]{:S(2)}) copy-start(bf16[64,768]{0,1:T(8,128)(2,1)S(1)} %copy.172) | copy-start | bytes 294916
  421.7 164.2 %reduce-scatter.27.cloned.1.call-start = ((), (), s32[]{:S(2)}) async-start(), calls=%async_computation.28 | async-start | bytes 2359296 | tf_op jit(solution)/shard_map/reduce_scatter | solution.py:59
  562.4 31.4 %reduce-scatter.33.cloned.1.call-start = ((), (), s32[]{:S(2)}) async-start(), calls=%async_computation.36 | async-start | bytes 2359296 | tf_op jit(solution)/shard_map/reduce_scatter | solution.py:59
  585.0 134.5 %all-gather.40.cloned.1.call-start = ((), (), s32[]{:S(2)}) async-start(), calls=%async_computation.30 | async-start | bytes 10027008 | tf_op jit(solution)/shard_map/all_gather | solution.py:224
  585.6 143.9 %all-gather.48.cloned.1.call-start = ((), (), s32[]{:S(2)}) async-start(), calls=%async_computation.37 | async-start | bytes 2359296 | tf_op jit(solution)/shard_map/all_gather | solution.py:51
  598.8 152.3 %all-gather.60.cloned.1.call-start = ((), (), s32[]{:S(2)}) async-start(), calls=%async_computation.56 | async-start | bytes 2359296 | tf_op jit(solution)/shard_map/all_gather | solution.py:55
  600.1 267.4 %all-gather.42.cloned.1.call-start = ((), (), s32[]{:S(2)}) async-start(), calls=%async_computation.31 | async-start | bytes 10027008 | tf_op jit(solution)/shard_map/all_gather | solution.py:225
  600.7 287.6 %all-gather.38.cloned.1.call-start = ((), (), s32[]{:S(2)}) async-start(), calls=%async_computation.29 | async-start | bytes 2359296 | tf_op jit(solution)/shard_map/all_gather | solution.py:51
  601.3 308.8 %all-gather.58.cloned.1.call-start = ((), (), s32[]{:S(2)}) async-start(), calls=%async_computation.55 | async-start | bytes 2359296 | tf_op jit(solution)/shard_map/all_gather | solution.py:55
  602.1 350.7 %reduce-scatter.43.cloned.1.call-start = ((), (), s32[]{:S(2)}) async-start(), calls=%async_computation.44 | async-start | bytes 2359296 | tf_op jit(solution)/shard_map/reduce_scatter | solution.py:69
  751.1 181.9 %copy-start.160 = (bf16[512,3072]{1,0:T(8,128)(2,1)}, bf16[512,3072]{1,0:T(8,128)(2,1)S(1)}, u32[]{:S(2)}) copy-start(bf16[512,3072]{1,0:T(8,128)(2,1)S(1)} %get-tuple-element.196) | copy-start | bytes 9437188
  887.8 65.0 %reduce-scatter.37.cloned.1.call-start = ((), (), s32[]{:S(2)}) async-start(), calls=%async_computation.39 | async-start | bytes 2359296 | tf_op jit(solution)/shard_map/reduce_scatter | solution.py:69
  932.9 24.3 reduce-scatter.35.cloned.1.call-start
  942.0 23.9 reduce-scatter.29.cloned.1.call-start
  952.7 30.2 %all-gather.54.cloned.1.call-start = ((), (), s32[]{:S(2)}) async-start(), calls=%async_computation.45 | async-start | bytes 2359296 | tf_op jit(solution)/shard_map/all_gather | solution.py:55
  971.7 23.8 all-gather.50.cloned.1.call-start
  972.5 35.4 %reduce-scatter.45.cloned.1.call-start = ((), (), s32[]{:S(2)}) async-start(), calls=%async_computation.46 | async-start | bytes 2359296 | tf_op jit(solution)/shard_map/reduce_scatter | solution.py:69
  993.0 27.3 %reduce-scatter.39.cloned.1.call-start = ((), (), s32[]{:S(2)}) async-start(), calls=%async_computation.41 | async-start | bytes 2359296 | tf_op jit(solution)/shard_map/reduce_scatter | solution.py:69
  1002.9 17.4 copy-start.10
  1002.9 17.4 copy-start.12
  1002.9 17.4 copy-start.82
  1002.9 17.4 copy-start.101
  1002.9 17.4 copy-start.103
  1005.6 17.9 copy-start.131
  1005.6 17.9 copy-start.139
  1005.6 18.0 copy-start.121
  1005.6 18.0 copy-start.123
  1005.6 34.0 %all-gather.52.cloned.1.call-start = ((), (), s32[]{:S(2)}) async-start(), calls=%async_computation.42 | async-start | bytes 2359296 | tf_op jit(solution)/shard_map/all_gather | solution.py:55
  1028.3 23.8 all-gather.56.cloned.1.call-start
  1032.6 184.1 %reduce-scatter.47.cloned.1.call-start = ((), (), s32[]{:S(2)}) async-start(), calls=%async_computation.48 | async-start | bytes 2359296 | tf_op jit(solution)/shard_map/reduce_scatter | solution.py:69
  1092.0 23.5 copy-start.28
  1128.5 88.2 %reduce-scatter.41.cloned.1.call-start = ((), (), s32[]{:S(2)}) async-start(), calls=%async_computation.43 | async-start | bytes 2359296 | tf_op jit(solution)/shard_map/reduce_scatter | solution.py:69
  1155.2 139.5 %all-reduce.8.cloned.1.call-start = ((), (), s32[]{:S(2)}) async-start(), calls=%async_computation.60 | async-start | bytes 786432 | tf_op jit(solution)/shard_map/psum | solution.py:293
  1174.8 205.5 %all-reduce.6.cloned.1.call-start = ((), (), s32[]{:S(2)}) async-start(), calls=%async_computation.59 | async-start | bytes 9437184
  1196.9 316.9 %reduce-scatter.53.cloned.1.call-start = ((), (), s32[]{:S(2)}) async-start(), calls=%async_computation.51 | async-start | bytes 2506752 | tf_op jit(solution)/shard_map/reduce_scatter | solution.py:354
  1203.8 443.3 %reduce-scatter.55.cloned.1.call-start = ((), (), s32[]{:S(2)}) async-start(), calls=%async_computation.52 | async-start | bytes 2506752 | tf_op jit(solution)/shard_map/reduce_scatter | solution.py:360
  1210.4 563.4 %reduce-scatter.61.cloned.1.call-start = ((), (), s32[]{:S(2)}) async-start(), calls=%async_computation.57 | async-start | bytes 417792
  1221.8 678.7 %reduce-scatter.63.cloned.1.call-start = ((), (), s32[]{:S(2)}) async-start(), calls=%async_computation.58 | async-start | bytes 417792
  1222.9 811.1 %reduce-scatter.51.cloned.1.call-start = ((), (), s32[]{:S(2)}) async-start(), calls=%async_computation.50 | async-start | bytes 2506752 | tf_op jit(solution)/shard_map/reduce_scatter | solution.py:351
  1229.0 981.1 %reduce-scatter.57.cloned.1.call-start = ((), (), s32[]{:S(2)}) async-start(), calls=%async_computation.53 | async-start | bytes 10027008 | tf_op jit(solution)/shard_map/reduce_scatter | solution.py:363
  1252.0 1134.2 %reduce-scatter.59.cloned.1.call-start = ((), (), s32[]{:S(2)}) async-start(), calls=%async_computation.54 | async-start | bytes 10027008 | tf_op jit(solution)/shard_map/reduce_scatter | solution.py:366
  1275.4 1267.7 %reduce-scatter.49.cloned.1.call-start = ((), (), s32[]{:S(2)}) async-start(), calls=%async_computation.49 | async-start | bytes 7520256 | tf_op jit(solution)/shard_map/reduce_scatter | solution.py:348
  (146 other events, 654.3 us)
Sparse Core Ops, SparseCore 0:
  91.4 7.5 all-gather.23
  101.7 101.7 all-gather.25
  206.4 60.5 all-gather.27
  271.3 7.3 reduce-scatter.24
  281.8 11.0 all-gather.43
  323.8 10.2 reduce-scatter.30
  336.7 80.9 all-gather.29
  420.5 60.8 all-gather.33
  483.6 8.1 all-gather.31
  494.4 63.3 all-gather.35
  559.9 8.1 all-gather.45
  570.8 10.2 reduce-scatter.26
  585.1 8.6 reduce-scatter.32
  596.5 123.0 all-gather.39
  721.5 7.9 all-gather.47
  730.9 10.9 all-gather.59
  744.6 122.8 all-gather.41
  869.5 7.9 all-gather.37
  879.0 10.9 all-gather.57
  892.1 10.1 reduce-scatter.42
  933.0 7.5 reduce-scatter.36
  942.9 10.3 reduce-scatter.34
  955.5 10.3 reduce-scatter.28
  971.9 11.0 all-gather.53
  984.5 10.9 all-gather.49
  997.6 10.1 reduce-scatter.44
  1010.0 10.3 reduce-scatter.38
  1028.5 11.0 all-gather.51
  1041.1 10.9 all-gather.55
  1128.6 10.2 reduce-scatter.46
  1155.3 10.1 reduce-scatter.40
  1174.9 19.5 all-reduce.7
  1200.1 180.0 all-reduce.5
  1385.2 128.5 reduce-scatter.52
  1518.7 128.4 reduce-scatter.54
  1651.6 122.0 reduce-scatter.60
  1778.3 122.2 reduce-scatter.62
  1905.5 128.5 reduce-scatter.50
  2039.6 170.4 reduce-scatter.56
  2215.8 170.3 reduce-scatter.58
  2391.5 151.4 reduce-scatter.48
where the time goes:
time: 2560 us; the launch traced here: 2550 us
  waiting for transfers between devices  1910 us (75%)
  matrix products  373 us (15%)
  other arithmetic  107 us (4%)
  blocking collectives  80.5 us (3%)
  local copies, waits for them, and re-layouts  63.5 us (2%)
    unnamed x44, waiting for transfers between devices  337 us
    reduce_scatter x1, waiting for transfers between devices, per_device(): lax.psum_scatter(grad_totals[7].astype(jnp.bfloat16), 'dp', scatter_dimen...  174 us
    reduce_scatter x1, waiting for transfers between devices, per_device(): lax.psum_scatter(grad_totals[8].astype(jnp.bfloat16), 'dp', scatter_dimen...  174 us
    reduce_scatter x1, waiting for transfers between devices, per_device(): lax.psum_scatter(grad_totals[2].astype(jnp.bfloat16), 'dp', scatter_dimen...  155 us
    reduce_scatter x1, waiting for transfers between devices, per_device(): lax.psum_scatter(grad_totals[6].astype(jnp.bfloat16), 'dp', scatter_dimen...  132 us
    reduce_scatter x1, waiting for transfers between devices, per_device(): lax.psum_scatter(grad_totals[4].astype(jnp.bfloat16), 'dp', scatter_dimen...  131 us
    reduce_scatter x1, waiting for transfers between devices, per_device(): lax.psum_scatter(grad_totals[3].astype(jnp.bfloat16), 'dp', scatter_dimen...  129 us
    dot_general x20, matrix products, product(): return jnp.dot(left_side, right_side, preferred_element_type=jnp.float32)  122 us
  transfers between devices with their start and end apart: 41, of which 30 were waited for; matrix products, arithmetic and copies ran while one was open for 15% of the time, Pallas kernels for 0%

commit v1 on v0

v1 whole, which is shorter than its diff:
```python
import math

import jax
import jax.numpy as jnp
from jax import lax
from jax.sharding import Mesh
from jax.sharding import PartitionSpec as P

HEAD_DIM = 64
EPS = 1e-05
BF = jnp.bfloat16
F32 = jnp.float32
SWAP = [(0, 1), (1, 0)]


def mm(left, right):
    return jnp.dot(left, right, preferred_element_type=F32)


def mm_t(left, right):
    return lax.dot_general(left, right, (((1,), (1,)), ((), ())), preferred_element_type=F32)


def mm_rows(left, right):
    return lax.dot_general(left, right, (((0,), (0,)), ((), ())), preferred_element_type=F32)


def norm_stats(values):
    mean = jnp.mean(values, axis=-1, keepdims=True)
    centred = values - mean
    inv = lax.rsqrt(jnp.mean(centred * centred, axis=-1, keepdims=True) + EPS)
    return mean, inv


def norm_apply(values, stats, gain, shift):
    return ((values - stats[0]) * stats[1] * gain + shift).astype(BF)


def norm_back(values, stats, gain, grad):
    xhat = (values - stats[0]) * stats[1]
    scaled = grad * gain
    part = jnp.mean(scaled, axis=-1, keepdims=True)
    cross = jnp.mean(scaled * xhat, axis=-1, keepdims=True)
    value_grad = (scaled - part - xhat * cross) * stats[1]
    return value_grad, jnp.sum(grad * xhat, axis=0), jnp.sum(grad, axis=0)


def gelu_pair(pre):
    phi = 0.5 * (1.0 + lax.erf(pre * (1.0 / math.sqrt(2.0))))
    dens = jnp.exp(-0.5 * pre * pre) * (1.0 / math.sqrt(2.0 * math.pi))
    return (pre * phi).astype(BF), (phi + pre * dens).astype(BF)


def heads(matrix):
    return matrix.reshape(*matrix.shape[:-1], matrix.shape[-1] // HEAD_DIM, HEAD_DIM)


def flat(matrix):
    return matrix.reshape(*matrix.shape[:-2], -1)


SCALE = 1.0 / math.sqrt(HEAD_DIM)


def causal_scores(q, k):
    scores = jnp.einsum("bqhd,bkhd->bhqk", heads(q), heads(k), preferred_element_type=F32) * SCALE
    n = q.shape[1]
    allowed = jnp.arange(n)[None, :] <= jnp.arange(n)[:, None]
    return jnp.where(allowed, scores, -1e30)


def attend(q, k, v):
    scores = causal_scores(q, k)
    top = jnp.max(scores, axis=-1, keepdims=True)
    terms = jnp.exp(scores - top)
    total = jnp.sum(terms, axis=-1, keepdims=True)
    out = jnp.einsum(
        "bhqk,bkhd->bqhd", (terms / total).astype(BF), heads(v), preferred_element_type=F32
    )
    return flat(out).astype(BF), top + jnp.log(total)


def probs_back(chances, dp, q, k, grad):
    dot = jnp.sum(chances * dp, axis=-1, keepdims=True)
    ds = (chances * (dp - dot)).astype(BF)
    dv = jnp.einsum("bhqk,bqhd->bkhd", chances.astype(BF), grad, preferred_element_type=F32)
    dq = jnp.einsum("bhqk,bkhd->bqhd", ds, heads(k), preferred_element_type=F32) * SCALE
    dk = jnp.einsum("bhqk,bqhd->bkhd", ds, heads(q), preferred_element_type=F32) * SCALE
    return flat(dq).astype(BF), flat(dk).astype(BF), flat(dv).astype(BF)


def attend_back(q, k, v, log_total, grad):
    chances = jnp.exp(causal_scores(q, k) - log_total)
    grad = heads(grad)
    dp = jnp.einsum("bqhd,bkhd->bhqk", grad, heads(v), preferred_element_type=F32)
    return probs_back(chances, dp, q, k, grad)


def cross_attend(q, k, v):
    scores = jnp.einsum("bqhd,bkhd->bhqk", heads(q), heads(k), preferred_element_type=F32) * SCALE
    chances = jax.nn.softmax(scores, axis=-1)
    out = jnp.einsum("bhqk,bkhd->bqhd", chances.astype(BF), heads(v), preferred_element_type=F32)
    return flat(out).astype(BF), chances


def cross_attend_back(q, k, v, chances, grad):
    grad = heads(grad)
    dp = jnp.einsum("bqhd,bkhd->bhqk", grad, heads(v), preferred_element_type=F32)
    return probs_back(chances, dp, q, k, grad)


class Whole:
    def __init__(self, dp, tensor):
        self.dp, self.tensor = dp, tensor

    def arrange(self, values):
        return values

    def restore(self, values):
        return values

    def gather_norms(self, packed):
        return lax.all_gather(packed, self.dp, axis=0, tiled=True)

    def gather_first(self, shard):
        return lax.all_gather(shard, self.dp, axis=0, tiled=True)

    gather_middle = gather_first

    def scatter_last(self, make):
        whole = make(slice(None), slice(None)).astype(BF)
        return lax.psum_scatter(whole, self.dp, scatter_dimension=0, tiled=True).astype(F32)

    scatter_middle = scatter_last

    def spread(self, rows, clips):
        local = rows.reshape(clips, -1, rows.shape[-1])
        return lax.all_gather(local, self.tensor, axis=1, tiled=True).reshape(-1, rows.shape[-1])

    def sequence(self, rows, clips):
        return rows.reshape(clips, -1, rows.shape[-1])

    def unsequence(self, rows):
        return rows.reshape(-1, rows.shape[-1])

    def clip_rows(self, rows, clips):
        return rows.reshape(clips, -1, rows.shape[-1])

    unclip_rows = unsequence

    def sum_own(self, left, right, product, clips):
        part = product(left, right).astype(BF).reshape(clips, -1, right_width(product, right))
        own = lax.psum_scatter(part, self.tensor, scatter_dimension=1, tiled=True)
        return own.reshape(-1, part.shape[-1]).astype(F32)

    def sum_all(self, values):
        return lax.psum(values.astype(BF), self.tensor).astype(F32)


def right_width(product, right):
    return right.shape[0] if product is mm_t else right.shape[1]


class Block(Whole):
    def __init__(self, width):
        self.width = width
        self.shard = width // 16
        self.core = lax.axis_index("core")

    def order(self):
        own_y, own_x = lax.axis_index("y"), lax.axis_index("x")
        place = jnp.arange(self.width, dtype=jnp.int32)
        quarter, rest = place // (4 * self.shard), place % (4 * self.shard)
        z, row = rest // self.shard, rest % self.shard
        y, x = (quarter // 2) ^ own_y, (quarter % 2) ^ own_x
        source = ((z * 2 + y) * 2 + x) * self.shard + row
        return (jnp.arange(self.width, dtype=jnp.int32)[:, None] == source[None, :]).astype(BF)

    def arrange(self, values):
        return mm(values, self.order()).astype(BF)

    def restore(self, values):
        if values.dtype == BF:
            return mm_t(values, self.order()).astype(BF)
        high = lax.reduce_precision(values, 8, 7)
        low = (values - high).astype(BF)
        order = self.order()
        return mm_t(high.astype(BF), order) + mm_t(low, order)

    def x(self, v):
        return lax.ppermute(v, "x", SWAP)

    def y(self, v):
        return lax.ppermute(v, "y", SWAP)

    def other(self, v):
        return lax.ppermute(v, "core", SWAP)

    def gather_norms(self, packed):
        pair = jnp.stack([packed, lax.ppermute(packed, "z", [(0, 1), (1, 0), (2, 3), (3, 2)])])
        far = lax.ppermute(pair, "z", [(0, 2), (1, 3), (2, 0), (3, 1)])
        own = lax.axis_index("z")
        four = jnp.concatenate([pair, far])
        four = jnp.stack([lax.dynamic_index_in_dim(four, own ^ p, 0, False) for p in range(4)])
        two = jnp.stack([four, self.x(four)])
        whole = jnp.stack([two, self.y(two)])
        return whole.reshape(self.width, packed.shape[-1])

    def halves(self, shard):
        half = shard.shape[1] // 256 * 128
        return shard[:, :half], shard[:, half:]

    def finish(self, first, second):
        n = first.shape[0] // 2
        far_first, far_second = self.y(first), self.x(second)
        left = jnp.concatenate([first, far_first])
        right = jnp.concatenate([second[:n], far_second[:n], second[n:], far_second[n:]])
        return jnp.concatenate([left, right], axis=1)

    def gather_first(self, shard):
        four = lax.all_gather(shard, "z", axis=0, tiled=True)
        a, b = self.halves(four)
        return self.finish(jnp.concatenate([a, self.x(a)]), jnp.concatenate([b, self.y(b)]))

    def gather_middle(self, shard):
        a, b = self.halves(shard)
        four = jnp.stack([a, self.x(a), b, self.y(b)])
        four = lax.all_gather(four, "z", axis=1, tiled=True)
        return self.finish(
            four[:2].reshape(-1, a.shape[1]), four[2:].reshape(-1, a.shape[1])
        )

    def scatter_open(self, make, columns):
        n = self.width // 4
        half = columns // 256 * 128
        left, right = slice(0, half), slice(half, columns)
        far_left = self.y(make(slice(2 * n, 4 * n), left).astype(BF))
        far_right = self.x(
            jnp.concatenate(
                [make(slice(n, 2 * n), right).astype(BF), make(slice(3 * n, 4 * n), right).astype(BF)]
            )
        )
        a = (make(slice(0, 2 * n), left) + far_left.astype(F32)).astype(BF)
        b = [
            (make(slice(0, n), right) + far_right[:n].astype(F32)).astype(BF),
            (make(slice(2 * n, 3 * n), right) + far_right[n:].astype(F32)).astype(BF),
        ]
        return a[:n], a[n:], b[0], b[1]

    def scatter_middle(self, make, columns):
        four = jnp.stack(self.scatter_open(make, columns))
        four = lax.psum_scatter(four, "z", scatter_dimension=1, tiled=True)
        left = four[0].astype(F32) + self.x(four[1]).astype(F32)
        right = four[2].astype(F32) + self.y(four[3]).astype(F32)
        return jnp.concatenate([left, right], axis=1)

    def scatter_last(self, make, columns):
        a0, a1, b0, b1 = self.scatter_open(make, columns)
        far_a, far_b = self.x(a1), self.y(b1)
        both = jnp.stack(
            [
                (a0.astype(F32) + far_a.astype(F32)).astype(BF),
                (b0.astype(F32) + far_b.astype(F32)).astype(BF),
            ]
        )
        both = lax.psum_scatter(both, "z", scatter_dimension=1, tiled=True).astype(F32)
        return jnp.concatenate([both[0], both[1]], axis=1)

    def spread(self, rows, clips):
        return jnp.concatenate([rows, self.other(rows)])

    def sequence(self, rows, clips):
        parts = rows.reshape(2, clips, -1, rows.shape[-1])
        swapped = jnp.where(self.core == 0, parts, parts[::-1])
        return jnp.swapaxes(swapped, 0, 1).reshape(clips, -1, rows.shape[-1])

    def unsequence(self, rows):
        parts = jnp.swapaxes(rows.reshape(rows.shape[0], 2, -1, rows.shape[-1]), 0, 1)
        return jnp.where(self.core == 0, parts, parts[::-1]).reshape(-1, rows.shape[-1])

    def clip_rows(self, rows, clips):
        parts = rows.reshape(2, clips, -1, rows.shape[-1])
        return jnp.swapaxes(parts, 0, 1).reshape(clips, -1, rows.shape[-1])

    def unclip_rows(self, rows):
        parts = rows.reshape(rows.shape[0], 2, -1, rows.shape[-1])
        return jnp.swapaxes(parts, 0, 1).reshape(-1, rows.shape[-1])

    def sum_own(self, left, right, product, clips):
        n = left.shape[0] // 2
        far = self.other(product(left[n:], right).astype(BF))
        return product(left[:n], right) + far.astype(F32)

    def sum_all(self, values):
        return values + self.other(values.astype(BF)).astype(F32)


def layer(
    comm,
    frames,
    text_states,
    norm_gain,
    norm_shift,
    self_project,
    self_output,
    cross_query,
    cross_memory,
    cross_output,
    feed_input,
    feed_output,
    upstream,
):
    clips, own_frames, width = frames.shape
    texts = text_states.shape[1]
    cols = cross_query.shape[1]
    own_rows = clips * own_frames

    def catenate(parts):
        return jnp.concatenate(parts, axis=1)

    norms = comm.gather_norms(
        jnp.pad(jnp.concatenate([norm_gain, norm_shift]).T, ((0, 0), (0, 122)))
    )
    norms = norms.T.astype(F32)
    gain, shift = norms[0:3], norms[3:6]
    first_set = catenate([self_project[0], self_project[1], self_project[2]])
    second_set = catenate(
        [self_output.T, cross_query, cross_memory[0], cross_memory[1], cross_output.T]
    )
    w_self = comm.gather_first(first_set)
    w_cross = comm.gather_first(second_set)
    w_in = comm.gather_middle(feed_input)
    w_out = comm.gather_middle(feed_output.T)
    w_so, w_cq = w_cross[:, :cols], w_cross[:, cols : 2 * cols]
    w_cm, w_co = w_cross[:, 2 * cols : 4 * cols], w_cross[:, 4 * cols :]

    values0 = comm.arrange(frames.reshape(own_rows, width)).astype(F32)
    up = comm.arrange(upstream.reshape(own_rows, width))
    text = comm.arrange(text_states.reshape(clips * texts, width))
    up_all = comm.spread(up, clips)

    stats0 = norm_stats(values0)
    n1 = comm.spread(norm_apply(values0, stats0, gain[0], shift[0]), clips)
    qkv = comm.sequence(mm(n1, w_self).astype(BF), clips)
    q, k, v = qkv[..., :cols], qkv[..., cols : 2 * cols], qkv[..., 2 * cols :]
    att, log_total = attend(q, k, v)
    att = comm.unsequence(att)
    values1 = values0 + comm.sum_own(att, w_so, mm_t, clips)

    stats1 = norm_stats(values1)
    n2 = comm.spread(norm_apply(values1, stats1, gain[1], shift[1]), clips)
    cq = comm.clip_rows(mm(n2, w_cq).astype(BF), clips)
    memory = mm(text, w_cm).astype(BF).reshape(clips, texts, 2 * cols)
    ck, cv = memory[..., :cols], memory[..., cols:]
    cross, chances = cross_attend(cq, ck, cv)
    cross = comm.unclip_rows(cross)
    values2 = values1 + comm.sum_own(cross, w_co, mm_t, clips)

    stats2 = norm_stats(values2)
    n3 = comm.spread(norm_apply(values2, stats2, gain[2], shift[2]), clips)
    hidden, slope = gelu_pair(mm(n3, w_in))
    layer_out = (values2 + comm.sum_own(hidden, w_out, mm_t, clips)).astype(BF)
    layer_out = comm.restore(layer_out).reshape(clips, own_frames, width)

    def wgrad(left, right):
        return lambda rows, columns: mm_rows(left[:, rows], right[:, columns])

    def scatter(method, left, right):
        if type(comm) is Whole:
            return method(wgrad(left, right))
        return method(wgrad(left, right), right.shape[1])

    grad_out = scatter(comm.scatter_middle, up_all, hidden)
    pre_grad = (mm(up_all, w_out) * slope.astype(F32)).astype(BF)
    grad_in = scatter(comm.scatter_middle, n3, pre_grad)
    e3 = comm.sum_own(pre_grad, w_in, mm_t, clips)
    dv2, gain2, shift2 = norm_back(values2, stats2, gain[2], e3)
    r2 = up.astype(F32) + dv2
    r2_all = comm.spread(r2.astype(BF), clips)
    dco = comm.clip_rows(mm(r2_all, w_co).astype(BF), clips)
    dcq, dck, dcv = cross_attend_back(cq, ck, cv, chances, dco)
    dcq = comm.unclip_rows(dcq)
    dmem = jnp.concatenate([dck, dcv], axis=-1).reshape(clips * texts, 2 * cols)
    text_grad = comm.sum_all(mm_t(dmem, w_cm))
    e2 = comm.sum_own(dcq, w_cq, mm_t, clips)
    dv1, gain1, shift1 = norm_back(values1, stats1, gain[1], e2)
    r1 = r2 + dv1
    r1_all = comm.spread(r1.astype(BF), clips)
    grad_co = scatter(comm.scatter_last, r2_all, cross)
    grad_cq = scatter(comm.scatter_last, n2, dcq)
    grad_cm = scatter(comm.scatter_last, text, dmem)
    grad_so = scatter(comm.scatter_last, r1_all, att)
    datt = comm.sequence(mm(r1_all, w_so).astype(BF), clips)
    dq, dk, dvv = attend_back(q, k, v, log_total, datt)
    dqkv = comm.unsequence(jnp.concatenate([dq, dk, dvv], axis=-1))
    grad_self = scatter(comm.scatter_last, n1, dqkv)
    e1 = comm.sum_own(dqkv, w_self, mm_t, clips)
    dv0, gain0, shift0 = norm_back(values0, stats0, gain[0], e1)
    input_grad = comm.restore(r1 + dv0).reshape(clips, own_frames, width)
    text_grad = comm.restore(text_grad).reshape(clips, texts, width)
    packed = jnp.stack([gain0, gain1, gain2, shift0, shift1, shift2]).T
    packed = jnp.pad(packed, ((0, 0), (0, 250)))

    def norm_sums(rows, columns):
        return packed[rows, columns]

    if type(comm) is Whole:
        norm_grad = comm.scatter_last(norm_sums)
    else:
        norm_grad = comm.scatter_last(norm_sums, packed.shape[1])
    norm_grad = comm.sum_all(norm_grad[:, :8]).T
    return (
        layer_out,
        input_grad,
        text_grad,
        norm_grad[0:3],
        norm_grad[3:6],
        jnp.stack([grad_self[:, i * cols : (i + 1) * cols] for i in range(3)]),
        grad_so.T,
        grad_cq,
        jnp.stack([grad_cm[:, :cols], grad_cm[:, cols:]]),
        grad_co.T,
        grad_in,
        grad_out.T,
    )


def specs(dp, tensor):
    in_specs = (
        P(dp, tensor, None),
        P(dp, None, None),
        P(None, dp),
        P(None, dp),
        P(None, dp, tensor),
        P(tensor, dp),
        P(dp, tensor),
        P(None, dp, tensor),
        P(tensor, dp),
        P(dp, tensor),
        P(tensor, dp),
        P(dp, tensor, None),
    )
    out_specs = (
        P(dp, tensor, None),
        P(dp, tensor, None),
        P(dp, None, None),
        P(None, dp),
        P(None, dp),
        P(None, dp, tensor),
        P(tensor, dp),
        P(dp, tensor),
        P(None, dp, tensor),
        P(tensor, dp),
        P(dp, tensor),
        P(tensor, dp),
    )
    return in_specs, out_specs


def solution(mesh):
    if mesh.shape["dp"] == 16 and mesh.shape["tensor"] == 2:
        mesh = Mesh(mesh.devices.reshape(4, 2, 2, 2), ("z", "y", "x", "core"))
        in_specs, out_specs = specs(("z", "y", "x"), "core")

        def per_device(frames, *rest):
            return layer(Block(frames.shape[-1]), frames, *rest)
    else:
        in_specs, out_specs = specs("dp", "tensor")

        def per_device(frames, *rest):
            return layer(Whole("dp", "tensor"), frames, *rest)

    return jax.shard_map(
        per_device, mesh=mesh, in_specs=in_specs, out_specs=out_specs, check_vma=False
    )
```

time: 2560 us -> 1310 us (0.51)
  waiting for transfers between devices: 1910 us -> 443 us
  matrix products: 373 us -> 460 us
  local copies, waits for them, and re-layouts: 63.5 us -> 144 us
  blocking collectives: 80.5 us -> 0 us
  other arithmetic: 107 us -> 171 us
  starting transfers between devices: 3.98 us -> 62 us
    reduce_scatter x18 -> x7, waiting for transfers between devices: 942 us -> 43.8 us  [the longest x5 29 us: scatter_last(): lax.psum_scatter(both, 'z', scatter_dimension=1, tiled=True).astype(F32)]
    all_gather x19 -> x4, waiting for transfers between devices: 627 us -> 51 us  [the longest x2 26.2 us: gather_first(): four = lax.all_gather(shard, 'z', axis=0, tiled=True)]
    ppermute x0 -> x66, waiting for transfers between devices: none -> 348 us  [the longest x25 198 us: x(): return lax.ppermute(v, 'x', SWAP)]
    unnamed x44 -> x13, waiting for transfers between devices: 337 us -> 0.22 us
    dot_general x82 -> x80, matrix products: 367 us -> 457 us  [the longest x17 162 us: mm_t(): lax.dot_general(left, right, (((1,), (1,)), ((), ())), preferred_element_...]
    concatenate x0 -> x20, other arithmetic: none -> 83.7 us  [the longest x2 55.5 us: finish(): return jnp.concatenate([left, right], axis=1)]
    all_gather x2 -> x0, blocking collectives: 78 us -> none  [the longest x1 42.5 us: per_device(): lax.all_gather(norm_gain, 'dp', axis=1, tiled=True)]
    ppermute x0 -> x66, starting transfers between devices: none -> 60.5 us  [the longest x25 30.8 us: x(): return lax.ppermute(v, 'x', SWAP)]
  transfers between devices with their start and end apart: 41 -> 78, of which waited for: 30 -> 28; matrix products, arithmetic and copies ran while one was open for 15% -> 56% of each run, Pallas kernels for 0% -> 0%
where the time goes in v1:
time: 1310 us; the launch traced here: 1300 us
  matrix products  460 us (35%)
  waiting for transfers between devices  443 us (34%)
  other arithmetic  171 us (13%)
  local copies, waits for them, and re-layouts  144 us (11%)
  starting transfers between devices  62 us (5%)
  between operations  18.3 us (1%)
    ppermute x25, waiting for transfers between devices, x(): return lax.ppermute(v, 'x', SWAP)  198 us
    dot_general x17, matrix products, mm_t(): lax.dot_general(left, right, (((1,), (1,)), ((), ())), preferred_element_...  162 us
    ppermute x25, waiting for transfers between devices, y(): return lax.ppermute(v, 'y', SWAP)  150 us
    dot_general x10, matrix products, mm(): return jnp.dot(left, right, preferred_element_type=F32)  110 us
    dot_general x42, matrix products, mm_rows(): lax.dot_general(left, right, (((0,), (0,)), ((), ())), preferred_element_...  101 us
    concatenate x2, other arithmetic, finish(): return jnp.concatenate([left, right], axis=1)  55.5 us
    convert_element_type x12, local copies, waits for them, and re-layouts, probs_back(): return (flat(dq).astype(BF), flat(dk).astype(BF), flat(dv).astype(BF))  35.1 us
    ppermute x25, starting transfers between devices, x(): return lax.ppermute(v, 'x', SWAP)  30.8 us
  transfers between devices with their start and end apart: 78, of which 28 were waited for; matrix products, arithmetic and copies ran while one was open for 56% of the time, Pallas kernels for 0%

profile of v1, /device:TPU:0, one launch (start us, length us, event | category | flops | bytes accessed | tf_op | source)
XLA Modules:
  0.0 1298.4 jit_solution(15556184022518571638)
XLA Ops:
  29.1 26.2 %all-gather.5.cloned.1.call-done = bf16[384,2304]{1,0:T(8,128)(2,1)} async-done(((bf16[96,2304]{1,0:T(8,128)(2,1)}), bf16[384,2304]{1,0:T(8,128)(2,1)}) %all-gather.5.cloned.1.call-update) | async-done | bytes 1769488 | tf_op jit(solution)/shard_map/all_gather | solution.py:221
  69.1 19.6 %collective-permute-done.3 = bf16[2,4,96,128]{3,2,1,0:T(8,128)(2,1)S(1)} collective-permute-done((bf16[2,4,96,128]{3,2,1,0:T(8,128)(2,1)S(1)}, bf16[2,4,96,128]{3,2,1,0:T(8,128)(2,1)S(1)}, u32[]{:S(2)}, u32[]{:S(2)}) %collective-permute-start.3) | collective-permute-done | bytes 196640 | tf_op jit(solution)/shard_map/ppermute | solution.py:194
  93.4 17.8 %collective-permute-done.5 = bf16[384,1152]{1,0:T(8,128)(2,1)S(1)} collective-permute-done((bf16[384,1152]{1,0:T(8,128)(2,1)S(1)}, bf16[384,1152]{1,0:T(8,128)(2,1)S(1)}, u32[]{:S(2)}, u32[]{:S(2)}) %collective-permute-start.5) | collective-permute-done | bytes 884768 | tf_op jit(solution)/shard_map/ppermute | solution.py:191
  120.6 26.7 %collective-permute-done.8 = bf16[768,1152]{1,0:T(8,128)(2,1)} collective-permute-done((bf16[768,1152]{1,0:T(8,128)(2,1)}, bf16[768,1152]{1,0:T(8,128)(2,1)}, u32[]{:S(2)}, u32[]{:S(2)}) %collective-permute-start.8) | collective-permute-done | bytes 1769504 | tf_op jit(solution)/shard_map/ppermute | solution.py:191
  151.2 41.1 %maximum_maximum_fusion.2 = bf16[1536,2304]{1,0:T(8,128)(2,1)S(1)} fusion(bf16[384,1152]{1,0:T(8,128)(2,1)S(1)} %get-tuple-element.86, bf16[384,1152]{1,0:T(8,128)(2,1)} %collective-permute-done.7, bf16[384,1152]{1,0:T(8,128)(2,1)S(1)} %get-tuple-element.85, bf16[384,1152]{1,0:T(8,128)(2,1)S(1)} %copy-done.46, bf16[768,1152]{1,0:T(8,128)(2,1)} %collective-permute-done.6, ...), kind=kLoop, calls=%fused_computation.34 | loop fusion | flops 49545216 | bytes 14155776 | tf_op jit(solution)/shard_map/concatenate | solution.py:218
  193.8 8.3 convolution_convert_fusion
  210.9 12.2 fusion.12
  223.1 11.1 fusion.1
  244.3 13.2 %fusion.170 = bf16[2,512,12,64]{1,3,2,0:T(8,128)(2,1)} fusion(bf16[2,512,12,64]{1,3,2,0:T(8,128)(2,1)S(1)} %bitcast.379, f32[2,12,512]{2,1,0:T(8,128)S(1)} %fusion.1, f32[2,12,512]{2,1,0:T(8,128)S(1)} %get-tuple-element.139, f32[2,12,512,512]{2,3,1,0:T(8,128)} %get-tuple-element.140, pred[512,512]{0,1:T(8,128)(4,1)S(1)} %iota_compare_fusion.12), kind=kOutput, calls=%fused_computation.313 | convolution fusion | flops 837550080 | bytes 28672000 | tf_op jit(solution)/shard_map/bhqk,bkhd->bqhd/dot_general | solution.py:77
  266.3 42.6 %collective-permute-done.10 = bf16[768,1920]{1,0:T(8,128)(2,1)} collective-permute-done((bf16[768,1920]{1,0:T(8,128)(2,1)}, bf16[768,1920]{1,0:T(8,128)(2,1)}, u32[]{:S(2)}, u32[]{:S(2)}) %collective-permute-start.10) | collective-permute-done | bytes 2949152 | tf_op jit(solution)/shard_map/ppermute | solution.py:194
  308.8 5.7 pad_maximum_fusion.24
  338.3 14.5 %fusion.25 = bf16[1536,1536]{1,0:T(8,128)(2,1)S(1)} fusion(bf16[384,1920]{1,0:T(8,128)(2,1)S(1)} %get-tuple-element.72, bf16[768,1920]{1,0:T(8,128)(2,1)} %collective-permute-done.10, bf16[384,1920]{1,0:T(8,128)(2,1)} %collective-permute-done.12, bf16[384,1920]{1,0:T(8,128)(2,1)} %collective-permute-done.9, bf16[384,1920]{1,0:T(8,128)(2,1)S(1)} %copy-done.27, ...), kind=kLoop, calls=%fused_computation.117 | loop fusion | flops 33030144 | bytes 16515072 | tf_op jit(solution)/shard_map/concatenate | solution.py:218
  362.3 4.0 fusion.123
  383.7 4.9 fusion.398
  390.7 24.8 %all-gather.11.cloned.1.call-done = bf16[4,384,1536]{2,1,0:T(8,128)(2,1)} async-done(((bf16[4,96,1536]{2,1,0:T(8,128)(2,1)}), bf16[4,384,1536]{2,1,0:T(8,128)(2,1)}) %all-gather.11.cloned.1.call-update) | async-done | bytes 4718608 | tf_op jit(solution)/shard_map/all_gather | solution.py:228
  427.8 15.2 %collective-permute-done.20 = bf16[768,1536]{1,0:T(8,128)(2,1)} collective-permute-done((bf16[768,1536]{1,0:T(8,128)(2,1)}, bf16[768,1536]{1,0:T(8,128)(2,1)}, u32[]{:S(2)}, u32[]{:S(2)}) %collective-permute-start.20) | collective-permute-done | bytes 2359328 | tf_op jit(solution)/shard_map/ppermute | solution.py:191
  445.6 47.5 %collective-permute-done.24 = bf16[768,1536]{1,0:T(8,128)(2,1)S(1)} collective-permute-done((bf16[768,1536]{1,0:T(8,128)(2,1)S(1)}, bf16[768,1536]{1,0:T(8,128)(2,1)S(1)}, u32[]{:S(2)}, u32[]{:S(2)}) %collective-permute-start.24) | collective-permute-done | bytes 2359328 | tf_op jit(solution)/shard_map/ppermute | solution.py:191
  495.1 31.4 %multiply_convert_fusion.2 = (bf16[1024,3072]{1,0:T(8,128)(2,1)}, f32[1024,3072]{1,0:T(8,128)}) fusion(bf16[384,1536]{1,0:T(8,128)(2,1)S(1)} %get-tuple-element.82, bf16[384,1536]{1,0:T(8,128)(2,1)S(1)} %get-tuple-element.67, bf16[384,1536]{1,0:T(8,128)(2,1)S(1)} %get-tuple-element.81, bf16[384,1536]{1,0:T(8,128)(2,1)S(1)} %get-tuple-element.66, ...), kind=kOutput, calls=%fused_computation.18 | convolution fusion | flops 9742319616 | bytes 31457280 | tf_op jit(solution)/shard_map/dot_general | solution.py:17
  526.6 19.3 %collective-permute-done.23 = bf16[768,1536]{1,0:T(8,128)(2,1)S(1)} collective-permute-done((bf16[768,1536]{1,0:T(8,128)(2,1)S(1)}, bf16[768,1536]{1,0:T(8,128)(2,1)S(1)}, u32[]{:S(2)}, u32[]{:S(2)}) %collective-permute-start.23) | collective-permute-done | bytes 2359328 | tf_op jit(solution)/shard_map/ppermute | solution.py:194
  547.4 48.5 %multiply_convert_fusion.1 = bf16[1024,3072]{1,0:T(8,128)(2,1)} fusion(f32[1024,3072]{1,0:T(8,128)} %get-tuple-element.148, bf16[512,1536]{0,1:T(8,128)(2,1)} %collective-permute-done.26, bf16[512,1536]{0,1:T(8,128)(2,1)} %fusion.95, bf16[384,1536]{1,0:T(8,128)(2,1)S(1)} %get-tuple-element.80, bf16[384,1536]{1,0:T(8,128)(2,1)S(1)} %get-tuple-element.63, ...), kind=kOutput, calls=%fused_computation.17 | convolution fusion | flops 9764339712 | bytes 31457280 | tf_op jit(solution)/shard_map/dot_general | solution.py:17
  595.9 27.6 %fusion.78 = bf16[512,1536]{0,1:T(8,128)(2,1)} fusion(bf16[1024,3072]{1,0:T(8,128)(2,1)} %multiply_convert_fusion.1, bf16[384,1536]{1,0:T(8,128)(2,1)} %copy-done.100, bf16[384,1536]{1,0:T(8,128)(2,1)S(1)} %copy-done.98, bf16[384,1536]{1,0:T(8,128)(2,1)} %copy-done.99, bf16[384,1536]{1,0:T(8,128)(2,1)S(1)} %get-tuple-element.66, ...), kind=kOutput, calls=%fused_computation.207 | convolution fusion | flops 4889247744 | bytes 14155776 | tf_op jit(solution)/shard_map/dot_general | solution.py:21
  623.5 6.5 convolution_convert_fusion.1
  638.6 30.1 %multiply_reduce_fusion.1 = (f32[1536]{0:T(1024)S(1)}, f32[512]{0:T(512)S(1)}, f32[512]{0:T(512)S(1)}, f32[1536]{0:T(1024)S(1)}, f32[512,1536]{0,1:T(8,128)}) fusion(f32[512,1536]{0,1:T(8,128)} %copy-done.2, f32[512]{0:T(512)S(1)} %add_rsqrt_fusion, f32[512]{0:T(512)S(1)} %broadcast_multiply_fusion.6, f32[1536]{0:T(1024)S(1)} %get-tuple-element.48, ...), kind=kOutput, calls=%fused_computation.180 | convolution fusion | flops 4897107968 | bytes 20473856 | tf_op jit(solution)/shard_map/dot_general | solution.py:21
  668.7 4.3 fusion.392
  676.5 14.3 %collective-permute-done.63 = bf16[768,1536]{1,0:T(8,128)(2,1)} collective-permute-done((bf16[768,1536]{1,0:T(8,128)(2,1)}, bf16[768,1536]{1,0:T(8,128)(2,1)}, u32[]{:S(2)}, u32[]{:S(2)}) %collective-permute-start.63) | collective-permute-done | bytes 2359328 | tf_op jit(solution)/shard_map/ppermute | solution.py:191
  690.9 4.9 fusion.101
  695.8 6.3 add_convert_fusion
  702.1 4.0 fusion.124
  735.6 5.2 copy.190
  760.8 24.1 %collective-permute-done.48 = bf16[768,384]{1,0:T(8,128)(2,1)S(1)} collective-permute-done((bf16[768,384]{1,0:T(8,128)(2,1)S(1)}, bf16[768,384]{1,0:T(8,128)(2,1)S(1)}, u32[]{:S(2)}, u32[]{:S(2)}) %collective-permute-start.48) | collective-permute-done | bytes 589856 | tf_op jit(solution)/shard_map/ppermute | solution.py:191
  796.2 6.6 multiply_reduce_fusion.2
  803.0 4.7 fusion.395
  811.3 12.1 collective-permute-done.49
  833.0 8.5 collective-permute-done.53
  844.1 4.1 fusion.125
  849.6 5.3 copy.193
  858.7 12.5 fusion.163
  871.2 17.3 %multiply_reduce_fusion = (f32[2,12,512]{2,1,0:T(8,128)S(1)}, f32[2,12,512,512]{2,3,1,0:T(8,128)}) fusion(f32[2,12,512]{2,1,0:T(8,128)S(1)} %copy-done.109, f32[2,12,512,512]{2,3,1,0:T(8,128)} %get-tuple-element.140, pred[512,512]{0,1:T(8,128)(4,1)S(1)} %copy-done.35, bf16[2,512,12,64]{1,3,2,0:T(8,128)(2,1)} %reshape_reshape.12, ...), kind=kOutput, calls=%fused_computation.2 | convolution fusion | flops 836751360 | bytes 53837824 | tf_op jit(solution)/shard_map/bqhd,bkhd->bhqk/dot_general | solution.py:95
  888.5 22.2 %multiply_convert_fusion = bf16[2,12,512,512]{2,3,1,0:T(8,128)(2,1)} fusion(f32[2,12,512,512]{2,3,1,0:T(8,128)} %get-tuple-element.154, f32[2,12,512]{2,1,0:T(8,128)S(1)} %get-tuple-element.153, f32[2,12,512]{2,1,0:T(8,128)S(1)} %copy-done.109, f32[2,12,512,512]{2,3,1,0:T(8,128)} %get-tuple-element.140, pred[512,512]{0,1:T(8,128)(4,1)S(1)} %copy-done.35), kind=kLoop, calls=%fused_computation.1 | loop fusion | flops 37748736 | bytes 63275008 | tf_op jit(solution)/shard_map/convert_element_type | solution.py:85
  910.7 9.7 fusion.167
  920.4 7.8 fusion.166
  931.9 5.0 copy.199
  938.7 5.1 copy.197
  947.4 4.9 copy.198
  960.2 4.9 convolution_convert_fusion.4
  976.7 8.6 collective-permute-done.44
  988.4 10.2 fusion.52
  1008.2 5.4 collective-permute-done.34
  1016.9 4.0 fusion.102
  1036.2 3.9 convolution_convert_fusion.2
  1040.9 17.6 %fusion.75 = bf16[512,1536]{0,1:T(8,128)(2,1)} fusion(bf16[1024,3072]{1,0:T(8,128)(2,1)} %get-tuple-element.147, bf16[384,1536]{1,0:T(8,128)(2,1)} %copy-done.96, bf16[384,1536]{1,0:T(8,128)(2,1)} %copy-done.93, bf16[384,1536]{1,0:T(8,128)(2,1)} %copy-done.95, bf16[384,1536]{1,0:T(8,128)(2,1)S(1)} %copy-done.92, bf16[768,1536]{1,0:T(8,128)(2,1)} %copy-done.154, ...), kind=kOutput, calls=%fused_computation.206 | convolution fusion | flops 4889247744 | bytes 14155776 | tf_op jit(solution)/shard_map/dot_general | solution.py:21
  1058.6 28.2 %collective-permute-done.59 = bf16[768,1536]{1,0:T(8,128)(2,1)} collective-permute-done((bf16[768,1536]{1,0:T(8,128)(2,1)}, bf16[768,1536]{1,0:T(8,128)(2,1)}, u32[]{:S(2)}, u32[]{:S(2)}) %collective-permute-start.59) | collective-permute-done | bytes 2359328 | tf_op jit(solution)/shard_map/ppermute | solution.py:191
  1086.8 3.9 fusion.103
  1091.7 5.1 add_convert_fusion.1
  1103.2 4.7 fusion.414
  1108.0 26.1 %fusion.74 = bf16[512,1536]{1,0:T(8,128)(2,1)} fusion(s32[1536]{0:T(1024)} %copy-done.147, f32[512,1536]{0,1:T(8,128)} %copy-done.2, bf16[512,1536]{0,1:T(8,128)(2,1)} %collective-permute-done.25, bf16[1024,3072]{1,0:T(8,128)(2,1)} %get-tuple-element.147, bf16[384,1536]{1,0:T(8,128)(2,1)} %copy-done.96, bf16[384,1536]{1,0:T(8,128)(2,1)S(1)} %copy-done.94, ...), kind=kOutput, calls=%fused_computation.201 | convolution fusion | flops 7310671872 | bytes 18882560 | tf_op jit(solution)/shard_map/dot_general | solution.py:21
  1137.3 4.0 fusion.105
  1157.9 7.0 fusion.13
  1164.9 27.5 %collective-permute-done.38 = bf16[768,1152]{1,0:T(8,128)(2,1)} collective-permute-done((bf16[768,1152]{1,0:T(8,128)(2,1)}, bf16[768,1152]{1,0:T(8,128)(2,1)}, u32[]{:S(2)}, u32[]{:S(2)}) %collective-permute-start.38) | collective-permute-done | bytes 1769504 | tf_op jit(solution)/shard_map/ppermute | solution.py:194
  1201.3 5.5 fusion.43
  1206.8 13.9 %collective-permute-done.41 = bf16[384,1152]{1,0:T(8,128)(2,1)S(1)} collective-permute-done((bf16[384,1152]{1,0:T(8,128)(2,1)S(1)}, bf16[384,1152]{1,0:T(8,128)(2,1)S(1)}, u32[]{:S(2)}, u32[]{:S(2)}) %collective-permute-start.41) | collective-permute-done | bytes 884768 | tf_op jit(solution)/shard_map/ppermute | solution.py:194
  1232.2 14.9 %reduce-scatter.18.cloned.1.call-done = bf16[4,96,1536]{2,1,0:T(8,128)(2,1)} async-done(((bf16[4,384,1536]{2,1,0:T(8,128)(2,1)}), bf16[4,96,1536]{2,1,0:T(8,128)(2,1)}) %reduce-scatter.18.cloned.1.call-update) | async-done | bytes 1179664 | tf_op jit(solution)/shard_map/reduce_scatter | solution.py:252
  1252.5 4.5 collective-permute-done.60
  1259.4 28.9 %reduce-scatter.8.cloned.1.call-done = bf16[2,96,1152]{2,1,0:T(8,128)(2,1)} async-done(((bf16[2,384,1152]{2,1,0:T(8,128)(2,1)}), bf16[2,96,1152]{2,1,0:T(8,128)(2,1)}) %reduce-scatter.8.cloned.1.call-update) | async-done | bytes 442384 | tf_op jit(solution)/shard_map/reduce_scatter | solution.py:266
  (727 shorter events, 363.0 us)
Async XLA Ops:
  7.2 48.1 %all-gather.5.cloned.1.call-start = ((), (), s32[]{:S(2)}) async-start(), calls=%async_computation.7 | async-start | bytes 2211840 | tf_op jit(solution)/shard_map/all_gather | solution.py:221
  9.3 109.0 %all-gather.7.cloned.1.call-start = ((), (), s32[]{:S(2)}) async-start(), calls=%async_computation.8 | async-start | bytes 3686400 | tf_op jit(solution)/shard_map/all_gather | solution.py:221
  11.3 372.4 %all-gather.9.cloned.1.call-start = ((), (), s32[]{:S(2)}) async-start(), calls=%async_computation.9 | async-start | bytes 5898240 | tf_op jit(solution)/shard_map/all_gather | solution.py:228
  15.5 307.7 %collective-permute-start.35 = (bf16[768,128]{1,0:T(8,128)(2,1)}, bf16[768,128]{1,0:T(8,128)(2,1)}, u32[]{:S(2)}, u32[]{:S(2)}) collective-permute-start(bf16[768,128]{1,0:T(8,128)(2,1)} %concatenate.162), channel_id=1, source_target_pairs={{0,2},{2,0},{1,3},{3,1},{4,6},{6,4},{5,7},{7,5},{8,10},{10,8},{9,1... | collective-permute-start | bytes 589832 | tf_op jit(solution)/shard_map/ppermute | solution.py:191
  19.0 44.8 %collective-permute-start.18 = (bf16[96,1536]{1,0:T(8,128)(2,1)}, bf16[96,1536]{1,0:T(8,128)(2,1)}, u32[]{:S(2)}, u32[]{:S(2)}) collective-permute-start(bf16[96,1536]{1,0:T(8,128)(2,1)} %get-tuple-element.109), channel_id=1, source_target_pairs={{0,4},{4,0},{1,5},{5,1},{2,6},{6,2},{3,7},{7,3},{8,12},{12,8},{9,1... | collective-permute-start | bytes 884744 | tf_op jit(solution)/shard_map/ppermute | solution.py:194
  20.5 44.9 %collective-permute-start.17 = (bf16[96,1536]{1,0:T(8,128)(2,1)}, bf16[96,1536]{1,0:T(8,128)(2,1)}, u32[]{:S(2)}, u32[]{:S(2)}) collective-permute-start(bf16[96,1536]{1,0:T(8,128)(2,1)} %get-tuple-element.110), channel_id=1, source_target_pairs={{0,2},{2,0},{1,3},{3,1},{4,6},{6,4},{5,7},{7,5},{8,10},{10,8},{9,1... | collective-permute-start | bytes 884744 | tf_op jit(solution)/shard_map/ppermute | solution.py:191
  26.5 32.0 %collective-permute-start.1 = (bf16[2,96,128]{2,1,0:T(8,128)(2,1)S(1)}, bf16[2,96,128]{2,1,0:T(8,128)(2,1)S(1)}, u32[]{:S(2)}, u32[]{:S(2)}) collective-permute-start(bf16[2,96,128]{2,1,0:T(8,128)(2,1)S(1)} %pad_maximum_fusion.59), channel_id=1, source_target_pairs={{0,16},{8,24},{16,0},{24,8},{1,17},{9,25},{17,1},{25,9},{2,18},{10... | collective-permute-start | bytes 147464 | tf_op jit(solution)/shard_map/ppermute | solution.py:201
  56.9 33.3 %collective-permute-start.7 = (bf16[384,1152]{1,0:T(8,128)(2,1)S(1)}, bf16[384,1152]{1,0:T(8,128)(2,1)}, u32[]{:S(2)}, u32[]{:S(2)}) collective-permute-start(bf16[384,1152]{1,0:T(8,128)(2,1)S(1)} %get-tuple-element.84), channel_id=1, source_target_pairs={{0,4},{4,0},{1,5},{5,1},{2,6},{6,2},{3,7},{7,3},{8,12},{12,8},{9,1... | collective-permute-start | bytes 2654216 | tf_op jit(solution)/shard_map/ppermute | solution.py:194
  63.2 262.1 %collective-permute-start.22 = (bf16[96,1536]{1,0:T(8,128)(2,1)}, bf16[96,1536]{1,0:T(8,128)(2,1)}, u32[]{:S(2)}, u32[]{:S(2)}) collective-permute-start(bf16[96,1536]{1,0:T(8,128)(2,1)} %get-tuple-element.105), channel_id=1, source_target_pairs={{0,4},{4,0},{1,5},{5,1},{2,6},{6,2},{3,7},{7,3},{8,12},{12,8},{9,1... | collective-permute-start | bytes 884744 | tf_op jit(solution)/shard_map/ppermute | solution.py:194
  63.8 261.5 %collective-permute-start.21 = (bf16[96,1536]{1,0:T(8,128)(2,1)}, bf16[96,1536]{1,0:T(8,128)(2,1)}, u32[]{:S(2)}, u32[]{:S(2)}) collective-permute-start(bf16[96,1536]{1,0:T(8,128)(2,1)} %get-tuple-element.106), channel_id=1, source_target_pairs={{0,2},{2,0},{1,3},{3,1},{4,6},{6,4},{5,7},{7,5},{8,10},{10,8},{9,1... | collective-permute-start | bytes 884744 | tf_op jit(solution)/shard_map/ppermute | solution.py:191
  65.3 23.4 %collective-permute-start.3 = (bf16[2,4,96,128]{3,2,1,0:T(8,128)(2,1)S(1)}, bf16[2,4,96,128]{3,2,1,0:T(8,128)(2,1)S(1)}, u32[]{:S(2)}, u32[]{:S(2)}) collective-permute-start(bf16[2,4,96,128]{3,2,1,0:T(8,128)(2,1)S(1)} %get-tuple-element.126), channel_id=1, source_target_pairs={{0,4},{4,0},{1,5},{5,1},{2,6},{6,2},{3,7},{7,3},{8,12},{12,8},{9,1... | collective-permute-start | bytes 589832 | tf_op jit(solution)/shard_map/ppermute | solution.py:194
  69.0 346.4 %all-gather.11.cloned.1.call-start = ((), (), s32[]{:S(2)}) async-start(), calls=%async_computation.10 | async-start | bytes 5898240 | tf_op jit(solution)/shard_map/all_gather | solution.py:228
  88.7 22.5 %collective-permute-start.5 = (bf16[384,1152]{1,0:T(8,128)(2,1)S(1)}, bf16[384,1152]{1,0:T(8,128)(2,1)S(1)}, u32[]{:S(2)}, u32[]{:S(2)}) collective-permute-start(bf16[384,1152]{1,0:T(8,128)(2,1)S(1)} %get-tuple-element.83), channel_id=1, source_target_pairs={{0,2},{2,0},{1,3},{3,1},{4,6},{6,4},{5,7},{7,5},{8,10},{10,8},{9,1... | collective-permute-start | bytes 2654216 | tf_op jit(solution)/shard_map/ppermute | solution.py:191
  92.8 54.4 %collective-permute-start.8 = (bf16[768,1152]{1,0:T(8,128)(2,1)}, bf16[768,1152]{1,0:T(8,128)(2,1)}, u32[]{:S(2)}, u32[]{:S(2)}) collective-permute-start(bf16[768,1152]{1,0:T(8,128)(2,1)} %pad_maximum_fusion.30), channel_id=1, source_target_pairs={{0,2},{2,0},{1,3},{3,1},{4,6},{6,4},{5,7},{7,5},{8,10},{10,8},{9,1... | collective-permute-start | bytes 5308424 | tf_op jit(solution)/shard_map/ppermute | solution.py:191
  112.8 37.0 %collective-permute-start.6 = (bf16[768,1152]{1,0:T(8,128)(2,1)}, bf16[768,1152]{1,0:T(8,128)(2,1)}, u32[]{:S(2)}, u32[]{:S(2)}) collective-permute-start(bf16[768,1152]{1,0:T(8,128)(2,1)} %pad_maximum_fusion.29), channel_id=1, source_target_pairs={{0,4},{4,0},{1,5},{5,1},{2,6},{6,2},{3,7},{7,3},{8,12},{12,8},{9,1... | collective-permute-start | bytes 5308424 | tf_op jit(solution)/shard_map/ppermute | solution.py:194
  147.2 45.0 %collective-permute-start.4 = (bf16[512,1536]{0,1:T(8,128)(2,1)S(1)}, bf16[512,1536]{0,1:T(8,128)(2,1)S(1)}, u32[]{:S(2)}, u32[]{:S(2)}) collective-permute-start(bf16[512,1536]{0,1:T(8,128)(2,1)S(1)} %copy-done.81), channel_id=1, source_target_pairs={{0,1},{1,0},{2,3},{3,2},{4,5},{5,4},{6,7},{7,6},{8,9},{9,8},{10,11... | collective-permute-start | bytes 4718600 | tf_op jit(solution)/shard_map/ppermute | solution.py:197
  149.7 87.1 %collective-permute-start.12 = (bf16[384,1920]{1,0:T(8,128)(2,1)S(1)}, bf16[384,1920]{1,0:T(8,128)(2,1)}, u32[]{:S(2)}, u32[]{:S(2)}) collective-permute-start(bf16[384,1920]{1,0:T(8,128)(2,1)S(1)} %get-tuple-element.73), channel_id=1, source_target_pairs={{0,4},{4,0},{1,5},{5,1},{2,6},{6,2},{3,7},{7,3},{8,12},{12,8},{9,1... | collective-permute-start | bytes 4423688 | tf_op jit(solution)/shard_map/ppermute | solution.py:194
  192.3 48.3 %collective-permute-start.9 = (bf16[384,1920]{1,0:T(8,128)(2,1)S(1)}, bf16[384,1920]{1,0:T(8,128)(2,1)}, u32[]{:S(2)}, u32[]{:S(2)}) collective-permute-start(bf16[384,1920]{1,0:T(8,128)(2,1)S(1)} %get-tuple-element.74), channel_id=1, source_target_pairs={{0,2},{2,0},{1,3},{3,1},{4,6},{6,4},{5,7},{7,5},{8,10},{10,8},{9,1... | collective-permute-start | bytes 4423688 | tf_op jit(solution)/shard_map/ppermute | solution.py:191
  240.0 88.1 %collective-permute-start.13 = (bf16[768,1920]{1,0:T(8,128)(2,1)}, bf16[768,1920]{1,0:T(8,128)(2,1)}, u32[]{:S(2)}, u32[]{:S(2)}) collective-permute-start(bf16[768,1920]{1,0:T(8,128)(2,1)} %pad_maximum_fusion.20), channel_id=1, source_target_pairs={{0,2},{2,0},{1,3},{3,1},{4,6},{6,4},{5,7},{7,5},{8,10},{10,8},{9,1... | collective-permute-start | bytes 8847368 | tf_op jit(solution)/shard_map/ppermute | solution.py:191
  243.7 65.1 %collective-permute-start.10 = (bf16[768,1920]{1,0:T(8,128)(2,1)}, bf16[768,1920]{1,0:T(8,128)(2,1)}, u32[]{:S(2)}, u32[]{:S(2)}) collective-permute-start(bf16[768,1920]{1,0:T(8,128)(2,1)} %pad_maximum_fusion.19), channel_id=1, source_target_pairs={{0,4},{4,0},{1,5},{5,1},{2,6},{6,2},{3,7},{7,3},{8,12},{12,8},{9,1... | collective-permute-start | bytes 8847368 | tf_op jit(solution)/shard_map/ppermute | solution.py:194
  323.2 203.3 %collective-permute-start.26 = (bf16[512,1536]{0,1:T(8,128)(2,1)}, bf16[512,1536]{0,1:T(8,128)(2,1)}, u32[]{:S(2)}, u32[]{:S(2)}) collective-permute-start(bf16[512,1536]{0,1:T(8,128)(2,1)} %fusion.95), channel_id=1, source_target_pairs={{0,1},{1,0},{2,3},{3,2},{4,5},{5,4},{6,7},{7,6},{8,9},{9,8},{10,11... | collective-permute-start | bytes 4718600 | tf_op jit(solution)/shard_map/ppermute | solution.py:197
  327.6 813.7 %reduce-scatter.16.cloned.1.call-start = ((), (), s32[]{:S(2)}) async-start(), calls=%async_computation.15 | async-start | bytes 737280 | tf_op jit(solution)/shard_map/reduce_scatter | solution.py:266
  336.3 26.0 %collective-permute-start.14 = (bf16[512,1536]{0,1:T(8,128)(2,1)S(1)}, bf16[512,1536]{0,1:T(8,128)(2,1)S(1)}, u32[]{:S(2)}, u32[]{:S(2)}) collective-permute-start(bf16[512,1536]{0,1:T(8,128)(2,1)S(1)} %add_convert_fusion.3), channel_id=1, source_target_pairs={{0,1},{1,0},{2,3},{3,2},{4,5},{5,4},{6,7},{7,6},{8,9},{9,8},{10,11... | collective-permute-start | bytes 4718600 | tf_op jit(solution)/shard_map/ppermute | solution.py:197
  383.7 36.3 %collective-permute-start.15 = (bf16[512,1536]{0,1:T(8,128)(2,1)}, bf16[512,1536]{0,1:T(8,128)(2,1)}, u32[]{:S(2)}, u32[]{:S(2)}) collective-permute-start(bf16[512,1536]{0,1:T(8,128)(2,1)} %convolution_convert_fusion.6), channel_id=1, source_target_pairs={{0,1},{1,0},{2,3},{3,2},{4,5},{5,4},{6,7},{7,6},{8,9},{9,8},{10,11... | collective-permute-start | bytes 4718600 | tf_op jit(solution)/shard_map/ppermute | solution.py:197
  388.7 54.4 %collective-permute-start.20 = (bf16[768,1536]{1,0:T(8,128)(2,1)}, bf16[768,1536]{1,0:T(8,128)(2,1)}, u32[]{:S(2)}, u32[]{:S(2)}) collective-permute-start(bf16[768,1536]{1,0:T(8,128)(2,1)} %bitcast.45), channel_id=1, source_target_pairs={{0,2},{2,0},{1,3},{3,1},{4,6},{6,4},{5,7},{7,5},{8,10},{10,8},{9,1... | collective-permute-start | bytes 7077896 | tf_op jit(solution)/shard_map/ppermute | solution.py:191
  390.0 103.9 %collective-permute-start.19 = (bf16[768,1536]{1,0:T(8,128)(2,1)}, bf16[768,1536]{1,0:T(8,128)(2,1)}, u32[]{:S(2)}, u32[]{:S(2)}) collective-permute-start(bf16[768,1536]{1,0:T(8,128)(2,1)} %bitcast.43), channel_id=1, source_target_pairs={{0,4},{4,0},{1,5},{5,1},{2,6},{6,2},{3,7},{7,3},{8,12},{12,8},{9,1... | collective-permute-start | bytes 7077896 | tf_op jit(solution)/shard_map/ppermute | solution.py:194
  418.3 74.7 %collective-permute-start.24 = (bf16[768,1536]{1,0:T(8,128)(2,1)S(1)}, bf16[768,1536]{1,0:T(8,128)(2,1)S(1)}, u32[]{:S(2)}, u32[]{:S(2)}) collective-permute-start(bf16[768,1536]{1,0:T(8,128)(2,1)S(1)} %bitcast.404), channel_id=1, source_target_pairs={{0,2},{2,0},{1,3},{3,1},{4,6},{6,4},{5,7},{7,5},{8,10},{10,8},{9,1... | collective-permute-start | bytes 7077896 | tf_op jit(solution)/shard_map/ppermute | solution.py:191
  427.6 66.3 %collective-permute-start.16 = (bf16[512,1536]{0,1:T(8,128)(2,1)S(1)}, bf16[512,1536]{0,1:T(8,128)(2,1)S(1)}, u32[]{:S(2)}, u32[]{:S(2)}) collective-permute-start(bf16[512,1536]{0,1:T(8,128)(2,1)S(1)} %add_convert_fusion.2), channel_id=1, source_target_pairs={{0,1},{1,0},{2,3},{3,2},{4,5},{5,4},{6,7},{7,6},{8,9},{9,8},{10,11... | collective-permute-start | bytes 4718600 | tf_op jit(solution)/shard_map/ppermute | solution.py:197
  443.1 230.0 %collective-permute-start.36 = (bf16[384,128]{1,0:T(8,128)(2,1)S(1)}, bf16[384,128]{1,0:T(8,128)(2,1)S(1)}, u32[]{:S(2)}, u32[]{:S(2)}) collective-permute-start(bf16[384,128]{1,0:T(8,128)(2,1)S(1)} %copy-done.120), channel_id=1, source_target_pairs={{0,4},{4,0},{1,5},{5,1},{2,6},{6,2},{3,7},{7,3},{8,12},{12,8},{9,1... | collective-permute-start | bytes 294920 | tf_op jit(solution)/shard_map/ppermute | solution.py:194
  493.1 52.8 %collective-permute-start.23 = (bf16[768,1536]{1,0:T(8,128)(2,1)S(1)}, bf16[768,1536]{1,0:T(8,128)(2,1)S(1)}, u32[]{:S(2)}, u32[]{:S(2)}) collective-permute-start(bf16[768,1536]{1,0:T(8,128)(2,1)S(1)} %bitcast.399), channel_id=1, source_target_pairs={{0,4},{4,0},{1,5},{5,1},{2,6},{6,2},{3,7},{7,3},{8,12},{12,8},{9,1... | collective-permute-start | bytes 7077896 | tf_op jit(solution)/shard_map/ppermute | solution.py:194
  630.0 65.8 %collective-permute-start.62 = (bf16[768,1536]{1,0:T(8,128)(2,1)}, bf16[768,1536]{1,0:T(8,128)(2,1)}, u32[]{:S(2)}, u32[]{:S(2)}) collective-permute-start(bf16[768,1536]{1,0:T(8,128)(2,1)} %convolution_convert_fusion.1), channel_id=1, source_target_pairs={{0,4},{4,0},{1,5},{5,1},{2,6},{6,2},{3,7},{7,3},{8,12},{12,8},{9,1... | collective-permute-start | bytes 7077896 | tf_op jit(solution)/shard_map/ppermute | solution.py:194
  637.2 53.7 %collective-permute-start.63 = (bf16[768,1536]{1,0:T(8,128)(2,1)}, bf16[768,1536]{1,0:T(8,128)(2,1)}, u32[]{:S(2)}, u32[]{:S(2)}) collective-permute-start(bf16[768,1536]{1,0:T(8,128)(2,1)} %pad_maximum_fusion.28), channel_id=1, source_target_pairs={{0,2},{2,0},{1,3},{3,1},{4,6},{6,4},{5,7},{7,5},{8,10},{10,8},{9,1... | collective-permute-start | bytes 7077896 | tf_op jit(solution)/shard_map/ppermute | solution.py:191
  673.0 29.1 %collective-permute-start.28 = (bf16[512,1536]{0,1:T(8,128)(2,1)S(1)}, bf16[512,1536]{0,1:T(8,128)(2,1)S(1)}, u32[]{:S(2)}, u32[]{:S(2)}) collective-permute-start(bf16[512,1536]{0,1:T(8,128)(2,1)S(1)} %fusion.392), channel_id=1, source_target_pairs={{0,1},{1,0},{2,3},{3,2},{4,5},{5,4},{6,7},{7,6},{8,9},{9,8},{10,11... | collective-permute-start | bytes 4718600 | tf_op jit(solution)/shard_map/ppermute | solution.py:197
  727.2 27.3 %collective-permute-start.54 = (bf16[768,384]{1,0:T(8,128)(2,1)}, bf16[768,384]{1,0:T(8,128)(2,1)}, u32[]{:S(2)}, u32[]{:S(2)}) collective-permute-start(bf16[768,384]{1,0:T(8,128)(2,1)} %fusion.192), channel_id=1, source_target_pairs={{0,4},{4,0},{1,5},{5,1},{2,6},{6,2},{3,7},{7,3},{8,12},{12,8},{9,1... | collective-permute-start | bytes 1769480 | tf_op jit(solution)/shard_map/ppermute | solution.py:194
  730.6 27.4 %collective-permute-start.56 = (bf16[768,384]{1,0:T(8,128)(2,1)}, bf16[768,384]{1,0:T(8,128)(2,1)}, u32[]{:S(2)}, u32[]{:S(2)}) collective-permute-start(bf16[768,384]{1,0:T(8,128)(2,1)} %pad_maximum_fusion.49), channel_id=1, source_target_pairs={{0,2},{2,0},{1,3},{3,1},{4,6},{6,4},{5,7},{7,5},{8,10},{10,8},{9,1... | collective-permute-start | bytes 1769480 | tf_op jit(solution)/shard_map/ppermute | solution.py:191
  732.9 92.0 %collective-permute-start.52 = (bf16[768,768]{1,0:T(8,128)(2,1)}, bf16[768,768]{1,0:T(8,128)(2,1)}, u32[]{:S(2)}, u32[]{:S(2)}) collective-permute-start(bf16[768,768]{1,0:T(8,128)(2,1)} %pad_maximum_fusion.41), channel_id=1, source_target_pairs={{0,2},{2,0},{1,3},{3,1},{4,6},{6,4},{5,7},{7,5},{8,10},{10,8},{9,1... | collective-permute-start | bytes 3538952 | tf_op jit(solution)/shard_map/ppermute | solution.py:191
  747.5 60.2 %collective-permute-start.46 = (bf16[768,384]{1,0:T(8,128)(2,1)}, bf16[768,384]{1,0:T(8,128)(2,1)}, u32[]{:S(2)}, u32[]{:S(2)}) collective-permute-start(bf16[768,384]{1,0:T(8,128)(2,1)} %fusion.189), channel_id=1, source_target_pairs={{0,4},{4,0},{1,5},{5,1},{2,6},{6,2},{3,7},{7,3},{8,12},{12,8},{9,1... | collective-permute-start | bytes 1769480 | tf_op jit(solution)/shard_map/ppermute | solution.py:194
  753.3 42.9 %collective-permute-start.29 = (bf16[512,1536]{0,1:T(8,128)(2,1)}, bf16[512,1536]{0,1:T(8,128)(2,1)}, u32[]{:S(2)}, u32[]{:S(2)}) collective-permute-start(bf16[512,1536]{0,1:T(8,128)(2,1)} %convolution_convert_fusion.5), channel_id=1, source_target_pairs={{0,1},{1,0},{2,3},{3,2},{4,5},{5,4},{6,7},{7,6},{8,9},{9,8},{10,11... | collective-permute-start | bytes 4718600 | tf_op jit(solution)/shard_map/ppermute | solution.py:197
  754.5 30.4 %collective-permute-start.48 = (bf16[768,384]{1,0:T(8,128)(2,1)S(1)}, bf16[768,384]{1,0:T(8,128)(2,1)S(1)}, u32[]{:S(2)}, u32[]{:S(2)}) collective-permute-start(bf16[768,384]{1,0:T(8,128)(2,1)S(1)} %pad_maximum_fusion.47), channel_id=1, source_target_pairs={{0,2},{2,0},{1,3},{3,1},{4,6},{6,4},{5,7},{7,5},{8,10},{10,8},{9,1... | collective-permute-start | bytes 1769480 | tf_op jit(solution)/shard_map/ppermute | solution.py:191
  758.1 31.3 %collective-permute-start.55 = (bf16[384,384]{1,0:T(8,128)(2,1)S(1)}, bf16[384,384]{1,0:T(8,128)(2,1)S(1)}, u32[]{:S(2)}, u32[]{:S(2)}) collective-permute-start(bf16[384,384]{1,0:T(8,128)(2,1)S(1)} %slice.907), channel_id=1, source_target_pairs={{0,2},{2,0},{1,3},{3,1},{4,6},{6,4},{5,7},{7,5},{8,10},{10,8},{9,1... | collective-permute-start | bytes 884744 | tf_op jit(solution)/shard_map/ppermute | solution.py:191
  789.4 39.6 %collective-permute-start.50 = (bf16[768,768]{1,0:T(8,128)(2,1)}, bf16[768,768]{1,0:T(8,128)(2,1)}, u32[]{:S(2)}, u32[]{:S(2)}) collective-permute-start(bf16[768,768]{1,0:T(8,128)(2,1)} %convolution_convert_fusion.16), channel_id=1, source_target_pairs={{0,4},{4,0},{1,5},{5,1},{2,6},{6,2},{3,7},{7,3},{8,12},{12,8},{9,1... | collective-permute-start | bytes 3538952 | tf_op jit(solution)/shard_map/ppermute | solution.py:194
  793.0 30.4 %collective-permute-start.49 = (bf16[384,384]{1,0:T(8,128)(2,1)}, bf16[384,384]{1,0:T(8,128)(2,1)}, u32[]{:S(2)}, u32[]{:S(2)}) collective-permute-start(bf16[384,384]{1,0:T(8,128)(2,1)} %fusion.202), channel_id=1, source_target_pairs={{0,4},{4,0},{1,5},{5,1},{2,6},{6,2},{3,7},{7,3},{8,12},{12,8},{9,1... | collective-permute-start | bytes 884744 | tf_op jit(solution)/shard_map/ppermute | solution.py:194
  796.1 346.2 %reduce-scatter.12.cloned.1.call-start = ((), (), s32[]{:S(2)}) async-start(), calls=%async_computation.13 | async-start | bytes 737280 | tf_op jit(solution)/shard_map/reduce_scatter | solution.py:266
  807.6 36.4 %collective-permute-start.30 = (bf16[512,1536]{0,1:T(8,128)(2,1)S(1)}, bf16[512,1536]{0,1:T(8,128)(2,1)}, u32[]{:S(2)}, u32[]{:S(2)}) collective-permute-start(bf16[512,1536]{0,1:T(8,128)(2,1)S(1)} %get-tuple-element.54), channel_id=1, source_target_pairs={{0,1},{1,0},{2,3},{3,2},{4,5},{5,4},{6,7},{7,6},{8,9},{9,8},{10,11... | collective-permute-start | bytes 4718600 | tf_op jit(solution)/shard_map/ppermute | solution.py:197
  828.9 327.0 %reduce-scatter.14.cloned.1.call-start = ((), (), s32[]{:S(2)}) async-start(), calls=%async_computation.14 | async-start | bytes 1474560 | tf_op jit(solution)/shard_map/reduce_scatter | solution.py:266
  831.6 138.9 %collective-permute-start.51 = (bf16[384,768]{1,0:T(8,128)(2,1)}, bf16[384,768]{1,0:T(8,128)(2,1)}, u32[]{:S(2)}, u32[]{:S(2)}) collective-permute-start(bf16[384,768]{1,0:T(8,128)(2,1)} %slice.894), channel_id=1, source_target_pairs={{0,2},{2,0},{1,3},{3,1},{4,6},{6,4},{5,7},{7,5},{8,10},{10,8},{9,1... | collective-permute-start | bytes 1769480 | tf_op jit(solution)/shard_map/ppermute | solution.py:191
  965.1 23.2 %collective-permute-start.31 = (bf16[512,1536]{0,1:T(8,128)(2,1)}, bf16[512,1536]{0,1:T(8,128)(2,1)}, u32[]{:S(2)}, u32[]{:S(2)}) collective-permute-start(bf16[512,1536]{0,1:T(8,128)(2,1)} %convolution_convert_fusion.4), channel_id=1, source_target_pairs={{0,1},{1,0},{2,3},{3,2},{4,5},{5,4},{6,7},{7,6},{8,9},{9,8},{10,11... | collective-permute-start | bytes 4718600 | tf_op jit(solution)/shard_map/ppermute | solution.py:197
  972.8 252.0 %all-reduce.6.cloned.1.call-start = ((), (), s32[]{:S(2)}) async-start(), calls=%async_computation.18 | async-start | bytes 393216
  975.8 24.3 %collective-permute-start.42 = (bf16[768,384]{1,0:T(8,128)(2,1)}, bf16[768,384]{1,0:T(8,128)(2,1)}, u32[]{:S(2)}, u32[]{:S(2)}) collective-permute-start(bf16[768,384]{1,0:T(8,128)(2,1)} %fusion.195), channel_id=1, source_target_pairs={{0,4},{4,0},{1,5},{5,1},{2,6},{6,2},{3,7},{7,3},{8,12},{12,8},{9,1... | collective-permute-start | bytes 1769480 | tf_op jit(solution)/shard_map/ppermute | solution.py:194
  987.7 18.8 %collective-permute-start.45 = (bf16[384,384]{1,0:T(8,128)(2,1)}, bf16[384,384]{1,0:T(8,128)(2,1)}, u32[]{:S(2)}, u32[]{:S(2)}) collective-permute-start(bf16[384,384]{1,0:T(8,128)(2,1)} %fusion.200), channel_id=1, source_target_pairs={{0,4},{4,0},{1,5},{5,1},{2,6},{6,2},{3,7},{7,3},{8,12},{12,8},{9,1... | collective-permute-start | bytes 884744 | tf_op jit(solution)/shard_map/ppermute | solution.py:194
  1014.7 211.1 %reduce-scatter.10.cloned.1.call-start = ((), (), s32[]{:S(2)}) async-start(), calls=%async_computation.12 | async-start | bytes 737280 | tf_op jit(solution)/shard_map/reduce_scatter | solution.py:266
  1016.8 212.1 %reduce-scatter.20.cloned.1.call-start = ((), (), s32[]{:S(2)}) async-start(), calls=%async_computation.17 | async-start | bytes 5898240 | tf_op jit(solution)/shard_map/reduce_scatter | solution.py:252
  1024.7 222.4 %reduce-scatter.18.cloned.1.call-start = ((), (), s32[]{:S(2)}) async-start(), calls=%async_computation.16 | async-start | bytes 5898240 | tf_op jit(solution)/shard_map/reduce_scatter | solution.py:252
  1035.0 51.8 %collective-permute-start.59 = (bf16[768,1536]{1,0:T(8,128)(2,1)}, bf16[768,1536]{1,0:T(8,128)(2,1)}, u32[]{:S(2)}, u32[]{:S(2)}) collective-permute-start(bf16[768,1536]{1,0:T(8,128)(2,1)} %pad_maximum_fusion.27), channel_id=1, source_target_pairs={{0,2},{2,0},{1,3},{3,1},{4,6},{6,4},{5,7},{7,5},{8,10},{10,8},{9,1... | collective-permute-start | bytes 7077896 | tf_op jit(solution)/shard_map/ppermute | solution.py:191
  1040.1 51.5 %collective-permute-start.58 = (bf16[768,1536]{1,0:T(8,128)(2,1)}, bf16[768,1536]{1,0:T(8,128)(2,1)}, u32[]{:S(2)}, u32[]{:S(2)}) collective-permute-start(bf16[768,1536]{1,0:T(8,128)(2,1)} %convolution_convert_fusion.2), channel_id=1, source_target_pairs={{0,4},{4,0},{1,5},{5,1},{2,6},{6,2},{3,7},{7,3},{8,12},{12,8},{9,1... | collective-permute-start | bytes 7077896 | tf_op jit(solution)/shard_map/ppermute | solution.py:194
  1058.6 49.4 %collective-permute-start.25 = (bf16[512,1536]{0,1:T(8,128)(2,1)}, bf16[512,1536]{0,1:T(8,128)(2,1)}, u32[]{:S(2)}, u32[]{:S(2)}) collective-permute-start(bf16[512,1536]{0,1:T(8,128)(2,1)} %fusion.75), channel_id=1, source_target_pairs={{0,1},{1,0},{2,3},{3,2},{4,5},{5,4},{6,7},{7,6},{8,9},{9,8},{10,11... | collective-permute-start | bytes 4718600 | tf_op jit(solution)/shard_map/ppermute | solution.py:197
  1102.2 186.1 %reduce-scatter.8.cloned.1.call-start = ((), (), s32[]{:S(2)}) async-start(), calls=%async_computation.11 | async-start | bytes 2211840 | tf_op jit(solution)/shard_map/reduce_scatter | solution.py:266
  1107.9 26.2 %collective-permute-start.32 = (bf16[128,1536]{1,0:T(8,128)(2,1)}, bf16[128,1536]{1,0:T(8,128)(2,1)}, u32[]{:S(2)}, u32[]{:S(2)}) collective-permute-start(bf16[128,1536]{1,0:T(8,128)(2,1)} %get-tuple-element.156), channel_id=1, source_target_pairs={{0,1},{1,0},{2,3},{3,2},{4,5},{5,4},{6,7},{7,6},{8,9},{9,8},{10,11... | collective-permute-start | bytes 1179656 | tf_op jit(solution)/shard_map/ppermute | solution.py:197
  1151.5 40.9 %collective-permute-start.38 = (bf16[768,1152]{1,0:T(8,128)(2,1)}, bf16[768,1152]{1,0:T(8,128)(2,1)}, u32[]{:S(2)}, u32[]{:S(2)}) collective-permute-start(bf16[768,1152]{1,0:T(8,128)(2,1)} %convolution_convert_fusion.3), channel_id=1, source_target_pairs={{0,4},{4,0},{1,5},{5,1},{2,6},{6,2},{3,7},{7,3},{8,12},{12,8},{9,1... | collective-permute-start | bytes 5308424 | tf_op jit(solution)/shard_map/ppermute | solution.py:194
  1154.9 42.6 %collective-permute-start.40 = (bf16[768,1152]{1,0:T(8,128)(2,1)S(1)}, bf16[768,1152]{1,0:T(8,128)(2,1)}, u32[]{:S(2)}, u32[]{:S(2)}) collective-permute-start(bf16[768,1152]{1,0:T(8,128)(2,1)S(1)} %pad_maximum_fusion.31), channel_id=1, source_target_pairs={{0,2},{2,0},{1,3},{3,1},{4,6},{6,4},{5,7},{7,5},{8,10},{10,8},{9,1... | collective-permute-start | bytes 5308424 | tf_op jit(solution)/shard_map/ppermute | solution.py:191
  1196.5 26.6 %collective-permute-start.39 = (bf16[384,1152]{1,0:T(8,128)(2,1)S(1)}, bf16[384,1152]{1,0:T(8,128)(2,1)S(1)}, u32[]{:S(2)}, u32[]{:S(2)}) collective-permute-start(bf16[384,1152]{1,0:T(8,128)(2,1)S(1)} %slice.835), channel_id=1, source_target_pairs={{0,2},{2,0},{1,3},{3,1},{4,6},{6,4},{5,7},{7,5},{8,10},{10,8},{9,1... | collective-permute-start | bytes 2654216 | tf_op jit(solution)/shard_map/ppermute | solution.py:191
  1200.3 20.4 %collective-permute-start.41 = (bf16[384,1152]{1,0:T(8,128)(2,1)S(1)}, bf16[384,1152]{1,0:T(8,128)(2,1)S(1)}, u32[]{:S(2)}, u32[]{:S(2)}) collective-permute-start(bf16[384,1152]{1,0:T(8,128)(2,1)S(1)} %fusion.86), channel_id=1, source_target_pairs={{0,4},{4,0},{1,5},{5,1},{2,6},{6,2},{3,7},{7,3},{8,12},{12,8},{9,1... | collective-permute-start | bytes 2654216 | tf_op jit(solution)/shard_map/ppermute | solution.py:194
  1230.1 21.1 %collective-permute-start.64 = (bf16[96,1536]{1,0:T(8,128)(2,1)S(1)}, bf16[96,1536]{1,0:T(8,128)(2,1)S(1)}, u32[]{:S(2)}, u32[]{:S(2)}) collective-permute-start(bf16[96,1536]{1,0:T(8,128)(2,1)S(1)} %get-tuple-element.95), channel_id=1, source_target_pairs={{0,2},{2,0},{1,3},{3,1},{4,6},{6,4},{5,7},{7,5},{8,10},{10,8},{9,1... | collective-permute-start | bytes 884744 | tf_op jit(solution)/shard_map/ppermute | solution.py:191
  1231.5 19.8 %collective-permute-start.65 = (bf16[96,1536]{1,0:T(8,128)(2,1)S(1)}, bf16[96,1536]{1,0:T(8,128)(2,1)S(1)}, u32[]{:S(2)}, u32[]{:S(2)}) collective-permute-start(bf16[96,1536]{1,0:T(8,128)(2,1)S(1)} %get-tuple-element.96), channel_id=1, source_target_pairs={{0,4},{4,0},{1,5},{5,1},{2,6},{6,2},{3,7},{7,3},{8,12},{12,8},{9,1... | collective-permute-start | bytes 884744 | tf_op jit(solution)/shard_map/ppermute | solution.py:194
  (193 other events, 4112.1 us)
Sparse Core Ops, SparseCore 0:
  10.2 45.0 all-gather.4
  57.5 58.9 all-gather.6
  118.6 88.0 all-gather.8
  327.7 87.7 all-gather.10
  796.2 21.2 reduce-scatter.15
  829.0 21.2 reduce-scatter.11
  973.0 27.1 reduce-scatter.13
  1014.8 33.3 all-reduce.5
  1051.1 21.9 reduce-scatter.9
  1075.3 83.6 reduce-scatter.19
  1161.3 85.7 reduce-scatter.17
  1249.3 38.9 reduce-scatter.7

commit v2 on v1

--- a/solution.py
+++ b/solution.py
@@ -3,6 +3,8 @@
 import jax
 import jax.numpy as jnp
 from jax import lax
+from jax.experimental import pallas as pl
+from jax.experimental.pallas import tpu as pltpu
 from jax.sharding import Mesh
 from jax.sharding import PartitionSpec as P
 
@@ -108,6 +110,217 @@
     dp = jnp.einsum("bqhd,bkhd->bhqk", grad, heads(v), preferred_element_type=F32)
     return probs_back(chances, dp, q, k, grad)
 
+ANY = pl.BlockSpec(memory_space=pl.ANY)
+NEG = -1e30
+
+
+def place_kernel(*refs, spots):
+    sources, out, sems = refs[: len(spots)], refs[len(spots)], refs[len(spots) + 1]
+    copies = []
+    for i, (source, (row, col)) in enumerate(zip(sources, spots)):
+        rows, cols = source.shape
+        copies.append(
+            pltpu.make_async_copy(
+                source, out.at[pl.ds(row, rows), pl.ds(col, cols)], sems.at[i]
+            )
+        )
+    for copy in copies:
+        copy.start()
+    for copy in copies:
+        copy.wait()
+
+
+def place(pieces, shape):
+    spots = tuple((row, col) for _, row, col in pieces)
+    return pl.pallas_call(
+        lambda *refs: place_kernel(*refs, spots=spots),
+        out_shape=jax.ShapeDtypeStruct(shape, pieces[0][0].dtype),
+        in_specs=[ANY] * len(pieces),
+        out_specs=ANY,
+        scratch_shapes=[pltpu.SemaphoreType.DMA((len(pieces),))],
+        name="place",
+    )(*[piece for piece, _, _ in pieces])
+
+
+def place_stacked_kernel(four, far_a, far_b, out, sems):
+    n, half = four.shape[0] // 4, four.shape[1]
+    spots = [
+        (four, 0, 2 * n, 0, 0),
+        (far_a, 0, 2 * n, 2 * n, 0),
+        (four, 2 * n, n, 0, half),
+        (far_b, 0, n, n, half),
+        (four, 3 * n, n, 2 * n, half),
+        (far_b, n, n, 3 * n, half),
+    ]
+    copies = [
+        pltpu.make_async_copy(
+            source.at[pl.ds(start, rows)], out.at[pl.ds(row, rows), pl.ds(col, half)], sems.at[i]
+        )
+        for i, (source, start, rows, row, col) in enumerate(spots)
+    ]
+    for copy in copies:
+        copy.start()
+    for copy in copies:
+        copy.wait()
+
+
+def place_stacked(four, far_a, far_b):
+    return pl.pallas_call(
+        place_stacked_kernel,
+        out_shape=jax.ShapeDtypeStruct((four.shape[0], 2 * four.shape[1]), four.dtype),
+        in_specs=[ANY] * 3,
+        out_specs=ANY,
+        scratch_shapes=[pltpu.SemaphoreType.DMA((6,))],
+        name="place_stacked",
+    )(four, far_a, far_b)
+
+
+def rows_of(matrix, grad):
+    return lax.dot_general(matrix, grad, (((0,), (0,)), ((), ())), preferred_element_type=F32)
+
+
+def head_of(ref, half, head):
+    return ref[half, 0, :, head * HEAD_DIM : (head + 1) * HEAD_DIM]
+
+
+def masked(scores):
+    n = scores.shape[0]
+    rows = lax.broadcasted_iota(jnp.int32, (n, n), 0)
+    cols = lax.broadcasted_iota(jnp.int32, (n, n), 1)
+    return jnp.where(cols <= rows, scores, NEG)
+
+
+def self_kernel(core_ref, q_ref, k_ref, v_ref, out_ref, log_ref):
+    halves = (core_ref[0], 1 - core_ref[0])
+    outs, logs = ([], []), ([], [])
+    for head in range(2):
+        q = [head_of(q_ref, h, head) * BF(SCALE) for h in halves]
+        k = [head_of(k_ref, h, head) for h in halves]
+        v = [head_of(v_ref, h, head) for h in halves]
+        first = masked(mm_t(q[0], k[0]))
+        for half, scores in enumerate([[first], [mm_t(q[1], k[0]), masked(mm_t(q[1], k[1]))]]):
+            top = jnp.max(scores[0], axis=-1, keepdims=True)
+            if half:
+                top = jnp.maximum(top, jnp.max(scores[1], axis=-1, keepdims=True))
+            terms = [jnp.exp(part - top) for part in scores]
+            total = sum(jnp.sum(part, axis=-1, keepdims=True) for part in terms)
+            inverse = 1.0 / total
+            out = sum(mm((part * inverse).astype(BF), v[i]) for i, part in enumerate(terms))
+            outs[half].append(out.astype(BF))
+            logs[half].append(jnp.broadcast_to(top + jnp.log(total), out.shape))
+    for half, h in enumerate(halves):
+        out_ref[h, 0] = jnp.concatenate(outs[half], axis=1)
+        log_ref[h, 0] = jnp.concatenate(logs[half], axis=1)
+
+
+def self_back_kernel(core_ref, q_ref, k_ref, v_ref, log_ref, grad_ref, out_ref):
+    halves = (core_ref[0], 1 - core_ref[0])
+    found = [[], [], [], [], [], []]
+    for head in range(2):
+        q = [head_of(q_ref, h, head) * BF(SCALE) for h in halves]
+        k = [head_of(k_ref, h, head) for h in halves]
+        ks = [part * BF(SCALE) for part in k]
+        v = [head_of(v_ref, h, head) for h in halves]
+        log = [head_of(log_ref, h, head)[:, :1] for h in halves]
+        grad = [head_of(grad_ref, h, head) for h in halves]
+        dq, dk, dv = [0.0, 0.0], [0.0, 0.0], [0.0, 0.0]
+        for half, parts in enumerate([(0,), (0, 1)]):
+            chances, dps = [], []
+            for i in parts:
+                scores = mm_t(q[half], k[i])
+                if i == half:
+                    scores = masked(scores)
+                chances.append(jnp.exp(scores - log[half]))
+                dps.append(mm_t(grad[half], v[i]))
+            dot = sum(
+                jnp.sum(c * dp, axis=-1, keepdims=True) for c, dp in zip(chances, dps)
+            )
+            for i, c, dp in zip(parts, chances, dps):
+                ds = (c * (dp - dot)).astype(BF)
+                dv[i] += rows_of(c.astype(BF), grad[half])
+                dk[i] += rows_of(ds, q[half])
+                dq[half] += mm(ds, ks[i])
+        for i, part in enumerate(dq + dk + dv):
+            found[i].append(part.astype(BF))
+    width = out_ref.shape[-1] // 3
+    for i in range(3):
+        col = pl.multiple_of(i * width + pl.program_id(1) * 2 * HEAD_DIM, 2 * HEAD_DIM)
+        for half, h in enumerate(halves):
+            out_ref[h, 0, :, pl.ds(col, 2 * HEAD_DIM)] = jnp.concatenate(
+                found[2 * i + half], axis=1
+            )
+
+
+def cross_parts(q_ref, k_ref, head):
+    cs = slice(head * HEAD_DIM, (head + 1) * HEAD_DIM)
+    q = jnp.concatenate([q_ref[0, 0, :, cs], q_ref[1, 0, :, cs]]) * BF(SCALE)
+    scores = mm_t(q, k_ref[0, :, cs])
+    terms = jnp.exp(scores - jnp.max(scores, axis=-1, keepdims=True))
+    return q, terms * (1.0 / jnp.sum(terms, axis=-1, keepdims=True)), cs
+
+
+def cross_kernel(q_ref, k_ref, v_ref, out_ref):
+    outs = []
+    for head in range(2):
+        _, chances, cs = cross_parts(q_ref, k_ref, head)
+        outs.append(mm(chances.astype(BF), v_ref[0, :, cs]).astype(BF))
+    out = jnp.concatenate(outs, axis=1)
+    n = out.shape[0] // 2
+    out_ref[0, 0], out_ref[1, 0] = out[:n], out[n:]
+
+
+def cross_back_kernel(q_ref, k_ref, v_ref, grad_ref, dq_ref, dkv_ref):
+    found = [[], [], []]
+    for head in range(2):
+        q, chances, cs = cross_parts(q_ref, k_ref, head)
+        grad = jnp.concatenate([grad_ref[0, 0, :, cs], grad_ref[1, 0, :, cs]])
+        dp = mm_t(grad, v_ref[0, :, cs])
+        ds = (chances * (dp - jnp.sum(chances * dp, axis=-1, keepdims=True))).astype(BF)
+        found[0].append(mm(ds, k_ref[0, :, cs] * BF(SCALE)).astype(BF))
+        found[1].append(rows_of(ds, q).astype(BF))
+        found[2].append(rows_of(chances.astype(BF), grad).astype(BF))
+    dq, dk, dv = [jnp.concatenate(parts, axis=1) for parts in found]
+    n = dq.shape[0] // 2
+    dq_ref[0, 0], dq_ref[1, 0] = dq[:n], dq[n:]
+    width = dkv_ref.shape[-1] // 2
+    for i, part in enumerate([dk, dv]):
+        col = pl.multiple_of(i * width + pl.program_id(1) * 2 * HEAD_DIM, 2 * HEAD_DIM)
+        dkv_ref[0, :, pl.ds(col, 2 * HEAD_DIM)] = part
+
+
+def feed_kernel(rows_ref, weight_ref, hidden_ref, slope_ref):
+    step = 256
+
+    def body(i, carry):
+        at = pl.ds(pl.multiple_of(i * step, step), step)
+        hidden_ref[at], slope_ref[at] = gelu_pair(mm(rows_ref[at], weight_ref[...]))
+        return carry
+
+    lax.fori_loop(0, rows_ref.shape[0] // step, body, 0, unroll=True)
+
+
+def feed(rows, weight):
+    count, depth = rows.shape
+    width = weight.shape[1]
+    block = 256
+    out = jax.ShapeDtypeStruct((count, width), BF)
+    return pl.pallas_call(
+        feed_kernel,
+        grid=(width // block,),
+        in_specs=[
+            pl.BlockSpec((count, depth), lambda j: (0, 0)),
+            pl.BlockSpec((depth, block), lambda j: (0, j)),
+        ],
+        out_specs=[pl.BlockSpec((count, block), lambda j: (0, j))] * 2,
+        out_shape=[out, out],
+        cost_estimate=pl.CostEstimate(
+            flops=2 * count * depth * width,
+            transcendentals=2 * count * width,
+            bytes_accessed=2 * (count * depth + depth * width + 2 * count * width),
+        ),
+        name="feed",
+    )(rows, weight)
+
 
 class Whole:
     def __init__(self, dp, tensor):
@@ -147,6 +360,32 @@
         return rows.reshape(clips, -1, rows.shape[-1])
 
     unclip_rows = unsequence
+
+    def self_attend(self, qkv, clips):
+        qkv = self.sequence(qkv, clips)
+        cols = qkv.shape[-1] // 3
+        q, k, v = qkv[..., :cols], qkv[..., cols : 2 * cols], qkv[..., 2 * cols :]
+        att, log_total = attend(q, k, v)
+        return self.unsequence(att), (q, k, v, log_total)
+
+    def self_back(self, saved, grad, clips):
+        dq, dk, dv = attend_back(*saved, self.sequence(grad, clips))
+        return self.unsequence(jnp.concatenate([dq, dk, dv], axis=-1))
+
+    def cross_attend(self, q, memory, clips):
+        q = self.clip_rows(q, clips)
+        memory = memory.reshape(clips, -1, memory.shape[-1])
+        cols = q.shape[-1]
+        k, v = memory[..., :cols], memory[..., cols:]
+        out, chances = cross_attend(q, k, v)
+        return self.unclip_rows(out), (q, k, v, chances)
+
+    def cross_back(self, saved, grad, clips):
+        dq, dk, dv = cross_attend_back(*saved, self.clip_rows(grad, clips))
+        return self.unclip_rows(dq), self.unsequence(jnp.concatenate([dk, dv], axis=-1))
+
+    def feed(self, rows, weight):
+        return gelu_pair(mm(rows, weight))
 
     def sum_own(self, left, right, product, clips):
         part = product(left, right).astype(BF).reshape(clips, -1, right_width(product, right))
@@ -210,25 +449,34 @@
         half = shard.shape[1] // 256 * 128
         return shard[:, :half], shard[:, half:]
 
-    def finish(self, first, second):
-        n = first.shape[0] // 2
-        far_first, far_second = self.y(first), self.x(second)
-        left = jnp.concatenate([first, far_first])
-        right = jnp.concatenate([second[:n], far_second[:n], second[n:], far_second[n:]])
-        return jnp.concatenate([left, right], axis=1)
-
     def gather_first(self, shard):
         four = lax.all_gather(shard, "z", axis=0, tiled=True)
         a, b = self.halves(four)
-        return self.finish(jnp.concatenate([a, self.x(a)]), jnp.concatenate([b, self.y(b)]))
+        n, half = a.shape
+        xa, yb, ya, xb = self.x(a), self.y(b), self.y(a), self.x(b)
+        far_a, far_b = self.y(xa), self.x(yb)
+        return place(
+            [
+                (four, 0, 0),
+                (xa, n, 0),
+                (ya, 2 * n, 0),
+                (far_a, 3 * n, 0),
+                (xb, n, half),
+                (yb, 2 * n, half),
+                (far_b, 3 * n, half),
+            ],
+            (4 * n, shard.shape[1]),
+        )
 
     def gather_middle(self, shard):
         a, b = self.halves(shard)
         four = jnp.stack([a, self.x(a), b, self.y(b)])
         four = lax.all_gather(four, "z", axis=1, tiled=True)
-        return self.finish(
-            four[:2].reshape(-1, a.shape[1]), four[2:].reshape(-1, a.shape[1])
-        )
+        _, n, half = four.shape
+        far_a, far_b = self.y(four[:2]), self.x(four[2:])
+        four = four.reshape(4 * n, half)
+        far_a, far_b = far_a.reshape(2 * n, half), far_b.reshape(2 * n, half)
+        return place_stacked(four, far_a, far_b)
 
     def scatter_open(self, make, columns):
         n = self.width // 4
@@ -269,22 +517,121 @@
     def spread(self, rows, clips):
         return jnp.concatenate([rows, self.other(rows)])
 
-    def sequence(self, rows, clips):
-        parts = rows.reshape(2, clips, -1, rows.shape[-1])
-        swapped = jnp.where(self.core == 0, parts, parts[::-1])
-        return jnp.swapaxes(swapped, 0, 1).reshape(clips, -1, rows.shape[-1])
-
-    def unsequence(self, rows):
-        parts = jnp.swapaxes(rows.reshape(rows.shape[0], 2, -1, rows.shape[-1]), 0, 1)
-        return jnp.where(self.core == 0, parts, parts[::-1]).reshape(-1, rows.shape[-1])
-
-    def clip_rows(self, rows, clips):
-        parts = rows.reshape(2, clips, -1, rows.shape[-1])
-        return jnp.swapaxes(parts, 0, 1).reshape(clips, -1, rows.shape[-1])
-
-    def unclip_rows(self, rows):
-        parts = rows.reshape(rows.shape[0], 2, -1, rows.shape[-1])
-        return jnp.swapaxes(parts, 0, 1).reshape(-1, rows.shape[-1])
+    def self_attend(self, qkv, clips):
+        cols = qkv.shape[-1] // 3
+        steps = cols // (2 * HEAD_DIM)
+        view = qkv.reshape(2, clips, -1, qkv.shape[-1])
+        frames = view.shape[2]
+
+        def block(part):
+            return pl.BlockSpec(
+                (2, 1, frames, 2 * HEAD_DIM), lambda c, j, _: (0, c, 0, part * steps + j)
+            )
+
+        shape = (2, clips, frames, cols)
+        core = self.core.reshape(1).astype(jnp.int32)
+        scores = clips * steps * 2 * 3 * frames * frames
+        out, log_total = pl.pallas_call(
+            self_kernel,
+            grid_spec=pltpu.PrefetchScalarGridSpec(
+                num_scalar_prefetch=1,
+                grid=(clips, steps),
+                in_specs=[block(0), block(1), block(2)],
+                out_specs=[block(0), block(0)],
+            ),
+            out_shape=[jax.ShapeDtypeStruct(shape, BF), jax.ShapeDtypeStruct(shape, F32)],
+            cost_estimate=pl.CostEstimate(
+                flops=4 * scores * HEAD_DIM,
+                transcendentals=scores,
+                bytes_accessed=2 * qkv.size + 6 * qkv.size // 3,
+            ),
+            name="self_attend",
+        )(core, view, view, view)
+        return out.reshape(-1, cols), (core, view, log_total)
+
+    def self_back(self, saved, grad, clips):
+        core, view, log_total = saved
+        cols = view.shape[-1] // 3
+        steps = cols // (2 * HEAD_DIM)
+        frames = view.shape[2]
+
+        def block(part):
+            return pl.BlockSpec(
+                (2, 1, frames, 2 * HEAD_DIM), lambda c, j, _: (0, c, 0, part * steps + j)
+            )
+
+        scores = clips * steps * 2 * 3 * frames * frames
+        out = pl.pallas_call(
+            self_back_kernel,
+            grid_spec=pltpu.PrefetchScalarGridSpec(
+                num_scalar_prefetch=1,
+                grid=(clips, steps),
+                in_specs=[block(0), block(1), block(2), block(0), block(0)],
+                out_specs=pl.BlockSpec((2, 1, frames, 3 * cols), lambda c, j, _: (0, c, 0, 0)),
+            ),
+            out_shape=jax.ShapeDtypeStruct(view.shape, BF),
+            cost_estimate=pl.CostEstimate(
+                flops=10 * scores * HEAD_DIM,
+                transcendentals=scores,
+                bytes_accessed=4 * view.size + 6 * view.size // 3,
+            ),
+            name="self_back",
+        )(core, view, view, view, log_total, grad.reshape(2, clips, frames, cols))
+        return out.reshape(-1, 3 * cols)
+
+    def cross_specs(self, q, clips, texts):
+        cols = q.shape[-1]
+        steps = cols // (2 * HEAD_DIM)
+        view = q.reshape(2, clips, -1, cols)
+        frames = view.shape[2]
+        wide = pl.BlockSpec((2, 1, frames, 2 * HEAD_DIM), lambda c, j: (0, c, 0, j))
+
+        def block(part):
+            return pl.BlockSpec((1, texts, 2 * HEAD_DIM), lambda c, j: (c, 0, part * steps + j))
+
+        return view, (clips, steps), wide, block, clips * 2 * frames * cols * texts
+
+    def cross_attend(self, q, memory, clips):
+        memory = memory.reshape(clips, -1, memory.shape[-1])
+        view, grid, wide, block, work = self.cross_specs(q, clips, memory.shape[1])
+        out = pl.pallas_call(
+            cross_kernel,
+            grid=grid,
+            in_specs=[wide, block(0), block(1)],
+            out_specs=wide,
+            out_shape=jax.ShapeDtypeStruct(view.shape, BF),
+            cost_estimate=pl.CostEstimate(
+                flops=4 * work, transcendentals=work // HEAD_DIM, bytes_accessed=4 * q.size
+            ),
+            name="cross_attend",
+        )(view, memory, memory)
+        return out.reshape(q.shape), (q, memory)
+
+    def cross_back(self, saved, grad, clips):
+        q, memory = saved
+        texts = memory.shape[1]
+        view, grid, wide, block, work = self.cross_specs(q, clips, texts)
+        dq, dkv = pl.pallas_call(
+            cross_back_kernel,
+            grid=grid,
+            in_specs=[wide, block(0), block(1), wide],
+            out_specs=[
+                wide,
+                pl.BlockSpec((1, texts, memory.shape[-1]), lambda c, j: (c, 0, 0)),
+            ],
+            out_shape=[
+                jax.ShapeDtypeStruct(view.shape, BF),
+                jax.ShapeDtypeStruct(memory.shape, BF),
+            ],
+            cost_estimate=pl.CostEstimate(
+                flops=10 * work, transcendentals=work // HEAD_DIM, bytes_accessed=6 * q.size
+            ),
+            name="cross_back",
+        )(view, memory, memory, grad.reshape(view.shape))
+        return dq.reshape(q.shape), dkv.reshape(-1, memory.shape[-1])
+
+    def feed(self, rows, weight):
+        return feed(rows, weight)
 
     def sum_own(self, left, right, product, clips):
         n = left.shape[0] // 2
@@ -341,24 +688,19 @@
 
     stats0 = norm_stats(values0)
     n1 = comm.spread(norm_apply(values0, stats0, gain[0], shift[0]), clips)
-    qkv = comm.sequence(mm(n1, w_self).astype(BF), clips)
-    q, k, v = qkv[..., :cols], qkv[..., cols : 2 * cols], qkv[..., 2 * cols :]
-    att, log_total = attend(q, k, v)
-    att = comm.unsequence(att)
+    att, self_saved = comm.self_attend(mm(n1, w_self).astype(BF), clips)
     values1 = values0 + comm.sum_own(att, w_so, mm_t, clips)
 
     stats1 = norm_stats(values1)
     n2 = comm.spread(norm_apply(values1, stats1, gain[1], shift[1]), clips)
-    cq = comm.clip_rows(mm(n2, w_cq).astype(BF), clips)
-    memory = mm(text, w_cm).astype(BF).reshape(clips, texts, 2 * cols)
-    ck, cv = memory[..., :cols], memory[..., cols:]
-    cross, chances = cross_attend(cq, ck, cv)
-    cross = comm.unclip_rows(cross)
+    cross, cross_saved = comm.cross_attend(
+        mm(n2, w_cq).astype(BF), mm(text, w_cm).astype(BF), clips
+    )
     values2 = values1 + comm.sum_own(cross, w_co, mm_t, clips)
 
     stats2 = norm_stats(values2)
     n3 = comm.spread(norm_apply(values2, stats2, gain[2], shift[2]), clips)
-    hidden, slope = gelu_pair(mm(n3, w_in))
+    hidden, slope = comm.feed(n3, w_in)
     layer_out = (values2 + comm.sum_own(hidden, w_out, mm_t, clips)).astype(BF)
     layer_out = comm.restore(layer_out).reshape(clips, own_frames, width)
 
@@ -377,10 +719,7 @@
     dv2, gain2, shift2 = norm_back(values2, stats2, gain[2], e3)
     r2 = up.astype(F32) + dv2
     r2_all = comm.spread(r2.astype(BF), clips)
-    dco = comm.clip_rows(mm(r2_all, w_co).astype(BF), clips)
-    dcq, dck, dcv = cross_attend_back(cq, ck, cv, chances, dco)
-    dcq = comm.unclip_rows(dcq)
-    dmem = jnp.concatenate([dck, dcv], axis=-1).reshape(clips * texts, 2 * cols)
+    dcq, dmem = comm.cross_back(cross_saved, mm(r2_all, w_co).astype(BF), clips)
     text_grad = comm.sum_all(mm_t(dmem, w_cm))
     e2 = comm.sum_own(dcq, w_cq, mm_t, clips)
     dv1, gain1, shift1 = norm_back(values1, stats1, gain[1], e2)
@@ -390,9 +729,7 @@
     grad_cq = scatter(comm.scatter_last, n2, dcq)
     grad_cm = scatter(comm.scatter_last, text, dmem)
     grad_so = scatter(comm.scatter_last, r1_all, att)
-    datt = comm.sequence(mm(r1_all, w_so).astype(BF), clips)
-    dq, dk, dvv = attend_back(q, k, v, log_total, datt)
-    dqkv = comm.unsequence(jnp.concatenate([dq, dk, dvv], axis=-1))
+    dqkv = comm.self_back(self_saved, mm(r1_all, w_so).astype(BF), clips)
     grad_self = scatter(comm.scatter_last, n1, dqkv)
     e1 = comm.sum_own(dqkv, w_self, mm_t, clips)
     dv0, gain0, shift0 = norm_back(values0, stats0, gain[0], e1)

time: 1310 us -> 2160 us (1.65)
  Pallas kernels: 0 us -> 1250 us
  matrix products: 460 us -> 266 us
  other arithmetic: 171 us -> 61 us
  local copies, waits for them, and re-layouts: 144 us -> 54.7 us
    pallas_call x0 -> x9, Pallas kernels: none -> 1250 us  [the longest x2 574 us: place(): pl.pallas_call(lambda *refs: place_kernel(*refs, spots=spots), out_shape=...]
    dot_general x11 -> x0, matrix products: 83.5 us -> none  [the longest x1 17.3 us: attend_back(): jnp.einsum('bqhd,bkhd->bhqk', grad, heads(v), preferred_element_type=F32)]
    concatenate x8 -> x1, other arithmetic: 74.9 us -> 3.23 us  [spread(): return jnp.concatenate([rows, self.other(rows)])]
    dot_general x10 -> x9, matrix products: 110 us -> 53.7 us  [mm(): return jnp.dot(left, right, preferred_element_type=F32)]
    dot_general x17, matrix products: 162 us -> 109 us  [mm_t(): lax.dot_general(left, right, (((1,), (1,)), ((), ())), preferred_element_...]
    ppermute x25 -> x27, waiting for transfers between devices: 198 us -> 151 us  [x(): return lax.ppermute(v, 'x', SWAP)]
    convert_element_type x16 -> x0, local copies, waits for them, and re-layouts: 42.1 us -> none  [the longest x12 35.1 us: probs_back(): return (flat(dq).astype(BF), flat(dk).astype(BF), flat(dv).astype(BF))]
    all_gather x2, waiting for transfers between devices: 26.2 us -> 65.3 us  [gather_first(): four = lax.all_gather(shard, 'z', axis=0, tiled=True)]
  transfers between devices with their start and end apart: 78 -> 82, of which waited for: 28 -> 30; matrix products, arithmetic and copies ran while one was open for 56% -> 16% of each run, Pallas kernels for 0% -> 57%
where the time goes in v2:
time: 2160 us
  Pallas kernels  1250 us (58%)
  waiting for transfers between devices  451 us (21%)
  matrix products  266 us (12%)
  starting transfers between devices  61 us (3%)
  other arithmetic  61 us (3%)
  local copies, waits for them, and re-layouts  54.7 us (3%)
    pallas_call x2, Pallas kernels, place(): pl.pallas_call(lambda *refs: place_kernel(*refs, spots=spots), out_shape=...  574 us
    pallas_call x2, Pallas kernels, place_stacked(): pl.pallas_call(place_stacked_kernel, out_shape=jax.ShapeDtypeStruct((four...  574 us
    ppermute x27, waiting for transfers between devices, x(): return lax.ppermute(v, 'x', SWAP)  151 us
    ppermute x27, waiting for transfers between devices, y(): return lax.ppermute(v, 'y', SWAP)  124 us
    dot_general x17, matrix products, mm_t(): lax.dot_general(left, right, (((1,), (1,)), ((), ())), preferred_element_...  109 us
    dot_general x42, matrix products, mm_rows(): lax.dot_general(left, right, (((0,), (0,)), ((), ())), preferred_element_...  103 us
    all_gather x2, waiting for transfers between devices, gather_first(): four = lax.all_gather(shard, 'z', axis=0, tiled=True)  65.3 us
    dot_general x9, matrix products, mm(): return jnp.dot(left, right, preferred_element_type=F32)  53.7 us
  transfers between devices with their start and end apart: 82, of which 30 were waited for; matrix products, arithmetic and copies ran while one was open for 16% of the time, Pallas kernels for 57%

profile of v2, /device:TPU:0, one launch (start us, length us, event | category | flops | bytes accessed | tf_op | source)
XLA Modules:
  0.0 2158.1 jit_solution(14902124264666992190)
XLA Ops:
  24.3 5.8 collective-permute-done.1
  43.1 11.9 all-gather.5.cloned.1.call-done.refs_0_
  62.6 53.4 %all-gather.7.cloned.1.call-done.refs_0_ = bf16[384,3840]{1,0:T(8,128)(2,1)} async-done(((bf16[96,3840]{1,0:T(8,128)(2,1)}), bf16[384,3840]{1,0:T(8,128)(2,1)}) %all-gather.7.cloned.1.call-update) | async-done | bytes 2949136 | tf_op jit(solution)/shard_map/all_gather | solution.py:453
  116.0 3.6 fusion.367
  125.8 48.2 %collective-permute-done.7.refs_3_ = bf16[384,1152]{1,0:T(8,128)(2,1)} collective-permute-done((bf16[384,1152]{1,0:T(8,128)(2,1)}, bf16[384,1152]{1,0:T(8,128)(2,1)}, u32[]{:S(2)}, u32[]{:S(2)}) %collective-permute-start.7) | collective-permute-done | bytes 884768 | tf_op jit(solution)/shard_map/ppermute | solution.py:433
  176.0 215.6 %place.2 = bf16[1536,2304]{1,0:T(8,128)(2,1)} custom-call(bf16[384,2304]{1,0:T(8,128)(2,1)} %all-gather.5.cloned.1.call-done.refs_0_, bf16[384,1152]{1,0:T(8,128)(2,1)} %collective-permute-done.5.refs_1_, bf16[384,1152]{1,0:T(8,128)(2,1)} %collective-permute-done.6.refs_2_, bf16[384,1152]{1,0:T(8,128)(2,1)} %collective-permute-done.7.refs_3_, ...), custom_call_target="tpu_custom_call" | custom-call | tf_op jit(solution)/shard_map/place/pallas_call | solution.py:135
  395.2 13.1 convolution_convert_fusion
  408.3 18.3 self_attend.1
  428.7 30.1 %collective-permute-done.16.refs_6_ = bf16[384,1920]{1,0:T(8,128)(2,1)} collective-permute-done((bf16[384,1920]{1,0:T(8,128)(2,1)}, bf16[384,1920]{1,0:T(8,128)(2,1)}, u32[]{:S(2)}, u32[]{:S(2)}) %collective-permute-start.16) | collective-permute-done | bytes 1474592 | tf_op jit(solution)/shard_map/ppermute | solution.py:430
  458.8 358.5 %place.3 = bf16[1536,3840]{1,0:T(8,128)(2,1)} custom-call(bf16[384,3840]{1,0:T(8,128)(2,1)} %all-gather.7.cloned.1.call-done.refs_0_, bf16[384,1920]{1,0:T(8,128)(2,1)} %collective-permute-done.11.refs_1_, bf16[384,1920]{1,0:T(8,128)(2,1)} %collective-permute-done.12.refs_2_, bf16[384,1920]{1,0:T(8,128)(2,1)} %collective-permute-done.13.refs_3_, ...), custom_call_target="tpu_custom_call" | custom-call | tf_op jit(solution)/shard_map/place/pallas_call | solution.py:135
  817.3 4.3 convolution_convert_fusion.7
  825.4 3.9 fusion.373
  835.4 4.6 fusion.109
  840.0 13.5 cross_attend.1
  855.0 4.3 convolution_convert_fusion.6
  859.4 4.9 fusion.366
  866.0 45.5 %all-gather.9.cloned.1.call-done = bf16[4,384,1536]{2,1,0:T(8,128)(2,1)} async-done(((bf16[4,96,1536]{2,1,0:T(8,128)(2,1)}), bf16[4,384,1536]{2,1,0:T(8,128)(2,1)}) %all-gather.9.cloned.1.call-update) | async-done | bytes 4718608 | tf_op jit(solution)/shard_map/all_gather | solution.py:474
  911.6 4.8 fusion.365
  919.3 4.1 fusion.374
  929.7 287.0 %place_stacked.3 = bf16[1536,3072]{1,0:T(8,128)(2,1)} custom-call(bf16[1536,1536]{1,0:T(8,128)(2,1)} %bitcast.255, bf16[768,1536]{1,0:T(8,128)(2,1)} %bitcast.41.far_a, bf16[768,1536]{1,0:T(8,128)(2,1)} %bitcast.42.far_b), custom_call_target="tpu_custom_call" | custom-call | tf_op jit(solution)/shard_map/place_stacked/pallas_call | solution.py:168
  1216.8 287.0 %place_stacked.2.weight_ref = bf16[1536,3072]{1,0:T(8,128)(2,1)} custom-call(bf16[1536,1536]{1,0:T(8,128)(2,1)} %bitcast.256, bf16[768,1536]{1,0:T(8,128)(2,1)} %bitcast.33.far_a, bf16[768,1536]{1,0:T(8,128)(2,1)} %bitcast.34.far_b), custom_call_target="tpu_custom_call" | custom-call | tf_op jit(solution)/shard_map/place_stacked/pallas_call | solution.py:168
  1507.1 19.8 feed.1
  1526.9 14.0 multiply_convert_fusion
  1541.0 10.1 fusion.61
  1559.2 5.2 convolution_convert_fusion.2
  1564.9 11.9 multiply_reduce_fusion
  1576.9 4.5 fusion.363
  1583.0 36.9 %collective-permute-done.40 = bf16[384,128]{1,0:T(8,128)(2,1)S(1)} collective-permute-done((bf16[384,128]{1,0:T(8,128)(2,1)S(1)}, bf16[384,128]{1,0:T(8,128)(2,1)S(1)}, u32[]{:S(2)}, u32[]{:S(2)}) %collective-permute-start.40) | collective-permute-done | bytes 98336 | tf_op jit(solution)/shard_map/ppermute | solution.py:433
  1621.7 3.9 fusion.81
  1625.6 5.6 add_convert_fusion.1
  1631.2 6.9 fusion.112
  1638.0 17.7 cross_back.1
  1663.2 4.4 convolution_convert_fusion.5
  1678.3 8.6 collective-permute-done.50
  1690.7 32.3 %collective-permute-done.60 = bf16[768,384]{1,0:T(8,128)(2,1)S(1)} collective-permute-done((bf16[768,384]{1,0:T(8,128)(2,1)S(1)}, bf16[768,384]{1,0:T(8,128)(2,1)S(1)}, u32[]{:S(2)}, u32[]{:S(2)}) %collective-permute-start.60) | collective-permute-done | bytes 589856 | tf_op jit(solution)/shard_map/ppermute | solution.py:430
  1725.0 4.0 collective-permute-done.51
  1733.4 6.1 multiply_reduce_fusion.1
  1761.6 7.0 collective-permute-done.57
  1770.9 6.4 fusion.115
  1777.3 30.0 %self_back.1 = bf16[2,2,256,2304]{3,2,1,0:T(8,128)(2,1)} custom-call(s32[1]{0:T(128)} %bitcast.2.core_ref, bf16[2,2,256,2304]{3,2,1,0:T(8,128)(2,1)} %bitcast.238, bf16[2,2,256,2304]{3,2,1,0:T(8,128)(2,1)} %bitcast.239, bf16[2,2,256,2304]{3,2,1,0:T(8,128)(2,1)} %bitcast.240, f32[2,2,256,768]{3,2,1,0:T(8,128)} %get-tuple-element.22.log_ref, ...), custom_call_target="tpu_custom_call" | custom-call | flops 3019898880 | bytes 14155776 | tf_op jit(solution)/shard_map/self_back/pallas_call | solution.py:564
  1807.3 4.1 fusion.364
  1811.4 8.1 convolution_convert_fusion.4
  1831.3 8.7 collective-permute-done.48
  1843.1 10.0 fusion.40
  1866.4 5.5 collective-permute-done.38
  1879.3 3.9 fusion.82
  1887.0 3.6 convolution_convert_fusion.10
  1890.6 3.6 convolution_convert_fusion.11
  1896.5 5.6 convolution_convert_fusion.1
  1904.1 10.3 fusion.58
  1914.5 33.1 %collective-permute-done.67 = bf16[768,1536]{1,0:T(8,128)(2,1)} collective-permute-done((bf16[768,1536]{1,0:T(8,128)(2,1)}, bf16[768,1536]{1,0:T(8,128)(2,1)}, u32[]{:S(2)}, u32[]{:S(2)}) %collective-permute-start.67) | collective-permute-done | bytes 2359328 | tf_op jit(solution)/shard_map/ppermute | solution.py:430
  1947.6 4.0 fusion.79
  1953.7 5.6 add_convert_fusion
  1965.1 4.0 fusion.375
  1969.2 14.8 fusion.56
  1992.8 3.6 convolution_convert_fusion.8
  2006.5 4.5 fusion.39
  2013.7 26.7 %collective-permute-done.44 = bf16[768,1152]{1,0:T(8,128)(2,1)} collective-permute-done((bf16[768,1152]{1,0:T(8,128)(2,1)}, bf16[768,1152]{1,0:T(8,128)(2,1)}, u32[]{:S(2)}, u32[]{:S(2)}) %collective-permute-start.44) | collective-permute-done | bytes 1769504 | tf_op jit(solution)/shard_map/ppermute | solution.py:430
  2044.9 3.7 fusion.30
  2049.5 4.7 fusion.31
  2054.2 9.8 collective-permute-done.45
  2078.2 28.8 %reduce-scatter.20.cloned.1.call-done = bf16[4,96,1536]{2,1,0:T(8,128)(2,1)} async-done(((bf16[4,384,1536]{2,1,0:T(8,128)(2,1)}), bf16[4,96,1536]{2,1,0:T(8,128)(2,1)}) %reduce-scatter.20.cloned.1.call-update) | async-done | bytes 1179664 | tf_op jit(solution)/shard_map/reduce_scatter | solution.py:500
  2112.3 4.5 collective-permute-done.68
  2119.2 28.9 %reduce-scatter.8.cloned.1.call-done = bf16[2,96,1152]{2,1,0:T(8,128)(2,1)} async-done(((bf16[2,384,1152]{2,1,0:T(8,128)(2,1)}), bf16[2,96,1152]{2,1,0:T(8,128)(2,1)}) %reduce-scatter.8.cloned.1.call-update) | async-done | bytes 442384 | tf_op jit(solution)/shard_map/reduce_scatter | solution.py:514
  (501 shorter events, 243.5 us)
Async XLA Ops:
  7.3 47.7 %all-gather.5.cloned.1.call-start = ((), (), s32[]{:S(2)}) async-start(), calls=%async_computation.7 | async-start | bytes 2211840 | tf_op jit(solution)/shard_map/all_gather | solution.py:453
  9.4 106.7 %all-gather.7.cloned.1.call-start = ((), (), s32[]{:S(2)}) async-start(), calls=%async_computation.8 | async-start | bytes 3686400 | tf_op jit(solution)/shard_map/all_gather | solution.py:453
  11.3 848.1 %all-gather.11.cloned.1.call-start = ((), (), s32[]{:S(2)}) async-start(), calls=%async_computation.10 | async-start | bytes 5898240 | tf_op jit(solution)/shard_map/all_gather | solution.py:474
  15.6 20.2 collective-permute-start.26
  17.2 18.7 collective-permute-start.25
  38.1 873.5 %all-gather.9.cloned.1.call-start = ((), (), s32[]{:S(2)}) async-start(), calls=%async_computation.9 | async-start | bytes 5898240 | tf_op jit(solution)/shard_map/all_gather | solution.py:474
  57.7 61.9 %collective-permute-start.5 = (bf16[384,1152]{1,0:T(8,128)(2,1)}, bf16[384,1152]{1,0:T(8,128)(2,1)}, u32[]{:S(2)}, u32[]{:S(2)}) collective-permute-start(bf16[384,1152]{1,0:T(8,128)(2,1)} %get-tuple-element.83), channel_id=1, source_target_pairs={{0,2},{2,0},{1,3},{3,1},{4,6},{6,4},{5,7},{7,5},{8,10},{10,8},{9,1... | collective-permute-start | bytes 2654216 | tf_op jit(solution)/shard_map/ppermute | solution.py:430
  58.8 62.3 %collective-permute-start.6 = (bf16[384,1152]{1,0:T(8,128)(2,1)}, bf16[384,1152]{1,0:T(8,128)(2,1)}, u32[]{:S(2)}, u32[]{:S(2)}) collective-permute-start(bf16[384,1152]{1,0:T(8,128)(2,1)} %get-tuple-element.83), channel_id=1, source_target_pairs={{0,4},{4,0},{1,5},{5,1},{2,6},{6,2},{3,7},{7,3},{8,12},{12,8},{9,1... | collective-permute-start | bytes 2654216 | tf_op jit(solution)/shard_map/ppermute | solution.py:433
  60.0 331.6 %collective-permute-start.4 = (bf16[512,1536]{1,0:T(8,128)(2,1)S(1)}, bf16[512,1536]{1,0:T(8,128)(2,1)S(1)}, u32[]{:S(2)}, u32[]{:S(2)}) collective-permute-start(bf16[512,1536]{1,0:T(8,128)(2,1)S(1)} %fusion.35), channel_id=1, source_target_pairs={{0,1},{1,0},{2,3},{3,2},{4,5},{5,4},{6,7},{7,6},{8,9},{9,8},{10,11... | collective-permute-start | bytes 4718600 | tf_op jit(solution)/shard_map/ppermute | solution.py:436
  60.1 62.5 %collective-permute-start.8 = (bf16[384,1152]{1,0:T(8,128)(2,1)}, bf16[384,1152]{1,0:T(8,128)(2,1)}, u32[]{:S(2)}, u32[]{:S(2)}) collective-permute-start(bf16[384,1152]{1,0:T(8,128)(2,1)} %get-tuple-element.82), channel_id=1, source_target_pairs={{0,2},{2,0},{1,3},{3,1},{4,6},{6,4},{5,7},{7,5},{8,10},{10,8},{9,1... | collective-permute-start | bytes 2654216 | tf_op jit(solution)/shard_map/ppermute | solution.py:430
  61.5 61.7 %collective-permute-start.9 = (bf16[384,1152]{1,0:T(8,128)(2,1)}, bf16[384,1152]{1,0:T(8,128)(2,1)}, u32[]{:S(2)}, u32[]{:S(2)}) collective-permute-start(bf16[384,1152]{1,0:T(8,128)(2,1)} %get-tuple-element.82), channel_id=1, source_target_pairs={{0,4},{4,0},{1,5},{5,1},{2,6},{6,2},{3,7},{7,3},{8,12},{12,8},{9,1... | collective-permute-start | bytes 2654216 | tf_op jit(solution)/shard_map/ppermute | solution.py:433
  119.7 272.6 %collective-permute-start.11 = (bf16[384,1920]{1,0:T(8,128)(2,1)}, bf16[384,1920]{1,0:T(8,128)(2,1)}, u32[]{:S(2)}, u32[]{:S(2)}) collective-permute-start(bf16[384,1920]{1,0:T(8,128)(2,1)} %get-tuple-element.77), channel_id=1, source_target_pairs={{0,2},{2,0},{1,3},{3,1},{4,6},{6,4},{5,7},{7,5},{8,10},{10,8},{9,1... | collective-permute-start | bytes 4423688 | tf_op jit(solution)/shard_map/ppermute | solution.py:430
  121.1 272.6 %collective-permute-start.15 = (bf16[384,1920]{1,0:T(8,128)(2,1)}, bf16[384,1920]{1,0:T(8,128)(2,1)}, u32[]{:S(2)}, u32[]{:S(2)}) collective-permute-start(bf16[384,1920]{1,0:T(8,128)(2,1)} %get-tuple-element.76), channel_id=1, source_target_pairs={{0,4},{4,0},{1,5},{5,1},{2,6},{6,2},{3,7},{7,3},{8,12},{12,8},{9,1... | collective-permute-start | bytes 4423688 | tf_op jit(solution)/shard_map/ppermute | solution.py:433
  122.6 51.4 %collective-permute-start.7 = (bf16[384,1152]{1,0:T(8,128)(2,1)}, bf16[384,1152]{1,0:T(8,128)(2,1)}, u32[]{:S(2)}, u32[]{:S(2)}) collective-permute-start(bf16[384,1152]{1,0:T(8,128)(2,1)} %collective-permute-done.5.refs_1_), channel_id=1, source_target_pairs={{0,4},{4,0},{1,5},{5,1},{2,6},{6,2},{3,7},{7,3},{8,12},{12,8},{9,1... | collective-permute-start | bytes 2654216 | tf_op jit(solution)/shard_map/ppermute | solution.py:433
  123.2 52.3 %collective-permute-start.10 = (bf16[384,1152]{1,0:T(8,128)(2,1)}, bf16[384,1152]{1,0:T(8,128)(2,1)}, u32[]{:S(2)}, u32[]{:S(2)}) collective-permute-start(bf16[384,1152]{1,0:T(8,128)(2,1)} %collective-permute-done.9.refs_5_), channel_id=1, source_target_pairs={{0,2},{2,0},{1,3},{3,1},{4,6},{6,4},{5,7},{7,5},{8,10},{10,8},{9,1... | collective-permute-start | bytes 2654216 | tf_op jit(solution)/shard_map/ppermute | solution.py:430
  174.0 647.6 %collective-permute-start.22 = (bf16[96,1536]{1,0:T(8,128)(2,1)}, bf16[96,1536]{1,0:T(8,128)(2,1)}, u32[]{:S(2)}, u32[]{:S(2)}) collective-permute-start(bf16[96,1536]{1,0:T(8,128)(2,1)} %get-tuple-element.102), channel_id=1, source_target_pairs={{0,4},{4,0},{1,5},{5,1},{2,6},{6,2},{3,7},{7,3},{8,12},{12,8},{9,1... | collective-permute-start | bytes 884744 | tf_op jit(solution)/shard_map/ppermute | solution.py:433
  175.5 252.6 %collective-permute-start.12 = (bf16[384,1920]{1,0:T(8,128)(2,1)}, bf16[384,1920]{1,0:T(8,128)(2,1)}, u32[]{:S(2)}, u32[]{:S(2)}) collective-permute-start(bf16[384,1920]{1,0:T(8,128)(2,1)} %get-tuple-element.77), channel_id=1, source_target_pairs={{0,4},{4,0},{1,5},{5,1},{2,6},{6,2},{3,7},{7,3},{8,12},{12,8},{9,1... | collective-permute-start | bytes 4423688 | tf_op jit(solution)/shard_map/ppermute | solution.py:433
  391.6 37.1 %collective-permute-start.14 = (bf16[384,1920]{1,0:T(8,128)(2,1)}, bf16[384,1920]{1,0:T(8,128)(2,1)}, u32[]{:S(2)}, u32[]{:S(2)}) collective-permute-start(bf16[384,1920]{1,0:T(8,128)(2,1)} %get-tuple-element.76), channel_id=1, source_target_pairs={{0,2},{2,0},{1,3},{3,1},{4,6},{6,4},{5,7},{7,5},{8,10},{10,8},{9,1... | collective-permute-start | bytes 4423688 | tf_op jit(solution)/shard_map/ppermute | solution.py:430
  392.3 36.5 %collective-permute-start.13 = (bf16[384,1920]{1,0:T(8,128)(2,1)}, bf16[384,1920]{1,0:T(8,128)(2,1)}, u32[]{:S(2)}, u32[]{:S(2)}) collective-permute-start(bf16[384,1920]{1,0:T(8,128)(2,1)} %collective-permute-done.11.refs_1_), channel_id=1, source_target_pairs={{0,4},{4,0},{1,5},{5,1},{2,6},{6,2},{3,7},{7,3},{8,12},{12,8},{9,1... | collective-permute-start | bytes 4423688 | tf_op jit(solution)/shard_map/ppermute | solution.py:433
  393.7 65.0 %collective-permute-start.16 = (bf16[384,1920]{1,0:T(8,128)(2,1)}, bf16[384,1920]{1,0:T(8,128)(2,1)}, u32[]{:S(2)}, u32[]{:S(2)}) collective-permute-start(bf16[384,1920]{1,0:T(8,128)(2,1)} %collective-permute-done.15.refs_5_), channel_id=1, source_target_pairs={{0,2},{2,0},{1,3},{3,1},{4,6},{6,4},{5,7},{7,5},{8,10},{10,8},{9,1... | collective-permute-start | bytes 4423688 | tf_op jit(solution)/shard_map/ppermute | solution.py:430
  428.0 393.6 %collective-permute-start.21 = (bf16[96,1536]{1,0:T(8,128)(2,1)}, bf16[96,1536]{1,0:T(8,128)(2,1)}, u32[]{:S(2)}, u32[]{:S(2)}) collective-permute-start(bf16[96,1536]{1,0:T(8,128)(2,1)} %get-tuple-element.103), channel_id=1, source_target_pairs={{0,2},{2,0},{1,3},{3,1},{4,6},{6,4},{5,7},{7,5},{8,10},{10,8},{9,1... | collective-permute-start | bytes 884744 | tf_op jit(solution)/shard_map/ppermute | solution.py:430
  824.0 1165.1 %reduce-scatter.12.cloned.1.call-start = ((), (), s32[]{:S(2)}) async-start(), calls=%async_computation.13 | async-start | bytes 737280 | tf_op jit(solution)/shard_map/reduce_scatter | solution.py:514
  859.3 60.0 %collective-permute-start.19 = (bf16[512,1536]{1,0:T(8,128)(2,1)}, bf16[512,1536]{1,0:T(8,128)(2,1)S(1)}, u32[]{:S(2)}, u32[]{:S(2)}) collective-permute-start(bf16[512,1536]{1,0:T(8,128)(2,1)} %convolution_convert_fusion.6), channel_id=1, source_target_pairs={{0,1},{1,0},{2,3},{3,2},{4,5},{5,4},{6,7},{7,6},{8,9},{9,8},{10,11... | collective-permute-start | bytes 4718600 | tf_op jit(solution)/shard_map/ppermute | solution.py:436
  864.3 64.5 %collective-permute-start.27 = (bf16[2,384,1536]{2,1,0:T(8,128)(2,1)}, bf16[2,384,1536]{2,1,0:T(8,128)(2,1)}, u32[]{:S(2)}, u32[]{:S(2)}) collective-permute-start(bf16[2,384,1536]{2,1,0:T(8,128)(2,1)} %get-tuple-element.75), channel_id=1, source_target_pairs={{0,4},{4,0},{1,5},{5,1},{2,6},{6,2},{3,7},{7,3},{8,12},{12,8},{9,1... | collective-permute-start | bytes 7077896 | tf_op jit(solution)/shard_map/ppermute | solution.py:433
  865.7 63.2 %collective-permute-start.28 = (bf16[2,384,1536]{2,1,0:T(8,128)(2,1)}, bf16[2,384,1536]{2,1,0:T(8,128)(2,1)}, u32[]{:S(2)}, u32[]{:S(2)}) collective-permute-start(bf16[2,384,1536]{2,1,0:T(8,128)(2,1)} %get-tuple-element.74), channel_id=1, source_target_pairs={{0,2},{2,0},{1,3},{3,1},{4,6},{6,4},{5,7},{7,5},{8,10},{10,8},{9,1... | collective-permute-start | bytes 7077896 | tf_op jit(solution)/shard_map/ppermute | solution.py:430
  916.4 300.4 %collective-permute-start.23 = (bf16[2,384,1536]{2,1,0:T(8,128)(2,1)}, bf16[2,384,1536]{2,1,0:T(8,128)(2,1)}, u32[]{:S(2)}, u32[]{:S(2)}) collective-permute-start(bf16[2,384,1536]{2,1,0:T(8,128)(2,1)} %get-tuple-element.73), channel_id=1, source_target_pairs={{0,4},{4,0},{1,5},{5,1},{2,6},{6,2},{3,7},{7,3},{8,12},{12,8},{9,1... | collective-permute-start | bytes 7077896 | tf_op jit(solution)/shard_map/ppermute | solution.py:433
  917.9 298.9 %collective-permute-start.24 = (bf16[2,384,1536]{2,1,0:T(8,128)(2,1)}, bf16[2,384,1536]{2,1,0:T(8,128)(2,1)}, u32[]{:S(2)}, u32[]{:S(2)}) collective-permute-start(bf16[2,384,1536]{2,1,0:T(8,128)(2,1)} %get-tuple-element.72), channel_id=1, source_target_pairs={{0,2},{2,0},{1,3},{3,1},{4,6},{6,4},{5,7},{7,5},{8,10},{10,8},{9,1... | collective-permute-start | bytes 7077896 | tf_op jit(solution)/shard_map/ppermute | solution.py:430
  925.1 578.7 %collective-permute-start.20 = (bf16[512,1536]{1,0:T(8,128)(2,1)S(1)}, bf16[512,1536]{1,0:T(8,128)(2,1)}, u32[]{:S(2)}, u32[]{:S(2)}) collective-permute-start(bf16[512,1536]{1,0:T(8,128)(2,1)S(1)} %add_convert_fusion.2), channel_id=1, source_target_pairs={{0,1},{1,0},{2,3},{3,2},{4,5},{5,4},{6,7},{7,6},{8,9},{9,8},{10,11... | collective-permute-start | bytes 4718600 | tf_op jit(solution)/shard_map/ppermute | solution.py:436
  928.8 598.1 %collective-permute-start.30 = (bf16[512,1536]{1,0:T(8,128)(2,1)S(1)}, bf16[512,1536]{1,0:T(8,128)(2,1)}, u32[]{:S(2)}, u32[]{:S(2)}) collective-permute-start(bf16[512,1536]{1,0:T(8,128)(2,1)S(1)} %fusion.77), channel_id=1, source_target_pairs={{0,1},{1,0},{2,3},{3,2},{4,5},{5,4},{6,7},{7,6},{8,9},{9,8},{10,11... | collective-permute-start | bytes 4718600 | tf_op jit(solution)/shard_map/ppermute | solution.py:436
  929.1 652.3 %collective-permute-start.39 = (bf16[768,128]{1,0:T(8,128)(2,1)S(1)}, bf16[768,128]{1,0:T(8,128)(2,1)S(1)}, u32[]{:S(2)}, u32[]{:S(2)}) collective-permute-start(bf16[768,128]{1,0:T(8,128)(2,1)S(1)} %concatenate.86), channel_id=1, source_target_pairs={{0,2},{2,0},{1,3},{3,1},{4,6},{6,4},{5,7},{7,5},{8,10},{10,8},{9,1... | collective-permute-start | bytes 589832 | tf_op jit(solution)/shard_map/ppermute | solution.py:430
  1557.7 64.0 %collective-permute-start.63 = (bf16[768,1536]{1,0:T(8,128)(2,1)}, bf16[768,1536]{1,0:T(8,128)(2,1)}, u32[]{:S(2)}, u32[]{:S(2)}) collective-permute-start(bf16[768,1536]{1,0:T(8,128)(2,1)} %pad_maximum_fusion.13), channel_id=1, source_target_pairs={{0,2},{2,0},{1,3},{3,1},{4,6},{6,4},{5,7},{7,5},{8,10},{10,8},{9,1... | collective-permute-start | bytes 7077896 | tf_op jit(solution)/shard_map/ppermute | solution.py:430
  1564.4 61.2 %collective-permute-start.62 = (bf16[768,1536]{1,0:T(8,128)(2,1)}, bf16[768,1536]{1,0:T(8,128)(2,1)}, u32[]{:S(2)}, u32[]{:S(2)}) collective-permute-start(bf16[768,1536]{1,0:T(8,128)(2,1)} %convolution_convert_fusion.2), channel_id=1, source_target_pairs={{0,4},{4,0},{1,5},{5,1},{2,6},{6,2},{3,7},{7,3},{8,12},{12,8},{9,1... | collective-permute-start | bytes 7077896 | tf_op jit(solution)/shard_map/ppermute | solution.py:433
  1581.4 49.8 %collective-permute-start.32 = (bf16[512,1536]{1,0:T(8,128)(2,1)S(1)}, bf16[512,1536]{1,0:T(8,128)(2,1)S(1)}, u32[]{:S(2)}, u32[]{:S(2)}) collective-permute-start(bf16[512,1536]{1,0:T(8,128)(2,1)S(1)} %get-tuple-element.68), channel_id=1, source_target_pairs={{0,1},{1,0},{2,3},{3,2},{4,5},{5,4},{6,7},{7,6},{8,9},{9,8},{10,11... | collective-permute-start | bytes 4718600 | tf_op jit(solution)/shard_map/ppermute | solution.py:436
  1581.4 38.4 %collective-permute-start.40 = (bf16[384,128]{1,0:T(8,128)(2,1)S(1)}, bf16[384,128]{1,0:T(8,128)(2,1)S(1)}, u32[]{:S(2)}, u32[]{:S(2)}) collective-permute-start(bf16[384,128]{1,0:T(8,128)(2,1)S(1)} %slice.724), channel_id=1, source_target_pairs={{0,4},{4,0},{1,5},{5,1},{2,6},{6,2},{3,7},{7,3},{8,12},{12,8},{9,1... | collective-permute-start | bytes 294920 | tf_op jit(solution)/shard_map/ppermute | solution.py:433
  1667.6 65.8 %collective-permute-start.33 = (bf16[512,1536]{1,0:T(8,128)(2,1)}, bf16[512,1536]{1,0:T(8,128)(2,1)}, u32[]{:S(2)}, u32[]{:S(2)}) collective-permute-start(bf16[512,1536]{1,0:T(8,128)(2,1)} %convolution_convert_fusion.5), channel_id=1, source_target_pairs={{0,1},{1,0},{2,3},{3,2},{4,5},{5,4},{6,7},{7,6},{8,9},{9,8},{10,11... | collective-permute-start | bytes 4718600 | tf_op jit(solution)/shard_map/ppermute | solution.py:436
  1668.9 20.5 collective-permute-start.52
  1670.7 16.3 collective-permute-start.50
  1672.4 79.6 %collective-permute-start.56 = (bf16[768,768]{1,0:T(8,128)(2,1)}, bf16[768,768]{1,0:T(8,128)(2,1)}, u32[]{:S(2)}, u32[]{:S(2)}) collective-permute-start(bf16[768,768]{1,0:T(8,128)(2,1)} %pad_maximum_fusion.25), channel_id=1, source_target_pairs={{0,2},{2,0},{1,3},{3,1},{4,6},{6,4},{5,7},{7,5},{8,10},{10,8},{9,1... | collective-permute-start | bytes 3538952 | tf_op jit(solution)/shard_map/ppermute | solution.py:430
  1673.7 82.2 %collective-permute-start.54 = (bf16[768,768]{1,0:T(8,128)(2,1)}, bf16[768,768]{1,0:T(8,128)(2,1)}, u32[]{:S(2)}, u32[]{:S(2)}) collective-permute-start(bf16[768,768]{1,0:T(8,128)(2,1)} %convolution_convert_fusion.14), channel_id=1, source_target_pairs={{0,4},{4,0},{1,5},{5,1},{2,6},{6,2},{3,7},{7,3},{8,12},{12,8},{9,1... | collective-permute-start | bytes 3538952 | tf_op jit(solution)/shard_map/ppermute | solution.py:433
  1687.0 36.1 %collective-permute-start.60 = (bf16[768,384]{1,0:T(8,128)(2,1)S(1)}, bf16[768,384]{1,0:T(8,128)(2,1)S(1)}, u32[]{:S(2)}, u32[]{:S(2)}) collective-permute-start(bf16[768,384]{1,0:T(8,128)(2,1)S(1)} %pad_maximum_fusion.33), channel_id=1, source_target_pairs={{0,2},{2,0},{1,3},{3,1},{4,6},{6,4},{5,7},{7,5},{8,10},{10,8},{9,1... | collective-permute-start | bytes 1769480 | tf_op jit(solution)/shard_map/ppermute | solution.py:430
  1689.4 39.6 %collective-permute-start.51 = (bf16[384,384]{1,0:T(8,128)(2,1)S(1)}, bf16[384,384]{1,0:T(8,128)(2,1)S(1)}, u32[]{:S(2)}, u32[]{:S(2)}) collective-permute-start(bf16[384,384]{1,0:T(8,128)(2,1)S(1)} %slice.776), channel_id=1, source_target_pairs={{0,2},{2,0},{1,3},{3,1},{4,6},{6,4},{5,7},{7,5},{8,10},{10,8},{9,1... | collective-permute-start | bytes 884744 | tf_op jit(solution)/shard_map/ppermute | solution.py:430
  1728.9 16.5 collective-permute-start.58
  1731.2 19.3 collective-permute-start.61
  1733.3 256.9 %reduce-scatter.16.cloned.1.call-start = ((), (), s32[]{:S(2)}) async-start(), calls=%async_computation.15 | async-start | bytes 737280 | tf_op jit(solution)/shard_map/reduce_scatter | solution.py:514
  1742.7 28.2 %collective-permute-start.34 = (bf16[512,1536]{1,0:T(8,128)(2,1)}, bf16[512,1536]{1,0:T(8,128)(2,1)}, u32[]{:S(2)}, u32[]{:S(2)}) collective-permute-start(bf16[512,1536]{1,0:T(8,128)(2,1)} %get-tuple-element.66), channel_id=1, source_target_pairs={{0,1},{1,0},{2,3},{3,2},{4,5},{5,4},{6,7},{7,6},{8,9},{9,8},{10,11... | collective-permute-start | bytes 4718600 | tf_op jit(solution)/shard_map/ppermute | solution.py:436
  1755.8 248.8 %reduce-scatter.14.cloned.1.call-start = ((), (), s32[]{:S(2)}) async-start(), calls=%async_computation.14 | async-start | bytes 1474560 | tf_op jit(solution)/shard_map/reduce_scatter | solution.py:514
  1759.7 65.0 %collective-permute-start.55 = (bf16[384,768]{1,0:T(8,128)(2,1)}, bf16[384,768]{1,0:T(8,128)(2,1)}, u32[]{:S(2)}, u32[]{:S(2)}) collective-permute-start(bf16[384,768]{1,0:T(8,128)(2,1)} %slice.794), channel_id=1, source_target_pairs={{0,2},{2,0},{1,3},{3,1},{4,6},{6,4},{5,7},{7,5},{8,10},{10,8},{9,1... | collective-permute-start | bytes 1769480 | tf_op jit(solution)/shard_map/ppermute | solution.py:430
  1819.5 23.6 %collective-permute-start.35 = (bf16[512,1536]{1,0:T(8,128)(2,1)}, bf16[512,1536]{1,0:T(8,128)(2,1)}, u32[]{:S(2)}, u32[]{:S(2)}) collective-permute-start(bf16[512,1536]{1,0:T(8,128)(2,1)} %convolution_convert_fusion.4), channel_id=1, source_target_pairs={{0,1},{1,0},{2,3},{3,2},{4,5},{5,4},{6,7},{7,6},{8,9},{9,8},{10,11... | collective-permute-start | bytes 4718600 | tf_op jit(solution)/shard_map/ppermute | solution.py:436
  1827.0 244.3 %all-reduce.6.cloned.1.call-start = ((), (), s32[]{:S(2)}) async-start(), calls=%async_computation.18 | async-start | bytes 393216
  1830.6 27.4 %collective-permute-start.46 = (bf16[768,384]{1,0:T(8,128)(2,1)}, bf16[768,384]{1,0:T(8,128)(2,1)}, u32[]{:S(2)}, u32[]{:S(2)}) collective-permute-start(bf16[768,384]{1,0:T(8,128)(2,1)} %fusion.177), channel_id=1, source_target_pairs={{0,4},{4,0},{1,5},{5,1},{2,6},{6,2},{3,7},{7,3},{8,12},{12,8},{9,1... | collective-permute-start | bytes 1769480 | tf_op jit(solution)/shard_map/ppermute | solution.py:433
  1842.5 21.3 collective-permute-start.49
  1876.1 196.2 %reduce-scatter.10.cloned.1.call-start = ((), (), s32[]{:S(2)}) async-start(), calls=%async_computation.12 | async-start | bytes 737280 | tf_op jit(solution)/shard_map/reduce_scatter | solution.py:514
  1879.2 196.2 %reduce-scatter.18.cloned.1.call-start = ((), (), s32[]{:S(2)}) async-start(), calls=%async_computation.16 | async-start | bytes 5898240 | tf_op jit(solution)/shard_map/reduce_scatter | solution.py:500
  1886.9 220.0 %reduce-scatter.20.cloned.1.call-start = ((), (), s32[]{:S(2)}) async-start(), calls=%async_computation.17 | async-start | bytes 5898240 | tf_op jit(solution)/shard_map/reduce_scatter | solution.py:500
  1895.8 51.9 %collective-permute-start.67 = (bf16[768,1536]{1,0:T(8,128)(2,1)}, bf16[768,1536]{1,0:T(8,128)(2,1)}, u32[]{:S(2)}, u32[]{:S(2)}) collective-permute-start(bf16[768,1536]{1,0:T(8,128)(2,1)} %pad_maximum_fusion.14), channel_id=1, source_target_pairs={{0,2},{2,0},{1,3},{3,1},{4,6},{6,4},{5,7},{7,5},{8,10},{10,8},{9,1... | collective-permute-start | bytes 7077896 | tf_op jit(solution)/shard_map/ppermute | solution.py:430
  1902.1 51.6 %collective-permute-start.66 = (bf16[768,1536]{1,0:T(8,128)(2,1)}, bf16[768,1536]{1,0:T(8,128)(2,1)}, u32[]{:S(2)}, u32[]{:S(2)}) collective-permute-start(bf16[768,1536]{1,0:T(8,128)(2,1)} %convolution_convert_fusion.1), channel_id=1, source_target_pairs={{0,4},{4,0},{1,5},{5,1},{2,6},{6,2},{3,7},{7,3},{8,12},{12,8},{9,1... | collective-permute-start | bytes 7077896 | tf_op jit(solution)/shard_map/ppermute | solution.py:433
  1914.5 54.7 %collective-permute-start.29 = (bf16[512,1536]{1,0:T(8,128)(2,1)}, bf16[512,1536]{1,0:T(8,128)(2,1)}, u32[]{:S(2)}, u32[]{:S(2)}) collective-permute-start(bf16[512,1536]{1,0:T(8,128)(2,1)} %fusion.58), channel_id=1, source_target_pairs={{0,1},{1,0},{2,3},{3,2},{4,5},{5,4},{6,7},{7,6},{8,9},{9,8},{10,11... | collective-permute-start | bytes 4718600 | tf_op jit(solution)/shard_map/ppermute | solution.py:436
  1964.9 183.3 %reduce-scatter.8.cloned.1.call-start = ((), (), s32[]{:S(2)}) async-start(), calls=%async_computation.11 | async-start | bytes 2211840 | tf_op jit(solution)/shard_map/reduce_scatter | solution.py:514
  1999.1 41.3 %collective-permute-start.44 = (bf16[768,1152]{1,0:T(8,128)(2,1)}, bf16[768,1152]{1,0:T(8,128)(2,1)}, u32[]{:S(2)}, u32[]{:S(2)}) collective-permute-start(bf16[768,1152]{1,0:T(8,128)(2,1)} %pad_maximum_fusion.15), channel_id=1, source_target_pairs={{0,2},{2,0},{1,3},{3,1},{4,6},{6,4},{5,7},{7,5},{8,10},{10,8},{9,1... | collective-permute-start | bytes 5308424 | tf_op jit(solution)/shard_map/ppermute | solution.py:430
  2003.9 41.0 %collective-permute-start.42 = (bf16[768,1152]{1,0:T(8,128)(2,1)}, bf16[768,1152]{1,0:T(8,128)(2,1)}, u32[]{:S(2)}, u32[]{:S(2)}) collective-permute-start(bf16[768,1152]{1,0:T(8,128)(2,1)} %convolution_convert_fusion.3), channel_id=1, source_target_pairs={{0,4},{4,0},{1,5},{5,1},{2,6},{6,2},{3,7},{7,3},{8,12},{12,8},{9,1... | collective-permute-start | bytes 5308424 | tf_op jit(solution)/shard_map/ppermute | solution.py:433
  2042.8 21.2 collective-permute-start.45
  2048.7 21.0 collective-permute-start.43
  2076.6 34.4 %collective-permute-start.64 = (bf16[96,1536]{1,0:T(8,128)(2,1)S(1)}, bf16[96,1536]{1,0:T(8,128)(2,1)S(1)}, u32[]{:S(2)}, u32[]{:S(2)}) collective-permute-start(bf16[96,1536]{1,0:T(8,128)(2,1)S(1)} %get-tuple-element.96), channel_id=1, source_target_pairs={{0,2},{2,0},{1,3},{3,1},{4,6},{6,4},{5,7},{7,5},{8,10},{10,8},{9,1... | collective-permute-start | bytes 884744 | tf_op jit(solution)/shard_map/ppermute | solution.py:430
  2077.4 33.6 %collective-permute-start.65 = (bf16[96,1536]{1,0:T(8,128)(2,1)S(1)}, bf16[96,1536]{1,0:T(8,128)(2,1)S(1)}, u32[]{:S(2)}, u32[]{:S(2)}) collective-permute-start(bf16[96,1536]{1,0:T(8,128)(2,1)S(1)} %get-tuple-element.97), channel_id=1, source_target_pairs={{0,4},{4,0},{1,5},{5,1},{2,6},{6,2},{3,7},{7,3},{8,12},{12,8},{9,1... | collective-permute-start | bytes 884744 | tf_op jit(solution)/shard_map/ppermute | solution.py:433
  (109 other events, 3106.1 us)
Sparse Core Ops, SparseCore 0:
  10.2 44.7 all-gather.4
  57.1 58.9 all-gather.6
  118.2 88.0 all-gather.10
  824.1 87.4 all-gather.8
  1733.4 19.7 reduce-scatter.11
  1755.9 19.9 reduce-scatter.15
  1827.1 26.6 reduce-scatter.13
  1876.3 31.8 all-reduce.5
  1911.0 21.9 reduce-scatter.9
  1935.1 83.6 reduce-scatter.17
  2021.1 85.7 reduce-scatter.19
  2109.1 38.9 reduce-scatter.7

commit v3 on v2

--- a/solution.py
+++ b/solution.py
@@ -136,7 +136,7 @@
         lambda *refs: place_kernel(*refs, spots=spots),
         out_shape=jax.ShapeDtypeStruct(shape, pieces[0][0].dtype),
         in_specs=[ANY] * len(pieces),
-        out_specs=ANY,
+        out_specs=pl.BlockSpec(memory_space=pltpu.VMEM),
         scratch_shapes=[pltpu.SemaphoreType.DMA((len(pieces),))],
         name="place",
     )(*[piece for piece, _, _ in pieces])
@@ -169,7 +169,7 @@
         place_stacked_kernel,
         out_shape=jax.ShapeDtypeStruct((four.shape[0], 2 * four.shape[1]), four.dtype),
         in_specs=[ANY] * 3,
-        out_specs=ANY,
+        out_specs=pl.BlockSpec(memory_space=pltpu.VMEM),
         scratch_shapes=[pltpu.SemaphoreType.DMA((6,))],
         name="place_stacked",
     )(four, far_a, far_b)

time: 2160 us -> 1080 us (0.50)
  Pallas kernels: 1250 us -> 129 us
  waiting for transfers between devices: 451 us -> 487 us
    pallas_call x2, Pallas kernels: 574 us -> 14.6 us  [place_stacked(): pl.pallas_call(place_stacked_kernel, out_shape=jax.ShapeDtypeStruct((four...]
    pallas_call x2, Pallas kernels: 574 us -> 14.8 us  [place(): pl.pallas_call(lambda *refs: place_kernel(*refs, spots=spots), out_shape=...]
    ppermute x27, waiting for transfers between devices: 124 us -> 183 us  [y(): return lax.ppermute(v, 'y', SWAP)]
    ppermute x27, waiting for transfers between devices: 151 us -> 128 us  [x(): return lax.ppermute(v, 'x', SWAP)]
  transfers between devices with their start and end apart: 82 -> 82, of which waited for: 30 -> 33; matrix products, arithmetic and copies ran while one was open for 16% -> 33% of each run, Pallas kernels for 57% -> 10%
where the time goes in v3:
time: 1080 us; the launch traced here: 1070 us
  waiting for transfers between devices  487 us (45%)
  matrix products  266 us (25%)
  Pallas kernels  129 us (12%)
  other arithmetic  61 us (6%)
  starting transfers between devices  60.6 us (6%)
  local copies, waits for them, and re-layouts  54.7 us (5%)
  between operations  16.8 us (2%)
    ppermute x27, waiting for transfers between devices, y(): return lax.ppermute(v, 'y', SWAP)  183 us
    ppermute x27, waiting for transfers between devices, x(): return lax.ppermute(v, 'x', SWAP)  128 us
    dot_general x17, matrix products, mm_t(): lax.dot_general(left, right, (((1,), (1,)), ((), ())), preferred_element_...  109 us
    dot_general x42, matrix products, mm_rows(): lax.dot_general(left, right, (((0,), (0,)), ((), ())), preferred_element_...  103 us
    all_gather x2, waiting for transfers between devices, gather_first(): four = lax.all_gather(shard, 'z', axis=0, tiled=True)  65.3 us
    dot_general x9, matrix products, mm(): return jnp.dot(left, right, preferred_element_type=F32)  53.7 us
    all_gather x2, waiting for transfers between devices, gather_middle(): four = lax.all_gather(four, 'z', axis=1, tiled=True)  45.5 us
    pallas_call x1, Pallas kernels, self_back(): pl.pallas_call(self_back_kernel, grid_spec=pltpu.PrefetchScalarGridSpec(n...  30 us
  transfers between devices with their start and end apart: 82, of which 33 were waited for; matrix products, arithmetic and copies ran while one was open for 33% of the time, Pallas kernels for 10%

profile of v3, /device:TPU:0, one launch (start us, length us, event | category | flops | bytes accessed | tf_op | source)
XLA Modules:
  0.0 1074.5 jit_solution(149300963861940936)
XLA Ops:
  24.3 5.8 collective-permute-done.1
  43.1 11.9 %all-gather.5.cloned.1.call-done.refs_0_ = bf16[384,2304]{1,0:T(8,128)(2,1)} async-done(((bf16[96,2304]{1,0:T(8,128)(2,1)}), bf16[384,2304]{1,0:T(8,128)(2,1)}) %all-gather.5.cloned.1.call-update) | async-done | bytes 1769488 | tf_op jit(solution)/shard_map/all_gather | solution.py:453
  62.6 53.4 %all-gather.7.cloned.1.call-done.refs_0_ = bf16[384,3840]{1,0:T(8,128)(2,1)} async-done(((bf16[96,3840]{1,0:T(8,128)(2,1)}), bf16[384,3840]{1,0:T(8,128)(2,1)}) %all-gather.7.cloned.1.call-update) | async-done | bytes 2949136 | tf_op jit(solution)/shard_map/all_gather | solution.py:453
  116.0 3.6 fusion.367
  125.8 48.2 %collective-permute-done.7.refs_3_ = bf16[384,1152]{1,0:T(8,128)(2,1)} collective-permute-done((bf16[384,1152]{1,0:T(8,128)(2,1)}, bf16[384,1152]{1,0:T(8,128)(2,1)}, u32[]{:S(2)}, u32[]{:S(2)}) %collective-permute-start.7) | collective-permute-done | bytes 884768 | tf_op jit(solution)/shard_map/ppermute | solution.py:433
  176.0 6.0 place.2
  185.6 13.1 %convolution_convert_fusion = bf16[1024,2304]{1,0:T(8,128)(2,1)} fusion(bf16[1536,2304]{1,0:T(8,128)(2,1)} %place.2, bf16[512,1536]{1,0:T(8,128)(2,1)S(1)} %collective-permute-done.4, bf16[512,1536]{1,0:T(8,128)(2,1)S(1)} %fusion.35), kind=kOutput, calls=%fused_computation.10 | convolution fusion | flops 7256408064 | bytes 14942208 | tf_op jit(solution)/shard_map/dot_general | solution.py:19
  198.7 18.3 %self_attend.1 = (bf16[2,2,256,768]{3,2,1,0:T(8,128)(2,1)}, f32[2,2,256,768]{3,2,1,0:T(8,128)}) custom-call(s32[1]{0:T(128)} %bitcast.2.core_ref, bf16[2,2,256,2304]{3,2,1,0:T(8,128)(2,1)} %bitcast.235, bf16[2,2,256,2304]{3,2,1,0:T(8,128)(2,1)} %bitcast.236, bf16[2,2,256,2304]{3,2,1,0:T(8,128)(2,1)} %bitcast.237), custom_call_target="tpu_custom_call" | custom-call | flops 1207959552 | bytes 9437184 | tf_op jit(solution)/shard_map/self_attend/pallas_call | solution.py:534
  219.1 25.8 %collective-permute-done.13.refs_3_ = bf16[384,1920]{1,0:T(8,128)(2,1)} collective-permute-done((bf16[384,1920]{1,0:T(8,128)(2,1)}, bf16[384,1920]{1,0:T(8,128)(2,1)}, u32[]{:S(2)}, u32[]{:S(2)}) %collective-permute-start.13) | collective-permute-done | bytes 1474592 | tf_op jit(solution)/shard_map/ppermute | solution.py:433
  245.0 4.2 collective-permute-done.16.refs_6_
  249.2 8.8 place.3
  258.0 4.3 convolution_convert_fusion.7
  266.1 3.9 fusion.373
  276.1 4.6 fusion.109
  280.7 13.5 %cross_attend.1 = bf16[2,2,256,768]{3,2,1,0:T(8,128)(2,1)} custom-call(bf16[2,2,256,768]{3,2,1,0:T(8,128)(2,1)} %bitcast.277, bf16[2,64,1536]{2,1,0:T(8,128)(2,1)} %bitcast.279, bf16[2,64,1536]{2,1,0:T(8,128)(2,1)} %bitcast.280), custom_call_target="tpu_custom_call" | custom-call | flops 201326592 | bytes 3145728 | tf_op jit(solution)/shard_map/cross_attend/pallas_call | solution.py:597
  295.7 4.3 convolution_convert_fusion.6
  300.1 4.9 fusion.366
  306.8 45.5 %all-gather.9.cloned.1.call-done = bf16[4,384,1536]{2,1,0:T(8,128)(2,1)} async-done(((bf16[4,96,1536]{2,1,0:T(8,128)(2,1)}), bf16[4,384,1536]{2,1,0:T(8,128)(2,1)}) %all-gather.9.cloned.1.call-update) | async-done | bytes 4718608 | tf_op jit(solution)/shard_map/all_gather | solution.py:474
  352.2 4.8 fusion.365
  360.0 4.1 fusion.374
  370.4 7.3 place_stacked.3
  377.7 32.6 %collective-permute-done.23 = bf16[2,384,1536]{2,1,0:T(8,128)(2,1)} collective-permute-done((bf16[2,384,1536]{2,1,0:T(8,128)(2,1)}, bf16[2,384,1536]{2,1,0:T(8,128)(2,1)}, u32[]{:S(2)}, u32[]{:S(2)}) %collective-permute-start.23) | collective-permute-done | bytes 2359328 | tf_op jit(solution)/shard_map/ppermute | solution.py:433
  413.0 7.3 place_stacked.2.weight_ref
  423.5 19.8 %feed.1 = (bf16[1024,3072]{1,0:T(8,128)(2,1)}, bf16[1024,3072]{1,0:T(8,128)(2,1)}) custom-call(bf16[1024,1536]{1,0:T(8,128)(2,1)} %pad_maximum_fusion.2.rows_ref, bf16[1536,3072]{1,0:T(8,128)(2,1)} %place_stacked.2.weight_ref), custom_call_target="tpu_custom_call" | custom-call | flops 9663676416 | bytes 25165824 | tf_op jit(solution)/shard_map/feed/pallas_call | solution.py:307
  443.4 14.0 %multiply_convert_fusion = bf16[1024,3072]{1,0:T(8,128)(2,1)S(1)} fusion(bf16[1024,3072]{1,0:T(8,128)(2,1)} %get-tuple-element.20, bf16[1536,3072]{1,0:T(8,128)(2,1)} %place_stacked.3, bf16[512,1536]{1,0:T(8,128)(2,1)} %collective-permute-done.30, bf16[512,1536]{1,0:T(8,128)(2,1)S(1)} %fusion.77), kind=kOutput, calls=%fused_computation | convolution fusion | flops 9679405056 | bytes 25165824 | tf_op jit(solution)/shard_map/dot_general | solution.py:19
  457.4 10.1 fusion.61
  475.5 5.2 convolution_convert_fusion.2
  481.2 11.9 %multiply_reduce_fusion = (f32[1536]{0:T(1024)}, f32[512]{0:T(512)S(1)}, f32[512]{0:T(512)S(1)}, f32[1536]{0:T(1024)}, f32[512,1536]{1,0:T(8,128)}) fusion(f32[512,1536]{1,0:T(8,128)S(1)} %copy-done.3, f32[512]{0:T(512)S(1)} %add_rsqrt_fusion, f32[512]{0:T(512)S(1)} %broadcast_multiply_fusion.6, f32[1536]{0:T(1024)S(1)} %get-tuple-element.60, ...), kind=kOutput, calls=%fused_computation.147 | convolution fusion | flops 4840484864 | bytes 20475904 | tf_op jit(solution)/shard_map/dot_general | solution.py:23
  493.2 4.5 fusion.363
  499.3 37.1 %collective-permute-done.40 = bf16[384,128]{1,0:T(8,128)(2,1)S(1)} collective-permute-done((bf16[384,128]{1,0:T(8,128)(2,1)S(1)}, bf16[384,128]{1,0:T(8,128)(2,1)S(1)}, u32[]{:S(2)}, u32[]{:S(2)}) %collective-permute-start.40) | collective-permute-done | bytes 98336 | tf_op jit(solution)/shard_map/ppermute | solution.py:433
  538.2 3.9 fusion.81
  542.1 5.6 add_convert_fusion.1
  547.7 6.9 fusion.112
  554.5 17.7 %cross_back.1 = (bf16[2,2,256,768]{3,2,1,0:T(8,128)(2,1)}, bf16[2,64,1536]{2,1,0:T(8,128)(2,1)}) custom-call(bf16[2,2,256,768]{3,2,1,0:T(8,128)(2,1)} %bitcast.278, bf16[2,64,1536]{2,1,0:T(8,128)(2,1)} %bitcast.281, bf16[2,64,1536]{2,1,0:T(8,128)(2,1)} %bitcast.282, bf16[2,2,256,768]{3,2,1,0:T(8,128)(2,1)} %bitcast.294), custom_call_target="tpu_custom_call" | custom-call | flops 503316480 | bytes 4718592 | tf_op jit(solution)/shard_map/cross_back/pallas_call | solution.py:614
  579.7 4.4 convolution_convert_fusion.5
  594.8 8.6 collective-permute-done.50
  607.2 32.3 %collective-permute-done.60 = bf16[768,384]{1,0:T(8,128)(2,1)S(1)} collective-permute-done((bf16[768,384]{1,0:T(8,128)(2,1)S(1)}, bf16[768,384]{1,0:T(8,128)(2,1)S(1)}, u32[]{:S(2)}, u32[]{:S(2)}) %collective-permute-start.60) | collective-permute-done | bytes 589856 | tf_op jit(solution)/shard_map/ppermute | solution.py:430
  641.4 4.0 collective-permute-done.51
  649.9 6.1 multiply_reduce_fusion.1
  678.1 7.0 collective-permute-done.57
  687.4 6.4 fusion.115
  693.7 30.0 %self_back.1 = bf16[2,2,256,2304]{3,2,1,0:T(8,128)(2,1)} custom-call(s32[1]{0:T(128)} %bitcast.2.core_ref, bf16[2,2,256,2304]{3,2,1,0:T(8,128)(2,1)} %bitcast.238, bf16[2,2,256,2304]{3,2,1,0:T(8,128)(2,1)} %bitcast.239, bf16[2,2,256,2304]{3,2,1,0:T(8,128)(2,1)} %bitcast.240, f32[2,2,256,768]{3,2,1,0:T(8,128)} %get-tuple-element.22.log_ref, ...), custom_call_target="tpu_custom_call" | custom-call | flops 3019898880 | bytes 14155776 | tf_op jit(solution)/shard_map/self_back/pallas_call | solution.py:564
  723.8 4.1 fusion.364
  727.8 8.1 convolution_convert_fusion.4
  747.7 8.7 collective-permute-done.48
  759.6 10.0 fusion.40
  782.9 5.5 collective-permute-done.38
  795.8 3.9 fusion.82
  803.5 3.6 convolution_convert_fusion.10
  813.0 5.6 convolution_convert_fusion.1
  820.6 10.4 fusion.58
  831.0 33.2 %collective-permute-done.67 = bf16[768,1536]{1,0:T(8,128)(2,1)} collective-permute-done((bf16[768,1536]{1,0:T(8,128)(2,1)}, bf16[768,1536]{1,0:T(8,128)(2,1)}, u32[]{:S(2)}, u32[]{:S(2)}) %collective-permute-start.67) | collective-permute-done | bytes 2359328 | tf_op jit(solution)/shard_map/ppermute | solution.py:430
  864.1 4.0 fusion.79
  870.2 5.6 add_convert_fusion
  881.6 4.0 fusion.375
  885.6 14.8 %fusion.56 = bf16[512,1536]{1,0:T(8,128)(2,1)} fusion(s32[1536]{0:T(1024)S(1)} %copy-done.70, f32[512,1536]{1,0:T(8,128)} %copy-done.2, bf16[512,1536]{1,0:T(8,128)(2,1)} %collective-permute-done.29, bf16[1536,3072]{1,0:T(8,128)(2,1)} %place_stacked.3, bf16[1024,3072]{1,0:T(8,128)(2,1)} %get-tuple-element.19), kind=kOutput, calls=%fused_computation.164 | convolution fusion | flops 7254048768 | bytes 18880512 | tf_op jit(solution)/shard_map/dot_general | solution.py:23
  923.0 4.5 fusion.39
  930.2 26.6 %collective-permute-done.44 = bf16[768,1152]{1,0:T(8,128)(2,1)} collective-permute-done((bf16[768,1152]{1,0:T(8,128)(2,1)}, bf16[768,1152]{1,0:T(8,128)(2,1)}, u32[]{:S(2)}, u32[]{:S(2)}) %collective-permute-start.44) | collective-permute-done | bytes 1769504 | tf_op jit(solution)/shard_map/ppermute | solution.py:430
  961.4 3.7 fusion.30
  966.0 4.7 fusion.31
  970.7 9.8 collective-permute-done.45
  994.6 28.8 %reduce-scatter.20.cloned.1.call-done = bf16[4,96,1536]{2,1,0:T(8,128)(2,1)} async-done(((bf16[4,384,1536]{2,1,0:T(8,128)(2,1)}), bf16[4,96,1536]{2,1,0:T(8,128)(2,1)}) %reduce-scatter.20.cloned.1.call-update) | async-done | bytes 1179664 | tf_op jit(solution)/shard_map/reduce_scatter | solution.py:500
  1028.8 4.5 collective-permute-done.68
  1035.7 28.9 %reduce-scatter.8.cloned.1.call-done = bf16[2,96,1152]{2,1,0:T(8,128)(2,1)} async-done(((bf16[2,384,1152]{2,1,0:T(8,128)(2,1)}), bf16[2,96,1152]{2,1,0:T(8,128)(2,1)}) %reduce-scatter.8.cloned.1.call-update) | async-done | bytes 442384 | tf_op jit(solution)/shard_map/reduce_scatter | solution.py:514
  (501 shorter events, 253.0 us)
Async XLA Ops:
  7.3 47.7 %all-gather.5.cloned.1.call-start = ((), (), s32[]{:S(2)}) async-start(), calls=%async_computation.7 | async-start | bytes 2211840 | tf_op jit(solution)/shard_map/all_gather | solution.py:453
  9.4 106.7 %all-gather.7.cloned.1.call-start = ((), (), s32[]{:S(2)}) async-start(), calls=%async_computation.8 | async-start | bytes 3686400 | tf_op jit(solution)/shard_map/all_gather | solution.py:453
  11.3 288.8 %all-gather.11.cloned.1.call-start = ((), (), s32[]{:S(2)}) async-start(), calls=%async_computation.10 | async-start | bytes 5898240 | tf_op jit(solution)/shard_map/all_gather | solution.py:474
  15.6 20.2 %collective-permute-start.26 = (bf16[96,1536]{1,0:T(8,128)(2,1)}, bf16[96,1536]{1,0:T(8,128)(2,1)}, u32[]{:S(2)}, u32[]{:S(2)}) collective-permute-start(bf16[96,1536]{1,0:T(8,128)(2,1)} %get-tuple-element.106), channel_id=1, source_target_pairs={{0,4},{4,0},{1,5},{5,1},{2,6},{6,2},{3,7},{7,3},{8,12},{12,8},{9,1... | collective-permute-start | bytes 884744 | tf_op jit(solution)/shard_map/ppermute | solution.py:433
  17.2 18.7 %collective-permute-start.25 = (bf16[96,1536]{1,0:T(8,128)(2,1)}, bf16[96,1536]{1,0:T(8,128)(2,1)}, u32[]{:S(2)}, u32[]{:S(2)}) collective-permute-start(bf16[96,1536]{1,0:T(8,128)(2,1)} %get-tuple-element.107), channel_id=1, source_target_pairs={{0,2},{2,0},{1,3},{3,1},{4,6},{6,4},{5,7},{7,5},{8,10},{10,8},{9,1... | collective-permute-start | bytes 884744 | tf_op jit(solution)/shard_map/ppermute | solution.py:430
  38.1 314.1 %all-gather.9.cloned.1.call-start = ((), (), s32[]{:S(2)}) async-start(), calls=%async_computation.9 | async-start | bytes 5898240 | tf_op jit(solution)/shard_map/all_gather | solution.py:474
  57.7 61.9 %collective-permute-start.5 = (bf16[384,1152]{1,0:T(8,128)(2,1)}, bf16[384,1152]{1,0:T(8,128)(2,1)}, u32[]{:S(2)}, u32[]{:S(2)}) collective-permute-start(bf16[384,1152]{1,0:T(8,128)(2,1)} %get-tuple-element.83), channel_id=1, source_target_pairs={{0,2},{2,0},{1,3},{3,1},{4,6},{6,4},{5,7},{7,5},{8,10},{10,8},{9,1... | collective-permute-start | bytes 2654216 | tf_op jit(solution)/shard_map/ppermute | solution.py:430
  58.8 62.3 %collective-permute-start.6 = (bf16[384,1152]{1,0:T(8,128)(2,1)}, bf16[384,1152]{1,0:T(8,128)(2,1)}, u32[]{:S(2)}, u32[]{:S(2)}) collective-permute-start(bf16[384,1152]{1,0:T(8,128)(2,1)} %get-tuple-element.83), channel_id=1, source_target_pairs={{0,4},{4,0},{1,5},{5,1},{2,6},{6,2},{3,7},{7,3},{8,12},{12,8},{9,1... | collective-permute-start | bytes 2654216 | tf_op jit(solution)/shard_map/ppermute | solution.py:433
  60.0 122.0 %collective-permute-start.4 = (bf16[512,1536]{1,0:T(8,128)(2,1)S(1)}, bf16[512,1536]{1,0:T(8,128)(2,1)S(1)}, u32[]{:S(2)}, u32[]{:S(2)}) collective-permute-start(bf16[512,1536]{1,0:T(8,128)(2,1)S(1)} %fusion.35), channel_id=1, source_target_pairs={{0,1},{1,0},{2,3},{3,2},{4,5},{5,4},{6,7},{7,6},{8,9},{9,8},{10,11... | collective-permute-start | bytes 4718600 | tf_op jit(solution)/shard_map/ppermute | solution.py:436
  60.1 62.5 %collective-permute-start.8 = (bf16[384,1152]{1,0:T(8,128)(2,1)}, bf16[384,1152]{1,0:T(8,128)(2,1)}, u32[]{:S(2)}, u32[]{:S(2)}) collective-permute-start(bf16[384,1152]{1,0:T(8,128)(2,1)} %get-tuple-element.82), channel_id=1, source_target_pairs={{0,2},{2,0},{1,3},{3,1},{4,6},{6,4},{5,7},{7,5},{8,10},{10,8},{9,1... | collective-permute-start | bytes 2654216 | tf_op jit(solution)/shard_map/ppermute | solution.py:430
  61.5 61.7 %collective-permute-start.9 = (bf16[384,1152]{1,0:T(8,128)(2,1)}, bf16[384,1152]{1,0:T(8,128)(2,1)}, u32[]{:S(2)}, u32[]{:S(2)}) collective-permute-start(bf16[384,1152]{1,0:T(8,128)(2,1)} %get-tuple-element.82), channel_id=1, source_target_pairs={{0,4},{4,0},{1,5},{5,1},{2,6},{6,2},{3,7},{7,3},{8,12},{12,8},{9,1... | collective-permute-start | bytes 2654216 | tf_op jit(solution)/shard_map/ppermute | solution.py:433
  119.7 63.0 %collective-permute-start.11 = (bf16[384,1920]{1,0:T(8,128)(2,1)}, bf16[384,1920]{1,0:T(8,128)(2,1)}, u32[]{:S(2)}, u32[]{:S(2)}) collective-permute-start(bf16[384,1920]{1,0:T(8,128)(2,1)} %get-tuple-element.77), channel_id=1, source_target_pairs={{0,2},{2,0},{1,3},{3,1},{4,6},{6,4},{5,7},{7,5},{8,10},{10,8},{9,1... | collective-permute-start | bytes 4423688 | tf_op jit(solution)/shard_map/ppermute | solution.py:430
  121.1 63.0 %collective-permute-start.15 = (bf16[384,1920]{1,0:T(8,128)(2,1)}, bf16[384,1920]{1,0:T(8,128)(2,1)}, u32[]{:S(2)}, u32[]{:S(2)}) collective-permute-start(bf16[384,1920]{1,0:T(8,128)(2,1)} %get-tuple-element.76), channel_id=1, source_target_pairs={{0,4},{4,0},{1,5},{5,1},{2,6},{6,2},{3,7},{7,3},{8,12},{12,8},{9,1... | collective-permute-start | bytes 4423688 | tf_op jit(solution)/shard_map/ppermute | solution.py:433
  122.6 51.4 %collective-permute-start.7 = (bf16[384,1152]{1,0:T(8,128)(2,1)}, bf16[384,1152]{1,0:T(8,128)(2,1)}, u32[]{:S(2)}, u32[]{:S(2)}) collective-permute-start(bf16[384,1152]{1,0:T(8,128)(2,1)} %collective-permute-done.5.refs_1_), channel_id=1, source_target_pairs={{0,4},{4,0},{1,5},{5,1},{2,6},{6,2},{3,7},{7,3},{8,12},{12,8},{9,1... | collective-permute-start | bytes 2654216 | tf_op jit(solution)/shard_map/ppermute | solution.py:433
  123.2 52.3 %collective-permute-start.10 = (bf16[384,1152]{1,0:T(8,128)(2,1)}, bf16[384,1152]{1,0:T(8,128)(2,1)}, u32[]{:S(2)}, u32[]{:S(2)}) collective-permute-start(bf16[384,1152]{1,0:T(8,128)(2,1)} %collective-permute-done.9.refs_5_), channel_id=1, source_target_pairs={{0,2},{2,0},{1,3},{3,1},{4,6},{6,4},{5,7},{7,5},{8,10},{10,8},{9,1... | collective-permute-start | bytes 2654216 | tf_op jit(solution)/shard_map/ppermute | solution.py:430
  174.0 88.4 %collective-permute-start.22 = (bf16[96,1536]{1,0:T(8,128)(2,1)}, bf16[96,1536]{1,0:T(8,128)(2,1)}, u32[]{:S(2)}, u32[]{:S(2)}) collective-permute-start(bf16[96,1536]{1,0:T(8,128)(2,1)} %get-tuple-element.102), channel_id=1, source_target_pairs={{0,4},{4,0},{1,5},{5,1},{2,6},{6,2},{3,7},{7,3},{8,12},{12,8},{9,1... | collective-permute-start | bytes 884744 | tf_op jit(solution)/shard_map/ppermute | solution.py:433
  175.5 43.0 %collective-permute-start.12 = (bf16[384,1920]{1,0:T(8,128)(2,1)}, bf16[384,1920]{1,0:T(8,128)(2,1)}, u32[]{:S(2)}, u32[]{:S(2)}) collective-permute-start(bf16[384,1920]{1,0:T(8,128)(2,1)} %get-tuple-element.77), channel_id=1, source_target_pairs={{0,4},{4,0},{1,5},{5,1},{2,6},{6,2},{3,7},{7,3},{8,12},{12,8},{9,1... | collective-permute-start | bytes 4423688 | tf_op jit(solution)/shard_map/ppermute | solution.py:433
  182.1 37.1 %collective-permute-start.14 = (bf16[384,1920]{1,0:T(8,128)(2,1)}, bf16[384,1920]{1,0:T(8,128)(2,1)}, u32[]{:S(2)}, u32[]{:S(2)}) collective-permute-start(bf16[384,1920]{1,0:T(8,128)(2,1)} %get-tuple-element.76), channel_id=1, source_target_pairs={{0,2},{2,0},{1,3},{3,1},{4,6},{6,4},{5,7},{7,5},{8,10},{10,8},{9,1... | collective-permute-start | bytes 4423688 | tf_op jit(solution)/shard_map/ppermute | solution.py:430
  182.7 62.3 %collective-permute-start.13 = (bf16[384,1920]{1,0:T(8,128)(2,1)}, bf16[384,1920]{1,0:T(8,128)(2,1)}, u32[]{:S(2)}, u32[]{:S(2)}) collective-permute-start(bf16[384,1920]{1,0:T(8,128)(2,1)} %collective-permute-done.11.refs_1_), channel_id=1, source_target_pairs={{0,4},{4,0},{1,5},{5,1},{2,6},{6,2},{3,7},{7,3},{8,12},{12,8},{9,1... | collective-permute-start | bytes 4423688 | tf_op jit(solution)/shard_map/ppermute | solution.py:433
  184.2 65.0 %collective-permute-start.16 = (bf16[384,1920]{1,0:T(8,128)(2,1)}, bf16[384,1920]{1,0:T(8,128)(2,1)}, u32[]{:S(2)}, u32[]{:S(2)}) collective-permute-start(bf16[384,1920]{1,0:T(8,128)(2,1)} %collective-permute-done.15.refs_5_), channel_id=1, source_target_pairs={{0,2},{2,0},{1,3},{3,1},{4,6},{6,4},{5,7},{7,5},{8,10},{10,8},{9,1... | collective-permute-start | bytes 4423688 | tf_op jit(solution)/shard_map/ppermute | solution.py:430
  218.5 43.9 %collective-permute-start.21 = (bf16[96,1536]{1,0:T(8,128)(2,1)}, bf16[96,1536]{1,0:T(8,128)(2,1)}, u32[]{:S(2)}, u32[]{:S(2)}) collective-permute-start(bf16[96,1536]{1,0:T(8,128)(2,1)} %get-tuple-element.103), channel_id=1, source_target_pairs={{0,2},{2,0},{1,3},{3,1},{4,6},{6,4},{5,7},{7,5},{8,10},{10,8},{9,1... | collective-permute-start | bytes 884744 | tf_op jit(solution)/shard_map/ppermute | solution.py:430
  264.7 640.9 %reduce-scatter.12.cloned.1.call-start = ((), (), s32[]{:S(2)}) async-start(), calls=%async_computation.13 | async-start | bytes 737280 | tf_op jit(solution)/shard_map/reduce_scatter | solution.py:514
  300.0 60.0 %collective-permute-start.19 = (bf16[512,1536]{1,0:T(8,128)(2,1)}, bf16[512,1536]{1,0:T(8,128)(2,1)S(1)}, u32[]{:S(2)}, u32[]{:S(2)}) collective-permute-start(bf16[512,1536]{1,0:T(8,128)(2,1)} %convolution_convert_fusion.6), channel_id=1, source_target_pairs={{0,1},{1,0},{2,3},{3,2},{4,5},{5,4},{6,7},{7,6},{8,9},{9,8},{10,11... | collective-permute-start | bytes 4718600 | tf_op jit(solution)/shard_map/ppermute | solution.py:436
  305.0 64.5 %collective-permute-start.27 = (bf16[2,384,1536]{2,1,0:T(8,128)(2,1)}, bf16[2,384,1536]{2,1,0:T(8,128)(2,1)}, u32[]{:S(2)}, u32[]{:S(2)}) collective-permute-start(bf16[2,384,1536]{2,1,0:T(8,128)(2,1)} %get-tuple-element.75), channel_id=1, source_target_pairs={{0,4},{4,0},{1,5},{5,1},{2,6},{6,2},{3,7},{7,3},{8,12},{12,8},{9,1... | collective-permute-start | bytes 7077896 | tf_op jit(solution)/shard_map/ppermute | solution.py:433
  306.4 63.2 %collective-permute-start.28 = (bf16[2,384,1536]{2,1,0:T(8,128)(2,1)}, bf16[2,384,1536]{2,1,0:T(8,128)(2,1)}, u32[]{:S(2)}, u32[]{:S(2)}) collective-permute-start(bf16[2,384,1536]{2,1,0:T(8,128)(2,1)} %get-tuple-element.74), channel_id=1, source_target_pairs={{0,2},{2,0},{1,3},{3,1},{4,6},{6,4},{5,7},{7,5},{8,10},{10,8},{9,1... | collective-permute-start | bytes 7077896 | tf_op jit(solution)/shard_map/ppermute | solution.py:430
  357.1 53.2 %collective-permute-start.23 = (bf16[2,384,1536]{2,1,0:T(8,128)(2,1)}, bf16[2,384,1536]{2,1,0:T(8,128)(2,1)}, u32[]{:S(2)}, u32[]{:S(2)}) collective-permute-start(bf16[2,384,1536]{2,1,0:T(8,128)(2,1)} %get-tuple-element.73), channel_id=1, source_target_pairs={{0,4},{4,0},{1,5},{5,1},{2,6},{6,2},{3,7},{7,3},{8,12},{12,8},{9,1... | collective-permute-start | bytes 7077896 | tf_op jit(solution)/shard_map/ppermute | solution.py:433
  358.5 54.4 %collective-permute-start.24 = (bf16[2,384,1536]{2,1,0:T(8,128)(2,1)}, bf16[2,384,1536]{2,1,0:T(8,128)(2,1)}, u32[]{:S(2)}, u32[]{:S(2)}) collective-permute-start(bf16[2,384,1536]{2,1,0:T(8,128)(2,1)} %get-tuple-element.72), channel_id=1, source_target_pairs={{0,2},{2,0},{1,3},{3,1},{4,6},{6,4},{5,7},{7,5},{8,10},{10,8},{9,1... | collective-permute-start | bytes 7077896 | tf_op jit(solution)/shard_map/ppermute | solution.py:430
  365.8 54.5 %collective-permute-start.20 = (bf16[512,1536]{1,0:T(8,128)(2,1)S(1)}, bf16[512,1536]{1,0:T(8,128)(2,1)}, u32[]{:S(2)}, u32[]{:S(2)}) collective-permute-start(bf16[512,1536]{1,0:T(8,128)(2,1)S(1)} %add_convert_fusion.2), channel_id=1, source_target_pairs={{0,1},{1,0},{2,3},{3,2},{4,5},{5,4},{6,7},{7,6},{8,9},{9,8},{10,11... | collective-permute-start | bytes 4718600 | tf_op jit(solution)/shard_map/ppermute | solution.py:436
  369.5 73.9 %collective-permute-start.30 = (bf16[512,1536]{1,0:T(8,128)(2,1)S(1)}, bf16[512,1536]{1,0:T(8,128)(2,1)}, u32[]{:S(2)}, u32[]{:S(2)}) collective-permute-start(bf16[512,1536]{1,0:T(8,128)(2,1)S(1)} %fusion.77), channel_id=1, source_target_pairs={{0,1},{1,0},{2,3},{3,2},{4,5},{5,4},{6,7},{7,6},{8,9},{9,8},{10,11... | collective-permute-start | bytes 4718600 | tf_op jit(solution)/shard_map/ppermute | solution.py:436
  369.8 127.9 %collective-permute-start.39 = (bf16[768,128]{1,0:T(8,128)(2,1)S(1)}, bf16[768,128]{1,0:T(8,128)(2,1)S(1)}, u32[]{:S(2)}, u32[]{:S(2)}) collective-permute-start(bf16[768,128]{1,0:T(8,128)(2,1)S(1)} %concatenate.86), channel_id=1, source_target_pairs={{0,2},{2,0},{1,3},{3,1},{4,6},{6,4},{5,7},{7,5},{8,10},{10,8},{9,1... | collective-permute-start | bytes 589832 | tf_op jit(solution)/shard_map/ppermute | solution.py:430
  474.0 64.2 %collective-permute-start.63 = (bf16[768,1536]{1,0:T(8,128)(2,1)}, bf16[768,1536]{1,0:T(8,128)(2,1)}, u32[]{:S(2)}, u32[]{:S(2)}) collective-permute-start(bf16[768,1536]{1,0:T(8,128)(2,1)} %pad_maximum_fusion.13), channel_id=1, source_target_pairs={{0,2},{2,0},{1,3},{3,1},{4,6},{6,4},{5,7},{7,5},{8,10},{10,8},{9,1... | collective-permute-start | bytes 7077896 | tf_op jit(solution)/shard_map/ppermute | solution.py:430
  480.7 61.4 %collective-permute-start.62 = (bf16[768,1536]{1,0:T(8,128)(2,1)}, bf16[768,1536]{1,0:T(8,128)(2,1)}, u32[]{:S(2)}, u32[]{:S(2)}) collective-permute-start(bf16[768,1536]{1,0:T(8,128)(2,1)} %convolution_convert_fusion.2), channel_id=1, source_target_pairs={{0,4},{4,0},{1,5},{5,1},{2,6},{6,2},{3,7},{7,3},{8,12},{12,8},{9,1... | collective-permute-start | bytes 7077896 | tf_op jit(solution)/shard_map/ppermute | solution.py:433
  497.7 50.0 %collective-permute-start.32 = (bf16[512,1536]{1,0:T(8,128)(2,1)S(1)}, bf16[512,1536]{1,0:T(8,128)(2,1)S(1)}, u32[]{:S(2)}, u32[]{:S(2)}) collective-permute-start(bf16[512,1536]{1,0:T(8,128)(2,1)S(1)} %get-tuple-element.68), channel_id=1, source_target_pairs={{0,1},{1,0},{2,3},{3,2},{4,5},{5,4},{6,7},{7,6},{8,9},{9,8},{10,11... | collective-permute-start | bytes 4718600 | tf_op jit(solution)/shard_map/ppermute | solution.py:436
  497.7 38.7 %collective-permute-start.40 = (bf16[384,128]{1,0:T(8,128)(2,1)S(1)}, bf16[384,128]{1,0:T(8,128)(2,1)S(1)}, u32[]{:S(2)}, u32[]{:S(2)}) collective-permute-start(bf16[384,128]{1,0:T(8,128)(2,1)S(1)} %slice.724), channel_id=1, source_target_pairs={{0,4},{4,0},{1,5},{5,1},{2,6},{6,2},{3,7},{7,3},{8,12},{12,8},{9,1... | collective-permute-start | bytes 294920 | tf_op jit(solution)/shard_map/ppermute | solution.py:433
  584.1 65.7 %collective-permute-start.33 = (bf16[512,1536]{1,0:T(8,128)(2,1)}, bf16[512,1536]{1,0:T(8,128)(2,1)}, u32[]{:S(2)}, u32[]{:S(2)}) collective-permute-start(bf16[512,1536]{1,0:T(8,128)(2,1)} %convolution_convert_fusion.5), channel_id=1, source_target_pairs={{0,1},{1,0},{2,3},{3,2},{4,5},{5,4},{6,7},{7,6},{8,9},{9,8},{10,11... | collective-permute-start | bytes 4718600 | tf_op jit(solution)/shard_map/ppermute | solution.py:436
  585.4 20.5 %collective-permute-start.52 = (bf16[768,384]{1,0:T(8,128)(2,1)S(1)}, bf16[768,384]{1,0:T(8,128)(2,1)S(1)}, u32[]{:S(2)}, u32[]{:S(2)}) collective-permute-start(bf16[768,384]{1,0:T(8,128)(2,1)S(1)} %pad_maximum_fusion.31), channel_id=1, source_target_pairs={{0,2},{2,0},{1,3},{3,1},{4,6},{6,4},{5,7},{7,5},{8,10},{10,8},{9,1... | collective-permute-start | bytes 1769480 | tf_op jit(solution)/shard_map/ppermute | solution.py:430
  587.2 16.3 %collective-permute-start.50 = (bf16[768,384]{1,0:T(8,128)(2,1)S(1)}, bf16[768,384]{1,0:T(8,128)(2,1)S(1)}, u32[]{:S(2)}, u32[]{:S(2)}) collective-permute-start(bf16[768,384]{1,0:T(8,128)(2,1)S(1)} %fusion.171), channel_id=1, source_target_pairs={{0,4},{4,0},{1,5},{5,1},{2,6},{6,2},{3,7},{7,3},{8,12},{12,8},{9,1... | collective-permute-start | bytes 1769480 | tf_op jit(solution)/shard_map/ppermute | solution.py:433
  588.9 79.6 %collective-permute-start.56 = (bf16[768,768]{1,0:T(8,128)(2,1)}, bf16[768,768]{1,0:T(8,128)(2,1)}, u32[]{:S(2)}, u32[]{:S(2)}) collective-permute-start(bf16[768,768]{1,0:T(8,128)(2,1)} %pad_maximum_fusion.25), channel_id=1, source_target_pairs={{0,2},{2,0},{1,3},{3,1},{4,6},{6,4},{5,7},{7,5},{8,10},{10,8},{9,1... | collective-permute-start | bytes 3538952 | tf_op jit(solution)/shard_map/ppermute | solution.py:430
  590.2 82.2 %collective-permute-start.54 = (bf16[768,768]{1,0:T(8,128)(2,1)}, bf16[768,768]{1,0:T(8,128)(2,1)}, u32[]{:S(2)}, u32[]{:S(2)}) collective-permute-start(bf16[768,768]{1,0:T(8,128)(2,1)} %convolution_convert_fusion.14), channel_id=1, source_target_pairs={{0,4},{4,0},{1,5},{5,1},{2,6},{6,2},{3,7},{7,3},{8,12},{12,8},{9,1... | collective-permute-start | bytes 3538952 | tf_op jit(solution)/shard_map/ppermute | solution.py:433
  603.4 36.1 %collective-permute-start.60 = (bf16[768,384]{1,0:T(8,128)(2,1)S(1)}, bf16[768,384]{1,0:T(8,128)(2,1)S(1)}, u32[]{:S(2)}, u32[]{:S(2)}) collective-permute-start(bf16[768,384]{1,0:T(8,128)(2,1)S(1)} %pad_maximum_fusion.33), channel_id=1, source_target_pairs={{0,2},{2,0},{1,3},{3,1},{4,6},{6,4},{5,7},{7,5},{8,10},{10,8},{9,1... | collective-permute-start | bytes 1769480 | tf_op jit(solution)/shard_map/ppermute | solution.py:430
  605.9 39.6 %collective-permute-start.51 = (bf16[384,384]{1,0:T(8,128)(2,1)S(1)}, bf16[384,384]{1,0:T(8,128)(2,1)S(1)}, u32[]{:S(2)}, u32[]{:S(2)}) collective-permute-start(bf16[384,384]{1,0:T(8,128)(2,1)S(1)} %slice.776), channel_id=1, source_target_pairs={{0,2},{2,0},{1,3},{3,1},{4,6},{6,4},{5,7},{7,5},{8,10},{10,8},{9,1... | collective-permute-start | bytes 884744 | tf_op jit(solution)/shard_map/ppermute | solution.py:430
  645.4 16.5 %collective-permute-start.58 = (bf16[768,384]{1,0:T(8,128)(2,1)}, bf16[768,384]{1,0:T(8,128)(2,1)}, u32[]{:S(2)}, u32[]{:S(2)}) collective-permute-start(bf16[768,384]{1,0:T(8,128)(2,1)} %fusion.174), channel_id=1, source_target_pairs={{0,4},{4,0},{1,5},{5,1},{2,6},{6,2},{3,7},{7,3},{8,12},{12,8},{9,1... | collective-permute-start | bytes 1769480 | tf_op jit(solution)/shard_map/ppermute | solution.py:433
  647.6 19.3 %collective-permute-start.61 = (bf16[384,384]{1,0:T(8,128)(2,1)}, bf16[384,384]{1,0:T(8,128)(2,1)}, u32[]{:S(2)}, u32[]{:S(2)}) collective-permute-start(bf16[384,384]{1,0:T(8,128)(2,1)} %fusion.185), channel_id=1, source_target_pairs={{0,4},{4,0},{1,5},{5,1},{2,6},{6,2},{3,7},{7,3},{8,12},{12,8},{9,1... | collective-permute-start | bytes 884744 | tf_op jit(solution)/shard_map/ppermute | solution.py:433
  649.8 256.9 %reduce-scatter.16.cloned.1.call-start = ((), (), s32[]{:S(2)}) async-start(), calls=%async_computation.15 | async-start | bytes 737280 | tf_op jit(solution)/shard_map/reduce_scatter | solution.py:514
  659.2 28.2 %collective-permute-start.34 = (bf16[512,1536]{1,0:T(8,128)(2,1)}, bf16[512,1536]{1,0:T(8,128)(2,1)}, u32[]{:S(2)}, u32[]{:S(2)}) collective-permute-start(bf16[512,1536]{1,0:T(8,128)(2,1)} %get-tuple-element.66), channel_id=1, source_target_pairs={{0,1},{1,0},{2,3},{3,2},{4,5},{5,4},{6,7},{7,6},{8,9},{9,8},{10,11... | collective-permute-start | bytes 4718600 | tf_op jit(solution)/shard_map/ppermute | solution.py:436
  672.3 248.8 %reduce-scatter.14.cloned.1.call-start = ((), (), s32[]{:S(2)}) async-start(), calls=%async_computation.14 | async-start | bytes 1474560 | tf_op jit(solution)/shard_map/reduce_scatter | solution.py:514
  676.2 64.9 %collective-permute-start.55 = (bf16[384,768]{1,0:T(8,128)(2,1)}, bf16[384,768]{1,0:T(8,128)(2,1)}, u32[]{:S(2)}, u32[]{:S(2)}) collective-permute-start(bf16[384,768]{1,0:T(8,128)(2,1)} %slice.794), channel_id=1, source_target_pairs={{0,2},{2,0},{1,3},{3,1},{4,6},{6,4},{5,7},{7,5},{8,10},{10,8},{9,1... | collective-permute-start | bytes 1769480 | tf_op jit(solution)/shard_map/ppermute | solution.py:430
  736.0 23.6 %collective-permute-start.35 = (bf16[512,1536]{1,0:T(8,128)(2,1)}, bf16[512,1536]{1,0:T(8,128)(2,1)}, u32[]{:S(2)}, u32[]{:S(2)}) collective-permute-start(bf16[512,1536]{1,0:T(8,128)(2,1)} %convolution_convert_fusion.4), channel_id=1, source_target_pairs={{0,1},{1,0},{2,3},{3,2},{4,5},{5,4},{6,7},{7,6},{8,9},{9,8},{10,11... | collective-permute-start | bytes 4718600 | tf_op jit(solution)/shard_map/ppermute | solution.py:436
  743.5 244.4 %all-reduce.6.cloned.1.call-start = ((), (), s32[]{:S(2)}) async-start(), calls=%async_computation.18 | async-start | bytes 393216
  747.1 27.4 %collective-permute-start.46 = (bf16[768,384]{1,0:T(8,128)(2,1)}, bf16[768,384]{1,0:T(8,128)(2,1)}, u32[]{:S(2)}, u32[]{:S(2)}) collective-permute-start(bf16[768,384]{1,0:T(8,128)(2,1)} %fusion.177), channel_id=1, source_target_pairs={{0,4},{4,0},{1,5},{5,1},{2,6},{6,2},{3,7},{7,3},{8,12},{12,8},{9,1... | collective-permute-start | bytes 1769480 | tf_op jit(solution)/shard_map/ppermute | solution.py:433
  759.0 21.3 %collective-permute-start.49 = (bf16[384,384]{1,0:T(8,128)(2,1)}, bf16[384,384]{1,0:T(8,128)(2,1)}, u32[]{:S(2)}, u32[]{:S(2)}) collective-permute-start(bf16[384,384]{1,0:T(8,128)(2,1)} %fusion.181), channel_id=1, source_target_pairs={{0,4},{4,0},{1,5},{5,1},{2,6},{6,2},{3,7},{7,3},{8,12},{12,8},{9,1... | collective-permute-start | bytes 884744 | tf_op jit(solution)/shard_map/ppermute | solution.py:433
  792.6 196.2 %reduce-scatter.10.cloned.1.call-start = ((), (), s32[]{:S(2)}) async-start(), calls=%async_computation.12 | async-start | bytes 737280 | tf_op jit(solution)/shard_map/reduce_scatter | solution.py:514
  795.7 196.2 %reduce-scatter.18.cloned.1.call-start = ((), (), s32[]{:S(2)}) async-start(), calls=%async_computation.16 | async-start | bytes 5898240 | tf_op jit(solution)/shard_map/reduce_scatter | solution.py:500
  803.4 220.0 %reduce-scatter.20.cloned.1.call-start = ((), (), s32[]{:S(2)}) async-start(), calls=%async_computation.17 | async-start | bytes 5898240 | tf_op jit(solution)/shard_map/reduce_scatter | solution.py:500
  812.3 51.9 %collective-permute-start.67 = (bf16[768,1536]{1,0:T(8,128)(2,1)}, bf16[768,1536]{1,0:T(8,128)(2,1)}, u32[]{:S(2)}, u32[]{:S(2)}) collective-permute-start(bf16[768,1536]{1,0:T(8,128)(2,1)} %pad_maximum_fusion.14), channel_id=1, source_target_pairs={{0,2},{2,0},{1,3},{3,1},{4,6},{6,4},{5,7},{7,5},{8,10},{10,8},{9,1... | collective-permute-start | bytes 7077896 | tf_op jit(solution)/shard_map/ppermute | solution.py:430
  818.6 51.6 %collective-permute-start.66 = (bf16[768,1536]{1,0:T(8,128)(2,1)}, bf16[768,1536]{1,0:T(8,128)(2,1)}, u32[]{:S(2)}, u32[]{:S(2)}) collective-permute-start(bf16[768,1536]{1,0:T(8,128)(2,1)} %convolution_convert_fusion.1), channel_id=1, source_target_pairs={{0,4},{4,0},{1,5},{5,1},{2,6},{6,2},{3,7},{7,3},{8,12},{12,8},{9,1... | collective-permute-start | bytes 7077896 | tf_op jit(solution)/shard_map/ppermute | solution.py:433
  831.0 54.7 %collective-permute-start.29 = (bf16[512,1536]{1,0:T(8,128)(2,1)}, bf16[512,1536]{1,0:T(8,128)(2,1)}, u32[]{:S(2)}, u32[]{:S(2)}) collective-permute-start(bf16[512,1536]{1,0:T(8,128)(2,1)} %fusion.58), channel_id=1, source_target_pairs={{0,1},{1,0},{2,3},{3,2},{4,5},{5,4},{6,7},{7,6},{8,9},{9,8},{10,11... | collective-permute-start | bytes 4718600 | tf_op jit(solution)/shard_map/ppermute | solution.py:436
  881.3 183.3 %reduce-scatter.8.cloned.1.call-start = ((), (), s32[]{:S(2)}) async-start(), calls=%async_computation.11 | async-start | bytes 2211840 | tf_op jit(solution)/shard_map/reduce_scatter | solution.py:514
  915.5 41.3 %collective-permute-start.44 = (bf16[768,1152]{1,0:T(8,128)(2,1)}, bf16[768,1152]{1,0:T(8,128)(2,1)}, u32[]{:S(2)}, u32[]{:S(2)}) collective-permute-start(bf16[768,1152]{1,0:T(8,128)(2,1)} %pad_maximum_fusion.15), channel_id=1, source_target_pairs={{0,2},{2,0},{1,3},{3,1},{4,6},{6,4},{5,7},{7,5},{8,10},{10,8},{9,1... | collective-permute-start | bytes 5308424 | tf_op jit(solution)/shard_map/ppermute | solution.py:430
  920.4 41.0 %collective-permute-start.42 = (bf16[768,1152]{1,0:T(8,128)(2,1)}, bf16[768,1152]{1,0:T(8,128)(2,1)}, u32[]{:S(2)}, u32[]{:S(2)}) collective-permute-start(bf16[768,1152]{1,0:T(8,128)(2,1)} %convolution_convert_fusion.3), channel_id=1, source_target_pairs={{0,4},{4,0},{1,5},{5,1},{2,6},{6,2},{3,7},{7,3},{8,12},{12,8},{9,1... | collective-permute-start | bytes 5308424 | tf_op jit(solution)/shard_map/ppermute | solution.py:433
  959.3 21.2 %collective-permute-start.45 = (bf16[384,1152]{1,0:T(8,128)(2,1)S(1)}, bf16[384,1152]{1,0:T(8,128)(2,1)S(1)}, u32[]{:S(2)}, u32[]{:S(2)}) collective-permute-start(bf16[384,1152]{1,0:T(8,128)(2,1)S(1)} %fusion.69), channel_id=1, source_target_pairs={{0,4},{4,0},{1,5},{5,1},{2,6},{6,2},{3,7},{7,3},{8,12},{12,8},{9,1... | collective-permute-start | bytes 2654216 | tf_op jit(solution)/shard_map/ppermute | solution.py:433
  965.2 21.0 %collective-permute-start.43 = (bf16[384,1152]{1,0:T(8,128)(2,1)S(1)}, bf16[384,1152]{1,0:T(8,128)(2,1)S(1)}, u32[]{:S(2)}, u32[]{:S(2)}) collective-permute-start(bf16[384,1152]{1,0:T(8,128)(2,1)S(1)} %slice.734), channel_id=1, source_target_pairs={{0,2},{2,0},{1,3},{3,1},{4,6},{6,4},{5,7},{7,5},{8,10},{10,8},{9,1... | collective-permute-start | bytes 2654216 | tf_op jit(solution)/shard_map/ppermute | solution.py:430
  993.1 34.4 %collective-permute-start.64 = (bf16[96,1536]{1,0:T(8,128)(2,1)S(1)}, bf16[96,1536]{1,0:T(8,128)(2,1)S(1)}, u32[]{:S(2)}, u32[]{:S(2)}) collective-permute-start(bf16[96,1536]{1,0:T(8,128)(2,1)S(1)} %get-tuple-element.96), channel_id=1, source_target_pairs={{0,2},{2,0},{1,3},{3,1},{4,6},{6,4},{5,7},{7,5},{8,10},{10,8},{9,1... | collective-permute-start | bytes 884744 | tf_op jit(solution)/shard_map/ppermute | solution.py:430
  993.9 33.6 %collective-permute-start.65 = (bf16[96,1536]{1,0:T(8,128)(2,1)S(1)}, bf16[96,1536]{1,0:T(8,128)(2,1)S(1)}, u32[]{:S(2)}, u32[]{:S(2)}) collective-permute-start(bf16[96,1536]{1,0:T(8,128)(2,1)S(1)} %get-tuple-element.97), channel_id=1, source_target_pairs={{0,4},{4,0},{1,5},{5,1},{2,6},{6,2},{3,7},{7,3},{8,12},{12,8},{9,1... | collective-permute-start | bytes 884744 | tf_op jit(solution)/shard_map/ppermute | solution.py:433
  (109 other events, 1778.3 us)
Sparse Core Ops, SparseCore 0:
  10.2 44.7 all-gather.4
  57.1 58.9 all-gather.6
  118.2 88.0 all-gather.10
  264.9 87.3 all-gather.8
  649.9 19.7 reduce-scatter.11
  672.4 19.9 reduce-scatter.15
  743.6 26.6 reduce-scatter.13
  792.8 31.7 all-reduce.5
  827.4 21.9 reduce-scatter.9
  851.6 83.5 reduce-scatter.17
  937.5 85.7 reduce-scatter.19
  1025.6 38.9 reduce-scatter.7

commit v4 on v3

--- a/solution.py
+++ b/solution.py
@@ -25,6 +25,10 @@
 
 def mm_rows(left, right):
     return lax.dot_general(left, right, (((0,), (0,)), ((), ())), preferred_element_type=F32)
+
+
+def tie(value, *others):
+    return lax.optimization_barrier((value, others))[0]
 
 
 def norm_stats(values):
@@ -322,6 +326,42 @@
     )(rows, weight)
 
 
+def slope_kernel(rows_ref, weight_ref, slope_ref, out_ref):
+    step = 256
+
+    def body(i, carry):
+        at = pl.ds(pl.multiple_of(i * step, step), step)
+        grad = mm(rows_ref[at], weight_ref[...])
+        out_ref[at] = (grad * slope_ref[at].astype(F32)).astype(BF)
+        return carry
+
+    lax.fori_loop(0, rows_ref.shape[0] // step, body, 0, unroll=True)
+
+
+def slope_product(rows, weight, slope):
+    count, depth = rows.shape
+    width = weight.shape[1]
+    block = 256
+    tall = pl.BlockSpec((count, block), lambda j: (0, j))
+    return pl.pallas_call(
+        slope_kernel,
+        grid=(width // block,),
+        in_specs=[
+            pl.BlockSpec((count, depth), lambda j: (0, 0)),
+            pl.BlockSpec((depth, block), lambda j: (0, j)),
+            tall,
+        ],
+        out_specs=tall,
+        out_shape=jax.ShapeDtypeStruct((count, width), BF),
+        cost_estimate=pl.CostEstimate(
+            flops=2 * count * depth * width,
+            transcendentals=0,
+            bytes_accessed=2 * (count * depth + depth * width + 2 * count * width),
+        ),
+        name="slope_product",
+    )(rows, weight, slope)
+
+
 class Whole:
     def __init__(self, dp, tensor):
         self.dp, self.tensor = dp, tensor
@@ -338,13 +378,61 @@
     def gather_first(self, shard):
         return lax.all_gather(shard, self.dp, axis=0, tiled=True)
 
-    gather_middle = gather_first
-
-    def scatter_last(self, make):
-        whole = make(slice(None), slice(None)).astype(BF)
-        return lax.psum_scatter(whole, self.dp, scatter_dimension=0, tiled=True).astype(F32)
-
-    scatter_middle = scatter_last
+    def gather_weights(self, *sets_and_rows):
+        *sets, rows = sets_and_rows
+        *first, last = [self.gather_first(shard) for shard in sets]
+        return *first, rows, None, None, (last, None)
+
+    def feed_out(self, pieces):
+        return pieces[0]
+
+    def after(self, value, *others):
+        return value
+
+    def stage(self, work, *values):
+        return work(*values)
+
+    def sends(self, left, right):
+        return ()
+
+    def exchange(self, sends):
+        return ()
+
+    def merged(self, *sends):
+        return ()
+
+    def parted(self, far, *widths):
+        return [()] * len(widths)
+
+    def adds(self, *products):
+        wholes = [mm_rows(left, right).astype(BF) for left, right, _ in products]
+        return jnp.concatenate(wholes, axis=1)
+
+    def second(self, whole):
+        return ()
+
+    def closing(self, whole, far):
+        return whole
+
+    middle = closing
+
+    def scatter_z(self, whole):
+        return lax.psum_scatter(whole, self.dp, scatter_dimension=0, tiled=True)
+
+    def close_middle(self, whole):
+        return whole.astype(F32)
+
+    def close_last(self, whole, *widths):
+        found, at = [], 0
+        for columns in widths:
+            found.append(whole[:, at : at + columns].astype(F32))
+            at += columns
+        return found
+
+    def norm_sums(self, sums):
+        sums = jnp.pad(sums.T, ((0, 0), (0, 122))).astype(BF)
+        sums = lax.psum_scatter(sums, self.dp, scatter_dimension=0, tiled=True)
+        return self.sum_all(sums)[:, :6].T
 
     def spread(self, rows, clips):
         local = rows.reshape(clips, -1, rows.shape[-1])
@@ -387,6 +475,9 @@
     def feed(self, rows, weight):
         return gelu_pair(mm(rows, weight))
 
+    def slope_product(self, rows, weight, slope):
+        return (mm(rows, weight) * slope.astype(F32)).astype(BF)
+
     def sum_own(self, left, right, product, clips):
         part = product(left, right).astype(BF).reshape(clips, -1, right_width(product, right))
         own = lax.psum_scatter(part, self.tensor, scatter_dimension=1, tiled=True)
@@ -405,6 +496,9 @@
         self.width = width
         self.shard = width // 16
         self.core = lax.axis_index("core")
+
+    def after(self, value, *others):
+        return tie(value, others)
 
     def order(self):
         own_y, own_x = lax.axis_index("y"), lax.axis_index("x")
@@ -449,70 +543,129 @@
         half = shard.shape[1] // 256 * 128
         return shard[:, :half], shard[:, half:]
 
-    def gather_first(self, shard):
-        four = lax.all_gather(shard, "z", axis=0, tiled=True)
-        a, b = self.halves(four)
-        n, half = a.shape
-        xa, yb, ya, xb = self.x(a), self.y(b), self.y(a), self.x(b)
-        far_a, far_b = self.y(xa), self.x(yb)
-        return place(
-            [
-                (four, 0, 0),
-                (xa, n, 0),
-                (ya, 2 * n, 0),
-                (far_a, 3 * n, 0),
-                (xb, n, half),
-                (yb, 2 * n, half),
-                (far_b, 3 * n, half),
-            ],
-            (4 * n, shard.shape[1]),
+    def gather_weights(self, first, second, feed_in, feed_out, rows):
+        opened = []
+        for shard in (feed_in, feed_out):
+            a, b = self.halves(shard)
+            opened.append(jnp.stack([a, self.x(a), b, self.y(b)]))
+        rows, opened = lax.optimization_barrier((rows, opened))
+        sets = [lax.all_gather(shard, "z", axis=0, tiled=True) for shard in (first, second)]
+        feeds = [lax.all_gather(four, "z", axis=1, tiled=True) for four in opened]
+        whole, last = [], rows
+        in_sides = feeds[0][:2], feeds[0][2:]
+        for four, ahead in zip(sets, ((), in_sides)):
+            a, b = self.halves(tie(four, last))
+            n, half = a.shape
+            xa, yb, ya, xb = self.x(a), self.y(b), self.y(a), self.x(b)
+            far_a, far_b = self.y(xa), self.x(yb)
+            last, before = (far_a, far_b, ya, xb), (xa, yb)
+            four = tie(four, ahead)
+            whole.append(
+                place(
+                    [
+                        (four, 0, 0),
+                        (xa, n, 0),
+                        (ya, 2 * n, 0),
+                        (far_a, 3 * n, 0),
+                        (xb, n, half),
+                        (yb, 2 * n, half),
+                        (far_b, 3 * n, half),
+                    ],
+                    (4 * n, four.shape[1]),
+                )
+            )
+        a, b = tie(in_sides, before)
+        in_far = self.y(a), self.x(b)
+        whole.append(self.place_feed(feeds[0], in_far))
+        out_sides = feeds[1][:2], feeds[1][2:]
+        a, b = tie(out_sides, in_far)
+        return *whole, rows, in_far, out_sides, (feeds[1], (self.y(a), self.x(b)))
+
+    def place_feed(self, four, far):
+        _, n, half = four.shape
+        return place_stacked(
+            four.reshape(4 * n, half), far[0].reshape(2 * n, half), far[1].reshape(2 * n, half)
         )
 
-    def gather_middle(self, shard):
-        a, b = self.halves(shard)
-        four = jnp.stack([a, self.x(a), b, self.y(b)])
-        four = lax.all_gather(four, "z", axis=1, tiled=True)
-        _, n, half = four.shape
-        far_a, far_b = self.y(four[:2]), self.x(four[2:])
-        four = four.reshape(4 * n, half)
-        far_a, far_b = far_a.reshape(2 * n, half), far_b.reshape(2 * n, half)
-        return place_stacked(four, far_a, far_b)
-
-    def scatter_open(self, make, columns):
-        n = self.width // 4
-        half = columns // 256 * 128
-        left, right = slice(0, half), slice(half, columns)
-        far_left = self.y(make(slice(2 * n, 4 * n), left).astype(BF))
-        far_right = self.x(
-            jnp.concatenate(
-                [make(slice(n, 2 * n), right).astype(BF), make(slice(3 * n, 4 * n), right).astype(BF)]
-            )
+    def feed_out(self, pieces):
+        return self.place_feed(*pieces)
+
+    def stage(self, work, *values):
+        shapes = jax.eval_shape(work, *values)
+
+        def nothing(*_):
+            return jax.tree.map(lambda leaf: jnp.zeros(leaf.shape, leaf.dtype), shapes)
+
+        return lax.cond(self.core < 2, work, nothing, *values)
+
+    def sends(self, left, right):
+        n, half = self.width // 4, right.shape[1] // 256 * 128
+        far = jnp.concatenate([left[:, n : 2 * n], left[:, 3 * n :]], axis=1)
+        return (
+            mm_rows(left[:, 2 * n :], right[:, :half]).astype(BF),
+            mm_rows(far, right[:, half:]).astype(BF),
         )
-        a = (make(slice(0, 2 * n), left) + far_left.astype(F32)).astype(BF)
-        b = [
-            (make(slice(0, n), right) + far_right[:n].astype(F32)).astype(BF),
-            (make(slice(2 * n, 3 * n), right) + far_right[n:].astype(F32)).astype(BF),
-        ]
-        return a[:n], a[n:], b[0], b[1]
-
-    def scatter_middle(self, make, columns):
-        four = jnp.stack(self.scatter_open(make, columns))
-        four = lax.psum_scatter(four, "z", scatter_dimension=1, tiled=True)
+
+    def exchange(self, sends):
+        return self.y(sends[0]), self.x(sends[1])
+
+    def merged(self, *sends):
+        return [jnp.concatenate(side, axis=1) for side in zip(*sends)]
+
+    def parted(self, far, *widths):
+        halves = [width // 256 * 128 for width in widths]
+        ends = [sum(halves[: i + 1]) for i in range(len(halves) - 1)]
+        lefts = jnp.split(far[0], ends, axis=1)
+        halves = [width - half for width, half in zip(widths, halves)]
+        ends = [sum(halves[: i + 1]) for i in range(len(halves) - 1)]
+        return list(zip(lefts, jnp.split(far[1], ends, axis=1)))
+
+    def adds(self, *products):
+        n, parts = self.width // 4, []
+        for left, right, (far_y, far_x) in products:
+            half = right.shape[1] // 256 * 128
+            first = (mm_rows(left[:, : 2 * n], right[:, :half]) + far_y.astype(F32)).astype(BF)
+            near = jnp.concatenate([left[:, :n], left[:, 2 * n : 3 * n]], axis=1)
+            last = (mm_rows(near, right[:, half:]) + far_x.astype(F32)).astype(BF)
+            parts.append((first[:n], first[n:], last[:n], last[n:]))
+        return [jnp.concatenate(part, axis=1) for part in zip(*parts)]
+
+    def middle(self, parts, _):
+        return jnp.stack(parts)
+
+    def second(self, parts):
+        return self.x(parts[1]), self.y(parts[3])
+
+    def closing(self, parts, far):
+        pairs = zip((parts[0], parts[2]), far)
+        return jnp.stack([(own.astype(F32) + other.astype(F32)).astype(BF) for own, other in pairs])
+
+    def scatter_z(self, parts):
+        return lax.psum_scatter(parts, "z", scatter_dimension=1, tiled=True)
+
+    def close_middle(self, four):
         left = four[0].astype(F32) + self.x(four[1]).astype(F32)
         right = four[2].astype(F32) + self.y(four[3]).astype(F32)
         return jnp.concatenate([left, right], axis=1)
 
-    def scatter_last(self, make, columns):
-        a0, a1, b0, b1 = self.scatter_open(make, columns)
-        far_a, far_b = self.x(a1), self.y(b1)
-        both = jnp.stack(
-            [
-                (a0.astype(F32) + far_a.astype(F32)).astype(BF),
-                (b0.astype(F32) + far_b.astype(F32)).astype(BF),
-            ]
-        )
-        both = lax.psum_scatter(both, "z", scatter_dimension=1, tiled=True).astype(F32)
-        return jnp.concatenate([both[0], both[1]], axis=1)
+    def close_last(self, both, *widths):
+        found, left, right = [], 0, 0
+        for columns in widths:
+            a = columns // 256 * 128
+            b = columns - a
+            found.append(
+                jnp.concatenate([both[0, :, left : left + a], both[1, :, right : right + b]], axis=1)
+            )
+            left, right = left + a, right + b
+        return [part.astype(F32) for part in found]
+
+    def norm_sums(self, sums):
+        n = self.width // 4
+        sums = self.sum_all(jnp.pad(sums.T, ((0, 0), (0, 122))))
+        sums = sums[: 2 * n] + self.y(sums[2 * n :].astype(BF)).astype(F32)
+        sums = sums[:n] + self.x(sums[n:].astype(BF)).astype(F32)
+        sums = lax.psum_scatter(sums.astype(BF), "z", scatter_dimension=0, tiled=True)
+        return sums[:, :6].T.astype(F32)
 
     def spread(self, rows, clips):
         return jnp.concatenate([rows, self.other(rows)])
@@ -633,6 +786,9 @@
     def feed(self, rows, weight):
         return feed(rows, weight)
 
+    def slope_product(self, rows, weight, slope):
+        return slope_product(rows, weight, slope)
+
     def sum_own(self, left, right, product, clips):
         n = left.shape[0] // 2
         far = self.other(product(left[n:], right).astype(BF))
@@ -674,78 +830,148 @@
     second_set = catenate(
         [self_output.T, cross_query, cross_memory[0], cross_memory[1], cross_output.T]
     )
-    w_self = comm.gather_first(first_set)
-    w_cross = comm.gather_first(second_set)
-    w_in = comm.gather_middle(feed_input)
-    w_out = comm.gather_middle(feed_output.T)
-    w_so, w_cq = w_cross[:, :cols], w_cross[:, cols : 2 * cols]
-    w_cm, w_co = w_cross[:, 2 * cols : 4 * cols], w_cross[:, 4 * cols :]
-
     values0 = comm.arrange(frames.reshape(own_rows, width)).astype(F32)
+    stats0 = norm_stats(values0)
+    own_n1 = norm_apply(values0, stats0, gain[0], shift[0])
+    w_self, w_cross, w_in, own_n1, mark_in, mark_out, out_pieces = comm.gather_weights(
+        first_set, second_set, feed_input, feed_output.T, own_n1
+    )
+
+    def split_cross(weights):
+        return jnp.split(weights, [cols, 2 * cols, 4 * cols], axis=1)
+
+
     up = comm.arrange(upstream.reshape(own_rows, width))
     text = comm.arrange(text_states.reshape(clips * texts, width))
     up_all = comm.spread(up, clips)
 
-    stats0 = norm_stats(values0)
-    n1 = comm.spread(norm_apply(values0, stats0, gain[0], shift[0]), clips)
+    n1 = comm.spread(own_n1, clips)
     att, self_saved = comm.self_attend(mm(n1, w_self).astype(BF), clips)
-    values1 = values0 + comm.sum_own(att, w_so, mm_t, clips)
-
-    stats1 = norm_stats(values1)
-    n2 = comm.spread(norm_apply(values1, stats1, gain[1], shift[1]), clips)
-    cross, cross_saved = comm.cross_attend(
-        mm(n2, w_cq).astype(BF), mm(text, w_cm).astype(BF), clips
-    )
-    values2 = values1 + comm.sum_own(cross, w_co, mm_t, clips)
-
-    stats2 = norm_stats(values2)
-    n3 = comm.spread(norm_apply(values2, stats2, gain[2], shift[2]), clips)
+
+    def stage0(values0, att, w_cross, text):
+        w_so, w_cq, w_cm, w_co = split_cross(w_cross)
+        values1 = values0 + comm.sum_own(att, w_so, mm_t, clips)
+        stats1 = norm_stats(values1)
+        n2 = comm.spread(norm_apply(values1, stats1, gain[1], shift[1]), clips)
+        cross, saved = comm.cross_attend(
+            mm(n2, w_cq).astype(BF), mm(text, w_cm).astype(BF), clips
+        )
+        values2 = values1 + comm.sum_own(cross, w_co, mm_t, clips)
+        stats2 = norm_stats(values2)
+        n3 = comm.spread(norm_apply(values2, stats2, gain[2], shift[2]), clips)
+        return values1, stats1, n2, cross, saved, values2, stats2, n3
+
+    values1, stats1, n2, cross, cross_saved, values2, stats2, n3 = comm.stage(
+        stage0, values0, att, w_cross, text
+    )
+    n3 = comm.after(n3, mark_in, mark_out)
     hidden, slope = comm.feed(n3, w_in)
-    layer_out = (values2 + comm.sum_own(hidden, w_out, mm_t, clips)).astype(BF)
-    layer_out = comm.restore(layer_out).reshape(clips, own_frames, width)
-
-    def wgrad(left, right):
-        return lambda rows, columns: mm_rows(left[:, rows], right[:, columns])
-
-    def scatter(method, left, right):
-        if type(comm) is Whole:
-            return method(wgrad(left, right))
-        return method(wgrad(left, right), right.shape[1])
-
-    grad_out = scatter(comm.scatter_middle, up_all, hidden)
-    pre_grad = (mm(up_all, w_out) * slope.astype(F32)).astype(BF)
-    grad_in = scatter(comm.scatter_middle, n3, pre_grad)
-    e3 = comm.sum_own(pre_grad, w_in, mm_t, clips)
-    dv2, gain2, shift2 = norm_back(values2, stats2, gain[2], e3)
-    r2 = up.astype(F32) + dv2
-    r2_all = comm.spread(r2.astype(BF), clips)
-    dcq, dmem = comm.cross_back(cross_saved, mm(r2_all, w_co).astype(BF), clips)
-    text_grad = comm.sum_all(mm_t(dmem, w_cm))
-    e2 = comm.sum_own(dcq, w_cq, mm_t, clips)
-    dv1, gain1, shift1 = norm_back(values1, stats1, gain[1], e2)
-    r1 = r2 + dv1
-    r1_all = comm.spread(r1.astype(BF), clips)
-    grad_co = scatter(comm.scatter_last, r2_all, cross)
-    grad_cq = scatter(comm.scatter_last, n2, dcq)
-    grad_cm = scatter(comm.scatter_last, text, dmem)
-    grad_so = scatter(comm.scatter_last, r1_all, att)
-    dqkv = comm.self_back(self_saved, mm(r1_all, w_so).astype(BF), clips)
-    grad_self = scatter(comm.scatter_last, n1, dqkv)
-    e1 = comm.sum_own(dqkv, w_self, mm_t, clips)
-    dv0, gain0, shift0 = norm_back(values0, stats0, gain[0], e1)
-    input_grad = comm.restore(r1 + dv0).reshape(clips, own_frames, width)
-    text_grad = comm.restore(text_grad).reshape(clips, texts, width)
-    packed = jnp.stack([gain0, gain1, gain2, shift0, shift1, shift2]).T
-    packed = jnp.pad(packed, ((0, 0), (0, 250)))
-
-    def norm_sums(rows, columns):
-        return packed[rows, columns]
-
-    if type(comm) is Whole:
-        norm_grad = comm.scatter_last(norm_sums)
-    else:
-        norm_grad = comm.scatter_last(norm_sums, packed.shape[1])
-    norm_grad = comm.sum_all(norm_grad[:, :8]).T
+    send_out = comm.sends(up_all, hidden)
+    hidden, slope = comm.after((hidden, slope), out_pieces[1], send_out)
+    far_out = comm.exchange(send_out)
+
+    def stage1(pieces, rows, slope, n3, w_in):
+        w_out = comm.feed_out(pieces)
+        pre_grad = comm.slope_product(rows, w_out, slope)
+        sends = [comm.sends(n3, part) for part in jnp.split(pre_grad, 2, axis=1)]
+        return w_out, pre_grad, sends, comm.sum_own(pre_grad, w_in, mm_t, clips)
+
+    w_out, pre_grad, send_in, e3 = comm.stage(stage1, out_pieces, up_all, slope, n3, w_in)
+    e3, send_in = comm.after((e3, send_in), far_out)
+    in_parts = jnp.split(pre_grad, 2, axis=1)
+    far_in = [comm.exchange(send_in[0])]
+
+    def stage2(rows, hidden, far, e3, values2, stats2, own):
+        sent = comm.middle(comm.adds((rows, hidden, far)), None)
+        grads = norm_back(values2, stats2, gain[2], e3)
+        r2 = own.astype(F32) + grads[0]
+        return sent, r2, r2.astype(BF), grads[1], grads[2]
+
+    sent_out, r2, r2_own, gain2, shift2 = comm.stage(
+        stage2, up_all, hidden, far_out, e3, values2, stats2, up
+    )
+    sent_out, r2_own, send_b = comm.after((sent_out, r2_own, send_in[1:]), far_in[0])
+    half_out = comm.scatter_z(sent_out)
+    far_in += [comm.exchange(sends) for sends in send_b]
+
+    def stage3(r2_own, saved, w_cross, n2, cross, text):
+        w_co = split_cross(w_cross)[3]
+        r2_all = comm.spread(r2_own, clips)
+        dcq, dmem = comm.cross_back(saved, mm(r2_all, w_co).astype(BF), clips)
+        pairs = (n2, dcq), (r2_all, cross), (text, dmem)
+        return r2_all, dcq, dmem, comm.merged(*[comm.sends(*pair) for pair in pairs])
+
+    r2_all, dcq, dmem, send_cross = comm.stage(
+        stage3, r2_own, cross_saved, w_cross, n2, cross, text
+    )
+    dcq, send_cross = comm.after((dcq, send_cross), far_in)
+    far_cross = comm.exchange(send_cross)
+    cross_pairs = (n2, dcq), (r2_all, cross), (text, dmem)
+
+    def stage4(n3, parts, far, dcq, w_cross, values1, stats1, r2):
+        w_so, w_cq, *_ = split_cross(w_cross)
+        in_sums = comm.adds(*[(n3, part, one) for part, one in zip(parts, far)])
+        e2 = comm.sum_own(dcq, w_cq, mm_t, clips)
+        grads = norm_back(values1, stats1, gain[1], e2)
+        r1 = r2 + grads[0]
+        r1_all = comm.spread(r1.astype(BF), clips)
+        return in_sums, r1, r1_all, mm(r1_all, w_so).astype(BF), grads[1], grads[2]
+
+    in_sums, r1, r1_all, datt, gain1, shift1 = comm.stage(
+        stage4, n3, in_parts, tuple(far_in), dcq, w_cross, values1, stats1, r2
+    )
+    in_sums, datt = comm.after((in_sums, datt), far_cross, half_out)
+    in_second = comm.second(in_sums)
+
+    def stage5(pairs, far, saved, datt, r1_all, att):
+        far = comm.parted(far, cols, cols, 2 * cols)
+        sums = comm.adds(*[(*pair, one) for pair, one in zip(pairs, far)])
+        return sums, comm.self_back(saved, datt, clips), comm.sends(r1_all, att)
+
+    cross_sums, dqkv, send_so = comm.stage(
+        stage5, cross_pairs, far_cross, self_saved, datt, r1_all, att
+    )
+    cross_sums, dqkv, send_so, in_sums = comm.after(
+        (cross_sums, dqkv, send_so, in_sums), in_second
+    )
+    half_in = comm.scatter_z(comm.closing(in_sums, in_second))
+    far_so = comm.exchange(send_so)
+    cross_second = comm.second(cross_sums)
+    send_self = comm.stage(comm.sends, n1, dqkv)
+    dmem, hidden, send_self, cross_sums = comm.after(
+        (dmem, hidden, send_self, cross_sums), cross_second, far_so
+    )
+    far_self = comm.exchange(send_self)
+    half_cross = comm.scatter_z(comm.closing(cross_sums, cross_second))
+
+    def stage6(dmem, w_cross, values2, hidden, w_out):
+        w_cm = split_cross(w_cross)[2]
+        text_grad = comm.sum_all(mm_t(dmem, w_cm))
+        layer_out = (values2 + comm.sum_own(hidden, w_out, mm_t, clips)).astype(BF)
+        return comm.restore(text_grad), comm.restore(layer_out)
+
+    text_grad, layer_out = comm.stage(stage6, dmem, w_cross, values2, hidden, w_out)
+    text_grad, layer_out, dqkv = comm.after((text_grad, layer_out, dqkv), far_self, half_in)
+    self_sums = comm.adds((r1_all, att, far_so), (n1, dqkv, far_self))
+    dqkv = comm.after(dqkv, self_sums)
+    self_second = comm.second(self_sums)
+
+    def stage7(dqkv, w_self, values0, stats0, r1):
+        e1 = comm.sum_own(dqkv, w_self, mm_t, clips)
+        grads = norm_back(values0, stats0, gain[0], e1)
+        return comm.restore(r1 + grads[0]), grads[1], grads[2]
+
+    input_grad, gain0, shift0 = comm.stage(stage7, dqkv, w_self, values0, stats0, r1)
+    input_grad, gain0 = comm.after((input_grad, gain0), self_second, half_cross)
+    half_self = comm.scatter_z(comm.closing(self_sums, self_second))
+    norm_grad = comm.norm_sums(jnp.stack([gain0, gain1, gain2, shift0, shift1, shift2]))
+    input_grad = input_grad.reshape(clips, own_frames, width)
+    text_grad = text_grad.reshape(clips, texts, width)
+    layer_out = layer_out.reshape(clips, own_frames, width)
+    grad_out = comm.close_middle(half_out)
+    grad_in = catenate(comm.close_last(half_in, *[part.shape[1] for part in in_parts]))
+    grad_cq, grad_co, grad_cm = comm.close_last(half_cross, cols, cols, 2 * cols)
+    grad_so, grad_self = comm.close_last(half_self, cols, 3 * cols)
     return (
         layer_out,
         input_grad,

time: 1080 us -> 916 us (0.85)
  waiting for transfers between devices: 487 us -> 234 us
  local copies, waits for them, and re-layouts: 54.7 us -> 118 us
  other arithmetic: 61 us -> 83.2 us
  Pallas kernels: 129 us -> 147 us
  matrix products: 266 us -> 249 us
    ppermute x27 -> x22, waiting for transfers between devices: 183 us -> 52.9 us  [y(): return lax.ppermute(v, 'y', SWAP)]
    ppermute x27 -> x22, waiting for transfers between devices: 128 us -> 47.4 us  [x(): return lax.ppermute(v, 'x', SWAP)]
    all_gather x4, waiting for transfers between devices: 111 us -> 70.5 us  [the longest x2 48.1 us: gather_weights(): feeds = [lax.all_gather(four, 'z', axis=1, tiled=True) for four in opened]]
    optimization_barrier x0 -> x11, local copies, waits for them, and re-layouts: none -> 23.5 us  [tie(): return lax.optimization_barrier((value, others))[0]]
    pallas_call x0 -> x1, Pallas kernels: none -> 18 us  [slope_product(): pl.pallas_call(slope_kernel, grid=(width // block,), in_specs=[pl.BlockSp...]
    slice x15 -> x37, local copies, waits for them, and re-layouts: 21.2 us -> 38.6 us  [the longest x6 10.9 us: sends(): far = jnp.concatenate([left[:, n:2 * n], left[:, 3 * n:]], axis=1)]
    dot_general x9 -> x8, matrix products: 53.7 us -> 41.1 us  [mm(): return jnp.dot(left, right, preferred_element_type=F32)]
    reduce_scatter x7 -> x4, waiting for transfers between devices: 57.7 us -> 46.8 us  [scatter_z(): return lax.psum_scatter(parts, 'z', scatter_dimension=1, tiled=True)]
  transfers between devices with their start and end apart: 82 -> 69, of which waited for: 33 -> 26; matrix products, arithmetic and copies ran while one was open for 33% -> 47% of each run, Pallas kernels for 10% -> 16%
where the time goes in v4:
time: 916 us; the launch traced here: 907 us
  matrix products  249 us (27%)
  waiting for transfers between devices  234 us (26%)
  Pallas kernels  147 us (16%)
  local copies, waits for them, and re-layouts  118 us (13%)
  other arithmetic  83.2 us (9%)
  starting transfers between devices  58.9 us (6%)
  between operations  15 us (2%)
    dot_general x17, matrix products, mm_t(): lax.dot_general(left, right, (((1,), (1,)), ((), ())), preferred_element_...  104 us
    dot_general x32, matrix products, mm_rows(): lax.dot_general(left, right, (((0,), (0,)), ((), ())), preferred_element_...  104 us
    ppermute x22, waiting for transfers between devices, y(): return lax.ppermute(v, 'y', SWAP)  52.9 us
    all_gather x2, waiting for transfers between devices, gather_weights(): feeds = [lax.all_gather(four, 'z', axis=1, tiled=True) for four in opened]  48.1 us
    ppermute x22, waiting for transfers between devices, x(): return lax.ppermute(v, 'x', SWAP)  47.4 us
    reduce_scatter x4, waiting for transfers between devices, scatter_z(): return lax.psum_scatter(parts, 'z', scatter_dimension=1, tiled=True)  46.8 us
    dot_general x8, matrix products, mm(): return jnp.dot(left, right, preferred_element_type=F32)  41.1 us
    pallas_call x1, Pallas kernels, self_back(): pl.pallas_call(self_back_kernel, grid_spec=pltpu.PrefetchScalarGridSpec(n...  30.5 us
  transfers between devices with their start and end apart: 69, of which 26 were waited for; matrix products, arithmetic and copies ran while one was open for 47% of the time, Pallas kernels for 16%

profile of v4, /device:TPU:0, one launch (start us, length us, event | category | flops | bytes accessed | tf_op | source)
XLA Modules:
  0.0 907.2 jit_solution(5434198121193177679)
XLA Ops:
  29.3 5.8 collective-permute-done.12
  49.3 6.0 all-gather.9.cloned.1.call-done.refs_0_
  61.0 18.6 %collective-permute-done.19.refs_1_ = bf16[384,1152]{1,0:T(8,128)(2,1)} collective-permute-done((bf16[384,1152]{1,0:T(8,128)(2,1)S(1)}, bf16[384,1152]{1,0:T(8,128)(2,1)}, u32[]{:S(2)}, u32[]{:S(2)}) %collective-permute-start.19) | collective-permute-done | bytes 884768 | tf_op jit(solution)/shard_map/ppermute | solution.py:524
  82.5 4.2 fusion.311
  86.8 13.2 %collective-permute-done.23.refs_2_ = bf16[384,1152]{1,0:T(8,128)(2,1)} collective-permute-done((bf16[384,1152]{1,0:T(8,128)(2,1)S(1)}, bf16[384,1152]{1,0:T(8,128)(2,1)}, u32[]{:S(2)}, u32[]{:S(2)}) %collective-permute-start.23) | collective-permute-done | bytes 884768 | tf_op jit(solution)/shard_map/ppermute | solution.py:527
  100.0 16.4 %all-gather.5.cloned.1.call-done.refs_0_ = bf16[384,3840]{1,0:T(8,128)(2,1)} async-done(((bf16[96,3840]{1,0:T(8,128)(2,1)}), bf16[384,3840]{1,0:T(8,128)(2,1)}) %all-gather.5.cloned.1.call-update) | async-done | bytes 2949136 | tf_op jit(solution)/shard_map/all_gather | solution.py:552
  136.6 6.0 place.3
  142.6 13.9 %collective-permute-done.25.refs_1_ = bf16[384,1920]{1,0:T(8,128)(2,1)} collective-permute-done((bf16[384,1920]{1,0:T(8,128)(2,1)}, bf16[384,1920]{1,0:T(8,128)(2,1)}, u32[]{:S(2)}, u32[]{:S(2)}) %collective-permute-start.25) | collective-permute-done | bytes 1474592 | tf_op jit(solution)/shard_map/ppermute | solution.py:524
  158.6 48.1 %all-gather.7.cloned.1.call-done = bf16[4,384,1536]{2,1,0:T(8,128)(2,1)} async-done(((bf16[4,96,1536]{2,1,0:T(8,128)(2,1)}), bf16[4,384,1536]{2,1,0:T(8,128)(2,1)}) %all-gather.7.cloned.1.call-update) | async-done | bytes 4718608 | tf_op jit(solution)/shard_map/all_gather | solution.py:553
  206.7 5.1 fusion.415
  214.7 11.7 %convolution_convert_fusion.8 = bf16[1024,2304]{1,0:T(8,128)(2,1)} fusion(bf16[1024,1536]{0,1:T(8,128)(2,1)} %constant_dynamic-update-slice_fusion.3, bf16[1536,2304]{1,0:T(8,128)(2,1)S(1)} %copy-done.7), kind=kOutput, calls=%fused_computation.340 | convolution fusion | flops 7250116608 | bytes 14942208 | tf_op jit(solution)/shard_map/dot_general | solution.py:19
  226.4 18.3 %self_attend.1 = (bf16[2,2,256,768]{3,2,1,0:T(8,128)(2,1)}, f32[2,2,256,768]{3,2,1,0:T(8,128)}) custom-call(s32[1]{0:T(128)} %bitcast.60.core_ref, bf16[2,2,256,2304]{3,2,1,0:T(8,128)(2,1)} %bitcast.197, bf16[2,2,256,2304]{3,2,1,0:T(8,128)(2,1)} %bitcast.198, bf16[2,2,256,2304]{3,2,1,0:T(8,128)(2,1)} %bitcast.199), custom_call_target="tpu_custom_call" | custom-call | flops 1207959552 | bytes 9437184 | tf_op jit(solution)/shard_map/self_attend/pallas_call | solution.py:687
  244.7 8.9 place.2
  253.5 72.0 %conditional.9 = (f32[512,1536]{1,0:T(8,128)}, f32[512,1]{0,1:T(1,128)S(1)}, f32[512,1]{0,1:T(1,128)S(1)}, bf16[1024,1536]{1,0:T(8,128)(2,1)}, bf16[1024,768]{1,...) conditional(s32[]{:T(128)} %convert_element_type.409, ...), branch_computations={%region_2.3_spmd, %region_3.8_spmd} | conditional | flops 8087077888 | bytes 115057208 | solution.py:599
  253.6 4.5 convolution_convert_fusion.5
  264.2 6.4 fusion.406
  281.2 6.4 fusion.216
  287.6 13.8 %cross_attend.1 = bf16[2,2,256,768]{3,2,1,0:T(8,128)(2,1)} custom-call(bf16[2,2,256,768]{3,2,1,0:T(8,128)(2,1)} %bitcast.2.q_ref, bf16[2,64,1536]{2,1,0:T(8,128)(2,1)S(1)} %bitcast.207, bf16[2,64,1536]{2,1,0:T(8,128)(2,1)S(1)} %bitcast.208), custom_call_target="tpu_custom_call" | custom-call | flops 201326592 | bytes 3145728 | tf_op jit(solution)/shard_map/cond/branch_1_fun/cross_attend/pallas_call | solution.py:750
  309.4 5.7 fusion.407
  325.6 4.8 fusion.414
  331.6 7.3 place_stacked.3.weight_ref
  338.9 19.8 %feed.1 = (bf16[1024,3072]{1,0:T(8,128)(2,1)}, bf16[1024,3072]{1,0:T(8,128)(2,1)}) custom-call(bf16[1024,1536]{1,0:T(8,128)(2,1)} %get-tuple-element.366.rows_ref, bf16[1536,3072]{1,0:T(8,128)(2,1)} %place_stacked.3.weight_ref), custom_call_target="tpu_custom_call" | custom-call | flops 9663676416 | bytes 25165824 | tf_op jit(solution)/shard_map/feed/pallas_call | solution.py:311
  358.7 6.3 convolution_convert_fusion.10
  375.3 9.6 %collective-permute-done.35 = bf16[2,384,1536]{2,1,0:T(8,128)(2,1)} collective-permute-done((bf16[2,384,1536]{2,1,0:T(8,128)(2,1)}, bf16[2,384,1536]{2,1,0:T(8,128)(2,1)}, u32[]{:S(2)}, u32[]{:S(2)}) %collective-permute-start.35) | collective-permute-done | bytes 2359328 | tf_op jit(solution)/shard_map/ppermute | solution.py:527
  385.6 67.2 %conditional.10 = (bf16[1536,3072]{1,0:T(8,128)(2,1)}, bf16[1024,3072]{1,0:T(8,128)(2,1)}, bf16[768,768]{0,1:T(8,128)(2,1)}, bf16[768,768]{1,0:T(8,128)(2,1)}, b...) conditional(s32[]{:T(128)} %convert_element_type.409, ...), branch_computations={%region_8.9_spmd, %region_9.10_spmd} | conditional | flops 24170201088 | bytes 124256440 | solution.py:599
  385.6 7.3 place_stacked.2.weight_ref
  392.9 18.0 %slope_product.1 = bf16[1024,3072]{1,0:T(8,128)(2,1)} custom-call(bf16[1024,1536]{1,0:T(8,128)(2,1)} %get-tuple-element.172.rows_ref, bf16[1536,3072]{1,0:T(8,128)(2,1)} %place_stacked.2.weight_ref, bf16[1024,3072]{1,0:T(8,128)(2,1)} %get-tuple-element.173.slope_ref), custom_call_target="tpu_custom_call" | custom-call | flops 9663676416 | bytes 25165824 | tf_op jit(solution)/shard_map/cond/branch_1_fun/slope_product/pallas_call | solution.py:346
  410.8 9.6 %fusion.4 = bf16[512,1536]{1,0:T(8,128)(2,1)S(1)} fusion(bf16[1536,3072]{1,0:T(8,128)(2,1)} %get-tuple-element.175, bf16[1024,3072]{1,0:T(8,128)(2,1)} %slope_product.1), kind=kOutput, calls=%fused_computation.5 | convolution fusion | flops 4832624640 | bytes 14155776 | tf_op jit(solution)/shard_map/cond/branch_1_fun/dot_general | solution.py:23
  429.9 4.3 fusion.30
  434.2 4.5 fusion.27
  438.7 6.1 fusion.388
  444.9 7.9 convert_add_fusion
  457.3 23.8 %conditional.11 = (bf16[4,384,1536]{2,1,0:T(8,128)(2,1)}, f32[512,1536]{1,0:T(8,128)}, bf16[512,1536]{1,0:T(8,128)(2,1)}, f32[1,1536]{1,0:T(1,128)S(1)}, f32[1,1536]{1,0:T(1,128)S(1)}) conditional(s32[]{:T(128)} %convert_element_type.409, () %tuple.116, (bf16[1024,1536]{1,0:T(8,128)(2,1)}, bf16[1024,3072]{1,0:T(8,128)(2,1)}, ...), branch_computations={%region_10.11_spmd, %region_11.16_spmd} | conditional | flops 4864078848 | bytes 91349112 | solution.py:599
  459.0 5.5 add_convert_fusion.5
  464.6 4.3 add_convert_fusion.6
  471.9 4.1 multiply_reduce_fusion.2
  476.1 5.0 fusion.386
  488.6 46.9 %conditional.12 = (bf16[1024,1536]{1,0:T(8,128)(2,1)}, bf16[1024,768]{1,0:T(8,128)(2,1)}, bf16[128,1536]{1,0:T(8,128)(2,1)S(1)}, bf16[768,1536]{0,1:T(8,128)(2,1)}, bf16[768,1536]{0,1:T(8,128)(2,1)}) conditional(s32[]{:T(128)} %convert_element_type.409, () %tuple.115, (bf16[512,1536]{1,0:T(8,128)(2,1)}, bf16[1024,768]{1,0:T(8,128)(2,1)}, ...), branch_computations={%region_16.17_spmd, %region_17.18_spmd} | conditional | flops 5661130752 | bytes 72745288 | solution.py:599
  498.6 6.4 fusion.39
  504.9 17.5 %cross_back.1 = (bf16[2,2,256,768]{3,2,1,0:T(8,128)(2,1)}, bf16[2,64,1536]{2,1,0:T(8,128)(2,1)S(1)}) custom-call(bf16[2,2,256,768]{3,2,1,0:T(8,128)(2,1)} %bitcast.20.q_ref, bf16[2,64,1536]{2,1,0:T(8,128)(2,1)S(1)} %get-tuple-element.188.k_ref.v_ref, bf16[2,64,1536]{2,1,0:T(8,128)(2,1)S(1)} %get-tuple-element.188.k_ref.v_ref, bf16[2,2,256,768]{3,2,1,0:T(8,128)(2,1)} %bitcast.225), custom_call_target="tpu_custom_call" | custom-call | flops 503316480 | bytes 4718592 | tf_op jit(solution)/shard_map/cond/branch_1_fun/cross_back/pallas_call | solution.py:767
  538.5 42.1 %conditional.13 = (bf16[384,1536]{0,1:T(8,128)(2,1)}, bf16[384,1536]{0,1:T(8,128)(2,1)}, bf16[384,1536]{0,1:T(8,128)(2,1)}, bf16[384,1536]{0,1:T(8,128)(2,1)}, f...) conditional(s32[]{:T(128)} %convert_element_type.409, ...), branch_computations={%region_18.19_spmd, %region_19.24_spmd} | conditional | flops 9710072832 | bytes 99999896 | solution.py:599
  538.5 4.6 convolution_convert_fusion.6
  555.8 5.4 multiply_reduce_fusion.5
  561.2 4.8 fusion.387
  575.4 5.2 fusion.235
  580.6 9.0 collective-permute-done.43
  597.8 59.3 %conditional.14 = (bf16[384,1536]{0,1:T(8,128)(2,1)S(1)}, bf16[384,1536]{0,1:T(8,128)(2,1)S(1)}, bf16[384,1536]{0,1:T(8,128)(2,1)S(1)}, bf16[384,1536]{0,1:T(8,1...) conditional(s32[]{:T(128)} %convert_element_type.409, ...), branch_computations={%region_25.26_spmd, %region_26.27_spmd} | conditional | flops 6977421312 | bytes 100663552 | solution.py:599
  620.4 30.5 %self_back.1 = bf16[2,2,256,2304]{3,2,1,0:T(8,128)(2,1)} custom-call(s32[1]{0:T(128)} %get-tuple-element.217.core_ref, bf16[2,2,256,2304]{3,2,1,0:T(8,128)(2,1)} %get-tuple-element.218.q_ref.k_ref.v_ref, bf16[2,2,256,2304]{3,2,1,0:T(8,128)(2,1)} %get-tuple-element.218.q_ref.k_ref.v_ref, bf16[2,2,256,2304]{3,2,1,0:T(8,128)(2,1)} %get-tuple-element.218.q_ref.k_ref.v_ref, ...), custom_call_target="tpu_custom_call" | custom-call | flops 3019898880 | bytes 14155776 | tf_op jit(solution)/shard_map/cond/branch_1_fun/self_back/pallas_call | solution.py:717
  684.4 14.2 %conditional.15 = (bf16[768,1152]{1,0:T(8,128)(2,1)}, bf16[768,1152]{1,0:T(8,128)(2,1)}) conditional(s32[]{:T(128)} %convert_element_type.409, () %tuple.129, (bf16[1024,1536]{0,1:T(8,128)(2,1)}, bf16[1024,2304]{1,0:T(8,128)(2,1)}) %tuple.137), branch_computations={%region_27.28_spmd, %region_28.29_spmd} | conditional | flops 3628793856 | bytes 47579228 | solution.py:599
  684.4 4.7 copy.124
  689.1 5.8 convolution_convert_fusion.3
  698.6 14.1 %collective-permute-done.49 = bf16[768,384]{0,1:T(8,128)(2,1)} collective-permute-done((bf16[768,384]{0,1:T(8,128)(2,1)}, bf16[768,384]{0,1:T(8,128)(2,1)}, u32[]{:S(2)}, u32[]{:S(2)}) %collective-permute-start.49) | collective-permute-done | bytes 589856 | tf_op jit(solution)/shard_map/ppermute | solution.py:527
  732.8 38.7 %conditional.16 = (f32[128,1536]{1,0:T(8,128)}, bf16[512,1536]{1,0:T(8,128)(2,1)S(1)}) conditional(s32[]{:T(128)} %convert_element_type.409, () %tuple.110, (bf16[1536,3840]{1,0:T(8,128)(2,1)}, bf16[128,1536]{1,0:T(8,128)(2,1)S(1)}, bf16[1024,3072]{1,0:T(8,128)(2,1)}, bf16[1536,3072]{1,0:T(8,128)(2,1)}, f32[512,1536]{1,0:T(8,128)}) %tuple.139), branch_computations={%region_29.30_spmd, %region_30.31_spmd} | conditional | flops 13905571840 | bytes 61366496 | solution.py:599
  732.8 10.5 %fusion.167 = bf16[512,1536]{1,0:T(8,128)(2,1)} fusion(bf16[1536,3072]{1,0:T(8,128)(2,1)} %get-tuple-element.229, bf16[1024,3072]{1,0:T(8,128)(2,1)} %get-tuple-element.228), kind=kOutput, calls=%fused_computation.139 | convolution fusion | flops 4832624640 | bytes 14155776 | tf_op jit(solution)/shard_map/cond/branch_1_fun/dot_general | solution.py:23
  743.3 5.0 fusion.404
  757.9 13.6 %fusion.166 = bf16[512,1536]{1,0:T(8,128)(2,1)S(1)} fusion(s32[1536]{0:T(1024)S(1)} %fusion.182, f32[512,1536]{1,0:T(8,128)} %get-tuple-element.227, bf16[512,1536]{1,0:T(8,128)(2,1)} %copy-done.75, bf16[1536,3072]{1,0:T(8,128)(2,1)} %get-tuple-element.229, bf16[1024,3072]{1,0:T(8,128)(2,1)} %get-tuple-element.228), kind=kOutput, calls=%fused_computation.138 | convolution fusion | flops 7254048768 | bytes 18880512 | tf_op jit(solution)/shard_map/cond/branch_1_fun/dot_general | solution.py:23
  771.6 5.6 fusion.303
  786.8 28.7 %conditional.17 = (f32[512,1536]{1,0:T(8,128)}, f32[1536]{0:T(1024)S(1)}, f32[1,1536]{1,0:T(1,128)S(1)}) conditional(s32[]{:T(128)} %convert_element_type.409, () %tuple.141, (bf16[1024,2304]{1,0:T(8,128)(2,1)S(1)}, bf16[1536,2304]{1,0:T(8,128)(2,1)S(1)}, f32[3,1536]{0,1:T(8,128)S(1)}, f32[512]{0:T(512)S(1)}, f32[512,1536]{0,1:T(8,128)}, ...), branch_computations={%region_32.33_spmd, %region_33.38_spmd} | conditional | flops 12104838144 | bytes 129112288 | solution.py:599
  786.8 5.0 convolution_convert_fusion.7
  795.7 9.6 %multiply_reduce_fusion.8 = (f32[1536]{0:T(1024)S(1)}, f32[512]{0:T(512)S(1)}, f32[512]{0:T(512)S(1)}, f32[1536]{0:T(1024)S(1)}, f32[512,1536]{1,0:T(8,128)S(1)}) fusion(f32[512,1536]{1,0:T(8,128)} %copy.134, f32[512]{0:T(512)S(1)} %get-tuple-element.810, f32[512]{0:T(512)S(1)} %get-tuple-element.811, f32[1536]{0:T(1024)S(1)} %slice_reduce_fusion.6, ...), kind=kOutput, calls=%fused_computation.284 | convolution fusion | flops 3632525312 | bytes 17328128 | tf_op jit(solution)/shard_map/cond/branch_1_fun/dot_general | solution.py:23
  811.1 4.4 fusion.264
  820.5 4.5 collective-permute-done.56
  836.3 4.6 collective-permute-done.58
  849.7 46.8 %reduce-scatter.14.cloned.1.call-done = bf16[2,96,1536]{2,1,0:T(8,128)(2,1)} async-done(((bf16[2,384,1536]{2,1,0:T(8,128)(2,1)}), bf16[2,96,1536]{2,1,0:T(8,128)(2,1)}) %reduce-scatter.14.cloned.1.call-update) | async-done | bytes 589840 | tf_op jit(solution)/shard_map/reduce_scatter | solution.py:644
  (511 shorter events, 336.4 us)
Async XLA Ops:
  7.2 48.1 %all-gather.9.cloned.1.call-start = ((), (), s32[]{:S(2)}) async-start(), calls=%async_computation.7 | async-start | bytes 2211840 | tf_op jit(solution)/shard_map/all_gather | solution.py:552
  9.3 107.1 %all-gather.5.cloned.1.call-start = ((), (), s32[]{:S(2)}) async-start(), calls=%async_computation.5 | async-start | bytes 3686400 | tf_op jit(solution)/shard_map/all_gather | solution.py:552
  10.2 15.9 %collective-permute-start.11 = (bf16[96,128]{1,0:T(8,128)(2,1)S(1)}, bf16[96,128]{1,0:T(8,128)(2,1)S(1)}, u32[]{:S(2)}, u32[]{:S(2)}) collective-permute-start(bf16[96,128]{1,0:T(8,128)(2,1)S(1)} %get-tuple-element.904), channel_id=1, source_target_pairs={{0,8},{8,0},{16,24},{24,16},{1,9},{9,1},{17,25},{25,17},{2,10},{10... | collective-permute-start | bytes 73736 | tf_op jit(solution)/shard_map/ppermute | solution.py:533
  16.2 190.5 %all-gather.7.cloned.1.call-start = ((), (), s32[]{:S(2)}) async-start(), calls=%async_computation.6 | async-start | bytes 5898240 | tf_op jit(solution)/shard_map/all_gather | solution.py:553
  17.3 24.2 %collective-permute-start.16 = (bf16[96,1536]{1,0:T(8,128)(2,1)}, bf16[96,1536]{1,0:T(8,128)(2,1)}, u32[]{:S(2)}, u32[]{:S(2)}) collective-permute-start(bf16[96,1536]{1,0:T(8,128)(2,1)} %get-tuple-element.890), channel_id=1, source_target_pairs={{0,4},{4,0},{1,5},{5,1},{2,6},{6,2},{3,7},{7,3},{8,12},{12,8},{9,1... | collective-permute-start | bytes 884744 | tf_op jit(solution)/shard_map/ppermute | solution.py:527
  18.8 22.7 %collective-permute-start.15 = (bf16[96,1536]{1,0:T(8,128)(2,1)}, bf16[96,1536]{1,0:T(8,128)(2,1)}, u32[]{:S(2)}, u32[]{:S(2)}) collective-permute-start(bf16[96,1536]{1,0:T(8,128)(2,1)} %get-tuple-element.891), channel_id=1, source_target_pairs={{0,2},{2,0},{1,3},{3,1},{4,6},{6,4},{5,7},{7,5},{8,10},{10,8},{9,1... | collective-permute-start | bytes 884744 | tf_op jit(solution)/shard_map/ppermute | solution.py:524
  22.3 21.4 %collective-permute-start.18 = (bf16[96,1536]{1,0:T(8,128)(2,1)}, bf16[96,1536]{1,0:T(8,128)(2,1)}, u32[]{:S(2)}, u32[]{:S(2)}) collective-permute-start(bf16[96,1536]{1,0:T(8,128)(2,1)} %get-tuple-element.886), channel_id=1, source_target_pairs={{0,4},{4,0},{1,5},{5,1},{2,6},{6,2},{3,7},{7,3},{8,12},{12,8},{9,1... | collective-permute-start | bytes 884744 | tf_op jit(solution)/shard_map/ppermute | solution.py:527
  22.8 20.9 %collective-permute-start.17 = (bf16[96,1536]{1,0:T(8,128)(2,1)}, bf16[96,1536]{1,0:T(8,128)(2,1)}, u32[]{:S(2)}, u32[]{:S(2)}) collective-permute-start(bf16[96,1536]{1,0:T(8,128)(2,1)} %get-tuple-element.887), channel_id=1, source_target_pairs={{0,2},{2,0},{1,3},{3,1},{4,6},{6,4},{5,7},{7,5},{8,10},{10,8},{9,1... | collective-permute-start | bytes 884744 | tf_op jit(solution)/shard_map/ppermute | solution.py:524
  26.1 9.0 collective-permute-start.12
  35.2 4.7 collective-permute-start.13
  39.9 6.1 collective-permute-start.14
  48.5 277.1 %all-gather.11.cloned.1.call-start = ((), (), s32[]{:S(2)}) async-start(), calls=%async_computation.8 | async-start | bytes 5898240 | tf_op jit(solution)/shard_map/all_gather | solution.py:553
  49.1 541.9 %reduce-scatter.8.cloned.1.call-start = ((), (), s32[]{:S(2)}) async-start(), calls=%async_computation.9 | async-start | bytes 5898240 | tf_op jit(solution)/shard_map/reduce_scatter | solution.py:644
  56.9 22.7 %collective-permute-start.19 = (bf16[384,1152]{1,0:T(8,128)(2,1)S(1)}, bf16[384,1152]{1,0:T(8,128)(2,1)}, u32[]{:S(2)}, u32[]{:S(2)}) collective-permute-start(bf16[384,1152]{1,0:T(8,128)(2,1)S(1)} %get-tuple-element.856), channel_id=1, source_target_pairs={{0,2},{2,0},{1,3},{3,1},{4,6},{6,4},{5,7},{7,5},{8,10},{10,8},{9,1... | collective-permute-start | bytes 2654216 | tf_op jit(solution)/shard_map/ppermute | solution.py:524
  58.4 22.6 %collective-permute-start.21 = (bf16[384,1152]{1,0:T(8,128)(2,1)S(1)}, bf16[384,1152]{1,0:T(8,128)(2,1)}, u32[]{:S(2)}, u32[]{:S(2)}) collective-permute-start(bf16[384,1152]{1,0:T(8,128)(2,1)S(1)} %get-tuple-element.855), channel_id=1, source_target_pairs={{0,4},{4,0},{1,5},{5,1},{2,6},{6,2},{3,7},{7,3},{8,12},{12,8},{9,1... | collective-permute-start | bytes 2654216 | tf_op jit(solution)/shard_map/ppermute | solution.py:527
  59.9 40.1 %collective-permute-start.23 = (bf16[384,1152]{1,0:T(8,128)(2,1)S(1)}, bf16[384,1152]{1,0:T(8,128)(2,1)}, u32[]{:S(2)}, u32[]{:S(2)}) collective-permute-start(bf16[384,1152]{1,0:T(8,128)(2,1)S(1)} %get-tuple-element.856), channel_id=1, source_target_pairs={{0,4},{4,0},{1,5},{5,1},{2,6},{6,2},{3,7},{7,3},{8,12},{12,8},{9,1... | collective-permute-start | bytes 2654216 | tf_op jit(solution)/shard_map/ppermute | solution.py:527
  60.4 39.6 %collective-permute-start.24 = (bf16[384,1152]{1,0:T(8,128)(2,1)S(1)}, bf16[384,1152]{1,0:T(8,128)(2,1)}, u32[]{:S(2)}, u32[]{:S(2)}) collective-permute-start(bf16[384,1152]{1,0:T(8,128)(2,1)S(1)} %get-tuple-element.855), channel_id=1, source_target_pairs={{0,2},{2,0},{1,3},{3,1},{4,6},{6,4},{5,7},{7,5},{8,10},{10,8},{9,1... | collective-permute-start | bytes 2654216 | tf_op jit(solution)/shard_map/ppermute | solution.py:524
  79.6 37.8 %collective-permute-start.20 = (bf16[384,1152]{1,0:T(8,128)(2,1)}, bf16[384,1152]{1,0:T(8,128)(2,1)}, u32[]{:S(2)}, u32[]{:S(2)}) collective-permute-start(bf16[384,1152]{1,0:T(8,128)(2,1)} %collective-permute-done.19.refs_1_), channel_id=1, source_target_pairs={{0,4},{4,0},{1,5},{5,1},{2,6},{6,2},{3,7},{7,3},{8,12},{12,8},{9,1... | collective-permute-start | bytes 2654216 | tf_op jit(solution)/shard_map/ppermute | solution.py:527
  81.0 36.3 %collective-permute-start.22 = (bf16[384,1152]{1,0:T(8,128)(2,1)}, bf16[384,1152]{1,0:T(8,128)(2,1)}, u32[]{:S(2)}, u32[]{:S(2)}) collective-permute-start(bf16[384,1152]{1,0:T(8,128)(2,1)} %collective-permute-done.21.refs_5_), channel_id=1, source_target_pairs={{0,2},{2,0},{1,3},{3,1},{4,6},{6,4},{5,7},{7,5},{8,10},{10,8},{9,1... | collective-permute-start | bytes 2654216 | tf_op jit(solution)/shard_map/ppermute | solution.py:524
  86.7 43.4 %collective-permute-start.31 = (bf16[512,1536]{1,0:T(8,128)(2,1)S(1)}, bf16[512,1536]{1,0:T(8,128)(2,1)}, u32[]{:S(2)}, u32[]{:S(2)}) collective-permute-start(bf16[512,1536]{1,0:T(8,128)(2,1)S(1)} %fusion.311), channel_id=1, source_target_pairs={{0,1},{1,0},{2,3},{3,2},{4,5},{5,4},{6,7},{7,6},{8,9},{9,8},{10,11... | collective-permute-start | bytes 4718600 | tf_op jit(solution)/shard_map/ppermute | solution.py:530
  100.0 32.5 %collective-permute-start.32 = (bf16[512,1536]{0,1:T(8,128)(2,1)}, bf16[512,1536]{0,1:T(8,128)(2,1)}, u32[]{:S(2)}, u32[]{:S(2)}) collective-permute-start(bf16[512,1536]{0,1:T(8,128)(2,1)} %add_convert_fusion.11), channel_id=1, source_target_pairs={{0,1},{1,0},{2,3},{3,2},{4,5},{5,4},{6,7},{7,6},{8,9},{9,8},{10,11... | collective-permute-start | bytes 4718600 | tf_op jit(solution)/shard_map/ppermute | solution.py:530
  121.0 35.5 %collective-permute-start.25 = (bf16[384,1920]{1,0:T(8,128)(2,1)}, bf16[384,1920]{1,0:T(8,128)(2,1)}, u32[]{:S(2)}, u32[]{:S(2)}) collective-permute-start(bf16[384,1920]{1,0:T(8,128)(2,1)} %get-tuple-element.850), channel_id=1, source_target_pairs={{0,2},{2,0},{1,3},{3,1},{4,6},{6,4},{5,7},{7,5},{8,10},{10,8},{9,1... | collective-permute-start | bytes 4423688 | tf_op jit(solution)/shard_map/ppermute | solution.py:524
  121.6 36.3 %collective-permute-start.29 = (bf16[384,1920]{1,0:T(8,128)(2,1)}, bf16[384,1920]{1,0:T(8,128)(2,1)}, u32[]{:S(2)}, u32[]{:S(2)}) collective-permute-start(bf16[384,1920]{1,0:T(8,128)(2,1)} %get-tuple-element.849), channel_id=1, source_target_pairs={{0,4},{4,0},{1,5},{5,1},{2,6},{6,2},{3,7},{7,3},{8,12},{12,8},{9,1... | collective-permute-start | bytes 4423688 | tf_op jit(solution)/shard_map/ppermute | solution.py:527
  125.3 88.0 %collective-permute-start.26 = (bf16[384,1920]{1,0:T(8,128)(2,1)}, bf16[384,1920]{1,0:T(8,128)(2,1)}, u32[]{:S(2)}, u32[]{:S(2)}) collective-permute-start(bf16[384,1920]{1,0:T(8,128)(2,1)} %get-tuple-element.850), channel_id=1, source_target_pairs={{0,4},{4,0},{1,5},{5,1},{2,6},{6,2},{3,7},{7,3},{8,12},{12,8},{9,1... | collective-permute-start | bytes 4423688 | tf_op jit(solution)/shard_map/ppermute | solution.py:527
  135.2 109.5 %collective-permute-start.28 = (bf16[384,1920]{1,0:T(8,128)(2,1)}, bf16[384,1920]{1,0:T(8,128)(2,1)}, u32[]{:S(2)}, u32[]{:S(2)}) collective-permute-start(bf16[384,1920]{1,0:T(8,128)(2,1)} %get-tuple-element.849), channel_id=1, source_target_pairs={{0,2},{2,0},{1,3},{3,1},{4,6},{6,4},{5,7},{7,5},{8,10},{10,8},{9,1... | collective-permute-start | bytes 4423688 | tf_op jit(solution)/shard_map/ppermute | solution.py:524
  156.5 88.2 %collective-permute-start.27 = (bf16[384,1920]{1,0:T(8,128)(2,1)}, bf16[384,1920]{1,0:T(8,128)(2,1)}, u32[]{:S(2)}, u32[]{:S(2)}) collective-permute-start(bf16[384,1920]{1,0:T(8,128)(2,1)} %collective-permute-done.25.refs_1_), channel_id=1, source_target_pairs={{0,4},{4,0},{1,5},{5,1},{2,6},{6,2},{3,7},{7,3},{8,12},{12,8},{9,1... | collective-permute-start | bytes 4423688 | tf_op jit(solution)/shard_map/ppermute | solution.py:527
  157.9 86.7 %collective-permute-start.30 = (bf16[384,1920]{1,0:T(8,128)(2,1)}, bf16[384,1920]{1,0:T(8,128)(2,1)}, u32[]{:S(2)}, u32[]{:S(2)}) collective-permute-start(bf16[384,1920]{1,0:T(8,128)(2,1)} %collective-permute-done.29.refs_5_), channel_id=1, source_target_pairs={{0,2},{2,0},{1,3},{3,1},{4,6},{6,4},{5,7},{7,5},{8,10},{10,8},{9,1... | collective-permute-start | bytes 4423688 | tf_op jit(solution)/shard_map/ppermute | solution.py:524
  211.8 118.6 %collective-permute-start.33 = (bf16[2,384,1536]{2,1,0:T(8,128)(2,1)}, bf16[2,384,1536]{2,1,0:T(8,128)(2,1)}, u32[]{:S(2)}, u32[]{:S(2)}) collective-permute-start(bf16[2,384,1536]{2,1,0:T(8,128)(2,1)} %get-tuple-element.363), channel_id=1, source_target_pairs={{0,4},{4,0},{1,5},{5,1},{2,6},{6,2},{3,7},{7,3},{8,12},{12,8},{9,1... | collective-permute-start | bytes 7077896 | tf_op jit(solution)/shard_map/ppermute | solution.py:527
  213.3 117.1 %collective-permute-start.34 = (bf16[2,384,1536]{2,1,0:T(8,128)(2,1)}, bf16[2,384,1536]{2,1,0:T(8,128)(2,1)}, u32[]{:S(2)}, u32[]{:S(2)}) collective-permute-start(bf16[2,384,1536]{2,1,0:T(8,128)(2,1)} %get-tuple-element.364), channel_id=1, source_target_pairs={{0,2},{2,0},{1,3},{3,1},{4,6},{6,4},{5,7},{7,5},{8,10},{10,8},{9,1... | collective-permute-start | bytes 7077896 | tf_op jit(solution)/shard_map/ppermute | solution.py:524
  258.1 6.2 collective-permute-start
  330.4 54.5 %collective-permute-start.35 = (bf16[2,384,1536]{2,1,0:T(8,128)(2,1)}, bf16[2,384,1536]{2,1,0:T(8,128)(2,1)}, u32[]{:S(2)}, u32[]{:S(2)}) collective-permute-start(bf16[2,384,1536]{2,1,0:T(8,128)(2,1)} %get-tuple-element.369), channel_id=1, source_target_pairs={{0,4},{4,0},{1,5},{5,1},{2,6},{6,2},{3,7},{7,3},{8,12},{12,8},{9,1... | collective-permute-start | bytes 7077896 | tf_op jit(solution)/shard_map/ppermute | solution.py:527
  331.1 54.4 %collective-permute-start.36 = (bf16[2,384,1536]{2,1,0:T(8,128)(2,1)}, bf16[2,384,1536]{2,1,0:T(8,128)(2,1)}, u32[]{:S(2)}, u32[]{:S(2)}) collective-permute-start(bf16[2,384,1536]{2,1,0:T(8,128)(2,1)} %get-tuple-element.370), channel_id=1, source_target_pairs={{0,2},{2,0},{1,3},{3,1},{4,6},{6,4},{5,7},{7,5},{8,10},{10,8},{9,1... | collective-permute-start | bytes 7077896 | tf_op jit(solution)/shard_map/ppermute | solution.py:524
  365.0 87.8 %collective-permute-start.37 = (bf16[768,1536]{1,0:T(8,128)(2,1)}, bf16[768,1536]{1,0:T(8,128)(2,1)}, u32[]{:S(2)}, u32[]{:S(2)}) collective-permute-start(bf16[768,1536]{1,0:T(8,128)(2,1)} %convolution_convert_fusion.10), channel_id=1, source_target_pairs={{0,4},{4,0},{1,5},{5,1},{2,6},{6,2},{3,7},{7,3},{8,12},{12,8},{9,1... | collective-permute-start | bytes 7077896 | tf_op jit(solution)/shard_map/ppermute | solution.py:527
  370.7 82.1 %collective-permute-start.38 = (bf16[768,1536]{1,0:T(8,128)(2,1)}, bf16[768,1536]{1,0:T(8,128)(2,1)}, u32[]{:S(2)}, u32[]{:S(2)}) collective-permute-start(bf16[768,1536]{1,0:T(8,128)(2,1)} %convolution_convert_fusion.9), channel_id=1, source_target_pairs={{0,2},{2,0},{1,3},{3,1},{4,6},{6,4},{5,7},{7,5},{8,10},{10,8},{9,1... | collective-permute-start | bytes 7077896 | tf_op jit(solution)/shard_map/ppermute | solution.py:524
  420.5 24.4 %collective-permute-start.7 = (bf16[512,1536]{1,0:T(8,128)(2,1)S(1)}, bf16[512,1536]{1,0:T(8,128)(2,1)S(1)}, u32[]{:S(2)}, u32[]{:S(2)}) collective-permute-start(bf16[512,1536]{1,0:T(8,128)(2,1)S(1)} %fusion.4), channel_id=1, source_target_pairs={{0,1},{1,0},{2,3},{3,2},{4,5},{5,4},{6,7},{7,6},{8,9},{9,8},{10,11... | collective-permute-start | bytes 4718600 | tf_op jit(solution)/shard_map/cond/branch_1_fun/ppermute | solution.py:530
  452.8 28.7 %collective-permute-start.39 = (bf16[768,768]{0,1:T(8,128)(2,1)}, bf16[768,768]{0,1:T(8,128)(2,1)}, u32[]{:S(2)}, u32[]{:S(2)}) collective-permute-start(bf16[768,768]{0,1:T(8,128)(2,1)} %get-tuple-element.386), channel_id=1, source_target_pairs={{0,4},{4,0},{1,5},{5,1},{2,6},{6,2},{3,7},{7,3},{8,12},{12,8},{9,1... | collective-permute-start | bytes 3538952 | tf_op jit(solution)/shard_map/ppermute | solution.py:527
  456.6 28.4 %collective-permute-start.40 = (bf16[768,768]{0,1:T(8,128)(2,1)}, bf16[768,768]{0,1:T(8,128)(2,1)}, u32[]{:S(2)}, u32[]{:S(2)}) collective-permute-start(bf16[768,768]{0,1:T(8,128)(2,1)} %copy.117), channel_id=1, source_target_pairs={{0,2},{2,0},{1,3},{3,1},{4,6},{6,4},{5,7},{7,5},{8,10},{10,8},{9,1... | collective-permute-start | bytes 3538952 | tf_op jit(solution)/shard_map/ppermute | solution.py:524
  485.0 286.5 %reduce-scatter.10.cloned.1.call-start = ((), (), s32[]{:S(2)}) async-start(), calls=%async_computation.10 | async-start | bytes 2949120 | tf_op jit(solution)/shard_map/reduce_scatter | solution.py:644
  485.1 50.4 %collective-permute-start.41 = (bf16[768,768]{0,1:T(8,128)(2,1)}, bf16[768,768]{0,1:T(8,128)(2,1)}, u32[]{:S(2)}, u32[]{:S(2)}) collective-permute-start(bf16[768,768]{0,1:T(8,128)(2,1)} %get-tuple-element.397), channel_id=1, source_target_pairs={{0,4},{4,0},{1,5},{5,1},{2,6},{6,2},{3,7},{7,3},{8,12},{12,8},{9,1... | collective-permute-start | bytes 3538952 | tf_op jit(solution)/shard_map/ppermute | solution.py:527
  488.2 47.3 %collective-permute-start.42 = (bf16[768,768]{0,1:T(8,128)(2,1)}, bf16[768,768]{0,1:T(8,128)(2,1)}, u32[]{:S(2)}, u32[]{:S(2)}) collective-permute-start(bf16[768,768]{0,1:T(8,128)(2,1)} %copy.119), channel_id=1, source_target_pairs={{0,2},{2,0},{1,3},{3,1},{4,6},{6,4},{5,7},{7,5},{8,10},{10,8},{9,1... | collective-permute-start | bytes 3538952 | tf_op jit(solution)/shard_map/ppermute | solution.py:524
  488.6 6.3 collective-permute-start.4
  535.5 54.2 %collective-permute-start.43 = (bf16[768,1536]{0,1:T(8,128)(2,1)}, bf16[768,1536]{0,1:T(8,128)(2,1)}, u32[]{:S(2)}, u32[]{:S(2)}) collective-permute-start(bf16[768,1536]{0,1:T(8,128)(2,1)} %get-tuple-element.400), channel_id=1, source_target_pairs={{0,4},{4,0},{1,5},{5,1},{2,6},{6,2},{3,7},{7,3},{8,12},{12,8},{9,1... | collective-permute-start | bytes 7077896 | tf_op jit(solution)/shard_map/ppermute | solution.py:527
  537.2 53.8 %collective-permute-start.44 = (bf16[768,1536]{0,1:T(8,128)(2,1)}, bf16[768,1536]{0,1:T(8,128)(2,1)}, u32[]{:S(2)}, u32[]{:S(2)}) collective-permute-start(bf16[768,1536]{0,1:T(8,128)(2,1)} %get-tuple-element.402), channel_id=1, source_target_pairs={{0,2},{2,0},{1,3},{3,1},{4,6},{6,4},{5,7},{7,5},{8,10},{10,8},{9,1... | collective-permute-start | bytes 7077896 | tf_op jit(solution)/shard_map/ppermute | solution.py:524
  543.1 12.7 %collective-permute-start.5 = (bf16[512,1536]{1,0:T(8,128)(2,1)}, bf16[512,1536]{1,0:T(8,128)(2,1)}, u32[]{:S(2)}, u32[]{:S(2)}) collective-permute-start(bf16[512,1536]{1,0:T(8,128)(2,1)} %convolution_convert_fusion.6), channel_id=1, source_target_pairs={{0,1},{1,0},{2,3},{3,2},{4,5},{5,4},{6,7},{7,6},{8,9},{9,8},{10,11... | collective-permute-start | bytes 4718600 | tf_op jit(solution)/shard_map/cond/branch_1_fun/ppermute | solution.py:530
  566.0 7.5 collective-permute-start.6
  593.4 63.7 %collective-permute-start.45 = (bf16[384,1536]{1,0:T(8,128)(2,1)}, bf16[384,1536]{1,0:T(8,128)(2,1)}, u32[]{:S(2)}, u32[]{:S(2)}) collective-permute-start(bf16[384,1536]{1,0:T(8,128)(2,1)} %copy.122), channel_id=1, source_target_pairs={{0,2},{2,0},{1,3},{3,1},{4,6},{6,4},{5,7},{7,5},{8,10},{10,8},{9,1... | collective-permute-start | bytes 3538952 | tf_op jit(solution)/shard_map/ppermute | solution.py:524
  597.2 60.0 %collective-permute-start.46 = (bf16[384,1536]{1,0:T(8,128)(2,1)}, bf16[384,1536]{1,0:T(8,128)(2,1)}, u32[]{:S(2)}, u32[]{:S(2)}) collective-permute-start(bf16[384,1536]{1,0:T(8,128)(2,1)} %copy.123), channel_id=1, source_target_pairs={{0,4},{4,0},{1,5},{5,1},{2,6},{6,2},{3,7},{7,3},{8,12},{12,8},{9,1... | collective-permute-start | bytes 3538952 | tf_op jit(solution)/shard_map/ppermute | solution.py:527
  667.5 148.1 %reduce-scatter.12.cloned.1.call-start = ((), (), s32[]{:S(2)}) async-start(), calls=%async_computation.11 | async-start | bytes 2949120 | tf_op jit(solution)/shard_map/reduce_scatter | solution.py:644
  670.2 45.9 %collective-permute-start.47 = (bf16[384,1536]{1,0:T(8,128)(2,1)}, bf16[384,1536]{1,0:T(8,128)(2,1)S(1)}, u32[]{:S(2)}, u32[]{:S(2)}) collective-permute-start(bf16[384,1536]{1,0:T(8,128)(2,1)} %copy.125), channel_id=1, source_target_pairs={{0,2},{2,0},{1,3},{3,1},{4,6},{6,4},{5,7},{7,5},{8,10},{10,8},{9,1... | collective-permute-start | bytes 3538952 | tf_op jit(solution)/shard_map/ppermute | solution.py:524
  673.1 42.9 %collective-permute-start.48 = (bf16[384,1536]{1,0:T(8,128)(2,1)}, bf16[384,1536]{1,0:T(8,128)(2,1)}, u32[]{:S(2)}, u32[]{:S(2)}) collective-permute-start(bf16[384,1536]{1,0:T(8,128)(2,1)} %copy.126), channel_id=1, source_target_pairs={{0,4},{4,0},{1,5},{5,1},{2,6},{6,2},{3,7},{7,3},{8,12},{12,8},{9,1... | collective-permute-start | bytes 3538952 | tf_op jit(solution)/shard_map/ppermute | solution.py:527
  676.9 35.7 %collective-permute-start.49 = (bf16[768,384]{0,1:T(8,128)(2,1)}, bf16[768,384]{0,1:T(8,128)(2,1)}, u32[]{:S(2)}, u32[]{:S(2)}) collective-permute-start(bf16[768,384]{0,1:T(8,128)(2,1)} %copy.127), channel_id=1, source_target_pairs={{0,4},{4,0},{1,5},{5,1},{2,6},{6,2},{3,7},{7,3},{8,12},{12,8},{9,1... | collective-permute-start | bytes 1769480 | tf_op jit(solution)/shard_map/ppermute | solution.py:527
  680.0 36.0 %collective-permute-start.50 = (bf16[768,384]{1,0:T(8,128)(2,1)}, bf16[768,384]{1,0:T(8,128)(2,1)}, u32[]{:S(2)}, u32[]{:S(2)}) collective-permute-start(bf16[768,384]{1,0:T(8,128)(2,1)} %get-tuple-element.437), channel_id=1, source_target_pairs={{0,2},{2,0},{1,3},{3,1},{4,6},{6,4},{5,7},{7,5},{8,10},{10,8},{9,1... | collective-permute-start | bytes 1769480 | tf_op jit(solution)/shard_map/ppermute | solution.py:524
  716.1 55.4 %collective-permute-start.51 = (bf16[768,1152]{1,0:T(8,128)(2,1)}, bf16[768,1152]{1,0:T(8,128)(2,1)}, u32[]{:S(2)}, u32[]{:S(2)}) collective-permute-start(bf16[768,1152]{1,0:T(8,128)(2,1)} %get-tuple-element.443), channel_id=1, source_target_pairs={{0,4},{4,0},{1,5},{5,1},{2,6},{6,2},{3,7},{7,3},{8,12},{12,8},{9,1... | collective-permute-start | bytes 5308424 | tf_op jit(solution)/shard_map/ppermute | solution.py:527
  717.6 53.9 %collective-permute-start.52 = (bf16[768,1152]{1,0:T(8,128)(2,1)}, bf16[768,1152]{1,0:T(8,128)(2,1)}, u32[]{:S(2)}, u32[]{:S(2)}) collective-permute-start(bf16[768,1152]{1,0:T(8,128)(2,1)} %get-tuple-element.444), channel_id=1, source_target_pairs={{0,2},{2,0},{1,3},{3,1},{4,6},{6,4},{5,7},{7,5},{8,10},{10,8},{9,1... | collective-permute-start | bytes 5308424 | tf_op jit(solution)/shard_map/ppermute | solution.py:524
  727.2 121.1 %reduce-scatter.16.cloned.1.call-start = ((), (), s32[]{:S(2)}) async-start(), calls=%async_computation.13 | async-start | bytes 122880
  743.3 13.5 %collective-permute-start.10 = (bf16[512,1536]{1,0:T(8,128)(2,1)}, bf16[512,1536]{1,0:T(8,128)(2,1)S(1)}, u32[]{:S(2)}, u32[]{:S(2)}) collective-permute-start(bf16[512,1536]{1,0:T(8,128)(2,1)} %fusion.167), channel_id=1, source_target_pairs={{0,1},{1,0},{2,3},{3,2},{4,5},{5,4},{6,7},{7,6},{8,9},{9,8},{10,11... | collective-permute-start | bytes 4718600 | tf_op jit(solution)/shard_map/cond/branch_1_fun/ppermute | solution.py:530
  779.4 36.1 %collective-permute-start.53 = (bf16[384,1536]{1,0:T(8,128)(2,1)}, bf16[384,1536]{1,0:T(8,128)(2,1)}, u32[]{:S(2)}, u32[]{:S(2)}) collective-permute-start(bf16[384,1536]{1,0:T(8,128)(2,1)} %pad_maximum_fusion.27), channel_id=1, source_target_pairs={{0,2},{2,0},{1,3},{3,1},{4,6},{6,4},{5,7},{7,5},{8,10},{10,8},{9,1... | collective-permute-start | bytes 3538952 | tf_op jit(solution)/shard_map/ppermute | solution.py:524
  785.7 29.8 %collective-permute-start.54 = (bf16[384,1536]{1,0:T(8,128)(2,1)}, bf16[384,1536]{1,0:T(8,128)(2,1)}, u32[]{:S(2)}, u32[]{:S(2)}) collective-permute-start(bf16[384,1536]{1,0:T(8,128)(2,1)} %pad_maximum_fusion.29), channel_id=1, source_target_pairs={{0,4},{4,0},{1,5},{5,1},{2,6},{6,2},{3,7},{7,3},{8,12},{12,8},{9,1... | collective-permute-start | bytes 3538952 | tf_op jit(solution)/shard_map/ppermute | solution.py:527
  791.8 3.9 collective-permute-start.8
  817.7 7.2 collective-permute-start.56
  825.0 4.7 collective-permute-start.57
  830.5 66.0 %reduce-scatter.14.cloned.1.call-start = ((), (), s32[]{:S(2)}) async-start(), calls=%async_computation.12 | async-start | bytes 2949120 | tf_op jit(solution)/shard_map/reduce_scatter | solution.py:644
  833.5 7.3 collective-permute-start.58
  834.9 7.0 collective-permute-start.59
  (95 other events, 685.3 us)
Sparse Core Ops, SparseCore 0:
  10.2 45.0 all-gather.8
  57.4 58.9 all-gather.4
  118.6 88.0 all-gather.6
  208.7 87.7 all-gather.10
  485.1 81.9 reduce-scatter.7
  667.6 45.2 reduce-scatter.9
  727.3 44.6 reduce-scatter.11
  830.6 17.6 reduce-scatter.15
  850.6 45.8 reduce-scatter.13

commit v5 on v4

--- a/solution.py
+++ b/solution.py
@@ -378,10 +378,15 @@
     def gather_first(self, shard):
         return lax.all_gather(shard, self.dp, axis=0, tiled=True)
 
-    def gather_weights(self, *sets_and_rows):
-        *sets, rows = sets_and_rows
-        *first, last = [self.gather_first(shard) for shard in sets]
-        return *first, rows, None, None, (last, None)
+    def gather_first_set(self, first, second, feed_in, feed_out, rows):
+        return first, rows, (second, feed_in, feed_out)
+
+    def place_pieces(self, first):
+        return self.gather_first(first)
+
+    def gather_rest(self, rest, value):
+        second, feed_in, feed_out = [self.gather_first(shard) for shard in rest]
+        return second, feed_in, None, None, (feed_out, None)
 
     def feed_out(self, pieces):
         return pieces[0]
@@ -543,7 +548,7 @@
         half = shard.shape[1] // 256 * 128
         return shard[:, :half], shard[:, half:]
 
-    def gather_weights(self, first, second, feed_in, feed_out, rows):
+    def gather_first_set(self, first, second, feed_in, feed_out, rows):
         opened = []
         for shard in (feed_in, feed_out):
             a, b = self.halves(shard)
@@ -551,35 +556,43 @@
         rows, opened = lax.optimization_barrier((rows, opened))
         sets = [lax.all_gather(shard, "z", axis=0, tiled=True) for shard in (first, second)]
         feeds = [lax.all_gather(four, "z", axis=1, tiled=True) for four in opened]
-        whole, last = [], rows
+        pieces, last, _ = self.gather_pieces(sets[0], rows)
+        pieces_next = self.gather_pieces(sets[1], last)
+        return pieces, rows, (pieces_next, feeds)
+
+    def gather_pieces(self, four, last):
+        a, b = self.halves(tie(four, last))
+        xa, yb, ya, xb = self.x(a), self.y(b), self.y(a), self.x(b)
+        far_a, far_b = self.y(xa), self.x(yb)
+        return (four, xa, ya, far_a, xb, yb, far_b), (far_a, far_b, ya, xb), (xa, yb)
+
+    def place_pieces(self, pieces):
+        four, xa, ya, far_a, xb, yb, far_b = pieces
+        n, half = xa.shape
+        return place(
+            [
+                (four, 0, 0),
+                (xa, n, 0),
+                (ya, 2 * n, 0),
+                (far_a, 3 * n, 0),
+                (xb, n, half),
+                (yb, 2 * n, half),
+                (far_b, 3 * n, half),
+            ],
+            (4 * n, four.shape[1]),
+        )
+
+    def gather_rest(self, rest, value):
+        (pieces, last, _), feeds = rest
+        feeds[0] = tie(feeds[0], value)
         in_sides = feeds[0][:2], feeds[0][2:]
-        for four, ahead in zip(sets, ((), in_sides)):
-            a, b = self.halves(tie(four, last))
-            n, half = a.shape
-            xa, yb, ya, xb = self.x(a), self.y(b), self.y(a), self.x(b)
-            far_a, far_b = self.y(xa), self.x(yb)
-            last, before = (far_a, far_b, ya, xb), (xa, yb)
-            four = tie(four, ahead)
-            whole.append(
-                place(
-                    [
-                        (four, 0, 0),
-                        (xa, n, 0),
-                        (ya, 2 * n, 0),
-                        (far_a, 3 * n, 0),
-                        (xb, n, half),
-                        (yb, 2 * n, half),
-                        (far_b, 3 * n, half),
-                    ],
-                    (4 * n, four.shape[1]),
-                )
-            )
-        a, b = tie(in_sides, before)
+        a, b = tie(in_sides, last)
         in_far = self.y(a), self.x(b)
-        whole.append(self.place_feed(feeds[0], in_far))
+        w_cross = self.place_pieces(pieces)
+        w_in = self.place_feed(feeds[0], in_far)
         out_sides = feeds[1][:2], feeds[1][2:]
         a, b = tie(out_sides, in_far)
-        return *whole, rows, in_far, out_sides, (feeds[1], (self.y(a), self.x(b)))
+        return w_cross, w_in, in_far, out_sides, (feeds[1], (self.y(a), self.x(b)))
 
     def place_feed(self, four, far):
         _, n, half = four.shape
@@ -664,8 +677,15 @@
         sums = self.sum_all(jnp.pad(sums.T, ((0, 0), (0, 122))))
         sums = sums[: 2 * n] + self.y(sums[2 * n :].astype(BF)).astype(F32)
         sums = sums[:n] + self.x(sums[n:].astype(BF)).astype(F32)
-        sums = lax.psum_scatter(sums.astype(BF), "z", scatter_dimension=0, tiled=True)
-        return sums[:, :6].T.astype(F32)
+        own = lax.axis_index("z")
+        for step, pairs, side in (
+            (n // 2, [(0, 2), (1, 3), (2, 0), (3, 1)], own // 2),
+            (n // 4, [(0, 1), (1, 0), (2, 3), (3, 2)], own % 2),
+        ):
+            near = lax.dynamic_slice_in_dim(sums, side * step, step)
+            away = lax.dynamic_slice_in_dim(sums, (1 - side) * step, step)
+            sums = near + lax.ppermute(away.astype(BF), "z", pairs).astype(F32)
+        return sums[:, :6].T
 
     def spread(self, rows, clips):
         return jnp.concatenate([rows, self.other(rows)])
@@ -833,20 +853,24 @@
     values0 = comm.arrange(frames.reshape(own_rows, width)).astype(F32)
     stats0 = norm_stats(values0)
     own_n1 = norm_apply(values0, stats0, gain[0], shift[0])
-    w_self, w_cross, w_in, own_n1, mark_in, mark_out, out_pieces = comm.gather_weights(
+    pieces, own_n1, rest = comm.gather_first_set(
         first_set, second_set, feed_input, feed_output.T, own_n1
     )
-
-    def split_cross(weights):
-        return jnp.split(weights, [cols, 2 * cols, 4 * cols], axis=1)
-
-
     up = comm.arrange(upstream.reshape(own_rows, width))
     text = comm.arrange(text_states.reshape(clips * texts, width))
     up_all = comm.spread(up, clips)
 
     n1 = comm.spread(own_n1, clips)
-    att, self_saved = comm.self_attend(mm(n1, w_self).astype(BF), clips)
+
+    def split_cross(weights):
+        return jnp.split(weights, [cols, 2 * cols, 4 * cols], axis=1)
+
+    def stage_self(pieces, n1):
+        w_self = comm.place_pieces(pieces)
+        return w_self, comm.self_attend(mm(n1, w_self).astype(BF), clips)
+
+    w_self, (att, self_saved) = comm.stage(stage_self, pieces, n1)
+    w_cross, w_in, mark_in, mark_out, out_pieces = comm.gather_rest(rest, att)
 
     def stage0(values0, att, w_cross, text):
         w_so, w_cq, w_cm, w_co = split_cross(w_cross)
@@ -923,23 +947,26 @@
     in_sums, datt = comm.after((in_sums, datt), far_cross, half_out)
     in_second = comm.second(in_sums)
 
-    def stage5(pairs, far, saved, datt, r1_all, att):
+    def stage5(pairs, far, r1_all, att):
         far = comm.parted(far, cols, cols, 2 * cols)
         sums = comm.adds(*[(*pair, one) for pair, one in zip(pairs, far)])
-        return sums, comm.self_back(saved, datt, clips), comm.sends(r1_all, att)
-
-    cross_sums, dqkv, send_so = comm.stage(
-        stage5, cross_pairs, far_cross, self_saved, datt, r1_all, att
-    )
-    cross_sums, dqkv, send_so, in_sums = comm.after(
-        (cross_sums, dqkv, send_so, in_sums), in_second
-    )
+        return sums, comm.sends(r1_all, att)
+
+    cross_sums, send_so = comm.stage(stage5, cross_pairs, far_cross, r1_all, att)
+    cross_sums, send_so, datt, in_sums = comm.after(
+        (cross_sums, send_so, datt, in_sums), in_second
+    )
+    cross_second = comm.second(cross_sums)
+    far_so = comm.exchange(send_so)
     half_in = comm.scatter_z(comm.closing(in_sums, in_second))
-    far_so = comm.exchange(send_so)
-    cross_second = comm.second(cross_sums)
-    send_self = comm.stage(comm.sends, n1, dqkv)
-    dmem, hidden, send_self, cross_sums = comm.after(
-        (dmem, hidden, send_self, cross_sums), cross_second, far_so
+
+    def stage_back(saved, datt, n1):
+        dqkv = comm.self_back(saved, datt, clips)
+        return dqkv, comm.sends(n1, dqkv)
+
+    dqkv, send_self = comm.stage(stage_back, self_saved, datt, n1)
+    dmem, hidden, send_self, cross_sums, dqkv = comm.after(
+        (dmem, hidden, send_self, cross_sums, dqkv), cross_second, far_so
     )
     far_self = comm.exchange(send_self)
     half_cross = comm.scatter_z(comm.closing(cross_sums, cross_second))

time: 916 us -> 880 us (0.961)
  waiting for transfers between devices: 234 us -> 175 us
  local copies, waits for them, and re-layouts: 118 us -> 133 us
  matrix products: 249 us -> 261 us
    all_gather x4, waiting for transfers between devices: 70.5 us -> 23 us  [the longest x2 21.8 us: gather_first_set(): lax.all_gather(shard, 'z', axis=0, tiled=True)]
    reduce_scatter x4, waiting for transfers between devices: 46.8 us -> 0.02 us  [scatter_z(): return lax.psum_scatter(parts, 'z', scatter_dimension=1, tiled=True)]
    ppermute x22, waiting for transfers between devices: 47.4 us -> 67.6 us  [x(): return lax.ppermute(v, 'x', SWAP)]
    ppermute x22, waiting for transfers between devices: 52.9 us -> 62.8 us  [y(): return lax.ppermute(v, 'y', SWAP)]
    optimization_barrier x11 -> x12, local copies, waits for them, and re-layouts: 23.5 us -> 30.5 us  [tie(): return lax.optimization_barrier((value, others))[0]]
  transfers between devices with their start and end apart: 69 -> 70, of which waited for: 26 -> 26; matrix products, arithmetic and copies ran while one was open for 47% -> 52% of each run, Pallas kernels for 16% -> 17%
where the time goes in v5:
time: 880 us; the launch traced here: 868 us
  matrix products  261 us (30%)
  waiting for transfers between devices  175 us (20%)
  Pallas kernels  147 us (17%)
  local copies, waits for them, and re-layouts  133 us (15%)
  other arithmetic  78.2 us (9%)
  starting transfers between devices  58.6 us (7%)
  between operations  15.1 us (2%)
    dot_general x32, matrix products, mm_rows(): lax.dot_general(left, right, (((0,), (0,)), ((), ())), preferred_element_...  110 us
    dot_general x17, matrix products, mm_t(): lax.dot_general(left, right, (((1,), (1,)), ((), ())), preferred_element_...  108 us
    ppermute x22, waiting for transfers between devices, x(): return lax.ppermute(v, 'x', SWAP)  67.6 us
    ppermute x22, waiting for transfers between devices, y(): return lax.ppermute(v, 'y', SWAP)  62.8 us
    dot_general x8, matrix products, mm(): return jnp.dot(left, right, preferred_element_type=F32)  42.9 us
    optimization_barrier x12, local copies, waits for them, and re-layouts, tie(): return lax.optimization_barrier((value, others))[0]  30.5 us
    pallas_call x1, Pallas kernels, self_back(): pl.pallas_call(self_back_kernel, grid_spec=pltpu.PrefetchScalarGridSpec(n...  30 us
    ppermute x22, starting transfers between devices, y(): return lax.ppermute(v, 'y', SWAP)  25.5 us
  transfers between devices with their start and end apart: 70, of which 26 were waited for; matrix products, arithmetic and copies ran while one was open for 52% of the time, Pallas kernels for 17%

profile of v5, /device:TPU:0, one launch (start us, length us, event | category | flops | bytes accessed | tf_op | source)
XLA Modules:
  0.0 868.2 jit_solution(17527433045922081659)
XLA Ops:
  29.3 5.8 collective-permute-done.12
  48.6 6.7 all-gather.7.cloned.1.call-done
  62.3 18.5 %collective-permute-done.19 = bf16[384,1152]{1,0:T(8,128)(2,1)S(1)} collective-permute-done((bf16[384,1152]{1,0:T(8,128)(2,1)}, bf16[384,1152]{1,0:T(8,128)(2,1)S(1)}, u32[]{:S(2)}, u32[]{:S(2)}) %collective-permute-start.19) | collective-permute-done | bytes 884768 | tf_op jit(solution)/shard_map/ppermute | solution.py:529
  83.7 17.6 %collective-permute-done.23 = bf16[384,1152]{1,0:T(8,128)(2,1)} collective-permute-done((bf16[384,1152]{1,0:T(8,128)(2,1)}, bf16[384,1152]{1,0:T(8,128)(2,1)}, u32[]{:S(2)}, u32[]{:S(2)}) %collective-permute-start.23) | collective-permute-done | bytes 884768 | tf_op jit(solution)/shard_map/ppermute | solution.py:532
  101.3 15.1 %all-gather.5.cloned.1.call-done.refs_0_ = bf16[384,3840]{1,0:T(8,128)(2,1)} async-done(((bf16[96,3840]{1,0:T(8,128)(2,1)}), bf16[384,3840]{1,0:T(8,128)(2,1)}) %all-gather.5.cloned.1.call-update) | async-done | bytes 2949136 | tf_op jit(solution)/shard_map/all_gather | solution.py:557
  126.4 31.4 %collective-permute-done.25.refs_1_ = bf16[384,1920]{1,0:T(8,128)(2,1)} collective-permute-done((bf16[384,1920]{1,0:T(8,128)(2,1)}, bf16[384,1920]{1,0:T(8,128)(2,1)}, u32[]{:S(2)}, u32[]{:S(2)}) %collective-permute-start.25) | collective-permute-done | bytes 1474592 | tf_op jit(solution)/shard_map/ppermute | solution.py:529
  168.6 36.8 %conditional.10 = (bf16[1536,2304]{1,0:T(8,128)(2,1)}, bf16[1024,768]{1,0:T(8,128)(2,1)}, s32[1]{0:T(128)}, bf16[2,2,256,2304]{3,2,1,0:T(8,128)(2,1)}, f32[2,2,256,768]{3,2,1,0:T(8,128)}) conditional(s32[]{:T(128)} %convert_element_type.419, () %tuple.125, (bf16[384,2304]{1,0:T(8,128)(2,1)}, bf16[384,1152]{1,0:T(8,128)(2,1)S(1)}, ...), branch_computations={%region_2.3_spmd, %region_3.4_spmd} | conditional | flops 8458076160 | bytes 24379432 | solution.py:612
  168.6 5.8 place.2
  174.5 12.8 %convolution_convert_fusion = bf16[2304,1024]{0,1:T(8,128)(2,1)} fusion(bf16[1536,2304]{1,0:T(8,128)(2,1)} %place.2, bf16[1024,1536]{0,1:T(8,128)(2,1)} %get-tuple-element.757), kind=kOutput, calls=%fused_computation | convolution fusion | flops 7250116608 | bytes 14942208 | tf_op jit(solution)/shard_map/cond/branch_1_fun/dot_general | solution.py:19
  187.2 18.2 %self_attend.1 = (bf16[2,2,256,768]{3,2,1,0:T(8,128)(2,1)}, f32[2,2,256,768]{3,2,1,0:T(8,128)}) custom-call(s32[1]{0:T(128)} %bitcast.core_ref, bf16[2,2,256,2304]{3,2,1,0:T(8,128)(2,1)} %bitcast.2.q_ref.k_ref.v_ref, bf16[2,2,256,2304]{3,2,1,0:T(8,128)(2,1)} %bitcast.2.q_ref.k_ref.v_ref, bf16[2,2,256,2304]{3,2,1,0:T(8,128)(2,1)} %bitcast.2.q_ref.k_ref.v_ref), custom_call_target="tpu_custom_call" | custom-call | flops 1207959552 | bytes 9437184 | tf_op jit(solution)/shard_map/cond/branch_1_fun/self_attend/pallas_call | solution.py:707
  206.7 5.0 fusion.416
  211.7 7.3 collective-permute-done.27.refs_3_
  228.5 8.9 %place.3 = bf16[1536,3840]{1,0:T(8,128)(2,1)} custom-call(bf16[384,3840]{1,0:T(8,128)(2,1)} %all-gather.5.cloned.1.call-done.refs_0_, bf16[384,1920]{1,0:T(8,128)(2,1)} %collective-permute-done.25.refs_1_, bf16[384,1920]{1,0:T(8,128)(2,1)} %collective-permute-done.26.refs_2_, bf16[384,1920]{1,0:T(8,128)(2,1)} %collective-permute-done.27.refs_3_, ...), custom_call_target="tpu_custom_call" | custom-call | tf_op jit(solution)/shard_map/place/pallas_call | solution.py:139
  237.4 65.2 %conditional.11 = (f32[512,1536]{1,0:T(8,128)}, f32[512,1]{0,1:T(1,128)S(1)}, f32[512,1]{0,1:T(1,128)S(1)}, bf16[1024,1536]{1,0:T(8,128)(2,1)}, bf16[1024,768]{1...) conditional(s32[]{:T(128)} %convert_element_type.419, ...), branch_computations={%region_4.5_spmd, %region_5.10_spmd} | conditional | flops 8087077888 | bytes 141820608 | solution.py:612
  237.4 4.6 convolution_convert_fusion.6
  246.9 6.0 fusion.407
  263.5 6.4 fusion.217
  269.9 13.4 %cross_attend.1 = bf16[2,2,256,768]{3,2,1,0:T(8,128)(2,1)} custom-call(bf16[2,2,256,768]{3,2,1,0:T(8,128)(2,1)} %bitcast.6.q_ref, bf16[2,64,1536]{2,1,0:T(8,128)(2,1)S(1)} %bitcast.205, bf16[2,64,1536]{2,1,0:T(8,128)(2,1)S(1)} %bitcast.206), custom_call_target="tpu_custom_call" | custom-call | flops 201326592 | bytes 3145728 | tf_op jit(solution)/shard_map/cond/branch_1_fun/cross_attend/pallas_call | solution.py:770
  302.6 4.8 fusion.415
  308.8 7.4 place_stacked.3.weight_ref
  316.2 20.0 %feed.1 = (bf16[1024,3072]{1,0:T(8,128)(2,1)}, bf16[1024,3072]{1,0:T(8,128)(2,1)}) custom-call(bf16[1024,1536]{1,0:T(8,128)(2,1)} %get-tuple-element.396.rows_ref, bf16[1536,3072]{1,0:T(8,128)(2,1)} %place_stacked.3.weight_ref), custom_call_target="tpu_custom_call" | custom-call | flops 9663676416 | bytes 25165824 | tf_op jit(solution)/shard_map/feed/pallas_call | solution.py:311
  336.2 6.6 convolution_convert_fusion.10
  352.8 9.1 %collective-permute-done.35 = bf16[2,384,1536]{2,1,0:T(8,128)(2,1)} collective-permute-done((bf16[2,384,1536]{2,1,0:T(8,128)(2,1)}, bf16[2,384,1536]{2,1,0:T(8,128)(2,1)}, u32[]{:S(2)}, u32[]{:S(2)}) %collective-permute-start.35) | collective-permute-done | bytes 2359328 | tf_op jit(solution)/shard_map/ppermute | solution.py:532
  362.5 67.3 %conditional.12 = (bf16[1536,3072]{1,0:T(8,128)(2,1)}, bf16[1024,3072]{1,0:T(8,128)(2,1)}, bf16[768,768]{0,1:T(8,128)(2,1)}, bf16[768,768]{1,0:T(8,128)(2,1)}, b...) conditional(s32[]{:T(128)} %convert_element_type.419, ...), branch_computations={%region_10.11_spmd, %region_11.12_spmd} | conditional | flops 24170201088 | bytes 124256440 | solution.py:612
  362.5 7.3 place_stacked.2.weight_ref
  369.8 18.0 %slope_product.1 = bf16[1024,3072]{1,0:T(8,128)(2,1)} custom-call(bf16[1024,1536]{1,0:T(8,128)(2,1)} %get-tuple-element.199.rows_ref, bf16[1536,3072]{1,0:T(8,128)(2,1)} %place_stacked.2.weight_ref, bf16[1024,3072]{1,0:T(8,128)(2,1)} %get-tuple-element.200.slope_ref), custom_call_target="tpu_custom_call" | custom-call | flops 9663676416 | bytes 25165824 | tf_op jit(solution)/shard_map/cond/branch_1_fun/slope_product/pallas_call | solution.py:346
  387.8 9.9 %fusion.4 = bf16[512,1536]{1,0:T(8,128)(2,1)S(1)} fusion(bf16[1536,3072]{1,0:T(8,128)(2,1)} %get-tuple-element.202, bf16[1024,3072]{1,0:T(8,128)(2,1)} %slope_product.1), kind=kOutput, calls=%fused_computation.6 | convolution fusion | flops 4832624640 | bytes 14155776 | tf_op jit(solution)/shard_map/cond/branch_1_fun/dot_general | solution.py:23
  407.1 4.3 fusion.30
  411.4 4.5 fusion.27
  415.9 6.0 fusion.389
  421.9 7.9 convert_add_fusion
  434.4 25.9 %conditional.13 = (bf16[4,384,1536]{2,1,0:T(8,128)(2,1)}, f32[512,1536]{1,0:T(8,128)}, bf16[512,1536]{1,0:T(8,128)(2,1)}, f32[1,1536]{1,0:T(1,128)}, f32[1,1536]{1,0:T(1,128)}) conditional(s32[]{:T(128)} %convert_element_type.419, () %tuple.123, (bf16[1024,1536]{1,0:T(8,128)(2,1)}, bf16[1024,3072]{1,0:T(8,128)(2,1)}, bf16[768,1536]{1,0:T(8,128)(2,1)}, ...), branch_computations={%region_12.13_spmd, %region_13.18_spmd} | conditional | flops 4864078848 | bytes 97640592 | solution.py:612
  436.1 5.3 add_convert_fusion.5
  441.5 4.5 add_convert_fusion.6
  454.7 4.4 fusion.387
  465.9 53.4 %conditional.14 = (bf16[1024,1536]{1,0:T(8,128)(2,1)}, bf16[1024,768]{1,0:T(8,128)(2,1)}, bf16[128,1536]{1,0:T(8,128)(2,1)}, bf16[768,1536]{0,1:T(8,128)(2,1)}, bf16[768,1536]{0,1:T(8,128)(2,1)}) conditional(s32[]{:T(128)} %convert_element_type.419, () %tuple.122, (bf16[512,1536]{1,0:T(8,128)(2,1)}, bf16[1024,768]{1,0:T(8,128)(2,1)}, ...), branch_computations={%region_18.19_spmd, %region_19.20_spmd} | conditional | flops 5661130752 | bytes 69599480 | solution.py:612
  480.3 6.5 fusion.39
  486.7 17.6 %cross_back.1 = (bf16[2,2,256,768]{3,2,1,0:T(8,128)(2,1)}, bf16[2,64,1536]{2,1,0:T(8,128)(2,1)}) custom-call(bf16[2,2,256,768]{3,2,1,0:T(8,128)(2,1)} %bitcast.24.q_ref, bf16[2,64,1536]{2,1,0:T(8,128)(2,1)S(1)} %get-tuple-element.215.k_ref.v_ref, bf16[2,64,1536]{2,1,0:T(8,128)(2,1)S(1)} %get-tuple-element.215.k_ref.v_ref, bf16[2,2,256,768]{3,2,1,0:T(8,128)(2,1)} %bitcast.211), custom_call_target="tpu_custom_call" | custom-call | flops 503316480 | bytes 4718592 | tf_op jit(solution)/shard_map/cond/branch_1_fun/cross_back/pallas_call | solution.py:787
  522.0 46.6 %conditional.15 = (bf16[384,1536]{0,1:T(8,128)(2,1)}, bf16[384,1536]{0,1:T(8,128)(2,1)}, bf16[384,1536]{0,1:T(8,128)(2,1)}, bf16[384,1536]{0,1:T(8,128)(2,1)}, f...) conditional(s32[]{:T(128)} %convert_element_type.419, ...), branch_computations={%region_20.21_spmd, %region_21.26_spmd} | conditional | flops 9710072832 | bytes 99999896 | solution.py:612
  522.0 4.5 convolution_convert_fusion.7
  526.6 4.7 add_convert_fusion.9
  542.5 5.5 multiply_reduce_fusion.5
  548.0 4.9 fusion.388
  562.2 6.4 fusion.236
  568.6 4.7 collective-permute-done.43
  581.8 29.0 %conditional.16 = (bf16[384,1536]{0,1:T(8,128)(2,1)}, bf16[384,1536]{0,1:T(8,128)(2,1)}, bf16[384,1536]{0,1:T(8,128)(2,1)}, bf16[384,1536]{0,1:T(8,128)(2,1)}, b...) conditional(s32[]{:T(128)} %convert_element_type.419, () %tuple.140, (bf16[1024,1536]{1,0:T(8,128)(2,1)}, ...), branch_computations={%region_26.27_spmd, %region_27.28_spmd} | conditional | flops 3957522432 | bytes 56623180 | solution.py:612
  636.6 45.6 %conditional.17 = (bf16[1024,2304]{1,0:T(8,128)(2,1)}, bf16[768,1152]{0,1:T(8,128)(2,1)}, bf16[768,1152]{1,0:T(8,128)(2,1)}) conditional(s32[]{:T(128)} %convert_element_type.419, () %tuple.139, (bf16[1024,768]{1,0:T(8,128)(2,1)}, s32[1]{0:T(128)}, bf16[2,2,256,2304]{3,2,1,0:T(8,128)(2,1)}, f32[2,2,256,768]{3,2,1,0:T(8,128)}, ...), branch_computations={%region_29.30_spmd, %region_30.31_spmd} | conditional | flops 6648692736 | bytes 47579188 | solution.py:612
  636.6 30.0 %self_back.1 = bf16[2,2,256,2304]{3,2,1,0:T(8,128)(2,1)} custom-call(s32[1]{0:T(128)} %get-tuple-element.246.core_ref, bf16[2,2,256,2304]{3,2,1,0:T(8,128)(2,1)} %get-tuple-element.247.q_ref.k_ref.v_ref, bf16[2,2,256,2304]{3,2,1,0:T(8,128)(2,1)} %get-tuple-element.247.q_ref.k_ref.v_ref, bf16[2,2,256,2304]{3,2,1,0:T(8,128)(2,1)} %get-tuple-element.247.q_ref.k_ref.v_ref, ...), custom_call_target="tpu_custom_call" | custom-call | flops 3019898880 | bytes 14155776 | tf_op jit(solution)/shard_map/cond/branch_1_fun/self_back/pallas_call | solution.py:737
  666.6 4.6 copy.135
  671.2 5.6 fusion.147
  677.0 5.1 convolution_convert_fusion.3
  703.1 39.1 %conditional.18 = (f32[128,1536]{1,0:T(8,128)}, bf16[512,1536]{1,0:T(8,128)(2,1)}) conditional(s32[]{:T(128)} %convert_element_type.419, () %tuple.118, (bf16[1536,3840]{1,0:T(8,128)(2,1)}, bf16[128,1536]{1,0:T(8,128)(2,1)}, bf16[1024,3072]{1,0:T(8,128)(2,1)}, bf16[1536,3072]{1,0:T(8,128)(2,1)}, f32[512,1536]{1,0:T(8,128)S(1)}) %tuple.149), branch_computations={%region_31.32_spmd, %region_32.33_spmd} | conditional | flops 13905571840 | bytes 55075012 | solution.py:612
  703.1 10.5 %fusion.168 = bf16[512,1536]{1,0:T(8,128)(2,1)} fusion(bf16[1536,3072]{1,0:T(8,128)(2,1)} %get-tuple-element.255, bf16[1024,3072]{1,0:T(8,128)(2,1)} %get-tuple-element.254), kind=kOutput, calls=%fused_computation.141 | convolution fusion | flops 4832624640 | bytes 14155776 | tf_op jit(solution)/shard_map/cond/branch_1_fun/dot_general | solution.py:23
  713.7 5.1 fusion.405
  728.5 13.7 %fusion.167 = bf16[512,1536]{1,0:T(8,128)(2,1)} fusion(s32[1536]{0:T(1024)S(1)} %fusion.183, f32[512,1536]{1,0:T(8,128)S(1)} %get-tuple-element.253, bf16[512,1536]{1,0:T(8,128)(2,1)} %collective-permute-done.10, bf16[1536,3072]{1,0:T(8,128)(2,1)} %get-tuple-element.255, bf16[1024,3072]{1,0:T(8,128)(2,1)} %get-tuple-element.254), kind=kOutput, calls=%fused_computation.140 | convolution fusion | flops 7254048768 | bytes 18880512 | tf_op jit(solution)/shard_map/cond/branch_1_fun/dot_general | solution.py:23
  748.2 4.4 fusion.305
  755.3 4.9 fusion.304
  767.9 15.9 %collective-permute-done.54 = bf16[384,1536]{1,0:T(8,128)(2,1)} collective-permute-done((bf16[384,1536]{1,0:T(8,128)(2,1)}, bf16[384,1536]{1,0:T(8,128)(2,1)}, u32[]{:S(2)}, u32[]{:S(2)}) %collective-permute-start.54) | collective-permute-done | bytes 1179680 | tf_op jit(solution)/shard_map/ppermute | solution.py:532
  785.4 5.0 collective-permute-done.53
  798.1 32.9 %conditional.19 = (f32[512,1536]{1,0:T(8,128)}, f32[1536]{0:T(1024)S(1)}, f32[1,1536]{1,0:T(1,128)S(1)}) conditional(s32[]{:T(128)} %convert_element_type.419, () %tuple.151, (bf16[1024,2304]{1,0:T(8,128)(2,1)}, bf16[1536,2304]{1,0:T(8,128)(2,1)}, f32[3,1536]{0,1:T(8,128)S(1)}, f32[512]{0:T(512)S(1)}, f32[512,1536]{0,1:T(8,128)}, ...), branch_computations={%region_34.35_spmd, %region_35.40_spmd} | conditional | flops 12104838144 | bytes 81926312 | solution.py:612
  798.1 9.3 %convolution_convert_fusion.8 = bf16[512,1536]{1,0:T(8,128)(2,1)} fusion(bf16[1536,2304]{1,0:T(8,128)(2,1)} %get-tuple-element.258, bf16[1024,2304]{1,0:T(8,128)(2,1)} %get-tuple-element.257), kind=kOutput, calls=%fused_computation.291 | convolution fusion | flops 3624665088 | bytes 11010048 | tf_op jit(solution)/shard_map/cond/branch_1_fun/dot_general | solution.py:23
  811.5 9.3 %multiply_reduce_fusion.8 = (f32[1536]{0:T(1024)S(1)}, f32[512]{0:T(512)S(1)}, f32[512]{0:T(512)S(1)}, f32[1536]{0:T(1024)S(1)}, f32[512,1536]{1,0:T(8,128)S(1)}) fusion(f32[512,1536]{1,0:T(8,128)} %copy.146, f32[512]{0:T(512)S(1)} %get-tuple-element.888, f32[512]{0:T(512)S(1)} %get-tuple-element.889, f32[1536]{0:T(1024)S(1)} %slice_reduce_fusion.6, ...), kind=kOutput, calls=%fused_computation.286 | convolution fusion | flops 3632525312 | bytes 17328128 | tf_op jit(solution)/shard_map/cond/branch_1_fun/dot_general | solution.py:23
  826.6 4.4 fusion.265
  836.5 5.8 collective-permute-done.56
  (468 shorter events, 360.5 us)
Async XLA Ops:
  7.2 48.1 %all-gather.7.cloned.1.call-start = ((), (), s32[]{:S(2)}) async-start(), calls=%async_computation.5 | async-start | bytes 2211840 | tf_op jit(solution)/shard_map/all_gather | solution.py:557
  9.3 107.1 %all-gather.5.cloned.1.call-start = ((), (), s32[]{:S(2)}) async-start(), calls=%async_computation.4 | async-start | bytes 3686400 | tf_op jit(solution)/shard_map/all_gather | solution.py:557
  10.2 15.9 %collective-permute-start.11 = (bf16[96,128]{1,0:T(8,128)(2,1)S(1)}, bf16[96,128]{1,0:T(8,128)(2,1)S(1)}, u32[]{:S(2)}, u32[]{:S(2)}) collective-permute-start(bf16[96,128]{1,0:T(8,128)(2,1)S(1)} %get-tuple-element.982), channel_id=1, source_target_pairs={{0,8},{8,0},{16,24},{24,16},{1,9},{9,1},{17,25},{25,17},{2,10},{10... | collective-permute-start | bytes 73736 | tf_op jit(solution)/shard_map/ppermute | solution.py:538
  16.2 190.5 %all-gather.9.cloned.1.call-start = ((), (), s32[]{:S(2)}) async-start(), calls=%async_computation.6 | async-start | bytes 5898240 | tf_op jit(solution)/shard_map/all_gather | solution.py:558
  17.3 24.2 %collective-permute-start.16 = (bf16[96,1536]{1,0:T(8,128)(2,1)}, bf16[96,1536]{1,0:T(8,128)(2,1)}, u32[]{:S(2)}, u32[]{:S(2)}) collective-permute-start(bf16[96,1536]{1,0:T(8,128)(2,1)} %get-tuple-element.968), channel_id=1, source_target_pairs={{0,4},{4,0},{1,5},{5,1},{2,6},{6,2},{3,7},{7,3},{8,12},{12,8},{9,1... | collective-permute-start | bytes 884744 | tf_op jit(solution)/shard_map/ppermute | solution.py:532
  18.8 22.7 %collective-permute-start.15 = (bf16[96,1536]{1,0:T(8,128)(2,1)}, bf16[96,1536]{1,0:T(8,128)(2,1)}, u32[]{:S(2)}, u32[]{:S(2)}) collective-permute-start(bf16[96,1536]{1,0:T(8,128)(2,1)} %get-tuple-element.969), channel_id=1, source_target_pairs={{0,2},{2,0},{1,3},{3,1},{4,6},{6,4},{5,7},{7,5},{8,10},{10,8},{9,1... | collective-permute-start | bytes 884744 | tf_op jit(solution)/shard_map/ppermute | solution.py:529
  22.3 21.4 %collective-permute-start.18 = (bf16[96,1536]{1,0:T(8,128)(2,1)}, bf16[96,1536]{1,0:T(8,128)(2,1)}, u32[]{:S(2)}, u32[]{:S(2)}) collective-permute-start(bf16[96,1536]{1,0:T(8,128)(2,1)} %get-tuple-element.964), channel_id=1, source_target_pairs={{0,4},{4,0},{1,5},{5,1},{2,6},{6,2},{3,7},{7,3},{8,12},{12,8},{9,1... | collective-permute-start | bytes 884744 | tf_op jit(solution)/shard_map/ppermute | solution.py:532
  22.8 20.9 %collective-permute-start.17 = (bf16[96,1536]{1,0:T(8,128)(2,1)}, bf16[96,1536]{1,0:T(8,128)(2,1)}, u32[]{:S(2)}, u32[]{:S(2)}) collective-permute-start(bf16[96,1536]{1,0:T(8,128)(2,1)} %get-tuple-element.965), channel_id=1, source_target_pairs={{0,2},{2,0},{1,3},{3,1},{4,6},{6,4},{5,7},{7,5},{8,10},{10,8},{9,1... | collective-permute-start | bytes 884744 | tf_op jit(solution)/shard_map/ppermute | solution.py:529
  26.2 9.0 %collective-permute-start.12 = (bf16[2,96,128]{2,1,0:T(8,128)(2,1)S(1)}, bf16[2,96,128]{2,1,0:T(8,128)(2,1)S(1)}, u32[]{:S(2)}, u32[]{:S(2)}) collective-permute-start(bf16[2,96,128]{2,1,0:T(8,128)(2,1)S(1)} %pad_maximum_fusion.37), channel_id=1, source_target_pairs={{0,16},{8,24},{16,0},{24,8},{1,17},{9,25},{17,1},{25,9},{2,18},{10... | collective-permute-start | bytes 147464 | tf_op jit(solution)/shard_map/ppermute | solution.py:539
  35.2 4.7 collective-permute-start.13
  39.9 6.0 collective-permute-start.14
  48.5 254.1 %all-gather.11.cloned.1.call-start = ((), (), s32[]{:S(2)}) async-start(), calls=%async_computation.7 | async-start | bytes 5898240 | tf_op jit(solution)/shard_map/all_gather | solution.py:558
  58.1 22.7 %collective-permute-start.19 = (bf16[384,1152]{1,0:T(8,128)(2,1)}, bf16[384,1152]{1,0:T(8,128)(2,1)S(1)}, u32[]{:S(2)}, u32[]{:S(2)}) collective-permute-start(bf16[384,1152]{1,0:T(8,128)(2,1)} %get-tuple-element.934), channel_id=1, source_target_pairs={{0,2},{2,0},{1,3},{3,1},{4,6},{6,4},{5,7},{7,5},{8,10},{10,8},{9,1... | collective-permute-start | bytes 2654216 | tf_op jit(solution)/shard_map/ppermute | solution.py:529
  59.5 22.7 %collective-permute-start.21 = (bf16[384,1152]{1,0:T(8,128)(2,1)}, bf16[384,1152]{1,0:T(8,128)(2,1)S(1)}, u32[]{:S(2)}, u32[]{:S(2)}) collective-permute-start(bf16[384,1152]{1,0:T(8,128)(2,1)} %get-tuple-element.933), channel_id=1, source_target_pairs={{0,4},{4,0},{1,5},{5,1},{2,6},{6,2},{3,7},{7,3},{8,12},{12,8},{9,1... | collective-permute-start | bytes 2654216 | tf_op jit(solution)/shard_map/ppermute | solution.py:532
  61.0 513.5 %reduce-scatter.5.cloned.1.call-start = ((), (), s32[]{:S(2)}) async-start(), calls=%async_computation.8 | async-start | bytes 5898240 | tf_op jit(solution)/shard_map/reduce_scatter | solution.py:657
  61.1 40.3 %collective-permute-start.23 = (bf16[384,1152]{1,0:T(8,128)(2,1)}, bf16[384,1152]{1,0:T(8,128)(2,1)}, u32[]{:S(2)}, u32[]{:S(2)}) collective-permute-start(bf16[384,1152]{1,0:T(8,128)(2,1)} %get-tuple-element.934), channel_id=1, source_target_pairs={{0,4},{4,0},{1,5},{5,1},{2,6},{6,2},{3,7},{7,3},{8,12},{12,8},{9,1... | collective-permute-start | bytes 2654216 | tf_op jit(solution)/shard_map/ppermute | solution.py:532
  61.7 39.6 %collective-permute-start.24 = (bf16[384,1152]{1,0:T(8,128)(2,1)}, bf16[384,1152]{1,0:T(8,128)(2,1)}, u32[]{:S(2)}, u32[]{:S(2)}) collective-permute-start(bf16[384,1152]{1,0:T(8,128)(2,1)} %get-tuple-element.933), channel_id=1, source_target_pairs={{0,2},{2,0},{1,3},{3,1},{4,6},{6,4},{5,7},{7,5},{8,10},{10,8},{9,1... | collective-permute-start | bytes 2654216 | tf_op jit(solution)/shard_map/ppermute | solution.py:529
  80.8 37.9 %collective-permute-start.20 = (bf16[384,1152]{1,0:T(8,128)(2,1)S(1)}, bf16[384,1152]{1,0:T(8,128)(2,1)}, u32[]{:S(2)}, u32[]{:S(2)}) collective-permute-start(bf16[384,1152]{1,0:T(8,128)(2,1)S(1)} %collective-permute-done.19), channel_id=1, source_target_pairs={{0,4},{4,0},{1,5},{5,1},{2,6},{6,2},{3,7},{7,3},{8,12},{12,8},{9,1... | collective-permute-start | bytes 2654216 | tf_op jit(solution)/shard_map/ppermute | solution.py:532
  82.3 36.4 %collective-permute-start.22 = (bf16[384,1152]{1,0:T(8,128)(2,1)S(1)}, bf16[384,1152]{1,0:T(8,128)(2,1)}, u32[]{:S(2)}, u32[]{:S(2)}) collective-permute-start(bf16[384,1152]{1,0:T(8,128)(2,1)S(1)} %collective-permute-done.21), channel_id=1, source_target_pairs={{0,2},{2,0},{1,3},{3,1},{4,6},{6,4},{5,7},{7,5},{8,10},{10,8},{9,1... | collective-permute-start | bytes 2654216 | tf_op jit(solution)/shard_map/ppermute | solution.py:529
  122.4 35.5 %collective-permute-start.25 = (bf16[384,1920]{1,0:T(8,128)(2,1)}, bf16[384,1920]{1,0:T(8,128)(2,1)}, u32[]{:S(2)}, u32[]{:S(2)}) collective-permute-start(bf16[384,1920]{1,0:T(8,128)(2,1)} %get-tuple-element.928), channel_id=1, source_target_pairs={{0,2},{2,0},{1,3},{3,1},{4,6},{6,4},{5,7},{7,5},{8,10},{10,8},{9,1... | collective-permute-start | bytes 4423688 | tf_op jit(solution)/shard_map/ppermute | solution.py:529
  122.9 36.4 %collective-permute-start.29 = (bf16[384,1920]{1,0:T(8,128)(2,1)}, bf16[384,1920]{1,0:T(8,128)(2,1)}, u32[]{:S(2)}, u32[]{:S(2)}) collective-permute-start(bf16[384,1920]{1,0:T(8,128)(2,1)} %get-tuple-element.927), channel_id=1, source_target_pairs={{0,4},{4,0},{1,5},{5,1},{2,6},{6,2},{3,7},{7,3},{8,12},{12,8},{9,1... | collective-permute-start | bytes 4423688 | tf_op jit(solution)/shard_map/ppermute | solution.py:532
  124.4 41.6 %collective-permute-start.32 = (bf16[512,1536]{0,1:T(8,128)(2,1)}, bf16[512,1536]{0,1:T(8,128)(2,1)}, u32[]{:S(2)}, u32[]{:S(2)}) collective-permute-start(bf16[512,1536]{0,1:T(8,128)(2,1)} %add_convert_fusion.11), channel_id=1, source_target_pairs={{0,1},{1,0},{2,3},{3,2},{4,5},{5,4},{6,7},{7,6},{8,9},{9,8},{10,11... | collective-permute-start | bytes 4718600 | tf_op jit(solution)/shard_map/ppermute | solution.py:535
  124.4 87.3 %collective-permute-start.26 = (bf16[384,1920]{1,0:T(8,128)(2,1)}, bf16[384,1920]{1,0:T(8,128)(2,1)}, u32[]{:S(2)}, u32[]{:S(2)}) collective-permute-start(bf16[384,1920]{1,0:T(8,128)(2,1)} %get-tuple-element.928), channel_id=1, source_target_pairs={{0,4},{4,0},{1,5},{5,1},{2,6},{6,2},{3,7},{7,3},{8,12},{12,8},{9,1... | collective-permute-start | bytes 4423688 | tf_op jit(solution)/shard_map/ppermute | solution.py:532
  124.9 86.8 %collective-permute-start.28 = (bf16[384,1920]{1,0:T(8,128)(2,1)}, bf16[384,1920]{1,0:T(8,128)(2,1)}, u32[]{:S(2)}, u32[]{:S(2)}) collective-permute-start(bf16[384,1920]{1,0:T(8,128)(2,1)} %get-tuple-element.927), channel_id=1, source_target_pairs={{0,2},{2,0},{1,3},{3,1},{4,6},{6,4},{5,7},{7,5},{8,10},{10,8},{9,1... | collective-permute-start | bytes 4423688 | tf_op jit(solution)/shard_map/ppermute | solution.py:529
  157.8 61.2 %collective-permute-start.27 = (bf16[384,1920]{1,0:T(8,128)(2,1)}, bf16[384,1920]{1,0:T(8,128)(2,1)}, u32[]{:S(2)}, u32[]{:S(2)}) collective-permute-start(bf16[384,1920]{1,0:T(8,128)(2,1)} %collective-permute-done.25.refs_1_), channel_id=1, source_target_pairs={{0,4},{4,0},{1,5},{5,1},{2,6},{6,2},{3,7},{7,3},{8,12},{12,8},{9,1... | collective-permute-start | bytes 4423688 | tf_op jit(solution)/shard_map/ppermute | solution.py:532
  159.3 59.7 %collective-permute-start.30 = (bf16[384,1920]{1,0:T(8,128)(2,1)}, bf16[384,1920]{1,0:T(8,128)(2,1)}, u32[]{:S(2)}, u32[]{:S(2)}) collective-permute-start(bf16[384,1920]{1,0:T(8,128)(2,1)} %collective-permute-done.29.refs_5_), channel_id=1, source_target_pairs={{0,2},{2,0},{1,3},{3,1},{4,6},{6,4},{5,7},{7,5},{8,10},{10,8},{9,1... | collective-permute-start | bytes 4423688 | tf_op jit(solution)/shard_map/ppermute | solution.py:529
  165.9 60.2 %collective-permute-start.31 = (bf16[512,1536]{1,0:T(8,128)(2,1)S(1)}, bf16[512,1536]{1,0:T(8,128)(2,1)}, u32[]{:S(2)}, u32[]{:S(2)}) collective-permute-start(bf16[512,1536]{1,0:T(8,128)(2,1)S(1)} %fusion.312), channel_id=1, source_target_pairs={{0,1},{1,0},{2,3},{3,2},{4,5},{5,4},{6,7},{7,6},{8,9},{9,8},{10,11... | collective-permute-start | bytes 4718600 | tf_op jit(solution)/shard_map/ppermute | solution.py:535
  219.0 88.4 %collective-permute-start.33 = (bf16[2,384,1536]{2,1,0:T(8,128)(2,1)}, bf16[2,384,1536]{2,1,0:T(8,128)(2,1)}, u32[]{:S(2)}, u32[]{:S(2)}) collective-permute-start(bf16[2,384,1536]{2,1,0:T(8,128)(2,1)} %get-tuple-element.393), channel_id=1, source_target_pairs={{0,4},{4,0},{1,5},{5,1},{2,6},{6,2},{3,7},{7,3},{8,12},{12,8},{9,1... | collective-permute-start | bytes 7077896 | tf_op jit(solution)/shard_map/ppermute | solution.py:532
  220.5 86.9 %collective-permute-start.34 = (bf16[2,384,1536]{2,1,0:T(8,128)(2,1)}, bf16[2,384,1536]{2,1,0:T(8,128)(2,1)}, u32[]{:S(2)}, u32[]{:S(2)}) collective-permute-start(bf16[2,384,1536]{2,1,0:T(8,128)(2,1)} %get-tuple-element.394), channel_id=1, source_target_pairs={{0,2},{2,0},{1,3},{3,1},{4,6},{6,4},{5,7},{7,5},{8,10},{10,8},{9,1... | collective-permute-start | bytes 7077896 | tf_op jit(solution)/shard_map/ppermute | solution.py:529
  242.0 4.9 collective-permute-start
  307.4 54.5 %collective-permute-start.35 = (bf16[2,384,1536]{2,1,0:T(8,128)(2,1)}, bf16[2,384,1536]{2,1,0:T(8,128)(2,1)}, u32[]{:S(2)}, u32[]{:S(2)}) collective-permute-start(bf16[2,384,1536]{2,1,0:T(8,128)(2,1)} %get-tuple-element.399), channel_id=1, source_target_pairs={{0,4},{4,0},{1,5},{5,1},{2,6},{6,2},{3,7},{7,3},{8,12},{12,8},{9,1... | collective-permute-start | bytes 7077896 | tf_op jit(solution)/shard_map/ppermute | solution.py:532
  308.1 54.4 %collective-permute-start.36 = (bf16[2,384,1536]{2,1,0:T(8,128)(2,1)}, bf16[2,384,1536]{2,1,0:T(8,128)(2,1)}, u32[]{:S(2)}, u32[]{:S(2)}) collective-permute-start(bf16[2,384,1536]{2,1,0:T(8,128)(2,1)} %get-tuple-element.400), channel_id=1, source_target_pairs={{0,2},{2,0},{1,3},{3,1},{4,6},{6,4},{5,7},{7,5},{8,10},{10,8},{9,1... | collective-permute-start | bytes 7077896 | tf_op jit(solution)/shard_map/ppermute | solution.py:529
  342.8 87.0 %collective-permute-start.37 = (bf16[768,1536]{1,0:T(8,128)(2,1)}, bf16[768,1536]{1,0:T(8,128)(2,1)}, u32[]{:S(2)}, u32[]{:S(2)}) collective-permute-start(bf16[768,1536]{1,0:T(8,128)(2,1)} %convolution_convert_fusion.10), channel_id=1, source_target_pairs={{0,4},{4,0},{1,5},{5,1},{2,6},{6,2},{3,7},{7,3},{8,12},{12,8},{9,1... | collective-permute-start | bytes 7077896 | tf_op jit(solution)/shard_map/ppermute | solution.py:532
  348.2 81.6 %collective-permute-start.38 = (bf16[768,1536]{1,0:T(8,128)(2,1)}, bf16[768,1536]{1,0:T(8,128)(2,1)}, u32[]{:S(2)}, u32[]{:S(2)}) collective-permute-start(bf16[768,1536]{1,0:T(8,128)(2,1)} %convolution_convert_fusion.9), channel_id=1, source_target_pairs={{0,2},{2,0},{1,3},{3,1},{4,6},{6,4},{5,7},{7,5},{8,10},{10,8},{9,1... | collective-permute-start | bytes 7077896 | tf_op jit(solution)/shard_map/ppermute | solution.py:529
  397.7 24.2 %collective-permute-start.7 = (bf16[512,1536]{1,0:T(8,128)(2,1)S(1)}, bf16[512,1536]{1,0:T(8,128)(2,1)S(1)}, u32[]{:S(2)}, u32[]{:S(2)}) collective-permute-start(bf16[512,1536]{1,0:T(8,128)(2,1)S(1)} %fusion.4), channel_id=1, source_target_pairs={{0,1},{1,0},{2,3},{3,2},{4,5},{5,4},{6,7},{7,6},{8,9},{9,8},{10,11... | collective-permute-start | bytes 4718600 | tf_op jit(solution)/shard_map/cond/branch_1_fun/ppermute | solution.py:535
  429.8 30.5 %collective-permute-start.39 = (bf16[768,768]{0,1:T(8,128)(2,1)}, bf16[768,768]{0,1:T(8,128)(2,1)}, u32[]{:S(2)}, u32[]{:S(2)}) collective-permute-start(bf16[768,768]{0,1:T(8,128)(2,1)} %get-tuple-element.416), channel_id=1, source_target_pairs={{0,4},{4,0},{1,5},{5,1},{2,6},{6,2},{3,7},{7,3},{8,12},{12,8},{9,1... | collective-permute-start | bytes 3538952 | tf_op jit(solution)/shard_map/ppermute | solution.py:532
  433.7 28.4 %collective-permute-start.40 = (bf16[768,768]{0,1:T(8,128)(2,1)}, bf16[768,768]{0,1:T(8,128)(2,1)}, u32[]{:S(2)}, u32[]{:S(2)}) collective-permute-start(bf16[768,768]{0,1:T(8,128)(2,1)} %copy.128), channel_id=1, source_target_pairs={{0,2},{2,0},{1,3},{3,1},{4,6},{6,4},{5,7},{7,5},{8,10},{10,8},{9,1... | collective-permute-start | bytes 3538952 | tf_op jit(solution)/shard_map/ppermute | solution.py:529
  462.1 285.3 %reduce-scatter.7.cloned.1.call-start = ((), (), s32[]{:S(2)}) async-start(), calls=%async_computation.9 | async-start | bytes 2949120 | tf_op jit(solution)/shard_map/reduce_scatter | solution.py:657
  462.1 57.1 %collective-permute-start.41 = (bf16[768,768]{0,1:T(8,128)(2,1)}, bf16[768,768]{0,1:T(8,128)(2,1)}, u32[]{:S(2)}, u32[]{:S(2)}) collective-permute-start(bf16[768,768]{0,1:T(8,128)(2,1)} %get-tuple-element.427), channel_id=1, source_target_pairs={{0,4},{4,0},{1,5},{5,1},{2,6},{6,2},{3,7},{7,3},{8,12},{12,8},{9,1... | collective-permute-start | bytes 3538952 | tf_op jit(solution)/shard_map/ppermute | solution.py:532
  465.2 54.1 %collective-permute-start.42 = (bf16[768,768]{0,1:T(8,128)(2,1)}, bf16[768,768]{0,1:T(8,128)(2,1)}, u32[]{:S(2)}, u32[]{:S(2)}) collective-permute-start(bf16[768,768]{0,1:T(8,128)(2,1)} %copy.130), channel_id=1, source_target_pairs={{0,2},{2,0},{1,3},{3,1},{4,6},{6,4},{5,7},{7,5},{8,10},{10,8},{9,1... | collective-permute-start | bytes 3538952 | tf_op jit(solution)/shard_map/ppermute | solution.py:529
  465.9 9.0 %collective-permute-start.4 = (bf16[512,1536]{1,0:T(8,128)(2,1)}, bf16[512,1536]{1,0:T(8,128)(2,1)}, u32[]{:S(2)}, u32[]{:S(2)}) collective-permute-start(bf16[512,1536]{1,0:T(8,128)(2,1)} %get-tuple-element.213), channel_id=1, source_target_pairs={{0,1},{1,0},{2,3},{3,2},{4,5},{5,4},{6,7},{7,6},{8,9},{9,8},{10,11... | collective-permute-start | bytes 4718600 | tf_op jit(solution)/shard_map/cond/branch_1_fun/ppermute | solution.py:535
  519.3 54.0 %collective-permute-start.43 = (bf16[768,1536]{0,1:T(8,128)(2,1)}, bf16[768,1536]{0,1:T(8,128)(2,1)}, u32[]{:S(2)}, u32[]{:S(2)}) collective-permute-start(bf16[768,1536]{0,1:T(8,128)(2,1)} %get-tuple-element.430), channel_id=1, source_target_pairs={{0,4},{4,0},{1,5},{5,1},{2,6},{6,2},{3,7},{7,3},{8,12},{12,8},{9,1... | collective-permute-start | bytes 7077896 | tf_op jit(solution)/shard_map/ppermute | solution.py:532
  520.8 53.7 %collective-permute-start.44 = (bf16[768,1536]{0,1:T(8,128)(2,1)}, bf16[768,1536]{0,1:T(8,128)(2,1)}, u32[]{:S(2)}, u32[]{:S(2)}) collective-permute-start(bf16[768,1536]{0,1:T(8,128)(2,1)} %get-tuple-element.432), channel_id=1, source_target_pairs={{0,2},{2,0},{1,3},{3,1},{4,6},{6,4},{5,7},{7,5},{8,10},{10,8},{9,1... | collective-permute-start | bytes 7077896 | tf_op jit(solution)/shard_map/ppermute | solution.py:529
  526.5 16.0 %collective-permute-start.5 = (bf16[512,1536]{1,0:T(8,128)(2,1)}, bf16[512,1536]{1,0:T(8,128)(2,1)}, u32[]{:S(2)}, u32[]{:S(2)}) collective-permute-start(bf16[512,1536]{1,0:T(8,128)(2,1)} %convolution_convert_fusion.7), channel_id=1, source_target_pairs={{0,1},{1,0},{2,3},{3,2},{4,5},{5,4},{6,7},{7,6},{8,9},{9,8},{10,11... | collective-permute-start | bytes 4718600 | tf_op jit(solution)/shard_map/cond/branch_1_fun/ppermute | solution.py:535
  553.0 7.4 collective-permute-start.6
  577.0 33.9 %collective-permute-start.45 = (bf16[384,1536]{1,0:T(8,128)(2,1)}, bf16[384,1536]{1,0:T(8,128)(2,1)}, u32[]{:S(2)}, u32[]{:S(2)}) collective-permute-start(bf16[384,1536]{1,0:T(8,128)(2,1)} %copy.133), channel_id=1, source_target_pairs={{0,2},{2,0},{1,3},{3,1},{4,6},{6,4},{5,7},{7,5},{8,10},{10,8},{9,1... | collective-permute-start | bytes 3538952 | tf_op jit(solution)/shard_map/ppermute | solution.py:529
  581.2 29.7 %collective-permute-start.46 = (bf16[384,1536]{1,0:T(8,128)(2,1)}, bf16[384,1536]{1,0:T(8,128)(2,1)}, u32[]{:S(2)}, u32[]{:S(2)}) collective-permute-start(bf16[384,1536]{1,0:T(8,128)(2,1)} %copy.134), channel_id=1, source_target_pairs={{0,4},{4,0},{1,5},{5,1},{2,6},{6,2},{3,7},{7,3},{8,12},{12,8},{9,1... | collective-permute-start | bytes 3538952 | tf_op jit(solution)/shard_map/ppermute | solution.py:532
  620.2 212.0 %reduce-scatter.9.cloned.1.call-start = ((), (), s32[]{:S(2)}) async-start(), calls=%async_computation.10 | async-start | bytes 2949120 | tf_op jit(solution)/shard_map/reduce_scatter | solution.py:657
  622.8 62.8 %collective-permute-start.47 = (bf16[384,1536]{1,0:T(8,128)(2,1)}, bf16[384,1536]{1,0:T(8,128)(2,1)}, u32[]{:S(2)}, u32[]{:S(2)}) collective-permute-start(bf16[384,1536]{1,0:T(8,128)(2,1)} %copy.136), channel_id=1, source_target_pairs={{0,2},{2,0},{1,3},{3,1},{4,6},{6,4},{5,7},{7,5},{8,10},{10,8},{9,1... | collective-permute-start | bytes 3538952 | tf_op jit(solution)/shard_map/ppermute | solution.py:529
  625.8 59.8 %collective-permute-start.48 = (bf16[384,1536]{1,0:T(8,128)(2,1)}, bf16[384,1536]{1,0:T(8,128)(2,1)}, u32[]{:S(2)}, u32[]{:S(2)}) collective-permute-start(bf16[384,1536]{1,0:T(8,128)(2,1)} %copy.137), channel_id=1, source_target_pairs={{0,4},{4,0},{1,5},{5,1},{2,6},{6,2},{3,7},{7,3},{8,12},{12,8},{9,1... | collective-permute-start | bytes 3538952 | tf_op jit(solution)/shard_map/ppermute | solution.py:532
  629.4 52.7 %collective-permute-start.49 = (bf16[768,384]{0,1:T(8,128)(2,1)}, bf16[768,384]{0,1:T(8,128)(2,1)}, u32[]{:S(2)}, u32[]{:S(2)}) collective-permute-start(bf16[768,384]{0,1:T(8,128)(2,1)} %copy.138), channel_id=1, source_target_pairs={{0,4},{4,0},{1,5},{5,1},{2,6},{6,2},{3,7},{7,3},{8,12},{12,8},{9,1... | collective-permute-start | bytes 1769480 | tf_op jit(solution)/shard_map/ppermute | solution.py:532
  632.6 53.0 %collective-permute-start.50 = (bf16[768,384]{1,0:T(8,128)(2,1)}, bf16[768,384]{1,0:T(8,128)(2,1)}, u32[]{:S(2)}, u32[]{:S(2)}) collective-permute-start(bf16[768,384]{1,0:T(8,128)(2,1)} %get-tuple-element.469), channel_id=1, source_target_pairs={{0,2},{2,0},{1,3},{3,1},{4,6},{6,4},{5,7},{7,5},{8,10},{10,8},{9,1... | collective-permute-start | bytes 1769480 | tf_op jit(solution)/shard_map/ppermute | solution.py:529
  689.5 57.9 %collective-permute-start.51 = (bf16[768,1152]{1,0:T(8,128)(2,1)}, bf16[768,1152]{1,0:T(8,128)(2,1)}, u32[]{:S(2)}, u32[]{:S(2)}) collective-permute-start(bf16[768,1152]{1,0:T(8,128)(2,1)} %copy.139), channel_id=1, source_target_pairs={{0,4},{4,0},{1,5},{5,1},{2,6},{6,2},{3,7},{7,3},{8,12},{12,8},{9,1... | collective-permute-start | bytes 5308424 | tf_op jit(solution)/shard_map/ppermute | solution.py:532
  690.9 56.4 %collective-permute-start.52 = (bf16[768,1152]{1,0:T(8,128)(2,1)}, bf16[768,1152]{1,0:T(8,128)(2,1)}, u32[]{:S(2)}, u32[]{:S(2)}) collective-permute-start(bf16[768,1152]{1,0:T(8,128)(2,1)} %get-tuple-element.477), channel_id=1, source_target_pairs={{0,2},{2,0},{1,3},{3,1},{4,6},{6,4},{5,7},{7,5},{8,10},{10,8},{9,1... | collective-permute-start | bytes 5308424 | tf_op jit(solution)/shard_map/ppermute | solution.py:529
  713.7 14.9 %collective-permute-start.10 = (bf16[512,1536]{1,0:T(8,128)(2,1)}, bf16[512,1536]{1,0:T(8,128)(2,1)}, u32[]{:S(2)}, u32[]{:S(2)}) collective-permute-start(bf16[512,1536]{1,0:T(8,128)(2,1)} %fusion.168), channel_id=1, source_target_pairs={{0,1},{1,0},{2,3},{3,2},{4,5},{5,4},{6,7},{7,6},{8,9},{9,8},{10,11... | collective-permute-start | bytes 4718600 | tf_op jit(solution)/shard_map/cond/branch_1_fun/ppermute | solution.py:535
  746.9 110.3 %reduce-scatter.11.cloned.1.call-start = ((), (), s32[]{:S(2)}) async-start(), calls=%async_computation.11 | async-start | bytes 2949120 | tf_op jit(solution)/shard_map/reduce_scatter | solution.py:657
  754.7 29.2 %collective-permute-start.54 = (bf16[384,1536]{1,0:T(8,128)(2,1)}, bf16[384,1536]{1,0:T(8,128)(2,1)}, u32[]{:S(2)}, u32[]{:S(2)}) collective-permute-start(bf16[384,1536]{1,0:T(8,128)(2,1)} %pad_maximum_fusion.29), channel_id=1, source_target_pairs={{0,4},{4,0},{1,5},{5,1},{2,6},{6,2},{3,7},{7,3},{8,12},{12,8},{9,1... | collective-permute-start | bytes 3538952 | tf_op jit(solution)/shard_map/ppermute | solution.py:532
  761.4 29.1 %collective-permute-start.53 = (bf16[384,1536]{1,0:T(8,128)(2,1)}, bf16[384,1536]{1,0:T(8,128)(2,1)S(1)}, u32[]{:S(2)}, u32[]{:S(2)}) collective-permute-start(bf16[384,1536]{1,0:T(8,128)(2,1)} %pad_maximum_fusion.27), channel_id=1, source_target_pairs={{0,2},{2,0},{1,3},{3,1},{4,6},{6,4},{5,7},{7,5},{8,10},{10,8},{9,1... | collective-permute-start | bytes 3538952 | tf_op jit(solution)/shard_map/ppermute | solution.py:529
  764.6 31.2 %collective-permute-start.60 = (bf16[96,1536]{1,0:T(8,128)(2,1)}, bf16[96,1536]{1,0:T(8,128)(2,1)S(1)}, u32[]{:S(2)}, u32[]{:S(2)}) collective-permute-start(bf16[96,1536]{1,0:T(8,128)(2,1)} %get-tuple-element.937), channel_id=1, source_target_pairs={{0,2},{2,0},{1,3},{3,1},{4,6},{6,4},{5,7},{7,5},{8,10},{10,8},{9,1... | collective-permute-start | bytes 884744 | tf_op jit(solution)/shard_map/ppermute | solution.py:529
  765.3 30.5 %collective-permute-start.61 = (bf16[96,1536]{1,0:T(8,128)(2,1)}, bf16[96,1536]{1,0:T(8,128)(2,1)}, u32[]{:S(2)}, u32[]{:S(2)}) collective-permute-start(bf16[96,1536]{1,0:T(8,128)(2,1)} %get-tuple-element.938), channel_id=1, source_target_pairs={{0,4},{4,0},{1,5},{5,1},{2,6},{6,2},{3,7},{7,3},{8,12},{12,8},{9,1... | collective-permute-start | bytes 884744 | tf_op jit(solution)/shard_map/ppermute | solution.py:532
  807.4 4.1 collective-permute-start.8
  835.0 7.2 collective-permute-start.56
  842.3 4.7 collective-permute-start.57
  847.1 5.2 collective-permute-start.58
  (74 other events, 755.6 us)
Sparse Core Ops, SparseCore 0:
  10.2 45.0 all-gather.6
  57.4 58.9 all-gather.4
  118.6 88.0 all-gather.8
  208.7 87.7 all-gather.10
  462.2 82.9 reduce-scatter.4
  620.3 46.2 reduce-scatter.6
  747.0 46.2 reduce-scatter.8
  795.6 47.0 reduce-scatter.10

commit v6 on v5

--- a/solution.py
+++ b/solution.py
@@ -150,11 +150,11 @@
     n, half = four.shape[0] // 4, four.shape[1]
     spots = [
         (four, 0, 2 * n, 0, 0),
-        (far_a, 0, 2 * n, 2 * n, 0),
+        (far_a, n, n, 2 * n, 0),
+        (far_a, 0, n, 3 * n, 0),
         (four, 2 * n, n, 0, half),
-        (far_b, 0, n, n, half),
-        (four, 3 * n, n, 2 * n, half),
-        (far_b, n, n, 3 * n, half),
+        (far_b, 0, 2 * n, n, half),
+        (four, 3 * n, n, 3 * n, half),
     ]
     copies = [
         pltpu.make_async_copy(
@@ -510,7 +510,7 @@
         place = jnp.arange(self.width, dtype=jnp.int32)
         quarter, rest = place // (4 * self.shard), place % (4 * self.shard)
         z, row = rest // self.shard, rest % self.shard
-        y, x = (quarter // 2) ^ own_y, (quarter % 2) ^ own_x
+        y, x = (quarter // 2) ^ own_y, (quarter // 2) ^ (quarter % 2) ^ own_x
         source = ((z * 2 + y) * 2 + x) * self.shard + row
         return (jnp.arange(self.width, dtype=jnp.int32)[:, None] == source[None, :]).astype(BF)
 
@@ -541,7 +541,8 @@
         four = jnp.concatenate([pair, far])
         four = jnp.stack([lax.dynamic_index_in_dim(four, own ^ p, 0, False) for p in range(4)])
         two = jnp.stack([four, self.x(four)])
-        whole = jnp.stack([two, self.y(two)])
+        far = self.y(two)
+        whole = jnp.stack([two[0], two[1], far[1], far[0]])
         return whole.reshape(self.width, packed.shape[-1])
 
     def halves(self, shard):
@@ -573,11 +574,11 @@
             [
                 (four, 0, 0),
                 (xa, n, 0),
-                (ya, 2 * n, 0),
-                (far_a, 3 * n, 0),
+                (far_a, 2 * n, 0),
+                (ya, 3 * n, 0),
                 (xb, n, half),
-                (yb, 2 * n, half),
-                (far_b, 3 * n, half),
+                (far_b, 2 * n, half),
+                (yb, 3 * n, half),
             ],
             (4 * n, four.shape[1]),
         )
@@ -613,10 +614,9 @@
 
     def sends(self, left, right):
         n, half = self.width // 4, right.shape[1] // 256 * 128
-        far = jnp.concatenate([left[:, n : 2 * n], left[:, 3 * n :]], axis=1)
         return (
             mm_rows(left[:, 2 * n :], right[:, :half]).astype(BF),
-            mm_rows(far, right[:, half:]).astype(BF),
+            mm_rows(left[:, n : 3 * n], right[:, half:]).astype(BF),
         )
 
     def exchange(self, sends):
@@ -637,10 +637,18 @@
         n, parts = self.width // 4, []
         for left, right, (far_y, far_x) in products:
             half = right.shape[1] // 256 * 128
-            first = (mm_rows(left[:, : 2 * n], right[:, :half]) + far_y.astype(F32)).astype(BF)
-            near = jnp.concatenate([left[:, :n], left[:, 2 * n : 3 * n]], axis=1)
-            last = (mm_rows(near, right[:, half:]) + far_x.astype(F32)).astype(BF)
-            parts.append((first[:n], first[n:], last[:n], last[n:]))
+            first, last = right[:, :half], right[:, half:]
+            parts.append(
+                [
+                    (mm_rows(own, side) + far.astype(F32)).astype(BF)
+                    for own, side, far in (
+                        (left[:, :n], first, far_y[n:]),
+                        (left[:, n : 2 * n], first, far_y[:n]),
+                        (left[:, :n], last, far_x[:n]),
+                        (left[:, 3 * n :], last, far_x[n:]),
+                    )
+                ]
+            )
         return [jnp.concatenate(part, axis=1) for part in zip(*parts)]
 
     def middle(self, parts, _):
@@ -675,8 +683,9 @@
     def norm_sums(self, sums):
         n = self.width // 4
         sums = self.sum_all(jnp.pad(sums.T, ((0, 0), (0, 122))))
-        sums = sums[: 2 * n] + self.y(sums[2 * n :].astype(BF)).astype(F32)
-        sums = sums[:n] + self.x(sums[n:].astype(BF)).astype(F32)
+        far = self.y(sums[2 * n :].astype(BF)).astype(F32)
+        away = (sums[n : 2 * n] + far[:n]).astype(BF)
+        sums = sums[:n] + far[n:] + self.x(away).astype(F32)
         own = lax.axis_index("z")
         for step, pairs, side in (
             (n // 2, [(0, 2), (1, 3), (2, 0), (3, 1)], own // 2),
@@ -897,13 +906,11 @@
     def stage1(pieces, rows, slope, n3, w_in):
         w_out = comm.feed_out(pieces)
         pre_grad = comm.slope_product(rows, w_out, slope)
-        sends = [comm.sends(n3, part) for part in jnp.split(pre_grad, 2, axis=1)]
-        return w_out, pre_grad, sends, comm.sum_own(pre_grad, w_in, mm_t, clips)
+        return w_out, pre_grad, comm.sends(n3, pre_grad), comm.sum_own(pre_grad, w_in, mm_t, clips)
 
     w_out, pre_grad, send_in, e3 = comm.stage(stage1, out_pieces, up_all, slope, n3, w_in)
     e3, send_in = comm.after((e3, send_in), far_out)
-    in_parts = jnp.split(pre_grad, 2, axis=1)
-    far_in = [comm.exchange(send_in[0])]
+    far_in = comm.exchange(send_in)
 
     def stage2(rows, hidden, far, e3, values2, stats2, own):
         sent = comm.middle(comm.adds((rows, hidden, far)), None)
@@ -914,9 +921,7 @@
     sent_out, r2, r2_own, gain2, shift2 = comm.stage(
         stage2, up_all, hidden, far_out, e3, values2, stats2, up
     )
-    sent_out, r2_own, send_b = comm.after((sent_out, r2_own, send_in[1:]), far_in[0])
     half_out = comm.scatter_z(sent_out)
-    far_in += [comm.exchange(sends) for sends in send_b]
 
     def stage3(r2_own, saved, w_cross, n2, cross, text):
         w_co = split_cross(w_cross)[3]
@@ -932,9 +937,9 @@
     far_cross = comm.exchange(send_cross)
     cross_pairs = (n2, dcq), (r2_all, cross), (text, dmem)
 
-    def stage4(n3, parts, far, dcq, w_cross, values1, stats1, r2):
+    def stage4(n3, pre_grad, far, dcq, w_cross, values1, stats1, r2):
         w_so, w_cq, *_ = split_cross(w_cross)
-        in_sums = comm.adds(*[(n3, part, one) for part, one in zip(parts, far)])
+        in_sums = comm.adds((n3, pre_grad, far))
         e2 = comm.sum_own(dcq, w_cq, mm_t, clips)
         grads = norm_back(values1, stats1, gain[1], e2)
         r1 = r2 + grads[0]
@@ -942,7 +947,7 @@
         return in_sums, r1, r1_all, mm(r1_all, w_so).astype(BF), grads[1], grads[2]
 
     in_sums, r1, r1_all, datt, gain1, shift1 = comm.stage(
-        stage4, n3, in_parts, tuple(far_in), dcq, w_cross, values1, stats1, r2
+        stage4, n3, pre_grad, far_in, dcq, w_cross, values1, stats1, r2
     )
     in_sums, datt = comm.after((in_sums, datt), far_cross, half_out)
     in_second = comm.second(in_sums)
@@ -989,14 +994,16 @@
         return comm.restore(r1 + grads[0]), grads[1], grads[2]
 
     input_grad, gain0, shift0 = comm.stage(stage7, dqkv, w_self, values0, stats0, r1)
-    input_grad, gain0 = comm.after((input_grad, gain0), self_second, half_cross)
+    input_grad, gain0, self_sums = comm.after(
+        (input_grad, gain0, self_sums), self_second, half_cross
+    )
     half_self = comm.scatter_z(comm.closing(self_sums, self_second))
     norm_grad = comm.norm_sums(jnp.stack([gain0, gain1, gain2, shift0, shift1, shift2]))
     input_grad = input_grad.reshape(clips, own_frames, width)
     text_grad = text_grad.reshape(clips, texts, width)
     layer_out = layer_out.reshape(clips, own_frames, width)
     grad_out = comm.close_middle(half_out)
-    grad_in = catenate(comm.close_last(half_in, *[part.shape[1] for part in in_parts]))
+    (grad_in,) = comm.close_last(half_in, pre_grad.shape[1])
     grad_cq, grad_co, grad_cm = comm.close_last(half_cross, cols, cols, 2 * cols)
     grad_so, grad_self = comm.close_last(half_self, cols, 3 * cols)
     return (

time: 880 us -> 906 us (1.030)
  matrix products: 261 us -> 292 us
    dot_general x32 -> x42, matrix products: 110 us -> 140 us  [mm_rows(): lax.dot_general(left, right, (((0,), (0,)), ((), ())), preferred_element_...]
    slice x30 -> x3, local copies, waits for them, and re-layouts: 28.6 us -> 2.44 us  [the longest x1 2.41 us: adds(): first, last = (right[:, :half], right[:, half:])]
    ppermute x22 -> x21, waiting for transfers between devices: 62.8 us -> 42.5 us  [y(): return lax.ppermute(v, 'y', SWAP)]
    another operation x11 -> x16, local copies, waits for them, and re-layouts: 19.5 us -> 38.6 us
    reduce_scatter x4, waiting for transfers between devices: 0.02 us -> 12.8 us  [scatter_z(): return lax.psum_scatter(parts, 'z', scatter_dimension=1, tiled=True)]
    convert_element_type x0 -> x10, local copies, waits for them, and re-layouts: none -> 12.6 us  [adds(): (mm_rows(own, side) + far.astype(F32)).astype(BF)]
    ppermute x22 -> x21, waiting for transfers between devices: 67.6 us -> 61.9 us  [x(): return lax.ppermute(v, 'x', SWAP)]
    optimization_barrier x12 -> x9, local copies, waits for them, and re-layouts: 30.5 us -> 28.6 us  [tie(): return lax.optimization_barrier((value, others))[0]]
  transfers between devices with their start and end apart: 70 -> 68, of which waited for: 26 -> 27; matrix products, arithmetic and copies ran while one was open for 52% -> 51% of each run, Pallas kernels for 17% -> 16%
where the time goes in v6:
time: 906 us; the launch traced here: 896 us
  matrix products  292 us (32%)
  waiting for transfers between devices  173 us (19%)
  Pallas kernels  147 us (16%)
  local copies, waits for them, and re-layouts  129 us (14%)
  other arithmetic  82.3 us (9%)
  starting transfers between devices  56.9 us (6%)
  between operations  15.3 us (2%)
    dot_general x42, matrix products, mm_rows(): lax.dot_general(left, right, (((0,), (0,)), ((), ())), preferred_element_...  140 us
    dot_general x17, matrix products, mm_t(): lax.dot_general(left, right, (((1,), (1,)), ((), ())), preferred_element_...  108 us
    ppermute x21, waiting for transfers between devices, x(): return lax.ppermute(v, 'x', SWAP)  61.9 us
    dot_general x8, matrix products, mm(): return jnp.dot(left, right, preferred_element_type=F32)  44.1 us
    ppermute x21, waiting for transfers between devices, y(): return lax.ppermute(v, 'y', SWAP)  42.5 us
    another operation x16, local copies, waits for them, and re-layouts  38.6 us
    pallas_call x1, Pallas kernels, self_back(): pl.pallas_call(self_back_kernel, grid_spec=pltpu.PrefetchScalarGridSpec(n...  30 us
    optimization_barrier x9, local copies, waits for them, and re-layouts, tie(): return lax.optimization_barrier((value, others))[0]  28.6 us
  transfers between devices with their start and end apart: 68, of which 27 were waited for; matrix products, arithmetic and copies ran while one was open for 51% of the time, Pallas kernels for 16%

profile of v6, /device:TPU:0, one launch (start us, length us, event | category | flops | bytes accessed | tf_op | source)
XLA Modules:
  0.0 896.3 jit_solution(17259369268794205201)
XLA Ops:
  28.3 5.1 collective-permute-done.12
  47.7 7.6 all-gather.7.cloned.1.call-done
  61.0 18.6 %collective-permute-done.19 = bf16[384,1152]{1,0:T(8,128)(2,1)} collective-permute-done((bf16[384,1152]{1,0:T(8,128)(2,1)S(1)}, bf16[384,1152]{1,0:T(8,128)(2,1)}, u32[]{:S(2)}, u32[]{:S(2)}) %collective-permute-start.19) | collective-permute-done | bytes 884768 | tf_op jit(solution)/shard_map/ppermute | solution.py:529
  82.5 17.5 %collective-permute-done.23 = bf16[384,1152]{1,0:T(8,128)(2,1)} collective-permute-done((bf16[384,1152]{1,0:T(8,128)(2,1)S(1)}, bf16[384,1152]{1,0:T(8,128)(2,1)}, u32[]{:S(2)}, u32[]{:S(2)}) %collective-permute-start.23) | collective-permute-done | bytes 884768 | tf_op jit(solution)/shard_map/ppermute | solution.py:532
  100.0 16.4 %all-gather.5.cloned.1.call-done.refs_0_ = bf16[384,3840]{1,0:T(8,128)(2,1)} async-done(((bf16[96,3840]{1,0:T(8,128)(2,1)}), bf16[384,3840]{1,0:T(8,128)(2,1)}) %all-gather.5.cloned.1.call-update) | async-done | bytes 2949136 | tf_op jit(solution)/shard_map/all_gather | solution.py:558
  125.1 31.4 %collective-permute-done.25.refs_1_ = bf16[384,1920]{1,0:T(8,128)(2,1)} collective-permute-done((bf16[384,1920]{1,0:T(8,128)(2,1)}, bf16[384,1920]{1,0:T(8,128)(2,1)}, u32[]{:S(2)}, u32[]{:S(2)}) %collective-permute-start.25) | collective-permute-done | bytes 1474592 | tf_op jit(solution)/shard_map/ppermute | solution.py:529
  164.0 39.7 %conditional.10 = (bf16[1536,2304]{1,0:T(8,128)(2,1)}, bf16[1024,768]{1,0:T(8,128)(2,1)}, s32[1]{0:T(128)}, bf16[2,2,256,2304]{3,2,1,0:T(8,128)(2,1)}, f32[2,2,2...) conditional(s32[]{:T(128)} %convert_element_type.497, () %tuple.124, ...), branch_computations={%region_2.3_spmd, %region_3.4_spmd} | conditional | flops 8458076160 | bytes 27525176 | solution.py:613
  164.0 6.0 place.2
  170.0 13.0 %convolution_convert_fusion = bf16[2304,1024]{0,1:T(8,128)(2,1)} fusion(bf16[1536,2304]{1,0:T(8,128)(2,1)} %place.2, bf16[1024,1536]{0,1:T(8,128)(2,1)} %get-tuple-element.705), kind=kOutput, calls=%fused_computation | convolution fusion | flops 7250116608 | bytes 14942208 | tf_op jit(solution)/shard_map/cond/branch_1_fun/dot_general | solution.py:19
  183.0 18.3 %self_attend.1 = (bf16[2,2,256,768]{3,2,1,0:T(8,128)(2,1)}, f32[2,2,256,768]{3,2,1,0:T(8,128)}) custom-call(s32[1]{0:T(128)} %bitcast.core_ref, bf16[2,2,256,2304]{3,2,1,0:T(8,128)(2,1)} %bitcast.2.q_ref.k_ref.v_ref, bf16[2,2,256,2304]{3,2,1,0:T(8,128)(2,1)} %bitcast.2.q_ref.k_ref.v_ref, bf16[2,2,256,2304]{3,2,1,0:T(8,128)(2,1)} %bitcast.2.q_ref.k_ref.v_ref), custom_call_target="tpu_custom_call" | custom-call | flops 1207959552 | bytes 9437184 | tf_op jit(solution)/shard_map/cond/branch_1_fun/self_attend/pallas_call | solution.py:716
  206.7 4.9 fusion.349
  211.6 7.0 collective-permute-done.26.refs_2_
  228.9 8.8 place.3
  237.7 65.6 %conditional.11 = (f32[512,1536]{1,0:T(8,128)}, f32[512,1]{0,1:T(1,128)S(1)}, f32[512,1]{0,1:T(1,128)S(1)}, bf16[1024,1536]{1,0:T(8,128)(2,1)}, bf16[1024,768]{1...) conditional(s32[]{:T(128)} %convert_element_type.497, ...), branch_computations={%region_4.5_spmd, %region_5.10_spmd} | conditional | flops 8087077888 | bytes 141820608 | solution.py:613
  247.8 6.0 fusion.346
  264.2 6.4 fusion.174
  270.5 13.4 %cross_attend.1 = bf16[2,2,256,768]{3,2,1,0:T(8,128)(2,1)} custom-call(bf16[2,2,256,768]{3,2,1,0:T(8,128)(2,1)} %bitcast.6.q_ref, bf16[2,64,1536]{2,1,0:T(8,128)(2,1)S(1)} %bitcast.208, bf16[2,64,1536]{2,1,0:T(8,128)(2,1)S(1)} %bitcast.209), custom_call_target="tpu_custom_call" | custom-call | flops 201326592 | bytes 3145728 | tf_op jit(solution)/shard_map/cond/branch_1_fun/cross_attend/pallas_call | solution.py:779
  303.3 4.9 fusion.348
  310.3 7.3 place_stacked.3.weight_ref
  317.7 20.1 %feed.1 = (bf16[1024,3072]{1,0:T(8,128)(2,1)}, bf16[1024,3072]{1,0:T(8,128)(2,1)}) custom-call(bf16[1024,1536]{1,0:T(8,128)(2,1)} %get-tuple-element.382.rows_ref, bf16[1536,3072]{1,0:T(8,128)(2,1)} %place_stacked.3.weight_ref), custom_call_target="tpu_custom_call" | custom-call | flops 9663676416 | bytes 25165824 | tf_op jit(solution)/shard_map/feed/pallas_call | solution.py:311
  337.8 6.6 convolution_convert_fusion.12
  345.8 5.4 convolution_convert_fusion.11
  355.5 7.2 collective-permute-done.35
  363.3 56.4 %conditional.12 = (bf16[1536,3072]{1,0:T(8,128)(2,1)}, bf16[1024,3072]{1,0:T(8,128)(2,1)}, bf16[768,1536]{0,1:T(8,128)(2,1)}, bf16[768,1536]{0,1:T(8,128)(2,1)}, f32[512,1536]{1,0:T(8,128)}) conditional(s32[]{:T(128)} %convert_element_type.497, () %tuple.132, (bf16[4,384,1536]{2,1,0:T(8,128)(2,1)}, bf16[2,384,1536]{2,1,0:T(8,128)(2,1)}, ...), branch_computations={%region_10.11_spmd, %region_11.12_spmd} | conditional | flops 24163909632 | bytes 105382040 | solution.py:613
  363.3 7.4 place_stacked.2.weight_ref
  370.7 17.9 %slope_product.1 = bf16[1024,3072]{1,0:T(8,128)(2,1)} custom-call(bf16[1024,1536]{1,0:T(8,128)(2,1)} %get-tuple-element.193.rows_ref, bf16[1536,3072]{1,0:T(8,128)(2,1)} %place_stacked.2.weight_ref, bf16[1024,3072]{1,0:T(8,128)(2,1)} %get-tuple-element.194.slope_ref), custom_call_target="tpu_custom_call" | custom-call | flops 9663676416 | bytes 25165824 | tf_op jit(solution)/shard_map/cond/branch_1_fun/slope_product/pallas_call | solution.py:346
  388.6 9.7 %fusion.12 = bf16[512,1536]{1,0:T(8,128)(2,1)S(1)} fusion(bf16[1536,3072]{1,0:T(8,128)(2,1)} %get-tuple-element.196, bf16[1024,3072]{1,0:T(8,128)(2,1)} %slope_product.1), kind=kOutput, calls=%fused_computation.12 | convolution fusion | flops 4832624640 | bytes 14155776 | tf_op jit(solution)/shard_map/cond/branch_1_fun/dot_general | solution.py:23
  398.4 6.6 fusion.6
  405.0 6.5 fusion.9
  411.6 8.1 convert_add_fusion
  419.7 27.5 %conditional.13 = (bf16[4,384,1536]{2,1,0:T(8,128)(2,1)}, f32[512,1536]{1,0:T(8,128)}, bf16[512,1536]{1,0:T(8,128)(2,1)}, f32[1,1536]{1,0:T(1,128)}, f32[1,1536]{1,0:T(1,128)}) conditional(s32[]{:T(128)} %convert_element_type.497, () %tuple.122, (bf16[1024,1536]{1,0:T(8,128)(2,1)}, bf16[1024,3072]{1,0:T(8,128)(2,1)}, bf16[768,1536]{1,0:T(8,128)(2,1)}, ...), branch_computations={%region_12.13_spmd, %region_13.18_spmd} | conditional | flops 4860933120 | bytes 91349088 | solution.py:613
  441.6 4.5 fusion.341
  447.4 4.7 copy.175
  459.3 46.6 %conditional.14 = (bf16[1024,1536]{1,0:T(8,128)(2,1)}, bf16[1024,768]{1,0:T(8,128)(2,1)}, bf16[128,1536]{1,0:T(8,128)(2,1)}, bf16[768,1536]{0,1:T(8,128)(2,1)}, bf16[768,1536]{0,1:T(8,128)(2,1)}) conditional(s32[]{:T(128)} %convert_element_type.497, () %tuple.121, (bf16[512,1536]{1,0:T(8,128)(2,1)}, bf16[1024,768]{1,0:T(8,128)(2,1)}, ...), branch_computations={%region_18.19_spmd, %region_19.20_spmd} | conditional | flops 5654446080 | bytes 49545296 | solution.py:613
  466.6 6.4 fusion.19
  473.0 17.6 %cross_back.1 = (bf16[2,2,256,768]{3,2,1,0:T(8,128)(2,1)}, bf16[2,64,1536]{2,1,0:T(8,128)(2,1)}) custom-call(bf16[2,2,256,768]{3,2,1,0:T(8,128)(2,1)} %bitcast.24.q_ref, bf16[2,64,1536]{2,1,0:T(8,128)(2,1)S(1)} %get-tuple-element.209.k_ref.v_ref, bf16[2,64,1536]{2,1,0:T(8,128)(2,1)S(1)} %get-tuple-element.209.k_ref.v_ref, bf16[2,2,256,768]{3,2,1,0:T(8,128)(2,1)} %bitcast.214), custom_call_target="tpu_custom_call" | custom-call | flops 503316480 | bytes 4718592 | tf_op jit(solution)/shard_map/cond/branch_1_fun/cross_back/pallas_call | solution.py:796
  506.0 5.5 collective-permute-done.40
  513.8 46.6 %conditional.15 = (bf16[384,1536]{1,0:T(8,128)(2,1)}, bf16[384,1536]{1,0:T(8,128)(2,1)}, bf16[384,1536]{1,0:T(8,128)(2,1)}, bf16[384,1536]{1,0:T(8,128)(2,1)}, f...) conditional(s32[]{:T(128)} %convert_element_type.497, ...), branch_computations={%region_20.21_spmd, %region_21.26_spmd} | conditional | flops 9694344192 | bytes 81125528 | solution.py:613
  513.8 4.5 convolution_convert_fusion.9
  522.1 5.4 multiply_reduce_fusion.5
  527.5 4.9 fusion.342
  532.6 4.9 fusion.203
  537.4 4.9 fusion.204
  542.3 4.9 fusion.205
  547.2 4.9 fusion.206
  554.0 6.4 fusion.218
  567.5 78.2 %conditional.16 = (bf16[384,1536]{0,1:T(8,128)(2,1)}, bf16[384,1536]{0,1:T(8,128)(2,1)}, bf16[384,1536]{0,1:T(8,128)(2,1)}, bf16[384,1536]{0,1:T(8,128)(2,1)}, b...) conditional(s32[]{:T(128)} %convert_element_type.497, () %tuple.138, (bf16[1024,1536]{1,0:T(8,128)(2,1)}, ...), branch_computations={%region_26.27_spmd, %region_27.28_spmd} | conditional | flops 3947692032 | bytes 64487500 | solution.py:613
  602.2 4.7 copy.157
  661.4 45.2 %conditional.17 = (bf16[1024,2304]{1,0:T(8,128)(2,1)}, bf16[768,1152]{0,1:T(8,128)(2,1)}, bf16[768,1152]{0,1:T(8,128)(2,1)}) conditional(s32[]{:T(128)} %convert_element_type.497, () %tuple.137, (bf16[1024,768]{1,0:T(8,128)(2,1)}, s32[1]{0:T(128)}, bf16[2,2,256,2304]{3,2,1,0:T(8,128)(2,1)}, f32[2,2,256,768]{3,2,1,0:T(8,128)}, ...), branch_computations={%region_29.30_spmd, %region_30.31_spmd} | conditional | flops 6645547008 | bytes 44433460 | solution.py:613
  661.4 30.0 %self_back.1 = bf16[2,2,256,2304]{3,2,1,0:T(8,128)(2,1)} custom-call(s32[1]{0:T(128)} %get-tuple-element.237.core_ref, bf16[2,2,256,2304]{3,2,1,0:T(8,128)(2,1)} %get-tuple-element.238.q_ref.k_ref.v_ref, bf16[2,2,256,2304]{3,2,1,0:T(8,128)(2,1)} %get-tuple-element.238.q_ref.k_ref.v_ref, bf16[2,2,256,2304]{3,2,1,0:T(8,128)(2,1)} %get-tuple-element.238.q_ref.k_ref.v_ref, ...), custom_call_target="tpu_custom_call" | custom-call | flops 3019898880 | bytes 14155776 | tf_op jit(solution)/shard_map/cond/branch_1_fun/self_back/pallas_call | solution.py:746
  691.4 4.6 copy.179
  696.0 5.6 fusion.106
  701.7 5.0 fusion.107
  728.5 39.3 %conditional.18 = (f32[128,1536]{1,0:T(8,128)}, bf16[512,1536]{1,0:T(8,128)(2,1)}) conditional(s32[]{:T(128)} %convert_element_type.497, () %tuple.117, (bf16[1536,3840]{1,0:T(8,128)(2,1)}, bf16[128,1536]{1,0:T(8,128)(2,1)}, bf16[1024,3072]{1,0:T(8,128)(2,1)}, bf16[1536,3072]{1,0:T(8,128)(2,1)}, f32[512,1536]{1,0:T(8,128)S(1)}) %tuple.147), branch_computations={%region_31.32_spmd, %region_32.33_spmd} | conditional | flops 13905573888 | bytes 55075012 | solution.py:613
  728.5 10.5 %fusion.125 = bf16[512,1536]{1,0:T(8,128)(2,1)} fusion(bf16[1536,3072]{1,0:T(8,128)(2,1)} %get-tuple-element.246, bf16[1024,3072]{1,0:T(8,128)(2,1)} %get-tuple-element.245), kind=kOutput, calls=%fused_computation.131 | convolution fusion | flops 4832624640 | bytes 14155776 | tf_op jit(solution)/shard_map/cond/branch_1_fun/dot_general | solution.py:23
  739.2 5.2 fusion.344
  754.0 13.9 %fusion.124 = bf16[512,1536]{1,0:T(8,128)(2,1)} fusion(s32[1536]{0:T(1024)S(1)} %fusion.140, f32[512,1536]{1,0:T(8,128)S(1)} %get-tuple-element.244, bf16[512,1536]{1,0:T(8,128)(2,1)} %collective-permute-done.10, bf16[1536,3072]{1,0:T(8,128)(2,1)} %get-tuple-element.246, bf16[1024,3072]{1,0:T(8,128)(2,1)} %get-tuple-element.245), kind=kOutput, calls=%fused_computation.130 | convolution fusion | flops 7254048768 | bytes 18880512 | tf_op jit(solution)/shard_map/cond/branch_1_fun/dot_general | solution.py:23
  797.2 33.9 %conditional.19 = (f32[512,1536]{1,0:T(8,128)}, f32[1536]{0:T(1024)S(1)}, f32[1,1536]{1,0:T(1,128)S(1)}) conditional(s32[]{:T(128)} %convert_element_type.497, () %tuple.149, (bf16[1024,2304]{1,0:T(8,128)(2,1)}, bf16[1536,2304]{1,0:T(8,128)(2,1)}, f32[3,1536]{0,1:T(8,128)S(1)}, f32[512]{0:T(512)S(1)}, f32[512,1536]{0,1:T(8,128)}, ...), branch_computations={%region_34.35_spmd, %region_35.40_spmd} | conditional | flops 12104839168 | bytes 88217792 | solution.py:613
  797.2 8.8 convolution_convert_fusion.10
  811.3 9.6 %multiply_reduce_fusion.8 = (f32[1536]{0:T(1024)S(1)}, f32[512]{0:T(512)S(1)}, f32[512]{0:T(512)S(1)}, f32[1536]{0:T(1024)S(1)}, f32[512,1536]{1,0:T(8,128)S(1)}) fusion(f32[512,1536]{1,0:T(8,128)} %copy.190, f32[512]{0:T(512)S(1)} %get-tuple-element.799, f32[512]{0:T(512)S(1)} %get-tuple-element.800, f32[1536]{0:T(1024)S(1)} %slice_reduce_fusion.6, ...), kind=kOutput, calls=%fused_computation.278 | convolution fusion | flops 3632525312 | bytes 17328128 | tf_op jit(solution)/shard_map/cond/branch_1_fun/dot_general | solution.py:23
  845.3 5.7 collective-permute-done.54
  857.5 7.8 collective-permute-done.56
  866.3 5.3 collective-permute-done.57
  872.3 12.7 %reduce-scatter.11.cloned.1.call-done = bf16[2,96,1536]{2,1,0:T(8,128)(2,1)} async-done(((bf16[2,384,1536]{2,1,0:T(8,128)(2,1)}), bf16[2,96,1536]{2,1,0:T(8,128)(2,1)}) %reduce-scatter.11.cloned.1.call-update) | async-done | bytes 589840 | tf_op jit(solution)/shard_map/reduce_scatter | solution.py:665
  (424 shorter events, 383.3 us)
Async XLA Ops:
  7.2 48.1 %all-gather.7.cloned.1.call-start = ((), (), s32[]{:S(2)}) async-start(), calls=%async_computation.5 | async-start | bytes 2211840 | tf_op jit(solution)/shard_map/all_gather | solution.py:558
  9.3 107.1 %all-gather.5.cloned.1.call-start = ((), (), s32[]{:S(2)}) async-start(), calls=%async_computation.4 | async-start | bytes 3686400 | tf_op jit(solution)/shard_map/all_gather | solution.py:558
  10.3 14.8 %collective-permute-start.11 = (bf16[96,128]{1,0:T(8,128)(2,1)S(1)}, bf16[96,128]{1,0:T(8,128)(2,1)S(1)}, u32[]{:S(2)}, u32[]{:S(2)}) collective-permute-start(bf16[96,128]{1,0:T(8,128)(2,1)S(1)} %get-tuple-element.855), channel_id=1, source_target_pairs={{0,8},{8,0},{16,24},{24,16},{1,9},{9,1},{17,25},{25,17},{2,10},{10... | collective-permute-start | bytes 73736 | tf_op jit(solution)/shard_map/ppermute | solution.py:538
  14.3 25.6 %collective-permute-start.16 = (bf16[96,1536]{1,0:T(8,128)(2,1)}, bf16[96,1536]{1,0:T(8,128)(2,1)}, u32[]{:S(2)}, u32[]{:S(2)}) collective-permute-start(bf16[96,1536]{1,0:T(8,128)(2,1)} %get-tuple-element.841), channel_id=1, source_target_pairs={{0,4},{4,0},{1,5},{5,1},{2,6},{6,2},{3,7},{7,3},{8,12},{12,8},{9,1... | collective-permute-start | bytes 884744 | tf_op jit(solution)/shard_map/ppermute | solution.py:532
  15.9 24.1 %collective-permute-start.15 = (bf16[96,1536]{1,0:T(8,128)(2,1)}, bf16[96,1536]{1,0:T(8,128)(2,1)}, u32[]{:S(2)}, u32[]{:S(2)}) collective-permute-start(bf16[96,1536]{1,0:T(8,128)(2,1)} %get-tuple-element.842), channel_id=1, source_target_pairs={{0,2},{2,0},{1,3},{3,1},{4,6},{6,4},{5,7},{7,5},{8,10},{10,8},{9,1... | collective-permute-start | bytes 884744 | tf_op jit(solution)/shard_map/ppermute | solution.py:529
  20.2 186.5 %all-gather.9.cloned.1.call-start = ((), (), s32[]{:S(2)}) async-start(), calls=%async_computation.6 | async-start | bytes 5898240 | tf_op jit(solution)/shard_map/all_gather | solution.py:559
  21.3 20.9 %collective-permute-start.18 = (bf16[96,1536]{1,0:T(8,128)(2,1)}, bf16[96,1536]{1,0:T(8,128)(2,1)}, u32[]{:S(2)}, u32[]{:S(2)}) collective-permute-start(bf16[96,1536]{1,0:T(8,128)(2,1)} %get-tuple-element.837), channel_id=1, source_target_pairs={{0,4},{4,0},{1,5},{5,1},{2,6},{6,2},{3,7},{7,3},{8,12},{12,8},{9,1... | collective-permute-start | bytes 884744 | tf_op jit(solution)/shard_map/ppermute | solution.py:532
  21.8 20.4 %collective-permute-start.17 = (bf16[96,1536]{1,0:T(8,128)(2,1)}, bf16[96,1536]{1,0:T(8,128)(2,1)}, u32[]{:S(2)}, u32[]{:S(2)}) collective-permute-start(bf16[96,1536]{1,0:T(8,128)(2,1)} %get-tuple-element.838), channel_id=1, source_target_pairs={{0,2},{2,0},{1,3},{3,1},{4,6},{6,4},{5,7},{7,5},{8,10},{10,8},{9,1... | collective-permute-start | bytes 884744 | tf_op jit(solution)/shard_map/ppermute | solution.py:529
  25.1 8.3 collective-permute-start.12
  33.5 4.7 collective-permute-start.13
  38.2 6.2 collective-permute-start.14
  47.0 256.3 %all-gather.11.cloned.1.call-start = ((), (), s32[]{:S(2)}) async-start(), calls=%async_computation.7 | async-start | bytes 5898240 | tf_op jit(solution)/shard_map/all_gather | solution.py:559
  47.6 517.2 %reduce-scatter.5.cloned.1.call-start = ((), (), s32[]{:S(2)}) async-start(), calls=%async_computation.8 | async-start | bytes 5898240 | tf_op jit(solution)/shard_map/reduce_scatter | solution.py:665
  56.9 22.7 %collective-permute-start.19 = (bf16[384,1152]{1,0:T(8,128)(2,1)S(1)}, bf16[384,1152]{1,0:T(8,128)(2,1)}, u32[]{:S(2)}, u32[]{:S(2)}) collective-permute-start(bf16[384,1152]{1,0:T(8,128)(2,1)S(1)} %get-tuple-element.813), channel_id=1, source_target_pairs={{0,2},{2,0},{1,3},{3,1},{4,6},{6,4},{5,7},{7,5},{8,10},{10,8},{9,1... | collective-permute-start | bytes 2654216 | tf_op jit(solution)/shard_map/ppermute | solution.py:529
  58.4 22.6 %collective-permute-start.21 = (bf16[384,1152]{1,0:T(8,128)(2,1)S(1)}, bf16[384,1152]{1,0:T(8,128)(2,1)}, u32[]{:S(2)}, u32[]{:S(2)}) collective-permute-start(bf16[384,1152]{1,0:T(8,128)(2,1)S(1)} %get-tuple-element.812), channel_id=1, source_target_pairs={{0,4},{4,0},{1,5},{5,1},{2,6},{6,2},{3,7},{7,3},{8,12},{12,8},{9,1... | collective-permute-start | bytes 2654216 | tf_op jit(solution)/shard_map/ppermute | solution.py:532
  59.9 40.1 %collective-permute-start.23 = (bf16[384,1152]{1,0:T(8,128)(2,1)S(1)}, bf16[384,1152]{1,0:T(8,128)(2,1)}, u32[]{:S(2)}, u32[]{:S(2)}) collective-permute-start(bf16[384,1152]{1,0:T(8,128)(2,1)S(1)} %get-tuple-element.813), channel_id=1, source_target_pairs={{0,4},{4,0},{1,5},{5,1},{2,6},{6,2},{3,7},{7,3},{8,12},{12,8},{9,1... | collective-permute-start | bytes 2654216 | tf_op jit(solution)/shard_map/ppermute | solution.py:532
  60.4 39.6 %collective-permute-start.24 = (bf16[384,1152]{1,0:T(8,128)(2,1)S(1)}, bf16[384,1152]{1,0:T(8,128)(2,1)}, u32[]{:S(2)}, u32[]{:S(2)}) collective-permute-start(bf16[384,1152]{1,0:T(8,128)(2,1)S(1)} %get-tuple-element.812), channel_id=1, source_target_pairs={{0,2},{2,0},{1,3},{3,1},{4,6},{6,4},{5,7},{7,5},{8,10},{10,8},{9,1... | collective-permute-start | bytes 2654216 | tf_op jit(solution)/shard_map/ppermute | solution.py:529
  79.5 37.8 %collective-permute-start.20 = (bf16[384,1152]{1,0:T(8,128)(2,1)}, bf16[384,1152]{1,0:T(8,128)(2,1)}, u32[]{:S(2)}, u32[]{:S(2)}) collective-permute-start(bf16[384,1152]{1,0:T(8,128)(2,1)} %collective-permute-done.19), channel_id=1, source_target_pairs={{0,4},{4,0},{1,5},{5,1},{2,6},{6,2},{3,7},{7,3},{8,12},{12,8},{9,1... | collective-permute-start | bytes 2654216 | tf_op jit(solution)/shard_map/ppermute | solution.py:532
  81.0 36.3 %collective-permute-start.22 = (bf16[384,1152]{1,0:T(8,128)(2,1)}, bf16[384,1152]{1,0:T(8,128)(2,1)}, u32[]{:S(2)}, u32[]{:S(2)}) collective-permute-start(bf16[384,1152]{1,0:T(8,128)(2,1)} %collective-permute-done.21), channel_id=1, source_target_pairs={{0,2},{2,0},{1,3},{3,1},{4,6},{6,4},{5,7},{7,5},{8,10},{10,8},{9,1... | collective-permute-start | bytes 2654216 | tf_op jit(solution)/shard_map/ppermute | solution.py:529
  121.0 35.5 %collective-permute-start.25 = (bf16[384,1920]{1,0:T(8,128)(2,1)}, bf16[384,1920]{1,0:T(8,128)(2,1)}, u32[]{:S(2)}, u32[]{:S(2)}) collective-permute-start(bf16[384,1920]{1,0:T(8,128)(2,1)} %get-tuple-element.811), channel_id=1, source_target_pairs={{0,2},{2,0},{1,3},{3,1},{4,6},{6,4},{5,7},{7,5},{8,10},{10,8},{9,1... | collective-permute-start | bytes 4423688 | tf_op jit(solution)/shard_map/ppermute | solution.py:529
  121.6 36.4 %collective-permute-start.29 = (bf16[384,1920]{1,0:T(8,128)(2,1)}, bf16[384,1920]{1,0:T(8,128)(2,1)}, u32[]{:S(2)}, u32[]{:S(2)}) collective-permute-start(bf16[384,1920]{1,0:T(8,128)(2,1)} %get-tuple-element.810), channel_id=1, source_target_pairs={{0,4},{4,0},{1,5},{5,1},{2,6},{6,2},{3,7},{7,3},{8,12},{12,8},{9,1... | collective-permute-start | bytes 4423688 | tf_op jit(solution)/shard_map/ppermute | solution.py:532
  123.0 38.2 %collective-permute-start.32 = (bf16[512,1536]{0,1:T(8,128)(2,1)}, bf16[512,1536]{0,1:T(8,128)(2,1)}, u32[]{:S(2)}, u32[]{:S(2)}) collective-permute-start(bf16[512,1536]{0,1:T(8,128)(2,1)} %add_convert_fusion.3), channel_id=1, source_target_pairs={{0,1},{1,0},{2,3},{3,2},{4,5},{5,4},{6,7},{7,6},{8,9},{9,8},{10,11... | collective-permute-start | bytes 4718600 | tf_op jit(solution)/shard_map/ppermute | solution.py:535
  123.0 88.5 %collective-permute-start.27 = (bf16[384,1920]{1,0:T(8,128)(2,1)}, bf16[384,1920]{1,0:T(8,128)(2,1)}, u32[]{:S(2)}, u32[]{:S(2)}) collective-permute-start(bf16[384,1920]{1,0:T(8,128)(2,1)} %get-tuple-element.811), channel_id=1, source_target_pairs={{0,4},{4,0},{1,5},{5,1},{2,6},{6,2},{3,7},{7,3},{8,12},{12,8},{9,1... | collective-permute-start | bytes 4423688 | tf_op jit(solution)/shard_map/ppermute | solution.py:532
  123.6 88.0 %collective-permute-start.28 = (bf16[384,1920]{1,0:T(8,128)(2,1)}, bf16[384,1920]{1,0:T(8,128)(2,1)}, u32[]{:S(2)}, u32[]{:S(2)}) collective-permute-start(bf16[384,1920]{1,0:T(8,128)(2,1)} %get-tuple-element.810), channel_id=1, source_target_pairs={{0,2},{2,0},{1,3},{3,1},{4,6},{6,4},{5,7},{7,5},{8,10},{10,8},{9,1... | collective-permute-start | bytes 4423688 | tf_op jit(solution)/shard_map/ppermute | solution.py:529
  156.5 62.1 %collective-permute-start.26 = (bf16[384,1920]{1,0:T(8,128)(2,1)}, bf16[384,1920]{1,0:T(8,128)(2,1)}, u32[]{:S(2)}, u32[]{:S(2)}) collective-permute-start(bf16[384,1920]{1,0:T(8,128)(2,1)} %collective-permute-done.25.refs_1_), channel_id=1, source_target_pairs={{0,4},{4,0},{1,5},{5,1},{2,6},{6,2},{3,7},{7,3},{8,12},{12,8},{9,1... | collective-permute-start | bytes 4423688 | tf_op jit(solution)/shard_map/ppermute | solution.py:532
  158.0 60.7 %collective-permute-start.30 = (bf16[384,1920]{1,0:T(8,128)(2,1)}, bf16[384,1920]{1,0:T(8,128)(2,1)}, u32[]{:S(2)}, u32[]{:S(2)}) collective-permute-start(bf16[384,1920]{1,0:T(8,128)(2,1)} %collective-permute-done.29.refs_6_), channel_id=1, source_target_pairs={{0,2},{2,0},{1,3},{3,1},{4,6},{6,4},{5,7},{7,5},{8,10},{10,8},{9,1... | collective-permute-start | bytes 4423688 | tf_op jit(solution)/shard_map/ppermute | solution.py:529
  218.6 89.6 %collective-permute-start.33 = (bf16[2,384,1536]{2,1,0:T(8,128)(2,1)}, bf16[2,384,1536]{2,1,0:T(8,128)(2,1)}, u32[]{:S(2)}, u32[]{:S(2)}) collective-permute-start(bf16[2,384,1536]{2,1,0:T(8,128)(2,1)} %get-tuple-element.379), channel_id=1, source_target_pairs={{0,4},{4,0},{1,5},{5,1},{2,6},{6,2},{3,7},{7,3},{8,12},{12,8},{9,1... | collective-permute-start | bytes 7077896 | tf_op jit(solution)/shard_map/ppermute | solution.py:532
  220.1 88.1 %collective-permute-start.34 = (bf16[2,384,1536]{2,1,0:T(8,128)(2,1)}, bf16[2,384,1536]{2,1,0:T(8,128)(2,1)}, u32[]{:S(2)}, u32[]{:S(2)}) collective-permute-start(bf16[2,384,1536]{2,1,0:T(8,128)(2,1)} %get-tuple-element.380), channel_id=1, source_target_pairs={{0,2},{2,0},{1,3},{3,1},{4,6},{6,4},{5,7},{7,5},{8,10},{10,8},{9,1... | collective-permute-start | bytes 7077896 | tf_op jit(solution)/shard_map/ppermute | solution.py:529
  224.6 113.2 %collective-permute-start.31 = (bf16[512,1536]{1,0:T(8,128)(2,1)}, bf16[512,1536]{1,0:T(8,128)(2,1)}, u32[]{:S(2)}, u32[]{:S(2)}) collective-permute-start(bf16[512,1536]{1,0:T(8,128)(2,1)} %fusion.280), channel_id=1, source_target_pairs={{0,1},{1,0},{2,3},{3,2},{4,5},{5,4},{6,7},{7,6},{8,9},{9,8},{10,11... | collective-permute-start | bytes 4718600 | tf_op jit(solution)/shard_map/ppermute | solution.py:535
  242.2 5.6 collective-permute-start
  258.8 3.5 collective-permute-start.1
  308.2 54.5 %collective-permute-start.35 = (bf16[2,384,1536]{2,1,0:T(8,128)(2,1)}, bf16[2,384,1536]{2,1,0:T(8,128)(2,1)}, u32[]{:S(2)}, u32[]{:S(2)}) collective-permute-start(bf16[2,384,1536]{2,1,0:T(8,128)(2,1)} %get-tuple-element.385), channel_id=1, source_target_pairs={{0,4},{4,0},{1,5},{5,1},{2,6},{6,2},{3,7},{7,3},{8,12},{12,8},{9,1... | collective-permute-start | bytes 7077896 | tf_op jit(solution)/shard_map/ppermute | solution.py:532
  308.9 54.4 %collective-permute-start.36 = (bf16[2,384,1536]{2,1,0:T(8,128)(2,1)}, bf16[2,384,1536]{2,1,0:T(8,128)(2,1)}, u32[]{:S(2)}, u32[]{:S(2)}) collective-permute-start(bf16[2,384,1536]{2,1,0:T(8,128)(2,1)} %get-tuple-element.386), channel_id=1, source_target_pairs={{0,2},{2,0},{1,3},{3,1},{4,6},{6,4},{5,7},{7,5},{8,10},{10,8},{9,1... | collective-permute-start | bytes 7077896 | tf_op jit(solution)/shard_map/ppermute | solution.py:529
  344.4 75.3 %collective-permute-start.37 = (bf16[768,1536]{1,0:T(8,128)(2,1)}, bf16[768,1536]{1,0:T(8,128)(2,1)}, u32[]{:S(2)}, u32[]{:S(2)}) collective-permute-start(bf16[768,1536]{1,0:T(8,128)(2,1)} %convolution_convert_fusion.12), channel_id=1, source_target_pairs={{0,4},{4,0},{1,5},{5,1},{2,6},{6,2},{3,7},{7,3},{8,12},{12,8},{9,1... | collective-permute-start | bytes 7077896 | tf_op jit(solution)/shard_map/ppermute | solution.py:532
  351.2 68.5 %collective-permute-start.38 = (bf16[768,1536]{1,0:T(8,128)(2,1)}, bf16[768,1536]{1,0:T(8,128)(2,1)}, u32[]{:S(2)}, u32[]{:S(2)}) collective-permute-start(bf16[768,1536]{1,0:T(8,128)(2,1)} %convolution_convert_fusion.11), channel_id=1, source_target_pairs={{0,2},{2,0},{1,3},{3,1},{4,6},{6,4},{5,7},{7,5},{8,10},{10,8},{9,1... | collective-permute-start | bytes 7077896 | tf_op jit(solution)/shard_map/ppermute | solution.py:529
  398.3 13.2 %collective-permute-start.7 = (bf16[512,1536]{1,0:T(8,128)(2,1)S(1)}, bf16[512,1536]{1,0:T(8,128)(2,1)S(1)}, u32[]{:S(2)}, u32[]{:S(2)}) collective-permute-start(bf16[512,1536]{1,0:T(8,128)(2,1)S(1)} %fusion.12), channel_id=1, source_target_pairs={{0,1},{1,0},{2,3},{3,2},{4,5},{5,4},{6,7},{7,6},{8,9},{9,8},{10,11... | collective-permute-start | bytes 4718600 | tf_op jit(solution)/shard_map/cond/branch_1_fun/ppermute | solution.py:535
  447.3 330.5 %reduce-scatter.7.cloned.1.call-start = ((), (), s32[]{:S(2)}) async-start(), calls=%async_computation.9 | async-start | bytes 2949120 | tf_op jit(solution)/shard_map/reduce_scatter | solution.py:665
  452.1 53.9 %collective-permute-start.39 = (bf16[768,1536]{1,0:T(8,128)(2,1)}, bf16[768,1536]{1,0:T(8,128)(2,1)}, u32[]{:S(2)}, u32[]{:S(2)}) collective-permute-start(bf16[768,1536]{1,0:T(8,128)(2,1)} %copy.175), channel_id=1, source_target_pairs={{0,4},{4,0},{1,5},{5,1},{2,6},{6,2},{3,7},{7,3},{8,12},{12,8},{9,1... | collective-permute-start | bytes 7077896 | tf_op jit(solution)/shard_map/ppermute | solution.py:532
  457.8 53.7 %collective-permute-start.40 = (bf16[768,1536]{1,0:T(8,128)(2,1)}, bf16[768,1536]{1,0:T(8,128)(2,1)}, u32[]{:S(2)}, u32[]{:S(2)}) collective-permute-start(bf16[768,1536]{1,0:T(8,128)(2,1)} %copy.176), channel_id=1, source_target_pairs={{0,2},{2,0},{1,3},{3,1},{4,6},{6,4},{5,7},{7,5},{8,10},{10,8},{9,1... | collective-permute-start | bytes 7077896 | tf_op jit(solution)/shard_map/ppermute | solution.py:529
  459.3 4.6 collective-permute-start.4
  511.5 52.8 %collective-permute-start.41 = (bf16[768,1536]{0,1:T(8,128)(2,1)}, bf16[768,1536]{0,1:T(8,128)(2,1)}, u32[]{:S(2)}, u32[]{:S(2)}) collective-permute-start(bf16[768,1536]{0,1:T(8,128)(2,1)} %get-tuple-element.408), channel_id=1, source_target_pairs={{0,4},{4,0},{1,5},{5,1},{2,6},{6,2},{3,7},{7,3},{8,12},{12,8},{9,1... | collective-permute-start | bytes 7077896 | tf_op jit(solution)/shard_map/ppermute | solution.py:532
  512.3 52.5 %collective-permute-start.42 = (bf16[768,1536]{0,1:T(8,128)(2,1)}, bf16[768,1536]{0,1:T(8,128)(2,1)}, u32[]{:S(2)}, u32[]{:S(2)}) collective-permute-start(bf16[768,1536]{0,1:T(8,128)(2,1)} %get-tuple-element.410), channel_id=1, source_target_pairs={{0,2},{2,0},{1,3},{3,1},{4,6},{6,4},{5,7},{7,5},{8,10},{10,8},{9,1... | collective-permute-start | bytes 7077896 | tf_op jit(solution)/shard_map/ppermute | solution.py:529
  518.3 3.8 collective-permute-start.5
  532.4 19.8 %collective-permute-start.6 = (bf16[512,1536]{1,0:T(8,128)(2,1)S(1)}, bf16[512,1536]{1,0:T(8,128)(2,1)S(1)}, u32[]{:S(2)}, u32[]{:S(2)}) collective-permute-start(bf16[512,1536]{1,0:T(8,128)(2,1)S(1)} %get-tuple-element.782), channel_id=1, source_target_pairs={{0,1},{1,0},{2,3},{3,2},{4,5},{5,4},{6,7},{7,6},{8,9},{9,8},{10,11... | collective-permute-start | bytes 4718600 | tf_op jit(solution)/shard_map/cond/branch_1_fun/ppermute | solution.py:535
  564.9 80.9 %collective-permute-start.43 = (bf16[384,1536]{1,0:T(8,128)(2,1)}, bf16[384,1536]{1,0:T(8,128)(2,1)}, u32[]{:S(2)}, u32[]{:S(2)}) collective-permute-start(bf16[384,1536]{1,0:T(8,128)(2,1)} %get-tuple-element.431), channel_id=1, source_target_pairs={{0,2},{2,0},{1,3},{3,1},{4,6},{6,4},{5,7},{7,5},{8,10},{10,8},{9,1... | collective-permute-start | bytes 3538952 | tf_op jit(solution)/shard_map/ppermute | solution.py:529
  566.3 79.4 %collective-permute-start.44 = (bf16[384,1536]{1,0:T(8,128)(2,1)}, bf16[384,1536]{1,0:T(8,128)(2,1)}, u32[]{:S(2)}, u32[]{:S(2)}) collective-permute-start(bf16[384,1536]{1,0:T(8,128)(2,1)} %get-tuple-element.433), channel_id=1, source_target_pairs={{0,4},{4,0},{1,5},{5,1},{2,6},{6,2},{3,7},{7,3},{8,12},{12,8},{9,1... | collective-permute-start | bytes 3538952 | tf_op jit(solution)/shard_map/ppermute | solution.py:532
  650.4 180.7 %reduce-scatter.9.cloned.1.call-start = ((), (), s32[]{:S(2)}) async-start(), calls=%async_computation.10 | async-start | bytes 2949120 | tf_op jit(solution)/shard_map/reduce_scatter | solution.py:665
  652.8 53.8 %collective-permute-start.45 = (bf16[384,1536]{1,0:T(8,128)(2,1)}, bf16[384,1536]{1,0:T(8,128)(2,1)}, u32[]{:S(2)}, u32[]{:S(2)}) collective-permute-start(bf16[384,1536]{1,0:T(8,128)(2,1)} %copy.180), channel_id=1, source_target_pairs={{0,2},{2,0},{1,3},{3,1},{4,6},{6,4},{5,7},{7,5},{8,10},{10,8},{9,1... | collective-permute-start | bytes 3538952 | tf_op jit(solution)/shard_map/ppermute | solution.py:529
  655.9 50.7 %collective-permute-start.46 = (bf16[384,1536]{1,0:T(8,128)(2,1)}, bf16[384,1536]{1,0:T(8,128)(2,1)}, u32[]{:S(2)}, u32[]{:S(2)}) collective-permute-start(bf16[384,1536]{1,0:T(8,128)(2,1)} %copy.181), channel_id=1, source_target_pairs={{0,4},{4,0},{1,5},{5,1},{2,6},{6,2},{3,7},{7,3},{8,12},{12,8},{9,1... | collective-permute-start | bytes 3538952 | tf_op jit(solution)/shard_map/ppermute | solution.py:532
  658.7 48.0 %collective-permute-start.47 = (bf16[768,384]{0,1:T(8,128)(2,1)}, bf16[768,384]{0,1:T(8,128)(2,1)}, u32[]{:S(2)}, u32[]{:S(2)}) collective-permute-start(bf16[768,384]{0,1:T(8,128)(2,1)} %copy.182), channel_id=1, source_target_pairs={{0,4},{4,0},{1,5},{5,1},{2,6},{6,2},{3,7},{7,3},{8,12},{12,8},{9,1... | collective-permute-start | bytes 1769480 | tf_op jit(solution)/shard_map/ppermute | solution.py:532
  660.1 46.6 %collective-permute-start.48 = (bf16[768,384]{1,0:T(8,128)(2,1)}, bf16[768,384]{1,0:T(8,128)(2,1)}, u32[]{:S(2)}, u32[]{:S(2)}) collective-permute-start(bf16[768,384]{1,0:T(8,128)(2,1)} %get-tuple-element.446), channel_id=1, source_target_pairs={{0,2},{2,0},{1,3},{3,1},{4,6},{6,4},{5,7},{7,5},{8,10},{10,8},{9,1... | collective-permute-start | bytes 1769480 | tf_op jit(solution)/shard_map/ppermute | solution.py:529
  716.0 169.0 %reduce-scatter.11.cloned.1.call-start = ((), (), s32[]{:S(2)}) async-start(), calls=%async_computation.11 | async-start | bytes 2949120 | tf_op jit(solution)/shard_map/reduce_scatter | solution.py:665
  720.0 57.8 %collective-permute-start.49 = (bf16[768,1152]{1,0:T(8,128)(2,1)}, bf16[768,1152]{1,0:T(8,128)(2,1)}, u32[]{:S(2)}, u32[]{:S(2)}) collective-permute-start(bf16[768,1152]{1,0:T(8,128)(2,1)} %copy.183), channel_id=1, source_target_pairs={{0,4},{4,0},{1,5},{5,1},{2,6},{6,2},{3,7},{7,3},{8,12},{12,8},{9,1... | collective-permute-start | bytes 5308424 | tf_op jit(solution)/shard_map/ppermute | solution.py:532
  724.6 53.2 %collective-permute-start.50 = (bf16[768,1152]{1,0:T(8,128)(2,1)}, bf16[768,1152]{1,0:T(8,128)(2,1)}, u32[]{:S(2)}, u32[]{:S(2)}) collective-permute-start(bf16[768,1152]{1,0:T(8,128)(2,1)} %copy.184), channel_id=1, source_target_pairs={{0,2},{2,0},{1,3},{3,1},{4,6},{6,4},{5,7},{7,5},{8,10},{10,8},{9,1... | collective-permute-start | bytes 5308424 | tf_op jit(solution)/shard_map/ppermute | solution.py:529
  727.2 109.1 %collective-permute-start.58 = (bf16[96,1536]{1,0:T(8,128)(2,1)}, bf16[96,1536]{1,0:T(8,128)(2,1)S(1)}, u32[]{:S(2)}, u32[]{:S(2)}) collective-permute-start(bf16[96,1536]{1,0:T(8,128)(2,1)} %get-tuple-element.816), channel_id=1, source_target_pairs={{0,2},{2,0},{1,3},{3,1},{4,6},{6,4},{5,7},{7,5},{8,10},{10,8},{9,1... | collective-permute-start | bytes 884744 | tf_op jit(solution)/shard_map/ppermute | solution.py:529
  739.1 14.9 %collective-permute-start.10 = (bf16[512,1536]{1,0:T(8,128)(2,1)}, bf16[512,1536]{1,0:T(8,128)(2,1)}, u32[]{:S(2)}, u32[]{:S(2)}) collective-permute-start(bf16[512,1536]{1,0:T(8,128)(2,1)} %fusion.125), channel_id=1, source_target_pairs={{0,1},{1,0},{2,3},{3,2},{4,5},{5,4},{6,7},{7,6},{8,9},{9,8},{10,11... | collective-permute-start | bytes 4718600 | tf_op jit(solution)/shard_map/cond/branch_1_fun/ppermute | solution.py:535
  767.8 68.5 %collective-permute-start.59 = (bf16[96,1536]{1,0:T(8,128)(2,1)}, bf16[96,1536]{1,0:T(8,128)(2,1)}, u32[]{:S(2)}, u32[]{:S(2)}) collective-permute-start(bf16[96,1536]{1,0:T(8,128)(2,1)} %get-tuple-element.817), channel_id=1, source_target_pairs={{0,4},{4,0},{1,5},{5,1},{2,6},{6,2},{3,7},{7,3},{8,12},{12,8},{9,1... | collective-permute-start | bytes 884744 | tf_op jit(solution)/shard_map/ppermute | solution.py:532
  782.2 48.9 %collective-permute-start.51 = (bf16[384,1536]{1,0:T(8,128)(2,1)}, bf16[384,1536]{1,0:T(8,128)(2,1)}, u32[]{:S(2)}, u32[]{:S(2)}) collective-permute-start(bf16[384,1536]{1,0:T(8,128)(2,1)} %pad_maximum_fusion.17), channel_id=1, source_target_pairs={{0,2},{2,0},{1,3},{3,1},{4,6},{6,4},{5,7},{7,5},{8,10},{10,8},{9,1... | collective-permute-start | bytes 3538952 | tf_op jit(solution)/shard_map/ppermute | solution.py:529
  787.4 43.6 %collective-permute-start.52 = (bf16[384,1536]{1,0:T(8,128)(2,1)}, bf16[384,1536]{1,0:T(8,128)(2,1)}, u32[]{:S(2)}, u32[]{:S(2)}) collective-permute-start(bf16[384,1536]{1,0:T(8,128)(2,1)} %pad_maximum_fusion.19), channel_id=1, source_target_pairs={{0,4},{4,0},{1,5},{5,1},{2,6},{6,2},{3,7},{7,3},{8,12},{12,8},{9,1... | collective-permute-start | bytes 3538952 | tf_op jit(solution)/shard_map/ppermute | solution.py:532
  806.0 4.1 collective-permute-start.8
  843.8 7.2 collective-permute-start.54
  851.1 4.7 collective-permute-start.55
  855.9 9.4 %collective-permute-start.56 = (bf16[192,128]{0,1:T(8,128)(2,1)S(1)}, bf16[192,128]{0,1:T(8,128)(2,1)S(1)}, u32[]{:S(2)}, u32[]{:S(2)}) collective-permute-start(bf16[192,128]{0,1:T(8,128)(2,1)S(1)} %dynamic-slice_convert_fusion), channel_id=1, source_target_pairs={{0,16},{8,24},{16,0},{24,8},{1,17},{9,25},{17,1},{25,9},{2,18},{10... | collective-permute-start | bytes 147464 | tf_op jit(solution)/shard_map/ppermute | solution.py:696
  865.5 6.1 collective-permute-start.57
  (55 other events, 548.4 us)
Sparse Core Ops, SparseCore 0:
  10.2 45.0 all-gather.6
  57.4 58.9 all-gather.4
  118.6 88.0 all-gather.8
  208.7 87.7 all-gather.10
  447.4 84.2 reduce-scatter.4
  650.5 45.2 reduce-scatter.6
  716.1 45.2 reduce-scatter.8
  836.4 48.5 reduce-scatter.10

commit v7 on v5

--- a/solution.py
+++ b/solution.py
@@ -897,13 +897,11 @@
     def stage1(pieces, rows, slope, n3, w_in):
         w_out = comm.feed_out(pieces)
         pre_grad = comm.slope_product(rows, w_out, slope)
-        sends = [comm.sends(n3, part) for part in jnp.split(pre_grad, 2, axis=1)]
-        return w_out, pre_grad, sends, comm.sum_own(pre_grad, w_in, mm_t, clips)
+        return w_out, pre_grad, comm.sends(n3, pre_grad), comm.sum_own(pre_grad, w_in, mm_t, clips)
 
     w_out, pre_grad, send_in, e3 = comm.stage(stage1, out_pieces, up_all, slope, n3, w_in)
-    e3, send_in = comm.after((e3, send_in), far_out)
-    in_parts = jnp.split(pre_grad, 2, axis=1)
-    far_in = [comm.exchange(send_in[0])]
+    e3 = comm.after(e3, far_out)
+    far_in = comm.exchange(send_in)
 
     def stage2(rows, hidden, far, e3, values2, stats2, own):
         sent = comm.middle(comm.adds((rows, hidden, far)), None)
@@ -914,9 +912,7 @@
     sent_out, r2, r2_own, gain2, shift2 = comm.stage(
         stage2, up_all, hidden, far_out, e3, values2, stats2, up
     )
-    sent_out, r2_own, send_b = comm.after((sent_out, r2_own, send_in[1:]), far_in[0])
     half_out = comm.scatter_z(sent_out)
-    far_in += [comm.exchange(sends) for sends in send_b]
 
     def stage3(r2_own, saved, w_cross, n2, cross, text):
         w_co = split_cross(w_cross)[3]
@@ -928,13 +924,13 @@
     r2_all, dcq, dmem, send_cross = comm.stage(
         stage3, r2_own, cross_saved, w_cross, n2, cross, text
     )
-    dcq, send_cross = comm.after((dcq, send_cross), far_in)
+    dcq = comm.after(dcq, far_in)
     far_cross = comm.exchange(send_cross)
     cross_pairs = (n2, dcq), (r2_all, cross), (text, dmem)
 
-    def stage4(n3, parts, far, dcq, w_cross, values1, stats1, r2):
+    def stage4(n3, pre_grad, far, dcq, w_cross, values1, stats1, r2):
         w_so, w_cq, *_ = split_cross(w_cross)
-        in_sums = comm.adds(*[(n3, part, one) for part, one in zip(parts, far)])
+        in_sums = comm.adds((n3, pre_grad, far))
         e2 = comm.sum_own(dcq, w_cq, mm_t, clips)
         grads = norm_back(values1, stats1, gain[1], e2)
         r1 = r2 + grads[0]
@@ -942,9 +938,9 @@
         return in_sums, r1, r1_all, mm(r1_all, w_so).astype(BF), grads[1], grads[2]
 
     in_sums, r1, r1_all, datt, gain1, shift1 = comm.stage(
-        stage4, n3, in_parts, tuple(far_in), dcq, w_cross, values1, stats1, r2
-    )
-    in_sums, datt = comm.after((in_sums, datt), far_cross, half_out)
+        stage4, n3, pre_grad, far_in, dcq, w_cross, values1, stats1, r2
+    )
+    datt = comm.after(datt, far_cross, half_out)
     in_second = comm.second(in_sums)
 
     def stage5(pairs, far, r1_all, att):
@@ -953,23 +949,21 @@
         return sums, comm.sends(r1_all, att)
 
     cross_sums, send_so = comm.stage(stage5, cross_pairs, far_cross, r1_all, att)
-    cross_sums, send_so, datt, in_sums = comm.after(
-        (cross_sums, send_so, datt, in_sums), in_second
-    )
+    datt, in_late = comm.after((datt, in_sums), in_second, send_so)
     cross_second = comm.second(cross_sums)
     far_so = comm.exchange(send_so)
-    half_in = comm.scatter_z(comm.closing(in_sums, in_second))
+    half_in = comm.scatter_z(comm.closing(in_late, in_second))
 
     def stage_back(saved, datt, n1):
         dqkv = comm.self_back(saved, datt, clips)
         return dqkv, comm.sends(n1, dqkv)
 
     dqkv, send_self = comm.stage(stage_back, self_saved, datt, n1)
-    dmem, hidden, send_self, cross_sums, dqkv = comm.after(
-        (dmem, hidden, send_self, cross_sums, dqkv), cross_second, far_so
+    dmem, hidden, send_self, cross_late, dqkv, far_so = comm.after(
+        (dmem, hidden, send_self, cross_sums, dqkv, far_so), cross_second, half_in
     )
     far_self = comm.exchange(send_self)
-    half_cross = comm.scatter_z(comm.closing(cross_sums, cross_second))
+    half_cross = comm.scatter_z(comm.closing(cross_late, cross_second))
 
     def stage6(dmem, w_cross, values2, hidden, w_out):
         w_cm = split_cross(w_cross)[2]
@@ -978,25 +972,27 @@
         return comm.restore(text_grad), comm.restore(layer_out)
 
     text_grad, layer_out = comm.stage(stage6, dmem, w_cross, values2, hidden, w_out)
-    text_grad, layer_out, dqkv = comm.after((text_grad, layer_out, dqkv), far_self, half_in)
+    text_grad, layer_out, dqkv, half_out, half_in = comm.after(
+        (text_grad, layer_out, dqkv, half_out, half_in), far_self, half_cross
+    )
     self_sums = comm.adds((r1_all, att, far_so), (n1, dqkv, far_self))
     dqkv = comm.after(dqkv, self_sums)
     self_second = comm.second(self_sums)
 
-    def stage7(dqkv, w_self, values0, stats0, r1):
-        e1 = comm.sum_own(dqkv, w_self, mm_t, clips)
-        grads = norm_back(values0, stats0, gain[0], e1)
-        return comm.restore(r1 + grads[0]), grads[1], grads[2]
-
-    input_grad, gain0, shift0 = comm.stage(stage7, dqkv, w_self, values0, stats0, r1)
-    input_grad, gain0 = comm.after((input_grad, gain0), self_second, half_cross)
-    half_self = comm.scatter_z(comm.closing(self_sums, self_second))
+    def stage7(dqkv, w_self):
+        return comm.sum_own(dqkv, w_self, mm_t, clips)
+
+    e1 = comm.stage(stage7, dqkv, w_self)
+    e1, self_late = comm.after((e1, self_sums), self_second)
+    half_self = comm.scatter_z(comm.closing(self_late, self_second))
+    dv0, gain0, shift0 = norm_back(values0, stats0, gain[0], e1)
+    input_grad = comm.restore(r1 + dv0)
     norm_grad = comm.norm_sums(jnp.stack([gain0, gain1, gain2, shift0, shift1, shift2]))
     input_grad = input_grad.reshape(clips, own_frames, width)
     text_grad = text_grad.reshape(clips, texts, width)
     layer_out = layer_out.reshape(clips, own_frames, width)
     grad_out = comm.close_middle(half_out)
-    grad_in = catenate(comm.close_last(half_in, *[part.shape[1] for part in in_parts]))
+    (grad_in,) = comm.close_last(half_in, pre_grad.shape[1])
     grad_cq, grad_co, grad_cm = comm.close_last(half_cross, cols, cols, 2 * cols)
     grad_so, grad_self = comm.close_last(half_self, cols, 3 * cols)
     return (

time: 880 us -> 850 us (0.966)
  waiting for transfers between devices: 175 us -> 158 us
  local copies, waits for them, and re-layouts: 133 us -> 124 us
    optimization_barrier x12 -> x4, local copies, waits for them, and re-layouts: 30.5 us -> 11.3 us  [tie(): return lax.optimization_barrier((value, others))[0]]
    ppermute x22 -> x21, waiting for transfers between devices: 62.8 us -> 45.8 us  [y(): return lax.ppermute(v, 'y', SWAP)]
    cond x65 -> x66, local copies, waits for them, and re-layouts: 3.37 us -> 19.1 us  [the longest x5 15.7 us: stage(): return lax.cond(self.core < 2, work, nothing, *values)]
    reduce_scatter x4, waiting for transfers between devices: 0.02 us -> 11.6 us  [scatter_z(): return lax.psum_scatter(parts, 'z', scatter_dimension=1, tiled=True)]
    ppermute x22 -> x21, waiting for transfers between devices: 67.6 us -> 58.2 us  [x(): return lax.ppermute(v, 'x', SWAP)]
    dot_general x32 -> x28, matrix products: 110 us -> 101 us  [mm_rows(): lax.dot_general(left, right, (((0,), (0,)), ((), ())), preferred_element_...]
    another operation x10 -> x8, local copies, waits for them, and re-layouts: 19.2 us -> 16 us
    ppermute x22 -> x21, starting transfers between devices: 25.5 us -> 23.8 us  [y(): return lax.ppermute(v, 'y', SWAP)]
  transfers between devices with their start and end apart: 70 -> 68, of which waited for: 26 -> 22; matrix products, arithmetic and copies ran while one was open for 52% -> 48% of each run, Pallas kernels for 17% -> 17%
where the time goes in v7:
time: 850 us; the launch traced here: 841 us
  matrix products  256 us (30%)
  waiting for transfers between devices  158 us (19%)
  Pallas kernels  147 us (17%)
  local copies, waits for them, and re-layouts  124 us (15%)
  other arithmetic  85.5 us (10%)
  starting transfers between devices  54.6 us (6%)
  between operations  15.4 us (2%)
    dot_general x17, matrix products, mm_t(): lax.dot_general(left, right, (((1,), (1,)), ((), ())), preferred_element_...  110 us
    dot_general x28, matrix products, mm_rows(): lax.dot_general(left, right, (((0,), (0,)), ((), ())), preferred_element_...  101 us
    ppermute x21, waiting for transfers between devices, x(): return lax.ppermute(v, 'x', SWAP)  58.2 us
    ppermute x21, waiting for transfers between devices, y(): return lax.ppermute(v, 'y', SWAP)  45.8 us
    dot_general x8, matrix products, mm(): return jnp.dot(left, right, preferred_element_type=F32)  44.2 us
    pallas_call x1, Pallas kernels, self_back(): pl.pallas_call(self_back_kernel, grid_spec=pltpu.PrefetchScalarGridSpec(n...  30 us
    ppermute x21, starting transfers between devices, y(): return lax.ppermute(v, 'y', SWAP)  23.8 us
    ppermute x21, starting transfers between devices, x(): return lax.ppermute(v, 'x', SWAP)  22 us
  transfers between devices with their start and end apart: 68, of which 22 were waited for; matrix products, arithmetic and copies ran while one was open for 48% of the time, Pallas kernels for 17%

profile of v7, /device:TPU:0, one launch (start us, length us, event | category | flops | bytes accessed | tf_op | source)
XLA Modules:
  0.0 840.5 jit_solution(2597946358867541445)
XLA Ops:
  30.2 5.1 collective-permute-done.12
  48.9 6.4 all-gather.7.cloned.1.call-done
  62.2 18.6 %collective-permute-done.19 = bf16[384,1152]{1,0:T(8,128)(2,1)} collective-permute-done((bf16[384,1152]{1,0:T(8,128)(2,1)}, bf16[384,1152]{1,0:T(8,128)(2,1)}, u32[]{:S(2)}, u32[]{:S(2)}) %collective-permute-start.19) | collective-permute-done | bytes 884768 | tf_op jit(solution)/shard_map/ppermute | solution.py:529
  83.8 17.5 %collective-permute-done.23 = bf16[384,1152]{1,0:T(8,128)(2,1)} collective-permute-done((bf16[384,1152]{1,0:T(8,128)(2,1)}, bf16[384,1152]{1,0:T(8,128)(2,1)}, u32[]{:S(2)}, u32[]{:S(2)}) %collective-permute-start.23) | collective-permute-done | bytes 884768 | tf_op jit(solution)/shard_map/ppermute | solution.py:532
  101.3 15.1 %all-gather.5.cloned.1.call-done.refs_0_ = bf16[384,3840]{1,0:T(8,128)(2,1)} async-done(((bf16[96,3840]{1,0:T(8,128)(2,1)}), bf16[384,3840]{1,0:T(8,128)(2,1)}) %all-gather.5.cloned.1.call-update) | async-done | bytes 2949136 | tf_op jit(solution)/shard_map/all_gather | solution.py:557
  126.4 31.4 %collective-permute-done.25.refs_1_ = bf16[384,1920]{1,0:T(8,128)(2,1)} collective-permute-done((bf16[384,1920]{1,0:T(8,128)(2,1)}, bf16[384,1920]{1,0:T(8,128)(2,1)}, u32[]{:S(2)}, u32[]{:S(2)}) %collective-permute-start.25) | collective-permute-done | bytes 1474592 | tf_op jit(solution)/shard_map/ppermute | solution.py:529
  169.5 37.1 %conditional.10 = (bf16[1536,2304]{1,0:T(8,128)(2,1)}, bf16[1024,768]{1,0:T(8,128)(2,1)}, s32[1]{0:T(128)}, bf16[2,2,256,2304]{3,2,1,0:T(8,128)(2,1)}, f32[2,2,256,768]{3,2,1,0:T(8,128)}) conditional(s32[]{:T(128)} %convert_element_type.399, () %tuple.117, (bf16[384,2304]{1,0:T(8,128)(2,1)}, bf16[384,1152]{1,0:T(8,128)(2,1)}, ...), branch_computations={%region_2.3_spmd, %region_3.4_spmd} | conditional | flops 8458076160 | bytes 24379432 | solution.py:612
  169.5 6.0 place.2
  175.5 12.8 %convolution_convert_fusion = bf16[2304,1024]{0,1:T(8,128)(2,1)} fusion(bf16[1536,2304]{1,0:T(8,128)(2,1)} %place.2, bf16[1024,1536]{0,1:T(8,128)(2,1)} %get-tuple-element.634), kind=kOutput, calls=%fused_computation | convolution fusion | flops 7250116608 | bytes 14942208 | tf_op jit(solution)/shard_map/cond/branch_1_fun/dot_general | solution.py:19
  188.3 18.3 %self_attend.1 = (bf16[2,2,256,768]{3,2,1,0:T(8,128)(2,1)}, f32[2,2,256,768]{3,2,1,0:T(8,128)}) custom-call(s32[1]{0:T(128)} %bitcast.core_ref, bf16[2,2,256,2304]{3,2,1,0:T(8,128)(2,1)} %bitcast.2.q_ref.k_ref.v_ref, bf16[2,2,256,2304]{3,2,1,0:T(8,128)(2,1)} %bitcast.2.q_ref.k_ref.v_ref, bf16[2,2,256,2304]{3,2,1,0:T(8,128)(2,1)} %bitcast.2.q_ref.k_ref.v_ref), custom_call_target="tpu_custom_call" | custom-call | flops 1207959552 | bytes 9437184 | tf_op jit(solution)/shard_map/cond/branch_1_fun/self_attend/pallas_call | solution.py:707
  206.7 4.8 fusion.358
  211.5 7.5 collective-permute-done.27.refs_3_
  228.8 8.8 %place.3 = bf16[1536,3840]{1,0:T(8,128)(2,1)} custom-call(bf16[384,3840]{1,0:T(8,128)(2,1)} %all-gather.5.cloned.1.call-done.refs_0_, bf16[384,1920]{1,0:T(8,128)(2,1)} %collective-permute-done.25.refs_1_, bf16[384,1920]{1,0:T(8,128)(2,1)} %collective-permute-done.26.refs_2_, bf16[384,1920]{1,0:T(8,128)(2,1)} %collective-permute-done.27.refs_3_, ...), custom_call_target="tpu_custom_call" | custom-call | tf_op jit(solution)/shard_map/place/pallas_call | solution.py:139
  237.6 65.5 %conditional.11 = (f32[512,1536]{1,0:T(8,128)}, f32[512,1]{0,1:T(1,128)S(1)}, f32[512,1]{0,1:T(1,128)S(1)}, bf16[1024,1536]{1,0:T(8,128)(2,1)}, bf16[1024,768]{1...) conditional(s32[]{:T(128)} %convert_element_type.399, ...), branch_computations={%region_4.5_spmd, %region_5.10_spmd} | conditional | flops 8087077888 | bytes 141820608 | solution.py:612
  237.7 4.5 convolution_convert_fusion.9
  247.4 6.0 fusion.351
  263.9 6.4 fusion.202
  270.3 13.4 %cross_attend.1 = bf16[2,2,256,768]{3,2,1,0:T(8,128)(2,1)} custom-call(bf16[2,2,256,768]{3,2,1,0:T(8,128)(2,1)} %bitcast.6.q_ref, bf16[2,64,1536]{2,1,0:T(8,128)(2,1)S(1)} %bitcast.206, bf16[2,64,1536]{2,1,0:T(8,128)(2,1)S(1)} %bitcast.207), custom_call_target="tpu_custom_call" | custom-call | flops 201326592 | bytes 3145728 | tf_op jit(solution)/shard_map/cond/branch_1_fun/cross_attend/pallas_call | solution.py:770
  303.1 4.8 fusion.357
  309.3 7.4 place_stacked.3.weight_ref
  316.7 19.9 %feed.1 = (bf16[1024,3072]{1,0:T(8,128)(2,1)}, bf16[1024,3072]{1,0:T(8,128)(2,1)}) custom-call(bf16[1024,1536]{1,0:T(8,128)(2,1)} %get-tuple-element.340.rows_ref, bf16[1536,3072]{1,0:T(8,128)(2,1)} %place_stacked.3.weight_ref), custom_call_target="tpu_custom_call" | custom-call | flops 9663676416 | bytes 25165824 | tf_op jit(solution)/shard_map/feed/pallas_call | solution.py:311
  336.7 6.6 convolution_convert_fusion.12
  353.8 8.6 %collective-permute-done.35 = bf16[2,384,1536]{2,1,0:T(8,128)(2,1)} collective-permute-done((bf16[2,384,1536]{2,1,0:T(8,128)(2,1)}, bf16[2,384,1536]{2,1,0:T(8,128)(2,1)}, u32[]{:S(2)}, u32[]{:S(2)}) %collective-permute-start.35) | collective-permute-done | bytes 2359328 | tf_op jit(solution)/shard_map/ppermute | solution.py:532
  363.0 57.1 %conditional.12 = (bf16[1536,3072]{1,0:T(8,128)(2,1)}, bf16[1024,3072]{1,0:T(8,128)(2,1)}, bf16[768,1536]{0,1:T(8,128)(2,1)}, bf16[768,1536]{1,0:T(8,128)(2,1)}, f32[512,1536]{1,0:T(8,128)}) conditional(s32[]{:T(128)} %convert_element_type.399, () %tuple.125, (bf16[4,384,1536]{2,1,0:T(8,128)(2,1)}, bf16[2,384,1536]{2,1,0:T(8,128)(2,1)}, ...), branch_computations={%region_10.11_spmd, %region_11.12_spmd} | conditional | flops 24167055360 | bytes 108527768 | solution.py:612
  363.0 7.3 place_stacked.2.weight_ref
  370.3 18.0 %slope_product.1 = bf16[1024,3072]{1,0:T(8,128)(2,1)} custom-call(bf16[1024,1536]{1,0:T(8,128)(2,1)} %get-tuple-element.172.rows_ref, bf16[1536,3072]{1,0:T(8,128)(2,1)} %place_stacked.2.weight_ref, bf16[1024,3072]{1,0:T(8,128)(2,1)} %get-tuple-element.173.slope_ref), custom_call_target="tpu_custom_call" | custom-call | flops 9663676416 | bytes 25165824 | tf_op jit(solution)/shard_map/cond/branch_1_fun/slope_product/pallas_call | solution.py:346
  388.3 9.5 %fusion.9 = bf16[512,1536]{1,0:T(8,128)(2,1)S(1)} fusion(bf16[1536,3072]{1,0:T(8,128)(2,1)} %get-tuple-element.175, bf16[1024,3072]{1,0:T(8,128)(2,1)} %slope_product.1), kind=kOutput, calls=%fused_computation.11 | convolution fusion | flops 4832624640 | bytes 14155776 | tf_op jit(solution)/shard_map/cond/branch_1_fun/dot_general | solution.py:23
  399.4 6.0 convolution_convert_fusion.1
  405.4 6.5 fusion.6
  411.9 8.2 convert_add_fusion
  420.1 25.8 %conditional.13 = (bf16[4,384,1536]{2,1,0:T(8,128)(2,1)}, f32[512,1536]{1,0:T(8,128)}, bf16[512,1536]{1,0:T(8,128)(2,1)}, f32[1,1536]{1,0:T(1,128)}, f32[1,1536]{1,0:T(1,128)}) conditional(s32[]{:T(128)} %convert_element_type.399, () %tuple.115, (bf16[1024,1536]{1,0:T(8,128)(2,1)}, bf16[1024,3072]{1,0:T(8,128)(2,1)}, bf16[768,1536]{1,0:T(8,128)(2,1)}, ...), branch_computations={%region_12.13_spmd, %region_13.18_spmd} | conditional | flops 4864078848 | bytes 91349112 | solution.py:612
  421.8 5.3 add_convert_fusion.5
  427.2 4.3 add_convert_fusion.6
  440.1 4.6 fusion.332
  445.9 4.7 copy.114
  452.8 53.0 %conditional.14 = (bf16[1024,1536]{1,0:T(8,128)(2,1)}, bf16[1024,768]{1,0:T(8,128)(2,1)}, bf16[128,1536]{1,0:T(8,128)(2,1)}, bf16[768,1536]{0,1:T(8,128)(2,1)}, bf16[768,1536]{0,1:T(8,128)(2,1)}) conditional(s32[]{:T(128)} %convert_element_type.399, () %tuple.114, (bf16[512,1536]{1,0:T(8,128)(2,1)}, bf16[1024,768]{1,0:T(8,128)(2,1)}, ...), branch_computations={%region_18.19_spmd, %region_19.20_spmd} | conditional | flops 5661130752 | bytes 69599480 | solution.py:612
  467.0 6.4 fusion.19
  473.5 17.6 %cross_back.1 = (bf16[2,2,256,768]{3,2,1,0:T(8,128)(2,1)}, bf16[2,64,1536]{2,1,0:T(8,128)(2,1)}) custom-call(bf16[2,2,256,768]{3,2,1,0:T(8,128)(2,1)} %bitcast.23.q_ref, bf16[2,64,1536]{2,1,0:T(8,128)(2,1)S(1)} %get-tuple-element.188.k_ref.v_ref, bf16[2,64,1536]{2,1,0:T(8,128)(2,1)S(1)} %get-tuple-element.188.k_ref.v_ref, bf16[2,2,256,768]{3,2,1,0:T(8,128)(2,1)} %bitcast.212), custom_call_target="tpu_custom_call" | custom-call | flops 503316480 | bytes 4718592 | tf_op jit(solution)/shard_map/cond/branch_1_fun/cross_back/pallas_call | solution.py:787
  507.8 47.1 %conditional.15 = (bf16[384,1536]{1,0:T(8,128)(2,1)}, bf16[384,1536]{1,0:T(8,128)(2,1)}, bf16[384,1536]{1,0:T(8,128)(2,1)}, bf16[384,1536]{1,0:T(8,128)(2,1)}, b...) conditional(s32[]{:T(128)} %convert_element_type.399, ...), branch_computations={%region_20.21_spmd, %region_21.26_spmd} | conditional | flops 9697489920 | bytes 93708440 | solution.py:612
  507.8 4.5 convolution_convert_fusion.10
  516.6 5.5 multiply_reduce_fusion.5
  522.2 5.2 fusion.333
  527.7 5.2 add_convert_fusion.7
  532.9 5.7 add_convert_fusion.8
  548.4 6.4 fusion.223
  560.9 29.0 %conditional.16 = (bf16[384,1536]{0,1:T(8,128)(2,1)}, bf16[384,1536]{0,1:T(8,128)(2,1)}, bf16[384,1536]{0,1:T(8,128)(2,1)}, bf16[384,1536]{0,1:T(8,128)(2,1)}, b...) conditional(s32[]{:T(128)} %convert_element_type.399, () %tuple.135, (bf16[1024,1536]{1,0:T(8,128)(2,1)}, ...), branch_computations={%region_27.28_spmd, %region_28.29_spmd} | conditional | flops 3957522432 | bytes 56623180 | solution.py:612
  605.9 45.6 %conditional.17 = (bf16[1024,2304]{1,0:T(8,128)(2,1)}, bf16[768,1152]{0,1:T(8,128)(2,1)}, bf16[768,1152]{1,0:T(8,128)(2,1)}) conditional(s32[]{:T(128)} %convert_element_type.399, () %tuple.130, (bf16[1024,768]{1,0:T(8,128)(2,1)}, s32[1]{0:T(128)}, bf16[2,2,256,2304]{3,2,1,0:T(8,128)(2,1)}, f32[2,2,256,768]{3,2,1,0:T(8,128)}, ...), branch_computations={%region_29.30_spmd, %region_30.31_spmd} | conditional | flops 6648692736 | bytes 47579188 | solution.py:612
  605.9 30.0 %self_back.1 = bf16[2,2,256,2304]{3,2,1,0:T(8,128)(2,1)} custom-call(s32[1]{0:T(128)} %get-tuple-element.216.core_ref, bf16[2,2,256,2304]{3,2,1,0:T(8,128)(2,1)} %get-tuple-element.217.q_ref.k_ref.v_ref, bf16[2,2,256,2304]{3,2,1,0:T(8,128)(2,1)} %get-tuple-element.217.q_ref.k_ref.v_ref, bf16[2,2,256,2304]{3,2,1,0:T(8,128)(2,1)} %get-tuple-element.217.q_ref.k_ref.v_ref, ...), custom_call_target="tpu_custom_call" | custom-call | flops 3019898880 | bytes 14155776 | tf_op jit(solution)/shard_map/cond/branch_1_fun/self_back/pallas_call | solution.py:737
  635.9 4.6 copy.117
  640.5 5.6 fusion.127
  646.3 5.2 convolution_convert_fusion.5
  680.0 39.2 %conditional.18 = (f32[128,1536]{1,0:T(8,128)}, bf16[512,1536]{1,0:T(8,128)(2,1)}) conditional(s32[]{:T(128)} %convert_element_type.399, () %tuple.110, (bf16[1536,3840]{1,0:T(8,128)(2,1)}, bf16[128,1536]{1,0:T(8,128)(2,1)}, bf16[1024,3072]{1,0:T(8,128)(2,1)}, bf16[1536,3072]{1,0:T(8,128)(2,1)}, f32[512,1536]{1,0:T(8,128)S(1)}) %tuple.140), branch_computations={%region_32.33_spmd, %region_33.34_spmd} | conditional | flops 13905571840 | bytes 55075012 | solution.py:612
  680.0 10.5 %fusion.148 = bf16[512,1536]{1,0:T(8,128)(2,1)} fusion(bf16[1536,3072]{1,0:T(8,128)(2,1)} %get-tuple-element.225, bf16[1024,3072]{1,0:T(8,128)(2,1)} %get-tuple-element.224), kind=kOutput, calls=%fused_computation.132 | convolution fusion | flops 4832624640 | bytes 14155776 | tf_op jit(solution)/shard_map/cond/branch_1_fun/dot_general | solution.py:23
  690.6 5.1 fusion.349
  705.4 13.8 %fusion.147 = bf16[512,1536]{1,0:T(8,128)(2,1)} fusion(s32[1536]{0:T(1024)S(1)} %fusion.163, f32[512,1536]{1,0:T(8,128)S(1)} %get-tuple-element.223, bf16[512,1536]{1,0:T(8,128)(2,1)} %collective-permute-done.10, bf16[1536,3072]{1,0:T(8,128)(2,1)} %get-tuple-element.225, bf16[1024,3072]{1,0:T(8,128)(2,1)} %get-tuple-element.224), kind=kOutput, calls=%fused_computation.131 | convolution fusion | flops 7254048768 | bytes 18880512 | tf_op jit(solution)/shard_map/cond/branch_1_fun/dot_general | solution.py:23
  722.9 5.1 fusion.246
  729.4 4.4 fusion.247
  744.1 17.9 %conditional.19 = (f32[512,1536]{1,0:T(8,128)S(1)}) conditional(s32[]{:T(128)} %convert_element_type.399, () %tuple.142, (bf16[1024,2304]{1,0:T(8,128)(2,1)}, bf16[1536,2304]{1,0:T(8,128)(2,1)}) %tuple.144), branch_computations={%region_35.36_spmd, %region_36.37_spmd} | conditional | flops 7250116608 | bytes 31457328 | solution.py:612
  744.1 7.6 convolution_convert_fusion.7
  755.2 6.8 convert_add_fusion.2
  787.5 6.7 collective-permute-done.54
  799.3 5.7 fusion.233
  809.4 7.7 fusion.248
  817.7 11.5 %reduce-scatter.11.cloned.1.call-done = bf16[2,96,1536]{2,1,0:T(8,128)(2,1)} async-done(((bf16[2,384,1536]{2,1,0:T(8,128)(2,1)}), bf16[2,96,1536]{2,1,0:T(8,128)(2,1)}) %reduce-scatter.11.cloned.1.call-update) | async-done | bytes 589840 | tf_op jit(solution)/shard_map/reduce_scatter | solution.py:657
  (458 shorter events, 333.1 us)
Async XLA Ops:
  7.2 48.1 %all-gather.7.cloned.1.call-start = ((), (), s32[]{:S(2)}) async-start(), calls=%async_computation.5 | async-start | bytes 2211840 | tf_op jit(solution)/shard_map/all_gather | solution.py:557
  9.3 107.1 %all-gather.5.cloned.1.call-start = ((), (), s32[]{:S(2)}) async-start(), calls=%async_computation.4 | async-start | bytes 3686400 | tf_op jit(solution)/shard_map/all_gather | solution.py:557
  10.2 16.8 %collective-permute-start.11 = (bf16[96,128]{1,0:T(8,128)(2,1)S(1)}, bf16[96,128]{1,0:T(8,128)(2,1)S(1)}, u32[]{:S(2)}, u32[]{:S(2)}) collective-permute-start(bf16[96,128]{1,0:T(8,128)(2,1)S(1)} %get-tuple-element.836), channel_id=1, source_target_pairs={{0,8},{8,0},{16,24},{24,16},{1,9},{9,1},{17,25},{25,17},{2,10},{10... | collective-permute-start | bytes 73736 | tf_op jit(solution)/shard_map/ppermute | solution.py:538
  17.0 189.6 %all-gather.9.cloned.1.call-start = ((), (), s32[]{:S(2)}) async-start(), calls=%async_computation.6 | async-start | bytes 5898240 | tf_op jit(solution)/shard_map/all_gather | solution.py:558
  18.2 23.6 %collective-permute-start.16 = (bf16[96,1536]{1,0:T(8,128)(2,1)}, bf16[96,1536]{1,0:T(8,128)(2,1)}, u32[]{:S(2)}, u32[]{:S(2)}) collective-permute-start(bf16[96,1536]{1,0:T(8,128)(2,1)} %get-tuple-element.822), channel_id=1, source_target_pairs={{0,4},{4,0},{1,5},{5,1},{2,6},{6,2},{3,7},{7,3},{8,12},{12,8},{9,1... | collective-permute-start | bytes 884744 | tf_op jit(solution)/shard_map/ppermute | solution.py:532
  19.7 22.1 %collective-permute-start.15 = (bf16[96,1536]{1,0:T(8,128)(2,1)}, bf16[96,1536]{1,0:T(8,128)(2,1)}, u32[]{:S(2)}, u32[]{:S(2)}) collective-permute-start(bf16[96,1536]{1,0:T(8,128)(2,1)} %get-tuple-element.823), channel_id=1, source_target_pairs={{0,2},{2,0},{1,3},{3,1},{4,6},{6,4},{5,7},{7,5},{8,10},{10,8},{9,1... | collective-permute-start | bytes 884744 | tf_op jit(solution)/shard_map/ppermute | solution.py:529
  23.2 20.8 %collective-permute-start.18 = (bf16[96,1536]{1,0:T(8,128)(2,1)}, bf16[96,1536]{1,0:T(8,128)(2,1)}, u32[]{:S(2)}, u32[]{:S(2)}) collective-permute-start(bf16[96,1536]{1,0:T(8,128)(2,1)} %get-tuple-element.818), channel_id=1, source_target_pairs={{0,4},{4,0},{1,5},{5,1},{2,6},{6,2},{3,7},{7,3},{8,12},{12,8},{9,1... | collective-permute-start | bytes 884744 | tf_op jit(solution)/shard_map/ppermute | solution.py:532
  23.7 20.3 %collective-permute-start.17 = (bf16[96,1536]{1,0:T(8,128)(2,1)}, bf16[96,1536]{1,0:T(8,128)(2,1)}, u32[]{:S(2)}, u32[]{:S(2)}) collective-permute-start(bf16[96,1536]{1,0:T(8,128)(2,1)} %get-tuple-element.819), channel_id=1, source_target_pairs={{0,2},{2,0},{1,3},{3,1},{4,6},{6,4},{5,7},{7,5},{8,10},{10,8},{9,1... | collective-permute-start | bytes 884744 | tf_op jit(solution)/shard_map/ppermute | solution.py:529
  27.1 8.2 collective-permute-start.12
  35.4 4.7 collective-permute-start.13
  40.1 6.1 collective-permute-start.14
  48.8 254.3 %all-gather.11.cloned.1.call-start = ((), (), s32[]{:S(2)}) async-start(), calls=%async_computation.7 | async-start | bytes 5898240 | tf_op jit(solution)/shard_map/all_gather | solution.py:558
  58.1 22.8 %collective-permute-start.19 = (bf16[384,1152]{1,0:T(8,128)(2,1)}, bf16[384,1152]{1,0:T(8,128)(2,1)}, u32[]{:S(2)}, u32[]{:S(2)}) collective-permute-start(bf16[384,1152]{1,0:T(8,128)(2,1)} %get-tuple-element.790), channel_id=1, source_target_pairs={{0,2},{2,0},{1,3},{3,1},{4,6},{6,4},{5,7},{7,5},{8,10},{10,8},{9,1... | collective-permute-start | bytes 2654216 | tf_op jit(solution)/shard_map/ppermute | solution.py:529
  59.5 22.8 %collective-permute-start.21 = (bf16[384,1152]{1,0:T(8,128)(2,1)}, bf16[384,1152]{1,0:T(8,128)(2,1)}, u32[]{:S(2)}, u32[]{:S(2)}) collective-permute-start(bf16[384,1152]{1,0:T(8,128)(2,1)} %get-tuple-element.789), channel_id=1, source_target_pairs={{0,4},{4,0},{1,5},{5,1},{2,6},{6,2},{3,7},{7,3},{8,12},{12,8},{9,1... | collective-permute-start | bytes 2654216 | tf_op jit(solution)/shard_map/ppermute | solution.py:532
  61.0 528.9 %reduce-scatter.5.cloned.1.call-start = ((), (), s32[]{:S(2)}) async-start(), calls=%async_computation.8 | async-start | bytes 5898240 | tf_op jit(solution)/shard_map/reduce_scatter | solution.py:657
  61.1 40.3 %collective-permute-start.23 = (bf16[384,1152]{1,0:T(8,128)(2,1)}, bf16[384,1152]{1,0:T(8,128)(2,1)}, u32[]{:S(2)}, u32[]{:S(2)}) collective-permute-start(bf16[384,1152]{1,0:T(8,128)(2,1)} %get-tuple-element.790), channel_id=1, source_target_pairs={{0,4},{4,0},{1,5},{5,1},{2,6},{6,2},{3,7},{7,3},{8,12},{12,8},{9,1... | collective-permute-start | bytes 2654216 | tf_op jit(solution)/shard_map/ppermute | solution.py:532
  61.7 39.6 %collective-permute-start.24 = (bf16[384,1152]{1,0:T(8,128)(2,1)}, bf16[384,1152]{1,0:T(8,128)(2,1)}, u32[]{:S(2)}, u32[]{:S(2)}) collective-permute-start(bf16[384,1152]{1,0:T(8,128)(2,1)} %get-tuple-element.789), channel_id=1, source_target_pairs={{0,2},{2,0},{1,3},{3,1},{4,6},{6,4},{5,7},{7,5},{8,10},{10,8},{9,1... | collective-permute-start | bytes 2654216 | tf_op jit(solution)/shard_map/ppermute | solution.py:529
  80.9 37.8 %collective-permute-start.20 = (bf16[384,1152]{1,0:T(8,128)(2,1)}, bf16[384,1152]{1,0:T(8,128)(2,1)}, u32[]{:S(2)}, u32[]{:S(2)}) collective-permute-start(bf16[384,1152]{1,0:T(8,128)(2,1)} %collective-permute-done.19), channel_id=1, source_target_pairs={{0,4},{4,0},{1,5},{5,1},{2,6},{6,2},{3,7},{7,3},{8,12},{12,8},{9,1... | collective-permute-start | bytes 2654216 | tf_op jit(solution)/shard_map/ppermute | solution.py:532
  82.4 36.3 %collective-permute-start.22 = (bf16[384,1152]{1,0:T(8,128)(2,1)}, bf16[384,1152]{1,0:T(8,128)(2,1)}, u32[]{:S(2)}, u32[]{:S(2)}) collective-permute-start(bf16[384,1152]{1,0:T(8,128)(2,1)} %collective-permute-done.21), channel_id=1, source_target_pairs={{0,2},{2,0},{1,3},{3,1},{4,6},{6,4},{5,7},{7,5},{8,10},{10,8},{9,1... | collective-permute-start | bytes 2654216 | tf_op jit(solution)/shard_map/ppermute | solution.py:529
  122.3 35.5 %collective-permute-start.25 = (bf16[384,1920]{1,0:T(8,128)(2,1)}, bf16[384,1920]{1,0:T(8,128)(2,1)}, u32[]{:S(2)}, u32[]{:S(2)}) collective-permute-start(bf16[384,1920]{1,0:T(8,128)(2,1)} %get-tuple-element.784), channel_id=1, source_target_pairs={{0,2},{2,0},{1,3},{3,1},{4,6},{6,4},{5,7},{7,5},{8,10},{10,8},{9,1... | collective-permute-start | bytes 4423688 | tf_op jit(solution)/shard_map/ppermute | solution.py:529
  122.9 36.4 %collective-permute-start.29 = (bf16[384,1920]{1,0:T(8,128)(2,1)}, bf16[384,1920]{1,0:T(8,128)(2,1)}, u32[]{:S(2)}, u32[]{:S(2)}) collective-permute-start(bf16[384,1920]{1,0:T(8,128)(2,1)} %get-tuple-element.783), channel_id=1, source_target_pairs={{0,4},{4,0},{1,5},{5,1},{2,6},{6,2},{3,7},{7,3},{8,12},{12,8},{9,1... | collective-permute-start | bytes 4423688 | tf_op jit(solution)/shard_map/ppermute | solution.py:532
  124.4 42.4 %collective-permute-start.32 = (bf16[512,1536]{0,1:T(8,128)(2,1)}, bf16[512,1536]{0,1:T(8,128)(2,1)}, u32[]{:S(2)}, u32[]{:S(2)}) collective-permute-start(bf16[512,1536]{0,1:T(8,128)(2,1)} %add_convert_fusion.9), channel_id=1, source_target_pairs={{0,1},{1,0},{2,3},{3,2},{4,5},{5,4},{6,7},{7,6},{8,9},{9,8},{10,11... | collective-permute-start | bytes 4718600 | tf_op jit(solution)/shard_map/ppermute | solution.py:535
  124.4 87.1 %collective-permute-start.26 = (bf16[384,1920]{1,0:T(8,128)(2,1)}, bf16[384,1920]{1,0:T(8,128)(2,1)}, u32[]{:S(2)}, u32[]{:S(2)}) collective-permute-start(bf16[384,1920]{1,0:T(8,128)(2,1)} %get-tuple-element.784), channel_id=1, source_target_pairs={{0,4},{4,0},{1,5},{5,1},{2,6},{6,2},{3,7},{7,3},{8,12},{12,8},{9,1... | collective-permute-start | bytes 4423688 | tf_op jit(solution)/shard_map/ppermute | solution.py:532
  124.9 86.6 %collective-permute-start.28 = (bf16[384,1920]{1,0:T(8,128)(2,1)}, bf16[384,1920]{1,0:T(8,128)(2,1)}, u32[]{:S(2)}, u32[]{:S(2)}) collective-permute-start(bf16[384,1920]{1,0:T(8,128)(2,1)} %get-tuple-element.783), channel_id=1, source_target_pairs={{0,2},{2,0},{1,3},{3,1},{4,6},{6,4},{5,7},{7,5},{8,10},{10,8},{9,1... | collective-permute-start | bytes 4423688 | tf_op jit(solution)/shard_map/ppermute | solution.py:529
  157.8 61.2 %collective-permute-start.27 = (bf16[384,1920]{1,0:T(8,128)(2,1)}, bf16[384,1920]{1,0:T(8,128)(2,1)}, u32[]{:S(2)}, u32[]{:S(2)}) collective-permute-start(bf16[384,1920]{1,0:T(8,128)(2,1)} %collective-permute-done.25.refs_1_), channel_id=1, source_target_pairs={{0,4},{4,0},{1,5},{5,1},{2,6},{6,2},{3,7},{7,3},{8,12},{12,8},{9,1... | collective-permute-start | bytes 4423688 | tf_op jit(solution)/shard_map/ppermute | solution.py:532
  159.3 59.7 %collective-permute-start.30 = (bf16[384,1920]{1,0:T(8,128)(2,1)}, bf16[384,1920]{1,0:T(8,128)(2,1)}, u32[]{:S(2)}, u32[]{:S(2)}) collective-permute-start(bf16[384,1920]{1,0:T(8,128)(2,1)} %collective-permute-done.29.refs_5_), channel_id=1, source_target_pairs={{0,2},{2,0},{1,3},{3,1},{4,6},{6,4},{5,7},{7,5},{8,10},{10,8},{9,1... | collective-permute-start | bytes 4423688 | tf_op jit(solution)/shard_map/ppermute | solution.py:529
  166.8 59.3 %collective-permute-start.31 = (bf16[512,1536]{1,0:T(8,128)(2,1)}, bf16[512,1536]{1,0:T(8,128)(2,1)}, u32[]{:S(2)}, u32[]{:S(2)}) collective-permute-start(bf16[512,1536]{1,0:T(8,128)(2,1)} %fusion.256), channel_id=1, source_target_pairs={{0,1},{1,0},{2,3},{3,2},{4,5},{5,4},{6,7},{7,6},{8,9},{9,8},{10,11... | collective-permute-start | bytes 4718600 | tf_op jit(solution)/shard_map/ppermute | solution.py:535
  219.0 88.9 %collective-permute-start.33 = (bf16[2,384,1536]{2,1,0:T(8,128)(2,1)}, bf16[2,384,1536]{2,1,0:T(8,128)(2,1)}, u32[]{:S(2)}, u32[]{:S(2)}) collective-permute-start(bf16[2,384,1536]{2,1,0:T(8,128)(2,1)} %get-tuple-element.337), channel_id=1, source_target_pairs={{0,4},{4,0},{1,5},{5,1},{2,6},{6,2},{3,7},{7,3},{8,12},{12,8},{9,1... | collective-permute-start | bytes 7077896 | tf_op jit(solution)/shard_map/ppermute | solution.py:532
  220.5 87.5 %collective-permute-start.34 = (bf16[2,384,1536]{2,1,0:T(8,128)(2,1)}, bf16[2,384,1536]{2,1,0:T(8,128)(2,1)}, u32[]{:S(2)}, u32[]{:S(2)}) collective-permute-start(bf16[2,384,1536]{2,1,0:T(8,128)(2,1)} %get-tuple-element.338), channel_id=1, source_target_pairs={{0,2},{2,0},{1,3},{3,1},{4,6},{6,4},{5,7},{7,5},{8,10},{10,8},{9,1... | collective-permute-start | bytes 7077896 | tf_op jit(solution)/shard_map/ppermute | solution.py:529
  242.1 5.2 collective-permute-start
  258.4 3.7 collective-permute-start.1
  307.9 54.5 %collective-permute-start.35 = (bf16[2,384,1536]{2,1,0:T(8,128)(2,1)}, bf16[2,384,1536]{2,1,0:T(8,128)(2,1)}, u32[]{:S(2)}, u32[]{:S(2)}) collective-permute-start(bf16[2,384,1536]{2,1,0:T(8,128)(2,1)} %get-tuple-element.343), channel_id=1, source_target_pairs={{0,4},{4,0},{1,5},{5,1},{2,6},{6,2},{3,7},{7,3},{8,12},{12,8},{9,1... | collective-permute-start | bytes 7077896 | tf_op jit(solution)/shard_map/ppermute | solution.py:532
  308.6 54.4 %collective-permute-start.36 = (bf16[2,384,1536]{2,1,0:T(8,128)(2,1)}, bf16[2,384,1536]{2,1,0:T(8,128)(2,1)}, u32[]{:S(2)}, u32[]{:S(2)}) collective-permute-start(bf16[2,384,1536]{2,1,0:T(8,128)(2,1)} %get-tuple-element.344), channel_id=1, source_target_pairs={{0,2},{2,0},{1,3},{3,1},{4,6},{6,4},{5,7},{7,5},{8,10},{10,8},{9,1... | collective-permute-start | bytes 7077896 | tf_op jit(solution)/shard_map/ppermute | solution.py:529
  343.2 76.9 %collective-permute-start.37 = (bf16[768,1536]{1,0:T(8,128)(2,1)}, bf16[768,1536]{1,0:T(8,128)(2,1)}, u32[]{:S(2)}, u32[]{:S(2)}) collective-permute-start(bf16[768,1536]{1,0:T(8,128)(2,1)} %convolution_convert_fusion.12), channel_id=1, source_target_pairs={{0,4},{4,0},{1,5},{5,1},{2,6},{6,2},{3,7},{7,3},{8,12},{12,8},{9,1... | collective-permute-start | bytes 7077896 | tf_op jit(solution)/shard_map/ppermute | solution.py:532
  348.8 71.3 %collective-permute-start.38 = (bf16[768,1536]{1,0:T(8,128)(2,1)}, bf16[768,1536]{1,0:T(8,128)(2,1)}, u32[]{:S(2)}, u32[]{:S(2)}) collective-permute-start(bf16[768,1536]{1,0:T(8,128)(2,1)} %convolution_convert_fusion.11), channel_id=1, source_target_pairs={{0,2},{2,0},{1,3},{3,1},{4,6},{6,4},{5,7},{7,5},{8,10},{10,8},{9,1... | collective-permute-start | bytes 7077896 | tf_op jit(solution)/shard_map/ppermute | solution.py:529
  397.8 14.1 %collective-permute-start.7 = (bf16[512,1536]{1,0:T(8,128)(2,1)S(1)}, bf16[512,1536]{1,0:T(8,128)(2,1)S(1)}, u32[]{:S(2)}, u32[]{:S(2)}) collective-permute-start(bf16[512,1536]{1,0:T(8,128)(2,1)S(1)} %fusion.9), channel_id=1, source_target_pairs={{0,1},{1,0},{2,3},{3,2},{4,5},{5,4},{6,7},{7,6},{8,9},{9,8},{10,11... | collective-permute-start | bytes 4718600 | tf_op jit(solution)/shard_map/cond/branch_1_fun/ppermute | solution.py:535
  445.9 205.7 %reduce-scatter.7.cloned.1.call-start = ((), (), s32[]{:S(2)}) async-start(), calls=%async_computation.9 | async-start | bytes 2949120 | tf_op jit(solution)/shard_map/reduce_scatter | solution.py:657
  450.7 57.1 %collective-permute-start.39 = (bf16[768,1536]{1,0:T(8,128)(2,1)}, bf16[768,1536]{1,0:T(8,128)(2,1)}, u32[]{:S(2)}, u32[]{:S(2)}) collective-permute-start(bf16[768,1536]{1,0:T(8,128)(2,1)} %copy.114), channel_id=1, source_target_pairs={{0,4},{4,0},{1,5},{5,1},{2,6},{6,2},{3,7},{7,3},{8,12},{12,8},{9,1... | collective-permute-start | bytes 7077896 | tf_op jit(solution)/shard_map/ppermute | solution.py:532
  452.1 55.7 %collective-permute-start.40 = (bf16[768,1536]{1,0:T(8,128)(2,1)}, bf16[768,1536]{1,0:T(8,128)(2,1)}, u32[]{:S(2)}, u32[]{:S(2)}) collective-permute-start(bf16[768,1536]{1,0:T(8,128)(2,1)} %get-tuple-element.360), channel_id=1, source_target_pairs={{0,2},{2,0},{1,3},{3,1},{4,6},{6,4},{5,7},{7,5},{8,10},{10,8},{9,1... | collective-permute-start | bytes 7077896 | tf_op jit(solution)/shard_map/ppermute | solution.py:529
  452.8 8.9 %collective-permute-start.4 = (bf16[512,1536]{1,0:T(8,128)(2,1)}, bf16[512,1536]{1,0:T(8,128)(2,1)}, u32[]{:S(2)}, u32[]{:S(2)}) collective-permute-start(bf16[512,1536]{1,0:T(8,128)(2,1)} %get-tuple-element.186), channel_id=1, source_target_pairs={{0,1},{1,0},{2,3},{3,2},{4,5},{5,4},{6,7},{7,6},{8,9},{9,8},{10,11... | collective-permute-start | bytes 4718600 | tf_op jit(solution)/shard_map/cond/branch_1_fun/ppermute | solution.py:535
  505.8 54.4 %collective-permute-start.41 = (bf16[768,1536]{0,1:T(8,128)(2,1)}, bf16[768,1536]{0,1:T(8,128)(2,1)}, u32[]{:S(2)}, u32[]{:S(2)}) collective-permute-start(bf16[768,1536]{0,1:T(8,128)(2,1)} %get-tuple-element.368), channel_id=1, source_target_pairs={{0,4},{4,0},{1,5},{5,1},{2,6},{6,2},{3,7},{7,3},{8,12},{12,8},{9,1... | collective-permute-start | bytes 7077896 | tf_op jit(solution)/shard_map/ppermute | solution.py:532
  506.5 54.4 %collective-permute-start.42 = (bf16[768,1536]{0,1:T(8,128)(2,1)}, bf16[768,1536]{0,1:T(8,128)(2,1)}, u32[]{:S(2)}, u32[]{:S(2)}) collective-permute-start(bf16[768,1536]{0,1:T(8,128)(2,1)} %get-tuple-element.369), channel_id=1, source_target_pairs={{0,2},{2,0},{1,3},{3,1},{4,6},{6,4},{5,7},{7,5},{8,10},{10,8},{9,1... | collective-permute-start | bytes 7077896 | tf_op jit(solution)/shard_map/ppermute | solution.py:529
  512.3 4.3 collective-permute-start.5
  527.4 17.3 %collective-permute-start.6 = (bf16[512,1536]{1,0:T(8,128)(2,1)}, bf16[512,1536]{1,0:T(8,128)(2,1)}, u32[]{:S(2)}, u32[]{:S(2)}) collective-permute-start(bf16[512,1536]{1,0:T(8,128)(2,1)} %get-tuple-element.704), channel_id=1, source_target_pairs={{0,1},{1,0},{2,3},{3,2},{4,5},{5,4},{6,7},{7,6},{8,9},{9,8},{10,11... | collective-permute-start | bytes 4718600 | tf_op jit(solution)/shard_map/cond/branch_1_fun/ppermute | solution.py:535
  554.9 35.1 %collective-permute-start.43 = (bf16[384,1536]{1,0:T(8,128)(2,1)}, bf16[384,1536]{1,0:T(8,128)(2,1)}, u32[]{:S(2)}, u32[]{:S(2)}) collective-permute-start(bf16[384,1536]{1,0:T(8,128)(2,1)} %get-tuple-element.373), channel_id=1, source_target_pairs={{0,2},{2,0},{1,3},{3,1},{4,6},{6,4},{5,7},{7,5},{8,10},{10,8},{9,1... | collective-permute-start | bytes 3538952 | tf_op jit(solution)/shard_map/ppermute | solution.py:529
  555.6 34.3 %collective-permute-start.44 = (bf16[384,1536]{1,0:T(8,128)(2,1)}, bf16[384,1536]{1,0:T(8,128)(2,1)}, u32[]{:S(2)}, u32[]{:S(2)}) collective-permute-start(bf16[384,1536]{1,0:T(8,128)(2,1)} %get-tuple-element.375), channel_id=1, source_target_pairs={{0,4},{4,0},{1,5},{5,1},{2,6},{6,2},{3,7},{7,3},{8,12},{12,8},{9,1... | collective-permute-start | bytes 3538952 | tf_op jit(solution)/shard_map/ppermute | solution.py:532
  594.5 128.4 %reduce-scatter.9.cloned.1.call-start = ((), (), s32[]{:S(2)}) async-start(), calls=%async_computation.10 | async-start | bytes 2949120 | tf_op jit(solution)/shard_map/reduce_scatter | solution.py:657
  597.3 54.2 %collective-permute-start.47 = (bf16[384,1536]{1,0:T(8,128)(2,1)}, bf16[384,1536]{1,0:T(8,128)(2,1)}, u32[]{:S(2)}, u32[]{:S(2)}) collective-permute-start(bf16[384,1536]{1,0:T(8,128)(2,1)} %copy.119), channel_id=1, source_target_pairs={{0,2},{2,0},{1,3},{3,1},{4,6},{6,4},{5,7},{7,5},{8,10},{10,8},{9,1... | collective-permute-start | bytes 3538952 | tf_op jit(solution)/shard_map/ppermute | solution.py:529
  601.0 50.5 %collective-permute-start.48 = (bf16[384,1536]{1,0:T(8,128)(2,1)}, bf16[384,1536]{1,0:T(8,128)(2,1)}, u32[]{:S(2)}, u32[]{:S(2)}) collective-permute-start(bf16[384,1536]{1,0:T(8,128)(2,1)} %copy.120), channel_id=1, source_target_pairs={{0,4},{4,0},{1,5},{5,1},{2,6},{6,2},{3,7},{7,3},{8,12},{12,8},{9,1... | collective-permute-start | bytes 3538952 | tf_op jit(solution)/shard_map/ppermute | solution.py:532
  604.5 47.0 %collective-permute-start.45 = (bf16[768,384]{0,1:T(8,128)(2,1)}, bf16[768,384]{0,1:T(8,128)(2,1)}, u32[]{:S(2)}, u32[]{:S(2)}) collective-permute-start(bf16[768,384]{0,1:T(8,128)(2,1)} %copy.118), channel_id=1, source_target_pairs={{0,4},{4,0},{1,5},{5,1},{2,6},{6,2},{3,7},{7,3},{8,12},{12,8},{9,1... | collective-permute-start | bytes 1769480 | tf_op jit(solution)/shard_map/ppermute | solution.py:532
  605.2 46.3 %collective-permute-start.46 = (bf16[768,384]{1,0:T(8,128)(2,1)}, bf16[768,384]{1,0:T(8,128)(2,1)}, u32[]{:S(2)}, u32[]{:S(2)}) collective-permute-start(bf16[768,384]{1,0:T(8,128)(2,1)} %get-tuple-element.379), channel_id=1, source_target_pairs={{0,2},{2,0},{1,3},{3,1},{4,6},{6,4},{5,7},{7,5},{8,10},{10,8},{9,1... | collective-permute-start | bytes 1769480 | tf_op jit(solution)/shard_map/ppermute | solution.py:529
  661.5 167.7 %reduce-scatter.11.cloned.1.call-start = ((), (), s32[]{:S(2)}) async-start(), calls=%async_computation.11 | async-start | bytes 2949120 | tf_op jit(solution)/shard_map/reduce_scatter | solution.py:657
  665.5 57.4 %collective-permute-start.49 = (bf16[768,1152]{1,0:T(8,128)(2,1)}, bf16[768,1152]{1,0:T(8,128)(2,1)}, u32[]{:S(2)}, u32[]{:S(2)}) collective-permute-start(bf16[768,1152]{1,0:T(8,128)(2,1)} %copy.121), channel_id=1, source_target_pairs={{0,4},{4,0},{1,5},{5,1},{2,6},{6,2},{3,7},{7,3},{8,12},{12,8},{9,1... | collective-permute-start | bytes 5308424 | tf_op jit(solution)/shard_map/ppermute | solution.py:532
  666.9 56.0 %collective-permute-start.50 = (bf16[768,1152]{1,0:T(8,128)(2,1)}, bf16[768,1152]{1,0:T(8,128)(2,1)}, u32[]{:S(2)}, u32[]{:S(2)}) collective-permute-start(bf16[768,1152]{1,0:T(8,128)(2,1)} %get-tuple-element.400), channel_id=1, source_target_pairs={{0,2},{2,0},{1,3},{3,1},{4,6},{6,4},{5,7},{7,5},{8,10},{10,8},{9,1... | collective-permute-start | bytes 5308424 | tf_op jit(solution)/shard_map/ppermute | solution.py:529
  690.5 14.9 %collective-permute-start.10 = (bf16[512,1536]{1,0:T(8,128)(2,1)}, bf16[512,1536]{1,0:T(8,128)(2,1)}, u32[]{:S(2)}, u32[]{:S(2)}) collective-permute-start(bf16[512,1536]{1,0:T(8,128)(2,1)} %fusion.148), channel_id=1, source_target_pairs={{0,1},{1,0},{2,3},{3,2},{4,5},{5,4},{6,7},{7,6},{8,9},{9,8},{10,11... | collective-permute-start | bytes 4718600 | tf_op jit(solution)/shard_map/cond/branch_1_fun/ppermute | solution.py:535
  735.9 31.8 %collective-permute-start.51 = (bf16[384,1536]{1,0:T(8,128)(2,1)}, bf16[384,1536]{1,0:T(8,128)(2,1)}, u32[]{:S(2)}, u32[]{:S(2)}) collective-permute-start(bf16[384,1536]{1,0:T(8,128)(2,1)} %pad_maximum_fusion.17), channel_id=1, source_target_pairs={{0,2},{2,0},{1,3},{3,1},{4,6},{6,4},{5,7},{7,5},{8,10},{10,8},{9,1... | collective-permute-start | bytes 3538952 | tf_op jit(solution)/shard_map/ppermute | solution.py:529
  737.8 29.9 %collective-permute-start.52 = (bf16[384,1536]{1,0:T(8,128)(2,1)}, bf16[384,1536]{1,0:T(8,128)(2,1)}, u32[]{:S(2)}, u32[]{:S(2)}) collective-permute-start(bf16[384,1536]{1,0:T(8,128)(2,1)} %pad_maximum_fusion.19), channel_id=1, source_target_pairs={{0,4},{4,0},{1,5},{5,1},{2,6},{6,2},{3,7},{7,3},{8,12},{12,8},{9,1... | collective-permute-start | bytes 3538952 | tf_op jit(solution)/shard_map/ppermute | solution.py:532
  741.8 39.4 %collective-permute-start.58 = (bf16[96,1536]{1,0:T(8,128)(2,1)}, bf16[96,1536]{1,0:T(8,128)(2,1)}, u32[]{:S(2)}, u32[]{:S(2)}) collective-permute-start(bf16[96,1536]{1,0:T(8,128)(2,1)} %get-tuple-element.793), channel_id=1, source_target_pairs={{0,2},{2,0},{1,3},{3,1},{4,6},{6,4},{5,7},{7,5},{8,10},{10,8},{9,1... | collective-permute-start | bytes 884744 | tf_op jit(solution)/shard_map/ppermute | solution.py:529
  742.8 38.4 %collective-permute-start.59 = (bf16[96,1536]{1,0:T(8,128)(2,1)}, bf16[96,1536]{1,0:T(8,128)(2,1)}, u32[]{:S(2)}, u32[]{:S(2)}) collective-permute-start(bf16[96,1536]{1,0:T(8,128)(2,1)} %get-tuple-element.794), channel_id=1, source_target_pairs={{0,4},{4,0},{1,5},{5,1},{2,6},{6,2},{3,7},{7,3},{8,12},{12,8},{9,1... | collective-permute-start | bytes 884744 | tf_op jit(solution)/shard_map/ppermute | solution.py:532
  775.9 8.9 %collective-permute-start.53 = (bf16[1536,128]{0,1:T(8,128)(2,1)S(1)}, bf16[1536,128]{0,1:T(8,128)(2,1)}, u32[]{:S(2)}, u32[]{:S(2)}) collective-permute-start(bf16[1536,128]{0,1:T(8,128)(2,1)S(1)} %pad_convert_fusion), channel_id=1, source_target_pairs={{0,1},{1,0},{2,3},{3,2},{4,5},{5,4},{6,7},{7,6},{8,9},{9,8},{10,11... | collective-permute-start | bytes 1179656 | tf_op jit(solution)/shard_map/ppermute | solution.py:535
  787.0 7.2 collective-permute-start.54
  794.3 4.7 collective-permute-start.55
  799.1 10.0 %collective-permute-start.56 = (bf16[192,128]{0,1:T(8,128)(2,1)S(1)}, bf16[192,128]{0,1:T(8,128)(2,1)S(1)}, u32[]{:S(2)}, u32[]{:S(2)}) collective-permute-start(bf16[192,128]{0,1:T(8,128)(2,1)S(1)} %dynamic-slice_convert_fusion), channel_id=1, source_target_pairs={{0,16},{8,24},{16,0},{24,8},{1,17},{9,25},{17,1},{25,9},{2,18},{10... | collective-permute-start | bytes 147464 | tf_op jit(solution)/shard_map/ppermute | solution.py:687
  809.3 7.7 collective-permute-start.57
  (76 other events, 1097.7 us)
Sparse Core Ops, SparseCore 0:
  10.2 45.0 all-gather.6
  57.4 58.9 all-gather.4
  118.6 88.0 all-gather.8
  208.7 87.7 all-gather.10
  446.0 83.9 reduce-scatter.4
  594.6 47.0 reduce-scatter.6
  661.6 47.0 reduce-scatter.8
  781.3 47.9 reduce-scatter.10

commit v8 on v7

--- a/solution.py
+++ b/solution.py
@@ -965,26 +965,34 @@
     far_self = comm.exchange(send_self)
     half_cross = comm.scatter_z(comm.closing(cross_late, cross_second))
 
-    def stage6(dmem, w_cross, values2, hidden, w_out):
+    def stage6(dmem, w_cross, values2, hidden, w_out, r1_all, att, far):
         w_cm = split_cross(w_cross)[2]
+        so_sums = comm.adds((r1_all, att, far))
         text_grad = comm.sum_all(mm_t(dmem, w_cm))
         layer_out = (values2 + comm.sum_own(hidden, w_out, mm_t, clips)).astype(BF)
-        return comm.restore(text_grad), comm.restore(layer_out)
-
-    text_grad, layer_out = comm.stage(stage6, dmem, w_cross, values2, hidden, w_out)
-    text_grad, layer_out, dqkv, half_out, half_in = comm.after(
-        (text_grad, layer_out, dqkv, half_out, half_in), far_self, half_cross
-    )
-    self_sums = comm.adds((r1_all, att, far_so), (n1, dqkv, far_self))
+        return comm.restore(text_grad), comm.restore(layer_out), so_sums
+
+    text_grad, layer_out, so_sums = comm.stage(
+        stage6, dmem, w_cross, values2, hidden, w_out, r1_all, att, far_so
+    )
+    text_grad, layer_out, dqkv, half_out, half_in, so_sums = comm.after(
+        (text_grad, layer_out, dqkv, half_out, half_in, so_sums), far_self, half_cross
+    )
+    so_second = comm.second(so_sums)
+    dqkv = comm.after(dqkv, so_second)
+    self_sums = comm.adds((n1, dqkv, far_self))
     dqkv = comm.after(dqkv, self_sums)
     self_second = comm.second(self_sums)
+    half_so = comm.scatter_z(comm.closing(so_sums, so_second))
 
     def stage7(dqkv, w_self):
         return comm.sum_own(dqkv, w_self, mm_t, clips)
 
     e1 = comm.stage(stage7, dqkv, w_self)
-    e1, self_late = comm.after((e1, self_sums), self_second)
-    half_self = comm.scatter_z(comm.closing(self_late, self_second))
+    e1, self_late = comm.after((e1, self_sums), self_second, half_so)
+    closed = comm.closing(self_late, self_second)
+    e1 = comm.after(e1, closed)
+    half_self = comm.scatter_z(closed)
     dv0, gain0, shift0 = norm_back(values0, stats0, gain[0], e1)
     input_grad = comm.restore(r1 + dv0)
     norm_grad = comm.norm_sums(jnp.stack([gain0, gain1, gain2, shift0, shift1, shift2]))
@@ -994,7 +1002,8 @@
     grad_out = comm.close_middle(half_out)
     (grad_in,) = comm.close_last(half_in, pre_grad.shape[1])
     grad_cq, grad_co, grad_cm = comm.close_last(half_cross, cols, cols, 2 * cols)
-    grad_so, grad_self = comm.close_last(half_self, cols, 3 * cols)
+    (grad_so,) = comm.close_last(half_so, cols)
+    (grad_self,) = comm.close_last(half_self, 3 * cols)
     return (
         layer_out,
         input_grad,

time: 850 us -> 830 us (0.976)
  waiting for transfers between devices: 158 us -> 148 us
  local copies, waits for them, and re-layouts: 124 us -> 115 us
    reduce_scatter x4 -> x5, waiting for transfers between devices: 11.6 us -> 0.05 us  [scatter_z(): return lax.psum_scatter(parts, 'z', scatter_dimension=1, tiled=True)]
    ppermute x2, waiting for transfers between devices: 4.16 us -> 12.8 us  [norm_sums(): sums = near + lax.ppermute(away.astype(BF), 'z', pairs).astype(F32)]
    ppermute x21 -> x22, waiting for transfers between devices: 45.8 us -> 39.9 us  [y(): return lax.ppermute(v, 'y', SWAP)]
    ppermute x21 -> x22, waiting for transfers between devices: 58.2 us -> 55.7 us  [x(): return lax.ppermute(v, 'x', SWAP)]
    ppermute x21 -> x22, starting transfers between devices: 23.8 us -> 25.4 us  [y(): return lax.ppermute(v, 'y', SWAP)]
    ppermute x21 -> x22, starting transfers between devices: 22 us -> 23.1 us  [x(): return lax.ppermute(v, 'x', SWAP)]
  transfers between devices with their start and end apart: 68 -> 71, of which waited for: 22 -> 21; matrix products, arithmetic and copies ran while one was open for 48% -> 49% of each run, Pallas kernels for 17% -> 18%
where the time goes in v8:
time: 830 us; the launch traced here: 820 us
  matrix products  257 us (31%)
  waiting for transfers between devices  148 us (18%)
  Pallas kernels  147 us (18%)
  local copies, waits for them, and re-layouts  115 us (14%)
  other arithmetic  80.2 us (10%)
  starting transfers between devices  58.2 us (7%)
  between operations  15.1 us (2%)
    dot_general x17, matrix products, mm_t(): lax.dot_general(left, right, (((1,), (1,)), ((), ())), preferred_element_...  110 us
    dot_general x28, matrix products, mm_rows(): lax.dot_general(left, right, (((0,), (0,)), ((), ())), preferred_element_...  102 us
    ppermute x22, waiting for transfers between devices, x(): return lax.ppermute(v, 'x', SWAP)  55.7 us
    dot_general x8, matrix products, mm(): return jnp.dot(left, right, preferred_element_type=F32)  44.2 us
    ppermute x22, waiting for transfers between devices, y(): return lax.ppermute(v, 'y', SWAP)  39.9 us
    pallas_call x1, Pallas kernels, self_back(): pl.pallas_call(self_back_kernel, grid_spec=pltpu.PrefetchScalarGridSpec(n...  30 us
    ppermute x22, starting transfers between devices, y(): return lax.ppermute(v, 'y', SWAP)  25.4 us
    ppermute x22, starting transfers between devices, x(): return lax.ppermute(v, 'x', SWAP)  23.1 us
  transfers between devices with their start and end apart: 71, of which 21 were waited for; matrix products, arithmetic and copies ran while one was open for 49% of the time, Pallas kernels for 18%

profile of v8, /device:TPU:0, one launch (start us, length us, event | category | flops | bytes accessed | tf_op | source)
XLA Modules:
  0.0 820.3 jit_solution(17069025153582174471)
XLA Ops:
  29.3 5.8 collective-permute-done.12
  48.6 6.7 all-gather.7.cloned.1.call-done
  62.3 18.6 %collective-permute-done.19 = bf16[384,1152]{1,0:T(8,128)(2,1)} collective-permute-done((bf16[384,1152]{1,0:T(8,128)(2,1)}, bf16[384,1152]{1,0:T(8,128)(2,1)}, u32[]{:S(2)}, u32[]{:S(2)}) %collective-permute-start.19) | collective-permute-done | bytes 884768 | tf_op jit(solution)/shard_map/ppermute | solution.py:529
  83.8 17.5 %collective-permute-done.23 = bf16[384,1152]{1,0:T(8,128)(2,1)} collective-permute-done((bf16[384,1152]{1,0:T(8,128)(2,1)}, bf16[384,1152]{1,0:T(8,128)(2,1)}, u32[]{:S(2)}, u32[]{:S(2)}) %collective-permute-start.23) | collective-permute-done | bytes 884768 | tf_op jit(solution)/shard_map/ppermute | solution.py:532
  101.3 15.1 %all-gather.5.cloned.1.call-done.refs_0_ = bf16[384,3840]{1,0:T(8,128)(2,1)} async-done(((bf16[96,3840]{1,0:T(8,128)(2,1)}), bf16[384,3840]{1,0:T(8,128)(2,1)}) %all-gather.5.cloned.1.call-update) | async-done | bytes 2949136 | tf_op jit(solution)/shard_map/all_gather | solution.py:557
  126.4 31.4 %collective-permute-done.25.refs_1_ = bf16[384,1920]{1,0:T(8,128)(2,1)} collective-permute-done((bf16[384,1920]{1,0:T(8,128)(2,1)}, bf16[384,1920]{1,0:T(8,128)(2,1)}, u32[]{:S(2)}, u32[]{:S(2)}) %collective-permute-start.25) | collective-permute-done | bytes 1474592 | tf_op jit(solution)/shard_map/ppermute | solution.py:529
  169.6 37.1 %conditional.10 = (bf16[1536,2304]{1,0:T(8,128)(2,1)}, bf16[1024,768]{1,0:T(8,128)(2,1)}, s32[1]{0:T(128)}, bf16[2,2,256,2304]{3,2,1,0:T(8,128)(2,1)}, f32[2,2,256,768]{3,2,1,0:T(8,128)}) conditional(s32[]{:T(128)} %convert_element_type.417, () %tuple.119, (bf16[384,2304]{1,0:T(8,128)(2,1)}, bf16[384,1152]{1,0:T(8,128)(2,1)}, ...), branch_computations={%region_2.3_spmd, %region_3.4_spmd} | conditional | flops 8458076160 | bytes 24379432 | solution.py:612
  169.6 6.0 place.2
  175.6 12.8 %convolution_convert_fusion = bf16[2304,1024]{0,1:T(8,128)(2,1)} fusion(bf16[1536,2304]{1,0:T(8,128)(2,1)} %place.2, bf16[1024,1536]{0,1:T(8,128)(2,1)} %get-tuple-element.666), kind=kOutput, calls=%fused_computation | convolution fusion | flops 7250116608 | bytes 14942208 | tf_op jit(solution)/shard_map/cond/branch_1_fun/dot_general | solution.py:19
  188.4 18.3 %self_attend.1 = (bf16[2,2,256,768]{3,2,1,0:T(8,128)(2,1)}, f32[2,2,256,768]{3,2,1,0:T(8,128)}) custom-call(s32[1]{0:T(128)} %bitcast.core_ref, bf16[2,2,256,2304]{3,2,1,0:T(8,128)(2,1)} %bitcast.2.q_ref.k_ref.v_ref, bf16[2,2,256,2304]{3,2,1,0:T(8,128)(2,1)} %bitcast.2.q_ref.k_ref.v_ref, bf16[2,2,256,2304]{3,2,1,0:T(8,128)(2,1)} %bitcast.2.q_ref.k_ref.v_ref), custom_call_target="tpu_custom_call" | custom-call | flops 1207959552 | bytes 9437184 | tf_op jit(solution)/shard_map/cond/branch_1_fun/self_attend/pallas_call | solution.py:707
  206.7 4.9 fusion.363
  211.6 7.5 collective-permute-done.27.refs_3_
  228.8 8.8 %place.3 = bf16[1536,3840]{1,0:T(8,128)(2,1)} custom-call(bf16[384,3840]{1,0:T(8,128)(2,1)} %all-gather.5.cloned.1.call-done.refs_0_, bf16[384,1920]{1,0:T(8,128)(2,1)} %collective-permute-done.25.refs_1_, bf16[384,1920]{1,0:T(8,128)(2,1)} %collective-permute-done.26.refs_2_, bf16[384,1920]{1,0:T(8,128)(2,1)} %collective-permute-done.27.refs_3_, ...), custom_call_target="tpu_custom_call" | custom-call | tf_op jit(solution)/shard_map/place/pallas_call | solution.py:139
  237.7 65.5 %conditional.11 = (f32[512,1536]{1,0:T(8,128)}, f32[512,1]{0,1:T(1,128)S(1)}, f32[512,1]{0,1:T(1,128)S(1)}, bf16[1024,1536]{1,0:T(8,128)(2,1)}, bf16[1024,768]{1...) conditional(s32[]{:T(128)} %convert_element_type.417, ...), branch_computations={%region_4.5_spmd, %region_5.10_spmd} | conditional | flops 8087077888 | bytes 141820608 | solution.py:612
  237.7 4.5 convolution_convert_fusion.9
  247.4 6.0 fusion.356
  264.0 6.4 fusion.223
  270.4 13.4 %cross_attend.1 = bf16[2,2,256,768]{3,2,1,0:T(8,128)(2,1)} custom-call(bf16[2,2,256,768]{3,2,1,0:T(8,128)(2,1)} %bitcast.6.q_ref, bf16[2,64,1536]{2,1,0:T(8,128)(2,1)S(1)} %bitcast.210, bf16[2,64,1536]{2,1,0:T(8,128)(2,1)S(1)} %bitcast.211), custom_call_target="tpu_custom_call" | custom-call | flops 201326592 | bytes 3145728 | tf_op jit(solution)/shard_map/cond/branch_1_fun/cross_attend/pallas_call | solution.py:770
  291.9 4.1 fusion.357
  303.2 4.8 fusion.362
  309.4 7.3 place_stacked.3.weight_ref
  316.7 20.0 %feed.1 = (bf16[1024,3072]{1,0:T(8,128)(2,1)}, bf16[1024,3072]{1,0:T(8,128)(2,1)}) custom-call(bf16[1024,1536]{1,0:T(8,128)(2,1)} %get-tuple-element.362.rows_ref, bf16[1536,3072]{1,0:T(8,128)(2,1)} %place_stacked.3.weight_ref), custom_call_target="tpu_custom_call" | custom-call | flops 9663676416 | bytes 25165824 | tf_op jit(solution)/shard_map/feed/pallas_call | solution.py:311
  336.8 6.6 convolution_convert_fusion.12
  353.9 8.6 %collective-permute-done.35 = bf16[2,384,1536]{2,1,0:T(8,128)(2,1)} collective-permute-done((bf16[2,384,1536]{2,1,0:T(8,128)(2,1)}, bf16[2,384,1536]{2,1,0:T(8,128)(2,1)}, u32[]{:S(2)}, u32[]{:S(2)}) %collective-permute-start.35) | collective-permute-done | bytes 2359328 | tf_op jit(solution)/shard_map/ppermute | solution.py:532
  363.1 57.2 %conditional.12 = (bf16[1536,3072]{1,0:T(8,128)(2,1)}, bf16[1024,3072]{1,0:T(8,128)(2,1)}, bf16[768,1536]{0,1:T(8,128)(2,1)}, bf16[768,1536]{1,0:T(8,128)(2,1)}, f32[512,1536]{1,0:T(8,128)}) conditional(s32[]{:T(128)} %convert_element_type.417, () %tuple.127, (bf16[4,384,1536]{2,1,0:T(8,128)(2,1)}, bf16[2,384,1536]{2,1,0:T(8,128)(2,1)}, ...), branch_computations={%region_10.11_spmd, %region_11.12_spmd} | conditional | flops 24167055360 | bytes 108527768 | solution.py:612
  363.1 7.3 place_stacked.2.weight_ref
  370.4 18.0 %slope_product.1 = bf16[1024,3072]{1,0:T(8,128)(2,1)} custom-call(bf16[1024,1536]{1,0:T(8,128)(2,1)} %get-tuple-element.180.rows_ref, bf16[1536,3072]{1,0:T(8,128)(2,1)} %place_stacked.2.weight_ref, bf16[1024,3072]{1,0:T(8,128)(2,1)} %get-tuple-element.181.slope_ref), custom_call_target="tpu_custom_call" | custom-call | flops 9663676416 | bytes 25165824 | tf_op jit(solution)/shard_map/cond/branch_1_fun/slope_product/pallas_call | solution.py:346
  388.4 9.5 %fusion.9 = bf16[512,1536]{1,0:T(8,128)(2,1)S(1)} fusion(bf16[1536,3072]{1,0:T(8,128)(2,1)} %get-tuple-element.183, bf16[1024,3072]{1,0:T(8,128)(2,1)} %slope_product.1), kind=kOutput, calls=%fused_computation.11 | convolution fusion | flops 4832624640 | bytes 14155776 | tf_op jit(solution)/shard_map/cond/branch_1_fun/dot_general | solution.py:23
  399.5 6.0 convolution_convert_fusion.1
  405.5 6.5 fusion.6
  412.0 8.2 convert_add_fusion
  420.2 25.8 %conditional.13 = (bf16[4,384,1536]{2,1,0:T(8,128)(2,1)}, f32[512,1536]{1,0:T(8,128)}, bf16[512,1536]{1,0:T(8,128)(2,1)}, f32[1,1536]{1,0:T(1,128)}, f32[1,1536]{1,0:T(1,128)}) conditional(s32[]{:T(128)} %convert_element_type.417, () %tuple.117, (bf16[1024,1536]{1,0:T(8,128)(2,1)}, bf16[1024,3072]{1,0:T(8,128)(2,1)}, bf16[768,1536]{1,0:T(8,128)(2,1)}, ...), branch_computations={%region_12.13_spmd, %region_13.18_spmd} | conditional | flops 4864078848 | bytes 91349112 | solution.py:612
  422.0 5.3 add_convert_fusion.5
  427.4 4.3 add_convert_fusion.6
  440.3 4.5 fusion.334
  446.1 4.7 copy.102
  453.0 52.9 %conditional.14 = (bf16[1024,1536]{1,0:T(8,128)(2,1)}, bf16[1024,768]{1,0:T(8,128)(2,1)}, bf16[128,1536]{1,0:T(8,128)(2,1)}, bf16[768,1536]{0,1:T(8,128)(2,1)}, bf16[768,1536]{0,1:T(8,128)(2,1)}) conditional(s32[]{:T(128)} %convert_element_type.417, () %tuple.116, (bf16[512,1536]{1,0:T(8,128)(2,1)}, bf16[1024,768]{1,0:T(8,128)(2,1)}, ...), branch_computations={%region_18.19_spmd, %region_19.20_spmd} | conditional | flops 5661130752 | bytes 69599480 | solution.py:612
  467.2 6.4 fusion.19
  473.6 17.6 %cross_back.1 = (bf16[2,2,256,768]{3,2,1,0:T(8,128)(2,1)}, bf16[2,64,1536]{2,1,0:T(8,128)(2,1)}) custom-call(bf16[2,2,256,768]{3,2,1,0:T(8,128)(2,1)} %bitcast.23.q_ref, bf16[2,64,1536]{2,1,0:T(8,128)(2,1)S(1)} %get-tuple-element.196.k_ref.v_ref, bf16[2,64,1536]{2,1,0:T(8,128)(2,1)S(1)} %get-tuple-element.196.k_ref.v_ref, bf16[2,2,256,768]{3,2,1,0:T(8,128)(2,1)} %bitcast.216), custom_call_target="tpu_custom_call" | custom-call | flops 503316480 | bytes 4718592 | tf_op jit(solution)/shard_map/cond/branch_1_fun/cross_back/pallas_call | solution.py:787
  507.9 47.1 %conditional.15 = (bf16[384,1536]{1,0:T(8,128)(2,1)}, bf16[384,1536]{1,0:T(8,128)(2,1)}, bf16[384,1536]{1,0:T(8,128)(2,1)}, bf16[384,1536]{1,0:T(8,128)(2,1)}, b...) conditional(s32[]{:T(128)} %convert_element_type.417, ...), branch_computations={%region_20.21_spmd, %region_21.26_spmd} | conditional | flops 9697489920 | bytes 93708440 | solution.py:612
  507.9 4.5 convolution_convert_fusion.10
  516.7 5.5 multiply_reduce_fusion.5
  522.2 5.2 fusion.335
  527.9 5.2 add_convert_fusion.7
  533.1 5.7 add_convert_fusion.8
  548.6 6.4 fusion.244
  561.0 29.1 %conditional.16 = (bf16[384,1536]{0,1:T(8,128)(2,1)}, bf16[384,1536]{0,1:T(8,128)(2,1)}, bf16[384,1536]{0,1:T(8,128)(2,1)}, bf16[384,1536]{0,1:T(8,128)(2,1)}, b...) conditional(s32[]{:T(128)} %convert_element_type.417, () %tuple.137, (bf16[1024,1536]{1,0:T(8,128)(2,1)}, ...), branch_computations={%region_27.28_spmd, %region_28.29_spmd} | conditional | flops 3957522432 | bytes 56623180 | solution.py:612
  603.8 45.5 %conditional.17 = (bf16[1024,2304]{1,0:T(8,128)(2,1)}, bf16[768,1152]{0,1:T(8,128)(2,1)}, bf16[768,1152]{1,0:T(8,128)(2,1)}) conditional(s32[]{:T(128)} %convert_element_type.417, () %tuple.132, (bf16[1024,768]{1,0:T(8,128)(2,1)}, s32[1]{0:T(128)}, bf16[2,2,256,2304]{3,2,1,0:T(8,128)(2,1)}, f32[2,2,256,768]{3,2,1,0:T(8,128)}, ...), branch_computations={%region_29.30_spmd, %region_30.31_spmd} | conditional | flops 6648692736 | bytes 47579188 | solution.py:612
  603.8 30.0 %self_back.1 = bf16[2,2,256,2304]{3,2,1,0:T(8,128)(2,1)} custom-call(s32[1]{0:T(128)} %get-tuple-element.224.core_ref, bf16[2,2,256,2304]{3,2,1,0:T(8,128)(2,1)} %get-tuple-element.225.q_ref.k_ref.v_ref, bf16[2,2,256,2304]{3,2,1,0:T(8,128)(2,1)} %get-tuple-element.225.q_ref.k_ref.v_ref, bf16[2,2,256,2304]{3,2,1,0:T(8,128)(2,1)} %get-tuple-element.225.q_ref.k_ref.v_ref, ...), custom_call_target="tpu_custom_call" | custom-call | flops 3019898880 | bytes 14155776 | tf_op jit(solution)/shard_map/cond/branch_1_fun/self_back/pallas_call | solution.py:737
  633.8 4.6 copy.105
  638.5 5.6 fusion.127
  644.2 5.2 convolution_convert_fusion.5
  668.7 46.8 %conditional.18 = (f32[128,1536]{1,0:T(8,128)}, bf16[512,1536]{1,0:T(8,128)(2,1)}, bf16[384,384]{1,0:T(8,128)(2,1)S(1)}, bf16[384,384]{1,0:T(8,128)(2,1)}, bf16[...) conditional(s32[]{:T(128)} %convert_element_type.417, () %tuple.112, (bf16[1536,3840]{1,0:T(8,128)(2,1)}, ...), branch_computations={%region_32.33_spmd, %region_33.34_spmd} | conditional | flops 15118446592 | bytes 92823808 | solution.py:612
  668.7 5.3 fusion.354
  673.9 9.1 %fusion.148 = bf16[512,1536]{1,0:T(8,128)(2,1)} fusion(bf16[1536,3072]{1,0:T(8,128)(2,1)} %get-tuple-element.233, bf16[1024,3072]{1,0:T(8,128)(2,1)S(1)} %copy-done.60), kind=kOutput, calls=%fused_computation.132 | convolution fusion | flops 4832624640 | bytes 14155776 | tf_op jit(solution)/shard_map/cond/branch_1_fun/dot_general | solution.py:23
  701.4 14.0 %fusion.147 = bf16[512,1536]{1,0:T(8,128)(2,1)} fusion(s32[1536]{0:T(1024)S(1)} %fusion.183, f32[512,1536]{1,0:T(8,128)S(1)} %get-tuple-element.231, bf16[512,1536]{1,0:T(8,128)(2,1)} %collective-permute-done.10, bf16[1536,3072]{1,0:T(8,128)(2,1)} %get-tuple-element.233, bf16[1024,3072]{1,0:T(8,128)(2,1)} %get-tuple-element.232), kind=kOutput, calls=%fused_computation.131 | convolution fusion | flops 7254048768 | bytes 18880512 | tf_op jit(solution)/shard_map/cond/branch_1_fun/dot_general | solution.py:23
  726.4 4.9 fusion.267
  734.9 4.4 fusion.268
  743.3 17.9 %conditional.19 = (f32[512,1536]{1,0:T(8,128)S(1)}) conditional(s32[]{:T(128)} %convert_element_type.417, () %tuple.144, (bf16[1024,2304]{1,0:T(8,128)(2,1)}, bf16[1536,2304]{1,0:T(8,128)(2,1)}) %tuple.147), branch_computations={%region_35.36_spmd, %region_36.37_spmd} | conditional | flops 7250116608 | bytes 31457328 | solution.py:612
  743.3 7.6 convolution_convert_fusion.7
  754.4 6.9 convert_add_fusion.2
  778.8 7.2 fusion.254
  786.9 7.7 fusion.269
  796.0 9.7 %collective-permute-done.58 = bf16[192,128]{0,1:T(8,128)(2,1)S(1)} collective-permute-done((bf16[192,128]{0,1:T(8,128)(2,1)S(1)}, bf16[192,128]{0,1:T(8,128)(2,1)S(1)}, u32[]{:S(2)}, u32[]{:S(2)}) %collective-permute-start.58) | collective-permute-done | bytes 49184 | tf_op jit(solution)/shard_map/ppermute | solution.py:687
  (448 shorter events, 316.3 us)
Async XLA Ops:
  7.2 48.1 %all-gather.7.cloned.1.call-start = ((), (), s32[]{:S(2)}) async-start(), calls=%async_computation.6 | async-start | bytes 2211840 | tf_op jit(solution)/shard_map/all_gather | solution.py:557
  9.3 107.1 %all-gather.5.cloned.1.call-start = ((), (), s32[]{:S(2)}) async-start(), calls=%async_computation.5 | async-start | bytes 3686400 | tf_op jit(solution)/shard_map/all_gather | solution.py:557
  10.2 15.9 %collective-permute-start.11 = (bf16[96,128]{1,0:T(8,128)(2,1)S(1)}, bf16[96,128]{1,0:T(8,128)(2,1)S(1)}, u32[]{:S(2)}, u32[]{:S(2)}) collective-permute-start(bf16[96,128]{1,0:T(8,128)(2,1)S(1)} %get-tuple-element.870), channel_id=1, source_target_pairs={{0,8},{8,0},{16,24},{24,16},{1,9},{9,1},{17,25},{25,17},{2,10},{10... | collective-permute-start | bytes 73736 | tf_op jit(solution)/shard_map/ppermute | solution.py:538
  16.2 190.5 %all-gather.9.cloned.1.call-start = ((), (), s32[]{:S(2)}) async-start(), calls=%async_computation.7 | async-start | bytes 5898240 | tf_op jit(solution)/shard_map/all_gather | solution.py:558
  17.3 24.2 %collective-permute-start.16 = (bf16[96,1536]{1,0:T(8,128)(2,1)}, bf16[96,1536]{1,0:T(8,128)(2,1)}, u32[]{:S(2)}, u32[]{:S(2)}) collective-permute-start(bf16[96,1536]{1,0:T(8,128)(2,1)} %get-tuple-element.852), channel_id=1, source_target_pairs={{0,4},{4,0},{1,5},{5,1},{2,6},{6,2},{3,7},{7,3},{8,12},{12,8},{9,1... | collective-permute-start | bytes 884744 | tf_op jit(solution)/shard_map/ppermute | solution.py:532
  18.8 22.7 %collective-permute-start.15 = (bf16[96,1536]{1,0:T(8,128)(2,1)}, bf16[96,1536]{1,0:T(8,128)(2,1)}, u32[]{:S(2)}, u32[]{:S(2)}) collective-permute-start(bf16[96,1536]{1,0:T(8,128)(2,1)} %get-tuple-element.853), channel_id=1, source_target_pairs={{0,2},{2,0},{1,3},{3,1},{4,6},{6,4},{5,7},{7,5},{8,10},{10,8},{9,1... | collective-permute-start | bytes 884744 | tf_op jit(solution)/shard_map/ppermute | solution.py:529
  22.3 21.4 %collective-permute-start.18 = (bf16[96,1536]{1,0:T(8,128)(2,1)}, bf16[96,1536]{1,0:T(8,128)(2,1)}, u32[]{:S(2)}, u32[]{:S(2)}) collective-permute-start(bf16[96,1536]{1,0:T(8,128)(2,1)} %get-tuple-element.848), channel_id=1, source_target_pairs={{0,4},{4,0},{1,5},{5,1},{2,6},{6,2},{3,7},{7,3},{8,12},{12,8},{9,1... | collective-permute-start | bytes 884744 | tf_op jit(solution)/shard_map/ppermute | solution.py:532
  22.8 20.9 %collective-permute-start.17 = (bf16[96,1536]{1,0:T(8,128)(2,1)}, bf16[96,1536]{1,0:T(8,128)(2,1)}, u32[]{:S(2)}, u32[]{:S(2)}) collective-permute-start(bf16[96,1536]{1,0:T(8,128)(2,1)} %get-tuple-element.849), channel_id=1, source_target_pairs={{0,2},{2,0},{1,3},{3,1},{4,6},{6,4},{5,7},{7,5},{8,10},{10,8},{9,1... | collective-permute-start | bytes 884744 | tf_op jit(solution)/shard_map/ppermute | solution.py:529
  26.2 8.9 %collective-permute-start.12 = (bf16[2,96,128]{2,1,0:T(8,128)(2,1)S(1)}, bf16[2,96,128]{2,1,0:T(8,128)(2,1)S(1)}, u32[]{:S(2)}, u32[]{:S(2)}) collective-permute-start(bf16[2,96,128]{2,1,0:T(8,128)(2,1)S(1)} %pad_maximum_fusion.24), channel_id=1, source_target_pairs={{0,16},{8,24},{16,0},{24,8},{1,17},{9,25},{17,1},{25,9},{2,18},{10... | collective-permute-start | bytes 147464 | tf_op jit(solution)/shard_map/ppermute | solution.py:539
  35.2 4.7 collective-permute-start.13
  39.9 6.0 collective-permute-start.14
  48.6 254.6 %all-gather.11.cloned.1.call-start = ((), (), s32[]{:S(2)}) async-start(), calls=%async_computation.8 | async-start | bytes 5898240 | tf_op jit(solution)/shard_map/all_gather | solution.py:558
  58.1 22.8 %collective-permute-start.19 = (bf16[384,1152]{1,0:T(8,128)(2,1)}, bf16[384,1152]{1,0:T(8,128)(2,1)}, u32[]{:S(2)}, u32[]{:S(2)}) collective-permute-start(bf16[384,1152]{1,0:T(8,128)(2,1)} %get-tuple-element.828), channel_id=1, source_target_pairs={{0,2},{2,0},{1,3},{3,1},{4,6},{6,4},{5,7},{7,5},{8,10},{10,8},{9,1... | collective-permute-start | bytes 2654216 | tf_op jit(solution)/shard_map/ppermute | solution.py:529
  59.5 22.8 %collective-permute-start.21 = (bf16[384,1152]{1,0:T(8,128)(2,1)}, bf16[384,1152]{1,0:T(8,128)(2,1)}, u32[]{:S(2)}, u32[]{:S(2)}) collective-permute-start(bf16[384,1152]{1,0:T(8,128)(2,1)} %get-tuple-element.827), channel_id=1, source_target_pairs={{0,4},{4,0},{1,5},{5,1},{2,6},{6,2},{3,7},{7,3},{8,12},{12,8},{9,1... | collective-permute-start | bytes 2654216 | tf_op jit(solution)/shard_map/ppermute | solution.py:532
  61.0 529.0 %reduce-scatter.6.cloned.1.call-start = ((), (), s32[]{:S(2)}) async-start(), calls=%async_computation.9 | async-start | bytes 5898240 | tf_op jit(solution)/shard_map/reduce_scatter | solution.py:657
  61.1 40.3 %collective-permute-start.23 = (bf16[384,1152]{1,0:T(8,128)(2,1)}, bf16[384,1152]{1,0:T(8,128)(2,1)}, u32[]{:S(2)}, u32[]{:S(2)}) collective-permute-start(bf16[384,1152]{1,0:T(8,128)(2,1)} %get-tuple-element.828), channel_id=1, source_target_pairs={{0,4},{4,0},{1,5},{5,1},{2,6},{6,2},{3,7},{7,3},{8,12},{12,8},{9,1... | collective-permute-start | bytes 2654216 | tf_op jit(solution)/shard_map/ppermute | solution.py:532
  61.7 39.6 %collective-permute-start.24 = (bf16[384,1152]{1,0:T(8,128)(2,1)}, bf16[384,1152]{1,0:T(8,128)(2,1)}, u32[]{:S(2)}, u32[]{:S(2)}) collective-permute-start(bf16[384,1152]{1,0:T(8,128)(2,1)} %get-tuple-element.827), channel_id=1, source_target_pairs={{0,2},{2,0},{1,3},{3,1},{4,6},{6,4},{5,7},{7,5},{8,10},{10,8},{9,1... | collective-permute-start | bytes 2654216 | tf_op jit(solution)/shard_map/ppermute | solution.py:529
  80.9 37.8 %collective-permute-start.20 = (bf16[384,1152]{1,0:T(8,128)(2,1)}, bf16[384,1152]{1,0:T(8,128)(2,1)}, u32[]{:S(2)}, u32[]{:S(2)}) collective-permute-start(bf16[384,1152]{1,0:T(8,128)(2,1)} %collective-permute-done.19), channel_id=1, source_target_pairs={{0,4},{4,0},{1,5},{5,1},{2,6},{6,2},{3,7},{7,3},{8,12},{12,8},{9,1... | collective-permute-start | bytes 2654216 | tf_op jit(solution)/shard_map/ppermute | solution.py:532
  82.4 36.3 %collective-permute-start.22 = (bf16[384,1152]{1,0:T(8,128)(2,1)}, bf16[384,1152]{1,0:T(8,128)(2,1)}, u32[]{:S(2)}, u32[]{:S(2)}) collective-permute-start(bf16[384,1152]{1,0:T(8,128)(2,1)} %collective-permute-done.21), channel_id=1, source_target_pairs={{0,2},{2,0},{1,3},{3,1},{4,6},{6,4},{5,7},{7,5},{8,10},{10,8},{9,1... | collective-permute-start | bytes 2654216 | tf_op jit(solution)/shard_map/ppermute | solution.py:529
  122.4 35.5 %collective-permute-start.25 = (bf16[384,1920]{1,0:T(8,128)(2,1)}, bf16[384,1920]{1,0:T(8,128)(2,1)}, u32[]{:S(2)}, u32[]{:S(2)}) collective-permute-start(bf16[384,1920]{1,0:T(8,128)(2,1)} %get-tuple-element.822), channel_id=1, source_target_pairs={{0,2},{2,0},{1,3},{3,1},{4,6},{6,4},{5,7},{7,5},{8,10},{10,8},{9,1... | collective-permute-start | bytes 4423688 | tf_op jit(solution)/shard_map/ppermute | solution.py:529
  122.9 36.4 %collective-permute-start.29 = (bf16[384,1920]{1,0:T(8,128)(2,1)}, bf16[384,1920]{1,0:T(8,128)(2,1)}, u32[]{:S(2)}, u32[]{:S(2)}) collective-permute-start(bf16[384,1920]{1,0:T(8,128)(2,1)} %get-tuple-element.821), channel_id=1, source_target_pairs={{0,4},{4,0},{1,5},{5,1},{2,6},{6,2},{3,7},{7,3},{8,12},{12,8},{9,1... | collective-permute-start | bytes 4423688 | tf_op jit(solution)/shard_map/ppermute | solution.py:532
  124.4 42.4 %collective-permute-start.32 = (bf16[512,1536]{0,1:T(8,128)(2,1)}, bf16[512,1536]{0,1:T(8,128)(2,1)}, u32[]{:S(2)}, u32[]{:S(2)}) collective-permute-start(bf16[512,1536]{0,1:T(8,128)(2,1)} %add_convert_fusion.9), channel_id=1, source_target_pairs={{0,1},{1,0},{2,3},{3,2},{4,5},{5,4},{6,7},{7,6},{8,9},{9,8},{10,11... | collective-permute-start | bytes 4718600 | tf_op jit(solution)/shard_map/ppermute | solution.py:535
  124.4 87.1 %collective-permute-start.26 = (bf16[384,1920]{1,0:T(8,128)(2,1)}, bf16[384,1920]{1,0:T(8,128)(2,1)}, u32[]{:S(2)}, u32[]{:S(2)}) collective-permute-start(bf16[384,1920]{1,0:T(8,128)(2,1)} %get-tuple-element.822), channel_id=1, source_target_pairs={{0,4},{4,0},{1,5},{5,1},{2,6},{6,2},{3,7},{7,3},{8,12},{12,8},{9,1... | collective-permute-start | bytes 4423688 | tf_op jit(solution)/shard_map/ppermute | solution.py:532
  125.0 86.6 %collective-permute-start.28 = (bf16[384,1920]{1,0:T(8,128)(2,1)}, bf16[384,1920]{1,0:T(8,128)(2,1)}, u32[]{:S(2)}, u32[]{:S(2)}) collective-permute-start(bf16[384,1920]{1,0:T(8,128)(2,1)} %get-tuple-element.821), channel_id=1, source_target_pairs={{0,2},{2,0},{1,3},{3,1},{4,6},{6,4},{5,7},{7,5},{8,10},{10,8},{9,1... | collective-permute-start | bytes 4423688 | tf_op jit(solution)/shard_map/ppermute | solution.py:529
  157.8 61.2 %collective-permute-start.27 = (bf16[384,1920]{1,0:T(8,128)(2,1)}, bf16[384,1920]{1,0:T(8,128)(2,1)}, u32[]{:S(2)}, u32[]{:S(2)}) collective-permute-start(bf16[384,1920]{1,0:T(8,128)(2,1)} %collective-permute-done.25.refs_1_), channel_id=1, source_target_pairs={{0,4},{4,0},{1,5},{5,1},{2,6},{6,2},{3,7},{7,3},{8,12},{12,8},{9,1... | collective-permute-start | bytes 4423688 | tf_op jit(solution)/shard_map/ppermute | solution.py:532
  159.3 59.7 %collective-permute-start.30 = (bf16[384,1920]{1,0:T(8,128)(2,1)}, bf16[384,1920]{1,0:T(8,128)(2,1)}, u32[]{:S(2)}, u32[]{:S(2)}) collective-permute-start(bf16[384,1920]{1,0:T(8,128)(2,1)} %collective-permute-done.29.refs_5_), channel_id=1, source_target_pairs={{0,2},{2,0},{1,3},{3,1},{4,6},{6,4},{5,7},{7,5},{8,10},{10,8},{9,1... | collective-permute-start | bytes 4423688 | tf_op jit(solution)/shard_map/ppermute | solution.py:529
  166.8 59.3 %collective-permute-start.31 = (bf16[512,1536]{1,0:T(8,128)(2,1)}, bf16[512,1536]{1,0:T(8,128)(2,1)}, u32[]{:S(2)}, u32[]{:S(2)}) collective-permute-start(bf16[512,1536]{1,0:T(8,128)(2,1)} %fusion.277), channel_id=1, source_target_pairs={{0,1},{1,0},{2,3},{3,2},{4,5},{5,4},{6,7},{7,6},{8,9},{9,8},{10,11... | collective-permute-start | bytes 4718600 | tf_op jit(solution)/shard_map/ppermute | solution.py:535
  219.0 89.0 %collective-permute-start.33 = (bf16[2,384,1536]{2,1,0:T(8,128)(2,1)}, bf16[2,384,1536]{2,1,0:T(8,128)(2,1)}, u32[]{:S(2)}, u32[]{:S(2)}) collective-permute-start(bf16[2,384,1536]{2,1,0:T(8,128)(2,1)} %get-tuple-element.359), channel_id=1, source_target_pairs={{0,4},{4,0},{1,5},{5,1},{2,6},{6,2},{3,7},{7,3},{8,12},{12,8},{9,1... | collective-permute-start | bytes 7077896 | tf_op jit(solution)/shard_map/ppermute | solution.py:532
  220.5 87.5 %collective-permute-start.34 = (bf16[2,384,1536]{2,1,0:T(8,128)(2,1)}, bf16[2,384,1536]{2,1,0:T(8,128)(2,1)}, u32[]{:S(2)}, u32[]{:S(2)}) collective-permute-start(bf16[2,384,1536]{2,1,0:T(8,128)(2,1)} %get-tuple-element.360), channel_id=1, source_target_pairs={{0,2},{2,0},{1,3},{3,1},{4,6},{6,4},{5,7},{7,5},{8,10},{10,8},{9,1... | collective-permute-start | bytes 7077896 | tf_op jit(solution)/shard_map/ppermute | solution.py:529
  242.2 5.2 collective-permute-start
  308.0 54.5 %collective-permute-start.35 = (bf16[2,384,1536]{2,1,0:T(8,128)(2,1)}, bf16[2,384,1536]{2,1,0:T(8,128)(2,1)}, u32[]{:S(2)}, u32[]{:S(2)}) collective-permute-start(bf16[2,384,1536]{2,1,0:T(8,128)(2,1)} %get-tuple-element.365), channel_id=1, source_target_pairs={{0,4},{4,0},{1,5},{5,1},{2,6},{6,2},{3,7},{7,3},{8,12},{12,8},{9,1... | collective-permute-start | bytes 7077896 | tf_op jit(solution)/shard_map/ppermute | solution.py:532
  308.6 54.4 %collective-permute-start.36 = (bf16[2,384,1536]{2,1,0:T(8,128)(2,1)}, bf16[2,384,1536]{2,1,0:T(8,128)(2,1)}, u32[]{:S(2)}, u32[]{:S(2)}) collective-permute-start(bf16[2,384,1536]{2,1,0:T(8,128)(2,1)} %get-tuple-element.366), channel_id=1, source_target_pairs={{0,2},{2,0},{1,3},{3,1},{4,6},{6,4},{5,7},{7,5},{8,10},{10,8},{9,1... | collective-permute-start | bytes 7077896 | tf_op jit(solution)/shard_map/ppermute | solution.py:529
  343.4 76.9 %collective-permute-start.37 = (bf16[768,1536]{1,0:T(8,128)(2,1)}, bf16[768,1536]{1,0:T(8,128)(2,1)}, u32[]{:S(2)}, u32[]{:S(2)}) collective-permute-start(bf16[768,1536]{1,0:T(8,128)(2,1)} %convolution_convert_fusion.12), channel_id=1, source_target_pairs={{0,4},{4,0},{1,5},{5,1},{2,6},{6,2},{3,7},{7,3},{8,12},{12,8},{9,1... | collective-permute-start | bytes 7077896 | tf_op jit(solution)/shard_map/ppermute | solution.py:532
  348.8 71.4 %collective-permute-start.38 = (bf16[768,1536]{1,0:T(8,128)(2,1)}, bf16[768,1536]{1,0:T(8,128)(2,1)}, u32[]{:S(2)}, u32[]{:S(2)}) collective-permute-start(bf16[768,1536]{1,0:T(8,128)(2,1)} %convolution_convert_fusion.11), channel_id=1, source_target_pairs={{0,2},{2,0},{1,3},{3,1},{4,6},{6,4},{5,7},{7,5},{8,10},{10,8},{9,1... | collective-permute-start | bytes 7077896 | tf_op jit(solution)/shard_map/ppermute | solution.py:529
  397.9 14.1 %collective-permute-start.7 = (bf16[512,1536]{1,0:T(8,128)(2,1)S(1)}, bf16[512,1536]{1,0:T(8,128)(2,1)S(1)}, u32[]{:S(2)}, u32[]{:S(2)}) collective-permute-start(bf16[512,1536]{1,0:T(8,128)(2,1)S(1)} %fusion.9), channel_id=1, source_target_pairs={{0,1},{1,0},{2,3},{3,2},{4,5},{5,4},{6,7},{7,6},{8,9},{9,8},{10,11... | collective-permute-start | bytes 4718600 | tf_op jit(solution)/shard_map/cond/branch_1_fun/ppermute | solution.py:535
  446.0 203.4 %reduce-scatter.8.cloned.1.call-start = ((), (), s32[]{:S(2)}) async-start(), calls=%async_computation.10 | async-start | bytes 2949120 | tf_op jit(solution)/shard_map/reduce_scatter | solution.py:657
  450.8 57.1 %collective-permute-start.39 = (bf16[768,1536]{1,0:T(8,128)(2,1)}, bf16[768,1536]{1,0:T(8,128)(2,1)}, u32[]{:S(2)}, u32[]{:S(2)}) collective-permute-start(bf16[768,1536]{1,0:T(8,128)(2,1)} %copy.102), channel_id=1, source_target_pairs={{0,4},{4,0},{1,5},{5,1},{2,6},{6,2},{3,7},{7,3},{8,12},{12,8},{9,1... | collective-permute-start | bytes 7077896 | tf_op jit(solution)/shard_map/ppermute | solution.py:532
  452.3 55.6 %collective-permute-start.40 = (bf16[768,1536]{1,0:T(8,128)(2,1)}, bf16[768,1536]{1,0:T(8,128)(2,1)}, u32[]{:S(2)}, u32[]{:S(2)}) collective-permute-start(bf16[768,1536]{1,0:T(8,128)(2,1)} %get-tuple-element.382), channel_id=1, source_target_pairs={{0,2},{2,0},{1,3},{3,1},{4,6},{6,4},{5,7},{7,5},{8,10},{10,8},{9,1... | collective-permute-start | bytes 7077896 | tf_op jit(solution)/shard_map/ppermute | solution.py:529
  453.0 8.9 %collective-permute-start.4 = (bf16[512,1536]{1,0:T(8,128)(2,1)}, bf16[512,1536]{1,0:T(8,128)(2,1)}, u32[]{:S(2)}, u32[]{:S(2)}) collective-permute-start(bf16[512,1536]{1,0:T(8,128)(2,1)} %get-tuple-element.194), channel_id=1, source_target_pairs={{0,1},{1,0},{2,3},{3,2},{4,5},{5,4},{6,7},{7,6},{8,9},{9,8},{10,11... | collective-permute-start | bytes 4718600 | tf_op jit(solution)/shard_map/cond/branch_1_fun/ppermute | solution.py:535
  505.9 54.4 %collective-permute-start.41 = (bf16[768,1536]{0,1:T(8,128)(2,1)}, bf16[768,1536]{0,1:T(8,128)(2,1)}, u32[]{:S(2)}, u32[]{:S(2)}) collective-permute-start(bf16[768,1536]{0,1:T(8,128)(2,1)} %get-tuple-element.390), channel_id=1, source_target_pairs={{0,4},{4,0},{1,5},{5,1},{2,6},{6,2},{3,7},{7,3},{8,12},{12,8},{9,1... | collective-permute-start | bytes 7077896 | tf_op jit(solution)/shard_map/ppermute | solution.py:532
  506.5 54.4 %collective-permute-start.42 = (bf16[768,1536]{0,1:T(8,128)(2,1)}, bf16[768,1536]{0,1:T(8,128)(2,1)}, u32[]{:S(2)}, u32[]{:S(2)}) collective-permute-start(bf16[768,1536]{0,1:T(8,128)(2,1)} %get-tuple-element.391), channel_id=1, source_target_pairs={{0,2},{2,0},{1,3},{3,1},{4,6},{6,4},{5,7},{7,5},{8,10},{10,8},{9,1... | collective-permute-start | bytes 7077896 | tf_op jit(solution)/shard_map/ppermute | solution.py:529
  527.5 17.4 %collective-permute-start.6 = (bf16[512,1536]{1,0:T(8,128)(2,1)}, bf16[512,1536]{1,0:T(8,128)(2,1)}, u32[]{:S(2)}, u32[]{:S(2)}) collective-permute-start(bf16[512,1536]{1,0:T(8,128)(2,1)} %get-tuple-element.736), channel_id=1, source_target_pairs={{0,1},{1,0},{2,3},{3,2},{4,5},{5,4},{6,7},{7,6},{8,9},{9,8},{10,11... | collective-permute-start | bytes 4718600 | tf_op jit(solution)/shard_map/cond/branch_1_fun/ppermute | solution.py:535
  555.0 35.0 %collective-permute-start.43 = (bf16[384,1536]{1,0:T(8,128)(2,1)}, bf16[384,1536]{1,0:T(8,128)(2,1)}, u32[]{:S(2)}, u32[]{:S(2)}) collective-permute-start(bf16[384,1536]{1,0:T(8,128)(2,1)} %get-tuple-element.395), channel_id=1, source_target_pairs={{0,2},{2,0},{1,3},{3,1},{4,6},{6,4},{5,7},{7,5},{8,10},{10,8},{9,1... | collective-permute-start | bytes 3538952 | tf_op jit(solution)/shard_map/ppermute | solution.py:529
  555.7 34.3 %collective-permute-start.44 = (bf16[384,1536]{1,0:T(8,128)(2,1)}, bf16[384,1536]{1,0:T(8,128)(2,1)}, u32[]{:S(2)}, u32[]{:S(2)}) collective-permute-start(bf16[384,1536]{1,0:T(8,128)(2,1)} %get-tuple-element.397), channel_id=1, source_target_pairs={{0,4},{4,0},{1,5},{5,1},{2,6},{6,2},{3,7},{7,3},{8,12},{12,8},{9,1... | collective-permute-start | bytes 3538952 | tf_op jit(solution)/shard_map/ppermute | solution.py:532
  594.6 120.9 %reduce-scatter.10.cloned.1.call-start = ((), (), s32[]{:S(2)}) async-start(), calls=%async_computation.11 | async-start | bytes 2949120 | tf_op jit(solution)/shard_map/reduce_scatter | solution.py:657
  597.4 52.0 %collective-permute-start.47 = (bf16[384,1536]{1,0:T(8,128)(2,1)}, bf16[384,1536]{1,0:T(8,128)(2,1)}, u32[]{:S(2)}, u32[]{:S(2)}) collective-permute-start(bf16[384,1536]{1,0:T(8,128)(2,1)} %copy.106), channel_id=1, source_target_pairs={{0,2},{2,0},{1,3},{3,1},{4,6},{6,4},{5,7},{7,5},{8,10},{10,8},{9,1... | collective-permute-start | bytes 3538952 | tf_op jit(solution)/shard_map/ppermute | solution.py:529
  601.1 48.3 %collective-permute-start.48 = (bf16[384,1536]{1,0:T(8,128)(2,1)}, bf16[384,1536]{1,0:T(8,128)(2,1)}, u32[]{:S(2)}, u32[]{:S(2)}) collective-permute-start(bf16[384,1536]{1,0:T(8,128)(2,1)} %copy.107), channel_id=1, source_target_pairs={{0,4},{4,0},{1,5},{5,1},{2,6},{6,2},{3,7},{7,3},{8,12},{12,8},{9,1... | collective-permute-start | bytes 3538952 | tf_op jit(solution)/shard_map/ppermute | solution.py:532
  602.5 46.9 %collective-permute-start.45 = (bf16[768,384]{1,0:T(8,128)(2,1)}, bf16[768,384]{1,0:T(8,128)(2,1)}, u32[]{:S(2)}, u32[]{:S(2)}) collective-permute-start(bf16[768,384]{1,0:T(8,128)(2,1)} %get-tuple-element.400), channel_id=1, source_target_pairs={{0,4},{4,0},{1,5},{5,1},{2,6},{6,2},{3,7},{7,3},{8,12},{12,8},{9,1... | collective-permute-start | bytes 1769480 | tf_op jit(solution)/shard_map/ppermute | solution.py:532
  603.1 46.2 %collective-permute-start.46 = (bf16[768,384]{1,0:T(8,128)(2,1)}, bf16[768,384]{1,0:T(8,128)(2,1)}, u32[]{:S(2)}, u32[]{:S(2)}) collective-permute-start(bf16[768,384]{1,0:T(8,128)(2,1)} %get-tuple-element.401), channel_id=1, source_target_pairs={{0,2},{2,0},{1,3},{3,1},{4,6},{6,4},{5,7},{7,5},{8,10},{10,8},{9,1... | collective-permute-start | bytes 1769480 | tf_op jit(solution)/shard_map/ppermute | solution.py:529
  659.4 104.4 %reduce-scatter.12.cloned.1.call-start = ((), (), s32[]{:S(2)}) async-start(), calls=%async_computation.12 | async-start | bytes 737280 | tf_op jit(solution)/shard_map/reduce_scatter | solution.py:657
  663.3 52.1 %collective-permute-start.49 = (bf16[768,1152]{1,0:T(8,128)(2,1)}, bf16[768,1152]{1,0:T(8,128)(2,1)}, u32[]{:S(2)}, u32[]{:S(2)}) collective-permute-start(bf16[768,1152]{1,0:T(8,128)(2,1)} %copy.108), channel_id=1, source_target_pairs={{0,4},{4,0},{1,5},{5,1},{2,6},{6,2},{3,7},{7,3},{8,12},{12,8},{9,1... | collective-permute-start | bytes 5308424 | tf_op jit(solution)/shard_map/ppermute | solution.py:532
  664.7 50.7 %collective-permute-start.50 = (bf16[768,1152]{1,0:T(8,128)(2,1)}, bf16[768,1152]{1,0:T(8,128)(2,1)}, u32[]{:S(2)}, u32[]{:S(2)}) collective-permute-start(bf16[768,1152]{1,0:T(8,128)(2,1)} %get-tuple-element.428), channel_id=1, source_target_pairs={{0,2},{2,0},{1,3},{3,1},{4,6},{6,4},{5,7},{7,5},{8,10},{10,8},{9,1... | collective-permute-start | bytes 5308424 | tf_op jit(solution)/shard_map/ppermute | solution.py:529
  673.9 20.3 %collective-permute-start.9 = (bf16[128,1536]{1,0:T(8,128)(2,1)}, bf16[128,1536]{1,0:T(8,128)(2,1)}, u32[]{:S(2)}, u32[]{:S(2)}) collective-permute-start(bf16[128,1536]{1,0:T(8,128)(2,1)} %get-tuple-element.780), channel_id=1, source_target_pairs={{0,1},{1,0},{2,3},{3,2},{4,5},{5,4},{6,7},{7,6},{8,9},{9,8},{10,11... | collective-permute-start | bytes 1179656 | tf_op jit(solution)/shard_map/cond/branch_1_fun/ppermute | solution.py:535
  683.1 18.3 %collective-permute-start.10 = (bf16[512,1536]{1,0:T(8,128)(2,1)}, bf16[512,1536]{1,0:T(8,128)(2,1)}, u32[]{:S(2)}, u32[]{:S(2)}) collective-permute-start(bf16[512,1536]{1,0:T(8,128)(2,1)} %fusion.148), channel_id=1, source_target_pairs={{0,1},{1,0},{2,3},{3,2},{4,5},{5,4},{6,7},{7,6},{8,9},{9,8},{10,11... | collective-permute-start | bytes 4718600 | tf_op jit(solution)/shard_map/cond/branch_1_fun/ppermute | solution.py:535
  715.5 10.2 %collective-permute-start.51 = (bf16[384,384]{1,0:T(8,128)(2,1)}, bf16[384,384]{1,0:T(8,128)(2,1)S(1)}, u32[]{:S(2)}, u32[]{:S(2)}) collective-permute-start(bf16[384,384]{1,0:T(8,128)(2,1)} %get-tuple-element.434), channel_id=1, source_target_pairs={{0,2},{2,0},{1,3},{3,1},{4,6},{6,4},{5,7},{7,5},{8,10},{10,8},{9,1... | collective-permute-start | bytes 884744 | tf_op jit(solution)/shard_map/ppermute | solution.py:529
  716.3 10.1 %collective-permute-start.52 = (bf16[384,384]{1,0:T(8,128)(2,1)}, bf16[384,384]{1,0:T(8,128)(2,1)S(1)}, u32[]{:S(2)}, u32[]{:S(2)}) collective-permute-start(bf16[384,384]{1,0:T(8,128)(2,1)} %get-tuple-element.435), channel_id=1, source_target_pairs={{0,4},{4,0},{1,5},{5,1},{2,6},{6,2},{3,7},{7,3},{8,12},{12,8},{9,1... | collective-permute-start | bytes 884744 | tf_op jit(solution)/shard_map/ppermute | solution.py:532
  719.3 41.9 %collective-permute-start.60 = (bf16[96,1536]{1,0:T(8,128)(2,1)}, bf16[96,1536]{1,0:T(8,128)(2,1)}, u32[]{:S(2)}, u32[]{:S(2)}) collective-permute-start(bf16[96,1536]{1,0:T(8,128)(2,1)} %get-tuple-element.831), channel_id=1, source_target_pairs={{0,2},{2,0},{1,3},{3,1},{4,6},{6,4},{5,7},{7,5},{8,10},{10,8},{9,1... | collective-permute-start | bytes 884744 | tf_op jit(solution)/shard_map/ppermute | solution.py:529
  720.4 40.9 %collective-permute-start.61 = (bf16[96,1536]{1,0:T(8,128)(2,1)}, bf16[96,1536]{1,0:T(8,128)(2,1)}, u32[]{:S(2)}, u32[]{:S(2)}) collective-permute-start(bf16[96,1536]{1,0:T(8,128)(2,1)} %get-tuple-element.832), channel_id=1, source_target_pairs={{0,4},{4,0},{1,5},{5,1},{2,6},{6,2},{3,7},{7,3},{8,12},{12,8},{9,1... | collective-permute-start | bytes 884744 | tf_op jit(solution)/shard_map/ppermute | solution.py:532
  734.8 75.8 %reduce-scatter.14.cloned.1.call-start = ((), (), s32[]{:S(2)}) async-start(), calls=%async_computation.13 | async-start | bytes 2211840 | tf_op jit(solution)/shard_map/reduce_scatter | solution.py:657
  740.6 23.2 %collective-permute-start.53 = (bf16[384,1152]{1,0:T(8,128)(2,1)}, bf16[384,1152]{1,0:T(8,128)(2,1)}, u32[]{:S(2)}, u32[]{:S(2)}) collective-permute-start(bf16[384,1152]{1,0:T(8,128)(2,1)} %get-tuple-element.825), channel_id=1, source_target_pairs={{0,2},{2,0},{1,3},{3,1},{4,6},{6,4},{5,7},{7,5},{8,10},{10,8},{9,1... | collective-permute-start | bytes 2654216 | tf_op jit(solution)/shard_map/ppermute | solution.py:529
  741.8 21.9 %collective-permute-start.54 = (bf16[384,1152]{1,0:T(8,128)(2,1)}, bf16[384,1152]{1,0:T(8,128)(2,1)}, u32[]{:S(2)}, u32[]{:S(2)}) collective-permute-start(bf16[384,1152]{1,0:T(8,128)(2,1)} %get-tuple-element.823), channel_id=1, source_target_pairs={{0,4},{4,0},{1,5},{5,1},{2,6},{6,2},{3,7},{7,3},{8,12},{12,8},{9,1... | collective-permute-start | bytes 2654216 | tf_op jit(solution)/shard_map/ppermute | solution.py:532
  777.5 8.5 %collective-permute-start.56 = (bf16[768,128]{0,1:T(8,128)(2,1)S(1)}, bf16[768,128]{0,1:T(8,128)(2,1)S(1)}, u32[]{:S(2)}, u32[]{:S(2)}) collective-permute-start(bf16[768,128]{0,1:T(8,128)(2,1)S(1)} %slice.864), channel_id=1, source_target_pairs={{0,4},{4,0},{1,5},{5,1},{2,6},{6,2},{3,7},{7,3},{8,12},{12,8},{9,1... | collective-permute-start | bytes 589832 | tf_op jit(solution)/shard_map/ppermute | solution.py:532
  786.1 8.5 %collective-permute-start.57 = (bf16[384,128]{0,1:T(8,128)(2,1)S(1)}, bf16[384,128]{0,1:T(8,128)(2,1)S(1)}, u32[]{:S(2)}, u32[]{:S(2)}) collective-permute-start(bf16[384,128]{0,1:T(8,128)(2,1)S(1)} %slice.865), channel_id=1, source_target_pairs={{0,2},{2,0},{1,3},{3,1},{4,6},{6,4},{5,7},{7,5},{8,10},{10,8},{9,1... | collective-permute-start | bytes 294920 | tf_op jit(solution)/shard_map/ppermute | solution.py:529
  794.7 10.9 %collective-permute-start.58 = (bf16[192,128]{0,1:T(8,128)(2,1)S(1)}, bf16[192,128]{0,1:T(8,128)(2,1)S(1)}, u32[]{:S(2)}, u32[]{:S(2)}) collective-permute-start(bf16[192,128]{0,1:T(8,128)(2,1)S(1)} %dynamic-slice_convert_fusion), channel_id=1, source_target_pairs={{0,16},{8,24},{16,0},{24,8},{1,17},{9,25},{17,1},{25,9},{2,18},{10... | collective-permute-start | bytes 147464 | tf_op jit(solution)/shard_map/ppermute | solution.py:687
  (73 other events, 1071.3 us)
Sparse Core Ops, SparseCore 0:
  10.2 45.0 all-gather.6
  57.4 58.9 all-gather.4
  118.6 88.0 all-gather.8
  208.7 87.7 all-gather.10
  446.2 83.9 reduce-scatter.5
  594.7 47.1 reduce-scatter.7
  659.5 47.1 reduce-scatter.9
  734.9 20.9 reduce-scatter.11
  768.5 38.6 reduce-scatter.13
